TPU v7x, 256 devices: a whole 4x4x8 slice. The times are simulated.
256 devices in a mesh: rows: 64 (over y, z, core), feat: 4 (over x).
Axes of the slice: x: 4, y: 4, z: 8, core: 2. Of those that a mesh axis runs over, the one named last changes fastest.
Arguments:
- feats: bfloat16 [256, 131072], P('feat', 'rows'), may hold values from -6 to 6
- weight: bfloat16 [256, 256], P('feat'), may hold values from -0.375 to 0.375
- bias: float32 [256], P('feat'), may hold values from -3 to 3
- tile_cols: int32 [8192], P('rows'), may hold values from 0 to 1023, as said below
- tile_values: bfloat16 [8192, 128, 128], P('rows'), may hold values from -0.1875 to 0.1875
- cotangent: bfloat16 [256, 131072], P('feat', 'rows'), may hold values from -6 to 6
Outputs:
- hidden_out: bfloat16 [256, 131072], P('feat', 'rows')
- grad_input: float32 [256, 131072], P('feat', 'rows')
- grad_weight: float32 [256, 256], P('feat')
- grad_bias: float32 [256], P('feat')
Inputs may be any that keep to these rules, and one draw needn't show every extreme that they name: `tile_cols`: column blocks of tiles. In each row block the first 4 tiles have column blocks on the same index of rows as the row block (index = column block // 16). Of the other tiles of one index of rows, at most 2 have column blocks on any one index, and in every draw one index receives exactly 2 such tiles from every index.
All inputs are finite; a program needn't handle non-finite values.
Results may differ from a plain program's by a relative error of at most 0.0058.
Values may be sent and summed in bfloat16 or wider, within the bound.
No kernel may reach another device: no remote copies, remote signals or barrier semaphores. Data moves between devices by JAX's collectives and lax.ppermute only.
A program may use at most 128 MiB of HBM per device.

v0:
```python
import math

import jax
import jax.numpy as jnp
from jax import lax
from jax.sharding import PartitionSpec as P

TL = 4


def local(feats, weight, bias, tile_cols, tile_values, cotangent):
    hid_dev = weight.shape[1] // lax.axis_size("feat")
    nodes_dev = feats.shape[1]
    block = tile_values.shape[1]
    row_blocks = nodes_dev // block
    peers = lax.axis_size("rows")
    tiles_dev = tile_cols.shape[0]
    per_block = tiles_dev // row_blocks
    remote_count = row_blocks * (per_block - TL)
    capacity = 2 * remote_count // peers
    num_slots = peers * capacity
    columns = weight
    mixed = lax.psum_scatter(
        lax.dot_general(
            columns, feats, (((0,), (0,)), ((), ())), preferred_element_type=jnp.float32
        ),
        "feat",
        scatter_dimension=0,
        tiled=True,
    )
    proj = mixed.astype(jnp.bfloat16)
    grid = tile_cols.reshape(row_blocks, per_block)
    tiles = tile_values.reshape(row_blocks, per_block, block, block)
    local_tiles = tiles[:, :TL]
    remote_tiles = tiles[:, TL:]
    local_cols = grid[:, :TL] % row_blocks
    remote_cols = grid[:, TL:].reshape(-1)
    remote_owner = remote_cols // row_blocks
    remote_local = remote_cols % row_blocks
    owner_onehot = (remote_owner[:, None] == jnp.arange(peers)[None, :]).astype(jnp.int32)
    before = jnp.cumsum(owner_onehot, axis=0) - owner_onehot
    ranks = jnp.sum(before * owner_onehot, axis=1)
    slots = remote_owner * capacity + ranks
    request = jnp.full((num_slots,), -1, jnp.int32).at[slots].set(remote_local)
    slot_tile = (
        jnp.full((num_slots,), -1, jnp.int32)
        .at[slots]
        .set(jnp.arange(remote_count, dtype=jnp.int32))
    )
    wanted = lax.all_to_all(
        request.reshape(peers, capacity), "rows", split_axis=0, concat_axis=0, tiled=True
    ).reshape(-1)
    gathered = lax.all_gather(proj, "rows", axis=1, tiled=True)
    gathered = gathered.reshape(hid_dev, -1, block)
    fetched = jnp.take(gathered, tile_cols, axis=1).reshape(hid_dev, row_blocks, per_block, block)
    local_part = jnp.einsum(
        "fbtk,btnk->bfn", fetched[:, :, :TL], local_tiles, preferred_element_type=jnp.float32
    )
    remote_part = jnp.einsum(
        "fbtk,btnk->bfn", fetched[:, :, TL:], remote_tiles, preferred_element_type=jnp.float32
    )
    summed = local_part + remote_part
    pre = summed.transpose(1, 0, 2).reshape(hid_dev, nodes_dev) + bias[:, None]
    hidden_out = jax.nn.silu(pre).astype(jnp.bfloat16)
    sigma = jax.nn.sigmoid(pre)
    grad_pre = cotangent.astype(jnp.float32) * (sigma * (1.0 + pre * (1.0 - sigma)))
    bias_part = jnp.sum(grad_pre, axis=1)
    grad_blocks = (
        grad_pre.astype(jnp.bfloat16).reshape(hid_dev, row_blocks, block).transpose(1, 0, 2)
    )
    local_back = jnp.einsum(
        "bfn,btnk->btfk", grad_blocks, local_tiles, preferred_element_type=jnp.float32
    )
    local_onehot = (local_cols[:, :, None] == jnp.arange(row_blocks)[None, None, :]).astype(
        jnp.float32
    )
    grad_proj_blocks = jnp.einsum(
        "bts,btfk->sfk", local_onehot, local_back, precision=lax.Precision.HIGHEST
    )
    remote_back = jnp.einsum(
        "bfn,btnk->btfk", grad_blocks, remote_tiles, preferred_element_type=jnp.float32
    )
    remote_back = remote_back.reshape(remote_count, hid_dev, block)
    filled = (slot_tile >= 0).astype(jnp.float32)
    outgoing_back = remote_back[jnp.maximum(slot_tile, 0)] * filled[:, None, None]
    outgoing_back = outgoing_back.reshape(peers, capacity, hid_dev, block)
    returned = lax.all_to_all(
        outgoing_back, "rows", split_axis=0, concat_axis=0, tiled=True
    ).reshape(num_slots, hid_dev, block)
    wanted_onehot = (wanted[:, None] == jnp.arange(row_blocks)[None, :]).astype(jnp.float32)
    grad_proj_blocks = grad_proj_blocks + jnp.einsum(
        "sb,sfk->bfk", wanted_onehot, returned, precision=lax.Precision.HIGHEST
    )
    grad_proj = grad_proj_blocks.transpose(1, 0, 2).reshape(hid_dev, nodes_dev).astype(jnp.bfloat16)
    piece = lax.all_gather(grad_proj, "feat", axis=0, tiled=True)
    columns = weight
    input_grad = jnp.dot(columns, piece, preferred_element_type=jnp.float32)
    partial_rows = lax.dot_general(
        feats, piece, (((1,), (1,)), ((), ())), preferred_element_type=jnp.float32
    )
    weight_total, bias_total = lax.psum((partial_rows, bias_part), "rows")
    divisor = math.sqrt(nodes_dev * peers)
    return (hidden_out, input_grad, weight_total / divisor, bias_total / divisor)


def solution(mesh):
    placed = (
        P("feat", "rows"),
        P("feat", None),
        P("feat"),
        P("rows"),
        P("rows", None, None),
        P("feat", "rows"),
    )
    return jax.shard_map(
        local,
        mesh=mesh,
        in_specs=placed,
        out_specs=(P("feat", "rows"), P("feat", "rows"), P("feat", None), P("feat")),
        check_vma=False,
    )
```

profile of v0, /device:TPU:1, one launch (start us, length us, event | category | flops | bytes accessed | tf_op | source)
XLA Modules:
  0.0 594.8 jit_solution(7321926682911000968)
XLA Ops:
  7.2 0.9 copy-done
  8.1 2.6 fusion.50
  10.8 36.1 %reduce-scatter.2.cloned.1.call-done = f32[64,2048]{1,0:T(8,128)} async-done(((f32[256,2048]{1,0:T(8,128)}), f32[64,2048]{1,0:T(8,128)}) %reduce-scatter.2.cloned.1.call-update) | async-done | bytes 524304 | tf_op jit(solution)/shard_map/reduce_scatter | solution.py:23
  46.9 1.8 convert_element_type.27
  49.4 0.8 scatter_custom_fusion
  50.2 0.8 all_to_all.9
  51.0 10.6 %all-to-all-start = ((s32[64,1,2]{2,1,0:T(1,128)}), s32[64,1,2]{2,1,0:T(1,128)S(1)}, u32[]{:S(2)}, u32[]{:S(2)}) async-start(s32[64,1,2]{2,1,0:T(1,128)} %bitcast.17), calls=%async_computation.1 | async-start | bytes 65536 | tf_op jit(solution)/shard_map/all_to_all | solution.py:50
  61.7 0.8 scatter_custom_fusion.1
  62.7 88.0 %all-gather.3.cloned.1.call-done = bf16[64,131072]{1,0:T(8,128)(2,1)} async-done(((bf16[64,2048]{1,0:T(8,128)(2,1)}), bf16[64,131072]{1,0:T(8,128)(2,1)}) %all-gather.3.cloned.1.call-update) | async-done | bytes 16777232 | tf_op jit(solution)/shard_map/all_gather | solution.py:53
  150.8 15.3 %copy_bitcast_fusion = bf16[64,1024,128]{2,0,1:T(8,128)(2,1)} fusion(bf16[64,131072]{1,0:T(8,128)(2,1)} %all-gather.3.cloned.1.call-done), kind=kLoop, calls=%fused_computation.4 | loop fusion | bytes 33554432 | tf_op jit(solution)/shard_map/reshape | solution.py:54
  166.0 6.7 %gather_fusion = bf16[128,64,128]{2,1,0:T(8,128)(2,1)S(1)} fusion(bf16[64,1024,128]{2,0,1:T(8,128)(2,1)} %copy_bitcast_fusion, s32[1024]{0:T(1024)S(1)} %pad_clamp_fusion.1), kind=kCustom, calls=%fused_computation | custom fusion | bytes 4194816 | tf_op jit(solution)/shard_map/jit(_take)/gather | solution.py:55
  172.8 2.6 fusion.16
  175.6 0.9 fusion.25
  176.5 1.1 fusion.48
  178.1 2.8 gather_fusion.1
  180.9 2.5 broadcast_multiply_fusion
  183.4 5.8 copy.32
  189.2 6.2 %all-to-all-start.1 = ((f32[64,2,64,128]{3,1,2,0:T(2,128)}), f32[64,2,64,128]{3,1,2,0:T(2,128)}, u32[]{:S(2)}, u32[]{:S(2)}) async-start(f32[64,2,64,128]{3,1,2,0:T(2,128)} %copy.32), calls=%async_computation.2 | async-start | bytes 8388608 | tf_op jit(solution)/shard_map/all_to_all | solution.py:87
  195.7 0.5 broadcast.163
  196.2 0.7 reduce.3
  197.1 2.0 fusion.10
  199.1 2.3 fusion.13
  201.4 89.9 %all-to-all-done.1 = f32[64,2,64,128]{3,1,2,0:T(2,128)} async-done(((f32[64,2,64,128]{3,1,2,0:T(2,128)}), f32[64,2,64,128]{3,1,2,0:T(2,128)}, u32[]{:S(2)}, u32[]{:S(2)}) %all-to-all-start.1) | async-done | bytes 4194336 | tf_op jit(solution)/shard_map/all_to_all | solution.py:87
  291.3 4.5 copy.33
  295.8 1.5 fusion.28
  297.3 0.8 copy.62
  298.2 123.7 %psum.15 = f32[64]{0:T(128)S(1)} all-reduce(f32[64]{0:T(128)S(1)} %get-tuple-element.4), channel_id=1, replica_groups=mesh['rows'=64,'feat'=4] {'rows'}, use_global_device_ids=true, to_apply=%region_7.8 | all-reduce | flops 64 | bytes 512 | tf_op jit(solution)/shard_map/psum | solution.py:101
  421.9 0.5 broadcast_multiply_fusion.2
  422.4 2.3 convolution_bitcast_fusion.1
  424.8 2.3 convolution_bitcast_fusion
  427.1 159.7 %all-reduce.2.cloned.1.call-done = f32[64,256]{1,0:T(8,128)} async-done(((f32[64,256]{1,0:T(8,128)}), f32[64,256]{1,0:T(8,128)}) %all-reduce.2.cloned.1.call-update) | async-done | bytes 65552 | tf_op jit(solution)/shard_map/psum | solution.py:101
  586.8 1.5 broadcast_multiply_fusion.1
  (42 shorter events, 2.3 us)
Async XLA Ops:
  7.2 1.0 copy-start
  7.2 39.7 %reduce-scatter.2.cloned.1.call-start = ((), (), s32[]{:S(2)}) async-start(), calls=%async_computation.3 | async-start | bytes 2621440 | tf_op jit(solution)/shard_map/reduce_scatter | solution.py:23
  10.7 38.0 %copy-start.5 = (s32[128]{0:T(128)S(1)}, s32[128]{0:T(128)}, u32[]{:S(2)}) copy-start(s32[128]{0:T(128)} %param.9) | copy-start | bytes 1540
  10.7 140.0 %all-gather.3.cloned.1.call-start = ((), (), s32[]{:S(2)}) async-start(), calls=%async_computation.4 | async-start | bytes 17039360 | tf_op jit(solution)/shard_map/all_gather | solution.py:53
  51.0 138.2 %all-to-all-start = ((s32[64,1,2]{2,1,0:T(1,128)}), s32[64,1,2]{2,1,0:T(1,128)S(1)}, u32[]{:S(2)}, u32[]{:S(2)}) async-start(s32[64,1,2]{2,1,0:T(1,128)} %bitcast.17), calls=%async_computation.1 | async-start | bytes 65536 | tf_op jit(solution)/shard_map/all_to_all | solution.py:50
  172.8 2.8 copy-start.1
  175.6 0.9 copy-start.2
  175.6 1.0 copy-start.4
  189.2 102.1 %all-to-all-start.1 = ((f32[64,2,64,128]{3,1,2,0:T(2,128)}), f32[64,2,64,128]{3,1,2,0:T(2,128)}, u32[]{:S(2)}, u32[]{:S(2)}) async-start(f32[64,2,64,128]{3,1,2,0:T(2,128)} %copy.32), calls=%async_computation.2 | async-start | bytes 8388608 | tf_op jit(solution)/shard_map/all_to_all | solution.py:87
  195.4 227.0 %all-gather.5.cloned.1.call-start = ((), (), s32[]{:S(2)}) async-start(), calls=%async_computation.5 | async-start | bytes 1310720 | tf_op jit(solution)/shard_map/all_gather | solution.py:95
  297.3 127.4 %copy-start.3 = (bf16[64,256]{1,0:T(8,128)(2,1)S(1)}, bf16[64,256]{1,0:T(8,128)(2,1)}, u32[]{:S(2)}) copy-start(bf16[64,256]{1,0:T(8,128)(2,1)} %param.7) | copy-start | bytes 98308
  298.1 288.7 %all-reduce.2.cloned.1.call-start = ((), (), s32[]{:S(2)}) async-start(), calls=%async_computation.6 | async-start | bytes 131072 | tf_op jit(solution)/shard_map/psum | solution.py:101
Sparse Core Ops, SparseCore 0:
  10.8 36.0 reduce-scatter.1
  50.7 100.0 all-gather.2
  298.2 21.9 all-gather.4
  424.9 161.8 all-reduce.1
where the time goes:
time: 596 us; the launch traced here: 595 us
  waiting for transfers between devices  374 us (63%)
  blocking collectives  124 us (21%)
  local copies, waits for them, and re-layouts  40.5 us (7%)
  starting transfers between devices  17.1 us (3%)
  matrix products  17 us (3%)
  between operations  14 us (2%)
  other arithmetic  8.64 us (1%)
    psum x1, waiting for transfers between devices, local(): weight_total, bias_total = lax.psum((partial_rows, bias_part), 'rows')  160 us
    psum x1, blocking collectives, local(): weight_total, bias_total = lax.psum((partial_rows, bias_part), 'rows')  124 us
    all_to_all x1, waiting for transfers between devices, local(): lax.all_to_all(outgoing_back, 'rows', split_axis=0, concat_axis=0, tiled=...  89.9 us
    all_gather x1, waiting for transfers between devices, local(): gathered = lax.all_gather(proj, 'rows', axis=1, tiled=True)  88 us
    reduce_scatter x1, waiting for transfers between devices, local(): lax.psum_scatter(lax.dot_general(columns, feats, (((0,), (0,)), ((), ()))...  36.1 us
    reshape x1, local copies, waits for them, and re-layouts, local(): gathered = gathered.reshape(hid_dev, -1, block)  15.3 us
  transfers between devices with their start and end apart: 6, of which 4 were waited for; matrix products, arithmetic and copies ran while one was open for 8% of the time, Pallas kernels for 0%

commit v1 on v0

v1 whole, which is shorter than its diff:
```python
import math

import jax
import jax.numpy as jnp
from jax import lax
from jax.experimental import pallas as pl
from jax.experimental.pallas import tpu as pltpu
from jax.sharding import PartitionSpec as P

TL = 4
BF = jnp.bfloat16
F32 = jnp.float32
VMEM = pl.BlockSpec(memory_space=pltpu.VMEM)
SMEM = pl.BlockSpec(memory_space=pltpu.SMEM)


def lanes(index, width):
    return pl.ds(pl.multiple_of(index * width, width), width)


def pack_kernel(wanted_ref, feats_ref, out_ref):
    block = out_ref.shape[2]

    def body(s, carry):
        w = jnp.maximum(wanted_ref[s], 0)
        out_ref[s] = feats_ref[:, lanes(w, block)]
        return carry

    lax.fori_loop(0, out_ref.shape[0], body, 0, unroll=8)


def pack(wanted, feats, block):
    slots = wanted.shape[0]
    return pl.pallas_call(
        pack_kernel,
        out_shape=jax.ShapeDtypeStruct((slots, feats.shape[0], block), feats.dtype),
        in_specs=[SMEM, VMEM],
        out_specs=VMEM,
        name="pack",
    )(wanted, feats)


def dot(a, b, dims):
    return lax.dot_general(a, b, ((dims[:1], dims[1:]), ((), ())), preferred_element_type=F32)


STEP = 4


def agg_local_kernel(cols_ref, feats_ref, tiles_ref, out_ref):
    i = pl.program_id(0)
    count, block = tiles_ref.shape[1], tiles_ref.shape[2]
    for rr in range(STEP):
        acc = None
        for t in range(0, count, 2):
            base = (i * STEP + rr) * count + t
            lhs = jnp.concatenate(
                [feats_ref[:, lanes(cols_ref[base + k], block)] for k in range(2)], axis=1
            )
            rhs = jnp.concatenate([tiles_ref[rr, t + k] for k in range(2)], axis=1)
            term = dot(lhs, rhs, (1, 1))
            acc = term if acc is None else acc + term
        out_ref[:, rr * block : (rr + 1) * block] = acc


def agg_local(cols, feats, tiles):
    row_blocks, _, block, _ = tiles.shape
    width = feats.shape[0]
    return pl.pallas_call(
        agg_local_kernel,
        grid=(row_blocks // STEP,),
        out_shape=jax.ShapeDtypeStruct((width, row_blocks * block), F32),
        in_specs=[
            SMEM,
            pl.BlockSpec(feats.shape, lambda i: (0, 0)),
            pl.BlockSpec((STEP, TL, block, block), lambda i: (i, 0, 0, 0)),
        ],
        out_specs=pl.BlockSpec((width, STEP * block), lambda i: (0, i)),
        name="agg_local",
        cost_estimate=pl.CostEstimate(
            flops=2 * width * row_blocks * TL * block * block, bytes_accessed=3 << 20, transcendentals=0
        ),
    )(cols, feats, tiles)


def agg_remote_kernel(slots_ref, recv_ref, tiles_ref, local_ref, out_ref):
    i = pl.program_id(0)
    count, block = tiles_ref.shape[1], tiles_ref.shape[2]
    for rr in range(STEP):
        acc = local_ref[:, rr * block : (rr + 1) * block]
        for t in range(0, count, 2):
            base = (i * STEP + rr) * count + t
            lhs = jnp.concatenate([recv_ref[slots_ref[base + k]] for k in range(2)], axis=1)
            rhs = jnp.concatenate([tiles_ref[rr, t + k] for k in range(2)], axis=1)
            acc = acc + dot(lhs, rhs, (1, 1))
        out_ref[:, rr * block : (rr + 1) * block] = acc.astype(out_ref.dtype)


def agg_remote(slots, recv, tiles, local):
    row_blocks, per_block, block, _ = tiles.shape
    rem = per_block - TL
    width = local.shape[0]
    return pl.pallas_call(
        agg_remote_kernel,
        grid=(row_blocks // STEP,),
        out_shape=jax.ShapeDtypeStruct(local.shape, BF),
        in_specs=[
            SMEM,
            pl.BlockSpec(recv.shape, lambda i: (0, 0, 0)),
            pl.BlockSpec((STEP, rem, block, block), lambda i: (i, 1, 0, 0)),
            pl.BlockSpec((width, STEP * block), lambda i: (0, i)),
        ],
        out_specs=pl.BlockSpec((width, STEP * block), lambda i: (0, i)),
        name="agg_remote",
        cost_estimate=pl.CostEstimate(
            flops=2 * width * row_blocks * rem * block * block, bytes_accessed=5 << 20, transcendentals=0
        ),
    )(slots, recv, tiles, local)


def mid_kernel(
    me_ref,
    own_ref,
    low_ref,
    high_ref,
    far_a_ref,
    far_b_ref,
    cot_ref,
    w_ref,
    bias_ref,
    wown_ref,
    hid_ref,
    g_ref,
    gw_ref,
    gb_ref,
    agg_scr,
    hid_scr,
    wt_scr,
    gb_scr,
):
    i = pl.program_id(0)
    width = own_ref.shape[0]
    half = width // 2
    me, below, above, far = me_ref[0], me_ref[1], me_ref[2], me_ref[3]

    def rows(index, size=width):
        return pl.ds(pl.multiple_of(index, half), size)

    @pl.when(i == 0)
    def _():
        wt_scr[...] = w_ref[...].astype(F32).T.astype(BF)
        gw_ref[...] = jnp.zeros_like(gw_ref)
        gb_scr[...] = jnp.zeros_like(gb_scr)

    agg_scr[rows(below * width)] = low_ref[...]
    agg_scr[rows(above * width)] = high_ref[...]
    agg_scr[rows(far * width, half)] = far_a_ref[...]
    agg_scr[rows(far * width + half, half)] = far_b_ref[...]
    agg_scr[rows(me * width)] = own_ref[...]
    pre = dot(wt_scr[...], agg_scr[...], (1, 0))
    bias = bias_ref[:, :3].astype(F32)
    pre = pre + ((bias[:, 2:3] + bias[:, 1:2]) + bias[:, 0:1])
    sigma = jax.nn.sigmoid(pre)
    hid_scr[...] = (pre * sigma).astype(BF)
    hid_ref[...] = hid_scr[rows(me * width)]
    grad_pre = cot_ref[...].astype(F32) * (sigma * (1.0 + pre * (1.0 - sigma)))
    total = grad_pre[:, :128]
    for k in range(1, grad_pre.shape[1] // 128):
        total = total + grad_pre[:, k * 128 : (k + 1) * 128]
    gb_scr[...] += total
    grad_b = grad_pre.astype(BF)
    g_ref[...] = dot(wown_ref[...], grad_b, (1, 0)).astype(BF)
    gw_ref[...] += dot(own_ref[...], grad_b, (1, 1))

    @pl.when(i == pl.num_programs(0) - 1)
    def _():
        gb_ref[...] = gb_scr[rows(me * width)]


def mid(me, pieces, packed, w_own):
    own, low, high, far_a, far_b = pieces
    width, nodes = own.shape
    hid_all = packed.shape[0]
    chunk = 512
    col = lambda i: (0, i)
    return pl.pallas_call(
        mid_kernel,
        grid=(nodes // chunk,),
        out_shape=(
            jax.ShapeDtypeStruct((width, nodes), BF),
            jax.ShapeDtypeStruct((width, nodes), BF),
            jax.ShapeDtypeStruct((width, hid_all), F32),
            jax.ShapeDtypeStruct((width, 128), F32),
        ),
        in_specs=[
            SMEM,
            pl.BlockSpec((width, chunk), col),
            pl.BlockSpec((width, chunk), col),
            pl.BlockSpec((width, chunk), col),
            pl.BlockSpec((width // 2, chunk), col),
            pl.BlockSpec((width // 2, chunk), col),
            pl.BlockSpec((hid_all, chunk), col),
            pl.BlockSpec((hid_all, hid_all), lambda i: (0, nodes // hid_all)),
            pl.BlockSpec((hid_all, 128), lambda i: (0, (nodes + hid_all) // 128)),
            pl.BlockSpec((width, hid_all), lambda i: (0, 0)),
        ],
        out_specs=(
            pl.BlockSpec((width, chunk), col),
            pl.BlockSpec((width, chunk), col),
            pl.BlockSpec((width, hid_all), lambda i: (0, 0)),
            pl.BlockSpec((width, 128), lambda i: (0, 0)),
        ),
        scratch_shapes=[
            pltpu.VMEM((hid_all, chunk), BF),
            pltpu.VMEM((hid_all, chunk), BF),
            pltpu.VMEM((hid_all, hid_all), BF),
            pltpu.VMEM((hid_all, 128), F32),
        ],
        name="mid",
        cost_estimate=pl.CostEstimate(
            flops=2 * nodes * hid_all * (hid_all + 2 * width),
            bytes_accessed=3 << 20,
            transcendentals=nodes * hid_all,
        ),
    )(me, own, low, high, far_a, far_b, packed, packed, packed, w_own)


def back_remote_kernel(slots_ref, g_ref, tiles_ref, out_ref):
    i = pl.program_id(0)
    count, block = tiles_ref.shape[1], tiles_ref.shape[2]

    @pl.when(i == 0)
    def _():
        out_ref[...] = jnp.zeros_like(out_ref)

    for rr in range(STEP):
        lhs = g_ref[:, rr * block : (rr + 1) * block]
        for t in range(0, count, 2):
            base = (i * STEP + rr) * count + t
            rhs = jnp.concatenate([tiles_ref[rr, t + k] for k in range(2)], axis=1)
            term = dot(lhs, rhs, (1, 0)).astype(BF)
            for k in range(2):
                out_ref[slots_ref[base + k]] = term[:, k * block : (k + 1) * block]


def back_remote(slots, g, tiles, num_slots):
    row_blocks, per_block, block, _ = tiles.shape
    rem = per_block - TL
    width = g.shape[0]
    return pl.pallas_call(
        back_remote_kernel,
        grid=(row_blocks // STEP,),
        out_shape=jax.ShapeDtypeStruct((num_slots, width, block), BF),
        in_specs=[
            SMEM,
            pl.BlockSpec((width, STEP * block), lambda i: (0, i)),
            pl.BlockSpec((STEP, rem, block, block), lambda i: (i, 1, 0, 0)),
        ],
        out_specs=pl.BlockSpec((num_slots, width, block), lambda i: (0, 0, 0)),
        name="back_remote",
        cost_estimate=pl.CostEstimate(
            flops=2 * width * row_blocks * rem * block * block, bytes_accessed=5 << 20, transcendentals=0
        ),
    )(slots, g, tiles)


def back_local_kernel(cols_ref, g_ref, tiles_ref, out_ref):
    i = pl.program_id(0)
    count, block = tiles_ref.shape[1], tiles_ref.shape[2]

    @pl.when(i == 0)
    def _():
        out_ref[...] = jnp.zeros_like(out_ref)

    for rr in range(STEP):
        lhs = g_ref[:, rr * block : (rr + 1) * block]
        for t in range(0, count, 2):
            base = (i * STEP + rr) * count + t
            rhs = jnp.concatenate([tiles_ref[rr, t + k] for k in range(2)], axis=1)
            term = dot(lhs, rhs, (1, 0))
            for k in range(2):
                out_ref[:, lanes(cols_ref[base + k], block)] += term[:, k * block : (k + 1) * block]


def back_local(cols, g, tiles):
    row_blocks, _, block, _ = tiles.shape
    width = g.shape[0]
    return pl.pallas_call(
        back_local_kernel,
        grid=(row_blocks // STEP,),
        out_shape=jax.ShapeDtypeStruct(g.shape, F32),
        in_specs=[
            SMEM,
            pl.BlockSpec((width, STEP * block), lambda i: (0, i)),
            pl.BlockSpec((STEP, TL, block, block), lambda i: (i, 0, 0, 0)),
        ],
        out_specs=pl.BlockSpec(g.shape, lambda i: (0, 0)),
        name="back_local",
        cost_estimate=pl.CostEstimate(
            flops=2 * width * row_blocks * TL * block * block, bytes_accessed=3 << 20, transcendentals=0
        ),
    )(cols, g, tiles)


def finish_kernel(wanted_ref, recv_ref, local_ref, out_ref):
    block = recv_ref.shape[2]
    out_ref[...] = local_ref[...]

    def body(s, carry):
        w = wanted_ref[s]

        @pl.when(w >= 0)
        def _():
            out_ref[:, lanes(w, block)] += recv_ref[s].astype(F32)

        return carry

    lax.fori_loop(0, recv_ref.shape[0], body, 0, unroll=4)


def finish(wanted, recv, local):
    return pl.pallas_call(
        finish_kernel,
        out_shape=jax.ShapeDtypeStruct(local.shape, F32),
        in_specs=[SMEM, VMEM, VMEM],
        out_specs=VMEM,
        name="finish",
    )(wanted, recv, local)


def split_bf16(x, terms):
    parts = []
    for _ in range(terms):
        part = lax.reduce_precision(x, 8, 7)
        parts.append(part.astype(BF))
        x = x - part
    return parts


def local(feats, weight, bias, tile_cols, tile_values, cotangent):
    width, nodes_dev = feats.shape
    hid_all = weight.shape[1]
    block = tile_values.shape[1]
    row_blocks = nodes_dev // block
    peers = lax.axis_size("rows")
    fpeers = lax.axis_size("feat")
    per_block = tile_cols.shape[0] // row_blocks
    remote_count = row_blocks * (per_block - TL)
    capacity = 2 * remote_count // peers
    num_slots = peers * capacity

    bias_cols = jnp.pad(jnp.stack(split_bf16(bias, 3), axis=1), ((0, 0), (0, 125)))
    packed = jnp.concatenate([cotangent, weight, bias_cols], axis=1)
    packed = lax.all_gather(packed, "feat", axis=0, tiled=True)

    grid = tile_cols.reshape(row_blocks, per_block)
    tiles = tile_values.reshape(row_blocks, per_block, block, block)
    local_cols = (grid[:, :TL] % row_blocks).reshape(-1)
    remote_cols = grid[:, TL:].reshape(-1)
    owner = remote_cols // row_blocks
    order = jnp.arange(remote_count)
    earlier = (owner[:, None] == owner[None, :]) & (order[None, :] < order[:, None])
    slots = owner * capacity + jnp.sum(earlier.astype(jnp.int32), axis=1)
    hit = slots[None, :] == jnp.arange(num_slots)[:, None]
    request = jnp.max(jnp.where(hit, (remote_cols % row_blocks)[None, :], -1), axis=1)
    wanted = lax.all_to_all(
        request.reshape(peers, capacity), "rows", split_axis=0, concat_axis=0, tiled=True
    ).reshape(-1)

    def exchange(x):
        x = x.reshape(peers, capacity, width, block)
        x = lax.all_to_all(x, "rows", split_axis=0, concat_axis=0, tiled=True)
        return x.reshape(num_slots, width, block)

    fetched = exchange(pack(wanted, feats, block))
    agg = agg_local(local_cols, feats, tiles)
    agg = agg_remote(slots, fetched, tiles, agg)

    up = [(k, (k + 1) % fpeers) for k in range(fpeers)]
    down = [(k, (k - 1) % fpeers) for k in range(fpeers)]
    low = lax.ppermute(agg, "feat", up)
    high = lax.ppermute(agg, "feat", down)
    far_a = lax.ppermute(low[: width // 2], "feat", up)
    far_b = lax.ppermute(high[width // 2 :], "feat", down)
    x = lax.axis_index("feat")
    me = jnp.stack([x, (x - 1) % fpeers, (x + 1) % fpeers, (x + 2) % fpeers]).astype(jnp.int32)
    hidden_out, g, grad_w, grad_b = mid(me, (agg, low, high, far_a, far_b), packed, weight)

    returned = exchange(back_remote(slots, g, tiles, num_slots))
    own = back_local(local_cols, g, tiles)
    grad_input = finish(wanted, returned, own)

    divisor = math.sqrt(nodes_dev * peers)
    sums = jnp.concatenate([grad_w.reshape(peers, -1), jnp.sum(grad_b, axis=1).reshape(peers, -1)], axis=1)
    sums = lax.all_to_all(sums, "rows", split_axis=0, concat_axis=0, tiled=True)
    total = jnp.sum(sums, axis=0, keepdims=True) / divisor
    total = jnp.broadcast_to(total, sums.shape)
    total = lax.all_to_all(total, "rows", split_axis=0, concat_axis=0, tiled=True)
    per = grad_w.size // peers
    return (
        hidden_out,
        grad_input,
        total[:, :per].reshape(width, hid_all),
        total[:, per:].reshape(width),
    )


def solution(mesh):
    placed = (
        P("feat", "rows"),
        P("feat", None),
        P("feat"),
        P("rows"),
        P("rows", None, None),
        P("feat", "rows"),
    )
    return jax.shard_map(
        local,
        mesh=mesh,
        in_specs=placed,
        out_specs=(P("feat", "rows"), P("feat", "rows"), P("feat", None), P("feat")),
        check_vma=False,
    )
```

time: 596 us -> 223 us (0.37)
  waiting for transfers between devices: 374 us -> 105 us
  blocking collectives: 124 us -> 40.3 us
  local copies, waits for them, and re-layouts: 40.5 us -> 9.08 us
  Pallas kernels: 0 us -> 29.6 us
  matrix products: 17 us -> 0 us
    psum x1 -> x0, waiting for transfers between devices: 160 us -> none  [local(): weight_total, bias_total = lax.psum((partial_rows, bias_part), 'rows')]
    psum x1 -> x0, blocking collectives: 124 us -> none  [local(): weight_total, bias_total = lax.psum((partial_rows, bias_part), 'rows')]
    all_gather x2 -> x1, waiting for transfers between devices: 88 us -> 0.01 us  [local(): packed = lax.all_gather(packed, 'feat', axis=0, tiled=True)]
    all_to_all x0 -> x2, blocking collectives: none -> 40.3 us  [the longest x1 22.2 us: local(): lax.all_to_all(request.reshape(peers, capacity), 'rows', split_axis=0, co...]
    reduce_scatter x1 -> x0, waiting for transfers between devices: 36.1 us -> none  [local(): lax.psum_scatter(lax.dot_general(columns, feats, (((0,), (0,)), ((), ()))...]
    pallas_call x0 -> x7, Pallas kernels: none -> 29.6 us  [the longest x1 4.92 us: mid(): pl.pallas_call(mid_kernel, grid=(nodes // chunk,), out_shape=(jax.ShapeDt...]
    dot_general x9 -> x0, matrix products: 17 us -> none  [the longest x1 2.62 us: local(): jnp.einsum('fbtk,btnk->bfn', fetched[:, :, :TL], local_tiles, preferred_e...]
    reshape x1 -> x3, local copies, waits for them, and re-layouts: 15.3 us -> 1.44 us  [the longest x1 0.68 us: local(): wanted = lax.all_to_all(request.reshape(peers, capacity), 'rows', split_a...]
  transfers between devices with their start and end apart: 6 -> 8, of which waited for: 4 -> 5; matrix products, arithmetic and copies ran while one was open for 8% -> 2% of each run, Pallas kernels for 0% -> 8%
where the time goes in v1:
time: 223 us; the launch traced here: 222 us
  waiting for transfers between devices  105 us (47%)
  blocking collectives  40.3 us (18%)
  Pallas kernels  29.6 us (13%)
  starting transfers between devices  19.6 us (9%)
  between operations  14.2 us (6%)
  local copies, waits for them, and re-layouts  9.08 us (4%)
  other arithmetic  4.31 us (2%)
    all_to_all x2, waiting for transfers between devices, exchange(): x = lax.all_to_all(x, 'rows', split_axis=0, concat_axis=0, tiled=True)  91.6 us
    all_to_all x1, blocking collectives, local(): lax.all_to_all(request.reshape(peers, capacity), 'rows', split_axis=0, co...  22.2 us
    all_to_all x1, blocking collectives, local(): sums = lax.all_to_all(sums, 'rows', split_axis=0, concat_axis=0, tiled=True)  18.1 us
    all_to_all x2, starting transfers between devices, exchange(): x = lax.all_to_all(x, 'rows', split_axis=0, concat_axis=0, tiled=True)  9.63 us
    ppermute x1, waiting for transfers between devices, local(): low = lax.ppermute(agg, 'feat', up)  6.24 us
    all_to_all x1, waiting for transfers between devices, local(): lax.all_to_all(total, 'rows', split_axis=0, concat_axis=0, tiled=True)  5.75 us
    pallas_call x1, Pallas kernels, mid(): pl.pallas_call(mid_kernel, grid=(nodes // chunk,), out_shape=(jax.ShapeDt...  4.92 us
    pallas_call x1, Pallas kernels, agg_remote(): pl.pallas_call(agg_remote_kernel, grid=(row_blocks // STEP,), out_shape=j...  4.81 us
  transfers between devices with their start and end apart: 8, of which 5 were waited for; matrix products, arithmetic and copies ran while one was open for 2% of the time, Pallas kernels for 8%

profile of v1, /device:TPU:1, one launch (start us, length us, event | category | flops | bytes accessed | tf_op | source)
XLA Modules:
  0.0 222.4 jit_solution(1473501579742887102)
XLA Ops:
  7.2 0.7 reshape.148
  8.5 22.2 %all_to_all.37 = s32[64,1,2]{2,1,0:T(1,128)S(1)} all-to-all(s32[64,1,2]{2,1,0:T(1,128)S(1)} %bitcast.32), channel_id=1, replica_groups=mesh['rows'=64,'feat'=4] {'rows'}, dimensions={0} | all-to-all | bytes 1024 | tf_op jit(solution)/shard_map/all_to_all | solution.py:366
  31.3 0.7 reduce.6
  32.0 0.7 reshape.150.wanted_ref
  32.7 3.0 %pack.1 = bf16[128,64,128]{2,1,0:T(8,128)(2,1)} custom-call(s32[128]{0:T(128)} %reshape.150.wanted_ref, bf16[64,2048]{1,0:T(8,128)(2,1)} %feats_ref.3), custom_call_target="tpu_custom_call" | custom-call | tf_op jit(solution)/shard_map/pack/pallas_call | solution.py:34
  35.7 4.9 %all-to-all-start.1 = ((bf16[64,2,64,128]{3,2,1,0:T(8,128)(2,1)}), bf16[64,2,64,128]{3,2,1,0:T(8,128)(2,1)S(1)}, u32[]{:S(2)}, u32[]{:S(2)}) async-start(bf16[64,2,64,128]{3,2,1,0:T(8,128)(2,1)} %bitcast.27), calls=%async_computation.1 | async-start | bytes 4194304 | tf_op jit(solution)/shard_map/all_to_all | solution.py:372
  40.8 0.7 fusion.1
  41.6 0.7 reshape.154.cols_ref
  42.3 4.1 %agg_local.1.local_ref = f32[64,2048]{1,0:T(8,128)} custom-call(s32[64]{0:T(128)} %reshape.154.cols_ref, bf16[64,2048]{1,0:T(8,128)(2,1)} %feats_ref.3, bf16[16,8,128,128]{3,2,1,0:T(8,128)(2,1)} %bitcast.22), custom_call_target="tpu_custom_call" | custom-call | flops 134217728 | bytes 3145728 | tf_op jit(solution)/shard_map/agg_local/pallas_call | solution.py:69
  46.4 45.6 %all-to-all-done.1 = bf16[64,2,64,128]{3,2,1,0:T(8,128)(2,1)S(1)} async-done(((bf16[64,2,64,128]{3,2,1,0:T(8,128)(2,1)}), bf16[64,2,64,128]{3,2,1,0:T(8,128)(2,1)S(1)}, u32[]{:S(2)}, u32[]{:S(2)}) %all-to-all-start.1) | async-done | bytes 2097184 | tf_op jit(solution)/shard_map/all_to_all | solution.py:372
  92.0 1.3 copy-done
  93.3 4.8 %agg_remote.1.own_ref = bf16[64,2048]{1,0:T(8,128)(2,1)} custom-call(s32[64]{0:T(128)} %copy-done.8, bf16[128,64,128]{2,1,0:T(8,128)(2,1)} %bitcast.26, bf16[16,8,128,128]{3,2,1,0:T(8,128)(2,1)} %bitcast.23, f32[64,2048]{1,0:T(8,128)} %agg_local.1.local_ref), custom_call_target="tpu_custom_call" | custom-call | flops 134217728 | bytes 5242880 | tf_op jit(solution)/shard_map/agg_remote/pallas_call | solution.py:103
  98.1 1.2 collective-permute-start
  99.3 1.5 collective-permute-start.1
  100.8 6.2 %collective-permute-done.low_ref = bf16[64,2048]{1,0:T(8,128)(2,1)S(1)} collective-permute-done((bf16[64,2048]{1,0:T(8,128)(2,1)}, bf16[64,2048]{1,0:T(8,128)(2,1)S(1)}, u32[]{:S(2)}, u32[]{:S(2)}) %collective-permute-start) | collective-permute-done | bytes 262176 | tf_op jit(solution)/shard_map/ppermute | solution.py:381
  107.2 2.7 %collective-permute-start.3 = (bf16[32,2048]{1,0:T(8,128)(2,1)S(1)}, bf16[32,2048]{1,0:T(8,128)(2,1)S(1)}, u32[]{:S(2)}, u32[]{:S(2)}) collective-permute-start(bf16[32,2048]{1,0:T(8,128)(2,1)S(1)} %slice.27), channel_id=1, source_target_pairs={{0,3},{1,0},{2,1},{3,2},{4,7},{5,4},{6,5},{7,6},{8,11},{9,8},{10,9... | collective-permute-start | bytes 393224 | tf_op jit(solution)/shard_map/ppermute | solution.py:384
  110.5 1.6 collective-permute-done.2.far_a_ref
  112.8 0.6 copy-done.7
  113.5 4.9 %mid.1 = (bf16[64,2048]{1,0:T(8,128)(2,1)}, bf16[64,2048]{1,0:T(8,128)(2,1)}, f32[64,256]{1,0:T(8,128)}, f32[64,128]{1,0:T(8,128)}) custom-call(s32[4]{0:T(128)} %pad_add_fusion.me_ref, bf16[64,2048]{1,0:T(8,128)(2,1)} %agg_remote.1.own_ref, bf16[64,2048]{1,0:T(8,128)(2,1)} %copy-done.2, bf16[64,2048]{1,0:T(8,128)(2,1)} %copy-done.3, ...), custom_call_target="tpu_custom_call" | custom-call | flops 402653184 | bytes 3145728 | tf_op jit(solution)/shard_map/mid/pallas_call | solution.py:186
  118.4 0.9 reduce_sum.28
  119.3 0.9 maximum_bitcast_fusion
  120.3 18.1 %all_to_all.38 = f32[64,1,257]{2,1,0:T(1,128)S(1)} all-to-all(f32[64,1,257]{2,1,0:T(1,128)S(1)} %copy.25), channel_id=1, replica_groups=mesh['rows'=64,'feat'=4] {'rows'}, dimensions={0} | all-to-all | bytes 131584 | tf_op jit(solution)/shard_map/all_to_all | solution.py:395
  138.5 0.7 broadcast_in_dim.16
  139.2 4.4 %all-to-all-start.4 = ((f32[64,1,257]{2,1,0:T(1,128)}), f32[64,1,257]{2,1,0:T(1,128)S(1)}, u32[]{:S(2)}, u32[]{:S(2)}) async-start(f32[64,1,257]{2,1,0:T(1,128)} %broadcast_in_dim.16), calls=%async_computation.4 | async-start | bytes 196608 | tf_op jit(solution)/shard_map/all_to_all | solution.py:398
  143.7 4.5 %back_remote.1 = bf16[128,64,128]{2,1,0:T(8,128)(2,1)} custom-call(s32[64]{0:T(128)} %copy-done.8, bf16[64,2048]{1,0:T(8,128)(2,1)} %get-tuple-element.9.g_ref, bf16[16,8,128,128]{3,2,1,0:T(8,128)(2,1)} %bitcast.24), custom_call_target="tpu_custom_call" | custom-call | flops 134217728 | bytes 5242880 | tf_op jit(solution)/shard_map/back_remote/pallas_call | solution.py:250
  148.2 5.7 %all-to-all-done.4 = f32[64,1,257]{2,1,0:T(1,128)S(1)} async-done(((f32[64,1,257]{2,1,0:T(1,128)}), f32[64,1,257]{2,1,0:T(1,128)S(1)}, u32[]{:S(2)}, u32[]{:S(2)}) %all-to-all-start.4) | async-done | bytes 65824 | tf_op jit(solution)/shard_map/all_to_all | solution.py:398
  154.0 4.7 %all-to-all-start.2 = ((bf16[64,2,64,128]{3,2,1,0:T(8,128)(2,1)}), bf16[64,2,64,128]{3,2,1,0:T(8,128)(2,1)S(1)}, u32[]{:S(2)}, u32[]{:S(2)}) async-start(bf16[64,2,64,128]{3,2,1,0:T(8,128)(2,1)} %bitcast.28), calls=%async_computation.2 | async-start | bytes 4194304 | tf_op jit(solution)/shard_map/all_to_all | solution.py:372
  158.7 3.9 %back_local.1.local_ref = f32[64,2048]{1,0:T(8,128)} custom-call(s32[64]{0:T(128)} %reshape.154.cols_ref, bf16[64,2048]{1,0:T(8,128)(2,1)} %get-tuple-element.9.g_ref, bf16[16,8,128,128]{3,2,1,0:T(8,128)(2,1)} %bitcast.25), custom_call_target="tpu_custom_call" | custom-call | flops 134217728 | bytes 3145728 | tf_op jit(solution)/shard_map/back_local/pallas_call | solution.py:288
  162.6 0.6 slice.28
  163.9 46.1 %all-to-all-done.2 = bf16[64,2,64,128]{3,2,1,0:T(8,128)(2,1)S(1)} async-done(((bf16[64,2,64,128]{3,2,1,0:T(8,128)(2,1)}), bf16[64,2,64,128]{3,2,1,0:T(8,128)(2,1)S(1)}, u32[]{:S(2)}, u32[]{:S(2)}) %all-to-all-start.2) | async-done | bytes 2097184 | tf_op jit(solution)/shard_map/all_to_all | solution.py:372
  209.9 1.3 copy-done.1
  211.3 4.3 %finish.1 = f32[64,2048]{1,0:T(8,128)} custom-call(s32[128]{0:T(128)} %reshape.150.wanted_ref, bf16[128,64,128]{2,1,0:T(8,128)(2,1)} %bitcast.29, f32[64,2048]{1,0:T(8,128)} %back_local.1.local_ref), custom_call_target="tpu_custom_call" | custom-call | tf_op jit(solution)/shard_map/finish/pallas_call | solution.py:322
  (43 shorter events, 3.6 us)
Async XLA Ops:
  8.3 27.4 %copy-start.8 = (s32[64]{0:T(128)}, s32[64]{0:T(128)S(1)}, u32[]{:S(2)}) copy-start(s32[64]{0:T(128)S(1)} %multiply_add_fusion.slots_ref) | copy-start | bytes 772
  35.7 5.0 %copy-start.9 = (f32[64]{0:T(128)S(1)}, f32[64]{0:T(128)}, u32[]{:S(2)}) copy-start(f32[64]{0:T(128)} %param.8) | copy-start | bytes 772
  35.7 5.2 %copy-start.4 = (bf16[64,2048]{1,0:T(8,128)(2,1)S(1)}, bf16[64,2048]{1,0:T(8,128)(2,1)}, u32[]{:S(2)}) copy-start(bf16[64,2048]{1,0:T(8,128)(2,1)} %param.11) | copy-start | bytes 786436
  35.7 5.2 %copy-start.5 = (bf16[64,256]{1,0:T(8,128)(2,1)S(1)}, bf16[64,256]{1,0:T(8,128)(2,1)}, u32[]{:S(2)}) copy-start(bf16[64,256]{1,0:T(8,128)(2,1)} %wown_ref.1) | copy-start | bytes 98308
  35.7 56.3 %all-to-all-start.1 = ((bf16[64,2,64,128]{3,2,1,0:T(8,128)(2,1)}), bf16[64,2,64,128]{3,2,1,0:T(8,128)(2,1)S(1)}, u32[]{:S(2)}, u32[]{:S(2)}) async-start(bf16[64,2,64,128]{3,2,1,0:T(8,128)(2,1)} %bitcast.27), calls=%async_computation.1 | async-start | bytes 4194304 | tf_op jit(solution)/shard_map/all_to_all | solution.py:372
  40.6 69.9 %all-gather.2.cloned.1.call-start = ((), (), s32[]{:S(2)}) async-start(), calls=%async_computation.5 | async-start | bytes 1556480 | tf_op jit(solution)/shard_map/all_gather | solution.py:354
  92.0 1.3 copy-start
  98.1 8.9 %collective-permute-start = (bf16[64,2048]{1,0:T(8,128)(2,1)}, bf16[64,2048]{1,0:T(8,128)(2,1)S(1)}, u32[]{:S(2)}, u32[]{:S(2)}) collective-permute-start(bf16[64,2048]{1,0:T(8,128)(2,1)} %agg_remote.1.own_ref), channel_id=1, source_target_pairs={{0,1},{1,2},{2,3},{3,0},{4,5},{5,6},{6,7},{7,4},{8,9},{9,10},{10,1... | collective-permute-start | bytes 786440 | tf_op jit(solution)/shard_map/ppermute | solution.py:381
  99.3 7.8 %collective-permute-start.1 = (bf16[64,2048]{1,0:T(8,128)(2,1)}, bf16[64,2048]{1,0:T(8,128)(2,1)S(1)}, u32[]{:S(2)}, u32[]{:S(2)}) collective-permute-start(bf16[64,2048]{1,0:T(8,128)(2,1)} %agg_remote.1.own_ref), channel_id=1, source_target_pairs={{0,3},{1,0},{2,1},{3,2},{4,7},{5,4},{6,5},{7,6},{8,11},{9,8},{10,9... | collective-permute-start | bytes 786440 | tf_op jit(solution)/shard_map/ppermute | solution.py:382
  107.0 5.1 %copy-start.2 = (bf16[64,2048]{1,0:T(8,128)(2,1)}, bf16[64,2048]{1,0:T(8,128)(2,1)S(1)}, u32[]{:S(2)}) copy-start(bf16[64,2048]{1,0:T(8,128)(2,1)S(1)} %collective-permute-done.low_ref) | copy-start | bytes 786436
  107.1 5.1 %collective-permute-start.2 = (bf16[32,2048]{1,0:T(8,128)(2,1)S(1)}, bf16[32,2048]{1,0:T(8,128)(2,1)S(1)}, u32[]{:S(2)}, u32[]{:S(2)}) collective-permute-start(bf16[32,2048]{1,0:T(8,128)(2,1)S(1)} %slice.26), channel_id=1, source_target_pairs={{0,1},{1,2},{2,3},{3,0},{4,5},{5,6},{6,7},{7,4},{8,9},{9,10},{10,1... | collective-permute-start | bytes 393224 | tf_op jit(solution)/shard_map/ppermute | solution.py:383
  107.2 5.0 %copy-start.3 = (bf16[64,2048]{1,0:T(8,128)(2,1)}, bf16[64,2048]{1,0:T(8,128)(2,1)S(1)}, u32[]{:S(2)}) copy-start(bf16[64,2048]{1,0:T(8,128)(2,1)S(1)} %collective-permute-done.1.high_ref) | copy-start | bytes 786436
  107.2 5.0 %collective-permute-start.3 = (bf16[32,2048]{1,0:T(8,128)(2,1)S(1)}, bf16[32,2048]{1,0:T(8,128)(2,1)S(1)}, u32[]{:S(2)}, u32[]{:S(2)}) collective-permute-start(bf16[32,2048]{1,0:T(8,128)(2,1)S(1)} %slice.27), channel_id=1, source_target_pairs={{0,3},{1,0},{2,1},{3,2},{4,7},{5,4},{6,5},{7,6},{8,11},{9,8},{10,9... | collective-permute-start | bytes 393224 | tf_op jit(solution)/shard_map/ppermute | solution.py:384
  112.2 0.6 copy-start.6
  112.8 0.7 copy-start.7
  139.2 14.7 %all-to-all-start.4 = ((f32[64,1,257]{2,1,0:T(1,128)}), f32[64,1,257]{2,1,0:T(1,128)S(1)}, u32[]{:S(2)}, u32[]{:S(2)}) async-start(f32[64,1,257]{2,1,0:T(1,128)} %broadcast_in_dim.16), calls=%async_computation.4 | async-start | bytes 196608 | tf_op jit(solution)/shard_map/all_to_all | solution.py:398
  154.0 55.9 %all-to-all-start.2 = ((bf16[64,2,64,128]{3,2,1,0:T(8,128)(2,1)}), bf16[64,2,64,128]{3,2,1,0:T(8,128)(2,1)S(1)}, u32[]{:S(2)}, u32[]{:S(2)}) async-start(bf16[64,2,64,128]{3,2,1,0:T(8,128)(2,1)} %bitcast.28), calls=%async_computation.2 | async-start | bytes 4194304 | tf_op jit(solution)/shard_map/all_to_all | solution.py:372
  209.9 1.3 copy-start.1
Sparse Core Ops, SparseCore 0:
  43.3 27.1 all-gather.1

commit v2 on v1

--- a/solution.py
+++ b/solution.py
@@ -1,3 +1,4 @@
+import functools
 import math
 
 import jax
@@ -11,6 +12,7 @@
 BF = jnp.bfloat16
 F32 = jnp.float32
 VMEM = pl.BlockSpec(memory_space=pltpu.VMEM)
+ANY = pl.BlockSpec(memory_space=pl.ANY)
 SMEM = pl.BlockSpec(memory_space=pltpu.SMEM)
 
 
@@ -18,26 +20,52 @@
     return pl.ds(pl.multiple_of(index * width, width), width)
 
 
-def pack_kernel(wanted_ref, feats_ref, out_ref):
-    block = out_ref.shape[2]
-
-    def body(s, carry):
-        w = jnp.maximum(wanted_ref[s], 0)
-        out_ref[s] = feats_ref[:, lanes(w, block)]
-        return carry
-
-    lax.fori_loop(0, out_ref.shape[0], body, 0, unroll=8)
-
-
-def pack(wanted, feats, block):
-    slots = wanted.shape[0]
-    return pl.pallas_call(
-        pack_kernel,
-        out_shape=jax.ShapeDtypeStruct((slots, feats.shape[0], block), feats.dtype),
-        in_specs=[SMEM, VMEM],
-        out_specs=VMEM,
+NY, NZ, NC = 4, 8, 2
+CAP = 2
+ORDER = (0, 1, 7, 2, 6, 3, 5, 4)
+GROUPS = ((0, 3), (3, 5), (5, 8))
+PER = NZ * CAP
+
+
+def shift(x, dy=0, dz=0, dc=0):
+    pairs = []
+    for y in range(NY):
+        for z in range(NZ):
+            for c in range(NC):
+                to = ((y + dy) % NY * NZ + (z + dz) % NZ) * NC + (c + dc) % NC
+                pairs.append(((y * NZ + z) * NC + c, to))
+    return lax.ppermute(x, "rows", pairs)
+
+
+def pack_kernel(first, count, split, *refs):
+    wanted_ref, sources, outs = refs[0], refs[1 : 1 + count + split], refs[-NY:]
+    width, block = outs[0].shape[2], outs[0].shape[3]
+    for ys in range(NY):
+        for cs in range(NC):
+            for q in range(count * CAP):
+                w = wanted_ref[(ys * NC + cs) * PER + first * CAP + q]
+                where = lanes(jnp.maximum(w, 0), block)
+                j = q // CAP
+                if split and j == count - 1:
+                    outs[ys][cs, q, : width // 2] = sources[j][:, where]
+                    outs[ys][cs, q, width // 2 :] = sources[j + 1][:, where]
+                else:
+                    outs[ys][cs, q] = sources[j][:, where]
+
+
+def pack(group, wanted, sources, block, after):
+    first, last = group
+    count = last - first
+    width = sources[0].shape[0]
+    shape = jax.ShapeDtypeStruct((NC, count * CAP, width, block), BF)
+    return pl.pallas_call(
+        functools.partial(pack_kernel, first, count, len(sources) > count),
+        out_shape=[shape] * NY,
+        in_specs=[SMEM] + [VMEM] * len(sources) + [ANY] * len(after),
+        out_specs=[VMEM] * NY,
         name="pack",
-    )(wanted, feats)
+        cost_estimate=pl.CostEstimate(flops=0, bytes_accessed=3 << 20, transcendentals=0),
+    )(wanted, *sources, *after)
 
 
 def dot(a, b, dims):
@@ -83,9 +111,21 @@
     )(cols, feats, tiles)
 
 
-def agg_remote_kernel(slots_ref, recv_ref, tiles_ref, local_ref, out_ref):
+def agg_remote_kernel(slots_ref, tiles_ref, local_ref, *refs):
+    parts, out_ref, recv_ref = refs[:-2], refs[-2], refs[-1]
     i = pl.program_id(0)
     count, block = tiles_ref.shape[1], tiles_ref.shape[2]
+
+    @pl.when(i == 0)
+    def _():
+        n = 0
+        for first, last in GROUPS:
+            size = (last - first) * CAP
+            for ys in range(NY):
+                recv_ref[pl.ds(ys * PER + first * CAP, size)] = parts[n + ys][0]
+                recv_ref[pl.ds((NY + ys) * PER + first * CAP, size)] = parts[n + NY][ys]
+            n += NY + 1
+
     for rr in range(STEP):
         acc = local_ref[:, rr * block : (rr + 1) * block]
         for t in range(0, count, 2):
@@ -96,26 +136,31 @@
         out_ref[:, rr * block : (rr + 1) * block] = acc.astype(out_ref.dtype)
 
 
-def agg_remote(slots, recv, tiles, local):
+def agg_remote(slots, parts, tiles, local):
     row_blocks, per_block, block, _ = tiles.shape
     rem = per_block - TL
     width = local.shape[0]
+    specs = []
+    for n, part in enumerate(parts):
+        lead = 1 if n % (NY + 1) < NY else NY
+        specs.append(pl.BlockSpec((lead,) + part.shape[1:], lambda i: (0, 0, 0, 0)))
     return pl.pallas_call(
         agg_remote_kernel,
         grid=(row_blocks // STEP,),
         out_shape=jax.ShapeDtypeStruct(local.shape, BF),
         in_specs=[
             SMEM,
-            pl.BlockSpec(recv.shape, lambda i: (0, 0, 0)),
             pl.BlockSpec((STEP, rem, block, block), lambda i: (i, 1, 0, 0)),
             pl.BlockSpec((width, STEP * block), lambda i: (0, i)),
-        ],
+        ]
+        + specs,
         out_specs=pl.BlockSpec((width, STEP * block), lambda i: (0, i)),
+        scratch_shapes=[pltpu.VMEM((NY * NC * PER, width, block), BF)],
         name="agg_remote",
         cost_estimate=pl.CostEstimate(
             flops=2 * width * row_blocks * rem * block * block, bytes_accessed=5 << 20, transcendentals=0
         ),
-    )(slots, recv, tiles, local)
+    )(slots, tiles, local, *parts)
 
 
 def mid_kernel(
@@ -123,8 +168,7 @@
     own_ref,
     low_ref,
     high_ref,
-    far_a_ref,
-    far_b_ref,
+    far_ref,
     cot_ref,
     w_ref,
     bias_ref,
@@ -140,11 +184,11 @@
 ):
     i = pl.program_id(0)
     width = own_ref.shape[0]
-    half = width // 2
-    me, below, above, far = me_ref[0], me_ref[1], me_ref[2], me_ref[3]
-
-    def rows(index, size=width):
-        return pl.ds(pl.multiple_of(index, half), size)
+    count = agg_scr.shape[0] // width
+    me = me_ref[0]
+
+    def rows(ahead):
+        return pl.ds(pl.multiple_of(lax.rem(me + ahead, count) * width, width), width)
 
     @pl.when(i == 0)
     def _():
@@ -152,17 +196,16 @@
         gw_ref[...] = jnp.zeros_like(gw_ref)
         gb_scr[...] = jnp.zeros_like(gb_scr)
 
-    agg_scr[rows(below * width)] = low_ref[...]
-    agg_scr[rows(above * width)] = high_ref[...]
-    agg_scr[rows(far * width, half)] = far_a_ref[...]
-    agg_scr[rows(far * width + half, half)] = far_b_ref[...]
-    agg_scr[rows(me * width)] = own_ref[...]
+    agg_scr[rows(3)] = low_ref[...]
+    agg_scr[rows(1)] = high_ref[...]
+    agg_scr[rows(2)] = far_ref[...]
+    agg_scr[rows(0)] = own_ref[...]
     pre = dot(wt_scr[...], agg_scr[...], (1, 0))
     bias = bias_ref[:, :3].astype(F32)
     pre = pre + ((bias[:, 2:3] + bias[:, 1:2]) + bias[:, 0:1])
     sigma = jax.nn.sigmoid(pre)
     hid_scr[...] = (pre * sigma).astype(BF)
-    hid_ref[...] = hid_scr[rows(me * width)]
+    hid_ref[...] = hid_scr[rows(0)]
     grad_pre = cot_ref[...].astype(F32) * (sigma * (1.0 + pre * (1.0 - sigma)))
     total = grad_pre[:, :128]
     for k in range(1, grad_pre.shape[1] // 128):
@@ -174,11 +217,11 @@
 
     @pl.when(i == pl.num_programs(0) - 1)
     def _():
-        gb_ref[...] = gb_scr[rows(me * width)]
+        gb_ref[...] = gb_scr[rows(0)]
 
 
 def mid(me, pieces, packed, w_own):
-    own, low, high, far_a, far_b = pieces
+    own, low, high, far = pieces
     width, nodes = own.shape
     hid_all = packed.shape[0]
     chunk = 512
@@ -197,8 +240,7 @@
             pl.BlockSpec((width, chunk), col),
             pl.BlockSpec((width, chunk), col),
             pl.BlockSpec((width, chunk), col),
-            pl.BlockSpec((width // 2, chunk), col),
-            pl.BlockSpec((width // 2, chunk), col),
+            pl.BlockSpec((width, chunk), col),
             pl.BlockSpec((hid_all, chunk), col),
             pl.BlockSpec((hid_all, hid_all), lambda i: (0, nodes // hid_all)),
             pl.BlockSpec((hid_all, 128), lambda i: (0, (nodes + hid_all) // 128)),
@@ -222,11 +264,12 @@
             bytes_accessed=3 << 20,
             transcendentals=nodes * hid_all,
         ),
-    )(me, own, low, high, far_a, far_b, packed, packed, packed, w_own)
+    )(me, own, low, high, far, packed, packed, packed, w_own)
 
 
 def back_remote_kernel(slots_ref, g_ref, tiles_ref, out_ref):
     i = pl.program_id(0)
+    width = g_ref.shape[0]
     count, block = tiles_ref.shape[1], tiles_ref.shape[2]
 
     @pl.when(i == 0)
@@ -240,23 +283,25 @@
             rhs = jnp.concatenate([tiles_ref[rr, t + k] for k in range(2)], axis=1)
             term = dot(lhs, rhs, (1, 0)).astype(BF)
             for k in range(2):
-                out_ref[slots_ref[base + k]] = term[:, k * block : (k + 1) * block]
-
-
-def back_remote(slots, g, tiles, num_slots):
+                slot = slots_ref[base + k]
+                row = pl.multiple_of((slot % CAP) * width, width)
+                out_ref[slot // CAP, pl.ds(row, width)] = term[:, k * block : (k + 1) * block]
+
+
+def back_remote(slots, g, tiles, peers, extra):
     row_blocks, per_block, block, _ = tiles.shape
     rem = per_block - TL
     width = g.shape[0]
     return pl.pallas_call(
         back_remote_kernel,
         grid=(row_blocks // STEP,),
-        out_shape=jax.ShapeDtypeStruct((num_slots, width, block), BF),
+        out_shape=jax.ShapeDtypeStruct((peers, CAP * width + extra, block), BF),
         in_specs=[
             SMEM,
             pl.BlockSpec((width, STEP * block), lambda i: (0, i)),
             pl.BlockSpec((STEP, rem, block, block), lambda i: (i, 1, 0, 0)),
         ],
-        out_specs=pl.BlockSpec((num_slots, width, block), lambda i: (0, 0, 0)),
+        out_specs=pl.BlockSpec((peers, CAP * width + extra, block), lambda i: (0, 0, 0)),
         name="back_remote",
         cost_estimate=pl.CostEstimate(
             flops=2 * width * row_blocks * rem * block * block, bytes_accessed=5 << 20, transcendentals=0
@@ -302,20 +347,20 @@
     )(cols, g, tiles)
 
 
-def finish_kernel(wanted_ref, recv_ref, local_ref, out_ref):
-    block = recv_ref.shape[2]
+def finish_kernel(wanted_ref, recv_ref, local_ref, out_ref, odd_scr):
+    width, block = out_ref.shape[0], recv_ref.shape[2]
     out_ref[...] = local_ref[...]
-
-    def body(s, carry):
-        w = wanted_ref[s]
-
-        @pl.when(w >= 0)
-        def _():
-            out_ref[:, lanes(w, block)] += recv_ref[s].astype(F32)
-
+    odd_scr[...] = jnp.zeros_like(odd_scr)
+
+    def body(p, carry):
+        even = lanes(jnp.maximum(wanted_ref[p * CAP], 0), block)
+        odd = lanes(jnp.maximum(wanted_ref[p * CAP + 1], 0), block)
+        out_ref[:, even] += recv_ref[p, :width].astype(F32)
+        odd_scr[:, odd] += recv_ref[p, width : 2 * width].astype(F32)
         return carry
 
     lax.fori_loop(0, recv_ref.shape[0], body, 0, unroll=4)
+    out_ref[...] += odd_scr[...]
 
 
 def finish(wanted, recv, local):
@@ -324,7 +369,9 @@
         out_shape=jax.ShapeDtypeStruct(local.shape, F32),
         in_specs=[SMEM, VMEM, VMEM],
         out_specs=VMEM,
+        scratch_shapes=[pltpu.VMEM(local.shape, F32)],
         name="finish",
+        cost_estimate=pl.CostEstimate(flops=recv.size, bytes_accessed=4 << 20, transcendentals=0),
     )(wanted, recv, local)
 
 
@@ -346,62 +393,93 @@
     fpeers = lax.axis_size("feat")
     per_block = tile_cols.shape[0] // row_blocks
     remote_count = row_blocks * (per_block - TL)
-    capacity = 2 * remote_count // peers
-    num_slots = peers * capacity
-
-    bias_cols = jnp.pad(jnp.stack(split_bf16(bias, 3), axis=1), ((0, 0), (0, 125)))
-    packed = jnp.concatenate([cotangent, weight, bias_cols], axis=1)
-    packed = lax.all_gather(packed, "feat", axis=0, tiled=True)
+    place = lax.axis_index("rows")
+    y, z, c = place // (NZ * NC), place // NC % NZ, place % NC
 
     grid = tile_cols.reshape(row_blocks, per_block)
     tiles = tile_values.reshape(row_blocks, per_block, block, block)
     local_cols = (grid[:, :TL] % row_blocks).reshape(-1)
     remote_cols = grid[:, TL:].reshape(-1)
     owner = remote_cols // row_blocks
+    inside = remote_cols % row_blocks
     order = jnp.arange(remote_count)
     earlier = (owner[:, None] == owner[None, :]) & (order[None, :] < order[:, None])
-    slots = owner * capacity + jnp.sum(earlier.astype(jnp.int32), axis=1)
-    hit = slots[None, :] == jnp.arange(num_slots)[:, None]
-    request = jnp.max(jnp.where(hit, (remote_cols % row_blocks)[None, :], -1), axis=1)
-    wanted = lax.all_to_all(
-        request.reshape(peers, capacity), "rows", split_axis=0, concat_axis=0, tiled=True
-    ).reshape(-1)
-
-    def exchange(x):
-        x = x.reshape(peers, capacity, width, block)
-        x = lax.all_to_all(x, "rows", split_axis=0, concat_axis=0, tiled=True)
-        return x.reshape(num_slots, width, block)
-
-    fetched = exchange(pack(wanted, feats, block))
+    rank = jnp.sum(earlier.astype(jnp.int32), axis=1)
+    slots = owner * CAP + rank
+    ahead = (owner // NC - z) & (NZ - 1)
+    pos = jnp.maximum(jnp.where(ahead <= NZ // 2, 2 * ahead - 1, 2 * (NZ - ahead)), 0)
+    back = (y - owner // (NZ * NC)) & (NY - 1)
+    other = (owner ^ c) & 1
+    near = ((other * NY + back) * NZ + pos) * CAP + rank
+
+    def table(index):
+        hit = index[None, :] == jnp.arange(peers * CAP)[:, None]
+        return jnp.max(jnp.where(hit, inside[None, :], -1), axis=1)
+
+    asked = table(near).reshape(NC, NY, PER)
+    asked = jnp.stack([asked[0], shift(asked[1], dc=1)], axis=1)
+    wanted = [asked[0]] + [shift(asked[ys], dy=-ys) for ys in range(1, NY)]
+    wanted = jnp.stack(wanted).reshape(-1)
+
+    up, down, parts = [feats], [feats], []
+    for k in range(1, NZ // 2):
+        up.append(shift(up[-1], dz=1))
+        down.append(shift(down[-1], dz=-1))
+    far_up = shift(up[-1][: width // 2], dz=1)
+    far_down = shift(down[-1][width // 2 :], dz=-1)
+    groups = ((feats, down[1], up[1]), (down[2], up[2]), (down[3], up[3], far_up, far_down))
+    after = []
     agg = agg_local(local_cols, feats, tiles)
-    agg = agg_remote(slots, fetched, tiles, agg)
-
-    up = [(k, (k + 1) % fpeers) for k in range(fpeers)]
-    down = [(k, (k - 1) % fpeers) for k in range(fpeers)]
-    low = lax.ppermute(agg, "feat", up)
-    high = lax.ppermute(agg, "feat", down)
-    far_a = lax.ppermute(low[: width // 2], "feat", up)
-    far_b = lax.ppermute(high[width // 2 :], "feat", down)
-    x = lax.axis_index("feat")
-    me = jnp.stack([x, (x - 1) % fpeers, (x + 1) % fpeers, (x + 2) % fpeers]).astype(jnp.int32)
-    hidden_out, g, grad_w, grad_b = mid(me, (agg, low, high, far_a, far_b), packed, weight)
-
-    returned = exchange(back_remote(slots, g, tiles, num_slots))
+    for group, sources in zip(GROUPS, groups):
+        packs = pack(group, wanted, sources, block, after)
+        after = [packs[0], agg]
+        moved = [packs[0]] + [shift(packs[ys], dy=ys) for ys in range(1, NY)]
+        parts += moved
+        parts.append(shift(jnp.concatenate([m[1:] for m in moved]), dc=1))
+
+    bias_cols = jnp.pad(jnp.stack(split_bf16(bias, 3), axis=1), ((0, 0), (0, 125)))
+    packed = jnp.concatenate([cotangent, weight, bias_cols], axis=1)
+    packed = lax.all_gather(packed, "feat", axis=0, tiled=True)
+
+    agg = agg_remote(near, parts, tiles, agg)
+
+    pieces = [agg] + [
+        lax.ppermute(agg, "feat", [(k, (k + s) % fpeers) for k in range(fpeers)]) for s in (1, 3, 2)
+    ]
+    me = lax.axis_index("feat").astype(jnp.int32).reshape(1)
+    hidden_out, g, grad_w, grad_b = mid(me, pieces, packed, weight)
+
+    divisor = math.sqrt(nodes_dev * peers)
+    per = grad_w.size // peers
+    per_b = width // peers
+    sums = jnp.concatenate(
+        [
+            grad_w.reshape(peers, per),
+            jnp.sum(grad_b, axis=1).reshape(peers, per_b),
+            table(slots).reshape(peers, CAP).astype(F32),
+        ],
+        axis=1,
+    )
+    sums = lax.all_to_all(sums, "rows", split_axis=0, concat_axis=0, tiled=True)
+    holders = sums[:, per + per_b :].astype(jnp.int32).reshape(-1)
+    total = jnp.sum(sums[:, : per + per_b], axis=0) / divisor
+    span = -(-total.size // block)
+    total = jnp.pad(total, (0, span * block - total.size)).reshape(span, block)
+    extra = -(-2 * span // 8) * 8
+    rider = jnp.concatenate(split_bf16(total, 2) + [jnp.zeros((extra - 2 * span, block), BF)])
+
+    send = back_remote(slots, g, tiles, peers, extra)
+    send = send.at[:, CAP * width :].set(jnp.broadcast_to(rider, (peers, extra, block)))
+    recv = lax.all_to_all(send, "rows", split_axis=0, concat_axis=0, tiled=True)
     own = back_local(local_cols, g, tiles)
-    grad_input = finish(wanted, returned, own)
-
-    divisor = math.sqrt(nodes_dev * peers)
-    sums = jnp.concatenate([grad_w.reshape(peers, -1), jnp.sum(grad_b, axis=1).reshape(peers, -1)], axis=1)
-    sums = lax.all_to_all(sums, "rows", split_axis=0, concat_axis=0, tiled=True)
-    total = jnp.sum(sums, axis=0, keepdims=True) / divisor
-    total = jnp.broadcast_to(total, sums.shape)
-    total = lax.all_to_all(total, "rows", split_axis=0, concat_axis=0, tiled=True)
-    per = grad_w.size // peers
+    grad_input = finish(holders, recv, own)
+    totals = recv[:, CAP * width :].astype(F32)
+    totals = (totals[:, :span] + totals[:, span : 2 * span]).reshape(peers, -1)
     return (
         hidden_out,
         grad_input,
-        total[:, :per].reshape(width, hid_all),
-        total[:, per:].reshape(width),
+        totals[:, :per].reshape(width, hid_all),
+        totals[:, per : per + per_b].reshape(width),
     )
 
 

time: 223 us -> 199 us (0.89)
  starting transfers between devices: 19.6 us -> 61 us
  blocking collectives: 40.3 us -> 0 us
  waiting for transfers between devices: 105 us -> 74.6 us
  Pallas kernels: 29.6 us -> 32.7 us
    ppermute x4 -> x27, starting transfers between devices: 5.48 us -> 49.1 us  [the longest x24 44.9 us: shift(): return lax.ppermute(x, 'rows', pairs)]
    all_to_all x3 -> x2, waiting for transfers between devices: 97.4 us -> 54.6 us  [the longest x1 49.1 us: local(): recv = lax.all_to_all(send, 'rows', split_axis=0, concat_axis=0, tiled=True)]
    all_to_all x2 -> x0, blocking collectives: 40.3 us -> none  [the longest x1 22.2 us: local(): lax.all_to_all(request.reshape(peers, capacity), 'rows', split_axis=0, co...]
    ppermute x4 -> x27, waiting for transfers between devices: 7.88 us -> 20 us  [the longest x3 11.2 us: local(): lax.ppermute(agg, 'feat', [(k, (k + s) % fpeers) for k in range(fpeers)])]
    pallas_call x1 -> x3, Pallas kernels: 2.96 us -> 6.53 us  [pack(): pl.pallas_call(functools.partial(pack_kernel, first, count, len(sources)...]
    all_to_all x3 -> x2, starting transfers between devices: 14.1 us -> 11.9 us  [the longest x1 7.1 us: local(): sums = lax.all_to_all(sums, 'rows', split_axis=0, concat_axis=0, tiled=True)]
  transfers between devices with their start and end apart: 8 -> 30, of which waited for: 5 -> 11; matrix products, arithmetic and copies ran while one was open for 2% -> 4% of each run, Pallas kernels for 8% -> 12%
where the time goes in v2:
time: 199 us; the launch traced here: 198 us
  waiting for transfers between devices  74.6 us (37%)
  starting transfers between devices  61 us (31%)
  Pallas kernels  32.7 us (16%)
  between operations  14.6 us (7%)
  local copies, waits for them, and re-layouts  10.1 us (5%)
  other arithmetic  4.99 us (3%)
    all_to_all x1, waiting for transfers between devices, local(): recv = lax.all_to_all(send, 'rows', split_axis=0, concat_axis=0, tiled=True)  49.1 us
    ppermute x24, starting transfers between devices, shift(): return lax.ppermute(x, 'rows', pairs)  44.9 us
    ppermute x3, waiting for transfers between devices, local(): lax.ppermute(agg, 'feat', [(k, (k + s) % fpeers) for k in range(fpeers)])  11.2 us
    ppermute x24, waiting for transfers between devices, shift(): return lax.ppermute(x, 'rows', pairs)  8.78 us
    all_to_all x1, starting transfers between devices, local(): sums = lax.all_to_all(sums, 'rows', split_axis=0, concat_axis=0, tiled=True)  7.1 us
    pallas_call x3, Pallas kernels, pack(): pl.pallas_call(functools.partial(pack_kernel, first, count, len(sources)...  6.53 us
    all_to_all x1, waiting for transfers between devices, local(): sums = lax.all_to_all(sums, 'rows', split_axis=0, concat_axis=0, tiled=True)  5.51 us
    pallas_call x1, Pallas kernels, agg_remote(): pl.pallas_call(agg_remote_kernel, grid=(row_blocks // STEP,), out_shape=j...  4.89 us
  transfers between devices with their start and end apart: 30, of which 11 were waited for; matrix products, arithmetic and copies ran while one was open for 4% of the time, Pallas kernels for 12%

profile of v2, /device:TPU:1, one launch (start us, length us, event | category | flops | bytes accessed | tf_op | source)
XLA Modules:
  0.0 198.1 jit_solution(3385823470504411805)
XLA Ops:
  7.2 6.5 %collective-permute-start.4 = (bf16[64,2048]{1,0:T(8,128)(2,1)}, bf16[64,2048]{1,0:T(8,128)(2,1)S(1)}, u32[]{:S(2)}, u32[]{:S(2)}) collective-permute-start(bf16[64,2048]{1,0:T(8,128)(2,1)} %refs_1_.1), channel_id=1, source_target_pairs={{0,56},{4,60},{8,0},{12,4},{16,8},{20,12},{24,16},{28,20},{32,24},... | collective-permute-start | bytes 786440 | tf_op jit(solution)/shard_map/ppermute | solution.py:37
  14.5 1.7 fusion.1
  17.4 1.5 collective-permute-done.4.refs_2_
  19.0 3.3 %collective-permute-start.10 = (bf16[64,2048]{1,0:T(8,128)(2,1)S(1)}, bf16[64,2048]{1,0:T(8,128)(2,1)S(1)}, u32[]{:S(2)}, u32[]{:S(2)}) collective-permute-start(bf16[64,2048]{1,0:T(8,128)(2,1)S(1)} %collective-permute-done.4.refs_2_), channel_id=1, source_target_pairs={{0,56},{4,60},{8,0},{12,4},{16,8},{20,12},{24,16},{28,20},{32,24},... | collective-permute-start | bytes 786440 | tf_op jit(solution)/shard_map/ppermute | solution.py:37
  22.6 1.8 collective-permute-start
  24.5 1.9 collective-permute-done.10.refs_1_
  26.3 3.4 %collective-permute-start.16 = (bf16[64,2048]{1,0:T(8,128)(2,1)S(1)}, bf16[64,2048]{1,0:T(8,128)(2,1)S(1)}, u32[]{:S(2)}, u32[]{:S(2)}) collective-permute-start(bf16[64,2048]{1,0:T(8,128)(2,1)S(1)} %collective-permute-done.10.refs_1_), channel_id=1, source_target_pairs={{0,56},{4,60},{8,0},{12,4},{16,8},{20,12},{24,16},{28,20},{32,24},... | collective-permute-start | bytes 786440 | tf_op jit(solution)/shard_map/ppermute | solution.py:37
  31.2 2.6 %collective-permute-start.2 = (s32[2,16]{1,0:T(2,128)S(1)}, s32[2,16]{1,0:T(2,128)S(1)}, u32[]{:S(2)}, u32[]{:S(2)}) collective-permute-start(s32[2,16]{1,0:T(2,128)S(1)} %bitcast.47), channel_id=1, source_target_pairs={{0,128},{4,132},{8,136},{12,140},{16,144},{20,148},{24,152},{28,15... | collective-permute-start | bytes 392 | tf_op jit(solution)/shard_map/ppermute | solution.py:37
  37.2 2.2 %pack.3 = (bf16[2,6,64,128]{3,2,1,0:T(8,128)(2,1)}, bf16[2,6,64,128]{3,2,1,0:T(8,128)(2,1)}, bf16[2,6,64,128]{3,2,1,0:T(8,128)(2,1)}, bf16[2,6,64,128]{3,2,1,0:T(8,128)(2,1)}) custom-call(s32[128]{0:T(128)} %reshape.245.refs_0_, bf16[64,2048]{1,0:T(8,128)(2,1)} %refs_1_.1, bf16[64,2048]{1,0:T(8,128)(2,1)} %copy-done.20, bf16[64,2048]{1,0:T(8,128)(2,1)} %copy-done.21), custom_call_target="tpu_custom_call" | custom-call | bytes 3145728 | tf_op jit(solution)/shard_map/pack/pallas_call | solution.py:61
  39.5 2.3 %collective-permute-start.8 = (bf16[2,6,64,128]{3,2,1,0:T(8,128)(2,1)}, bf16[2,6,64,128]{3,2,1,0:T(8,128)(2,1)S(1)}, u32[]{:S(2)}, u32[]{:S(2)}) collective-permute-start(bf16[2,6,64,128]{3,2,1,0:T(8,128)(2,1)} %get-tuple-element.35), channel_id=1, source_target_pairs={{0,192},{4,196},{8,200},{12,204},{16,208},{20,212},{24,216},{28,22... | collective-permute-start | bytes 589832 | tf_op jit(solution)/shard_map/ppermute | solution.py:37
  41.9 2.7 %collective-permute-start.19 = (bf16[32,2048]{1,0:T(8,128)(2,1)S(1)}, bf16[32,2048]{1,0:T(8,128)(2,1)S(1)}, u32[]{:S(2)}, u32[]{:S(2)}) collective-permute-start(bf16[32,2048]{1,0:T(8,128)(2,1)S(1)} %slice.171), channel_id=1, source_target_pairs={{0,56},{4,60},{8,0},{12,4},{16,8},{20,12},{24,16},{28,20},{32,24},... | collective-permute-start | bytes 393224 | tf_op jit(solution)/shard_map/ppermute | solution.py:37
  45.8 4.1 %agg_local.1.refs_4_.refs_6_.local_ref = f32[64,2048]{1,0:T(8,128)} custom-call(s32[64]{0:T(128)} %reshape.244.cols_ref, bf16[64,2048]{1,0:T(8,128)(2,1)} %refs_1_.1, bf16[16,8,128,128]{3,2,1,0:T(8,128)(2,1)} %bitcast.34), custom_call_target="tpu_custom_call" | custom-call | flops 134217728 | bytes 3145728 | tf_op jit(solution)/shard_map/agg_local/pallas_call | solution.py:97
  50.0 2.0 %pack.4 = (bf16[2,4,64,128]{3,2,1,0:T(8,128)(2,1)}, bf16[2,4,64,128]{3,2,1,0:T(8,128)(2,1)}, bf16[2,4,64,128]{3,2,1,0:T(8,128)(2,1)}, bf16[2,4,64,128]{3,2,1,0:T(8,128)(2,1)}) custom-call(s32[128]{0:T(128)} %reshape.245.refs_0_, bf16[64,2048]{1,0:T(8,128)(2,1)} %copy-done.22, bf16[64,2048]{1,0:T(8,128)(2,1)} %copy-done.23, ...), custom_call_target="tpu_custom_call" | custom-call | bytes 3145728 | tf_op jit(solution)/shard_map/pack/pallas_call | solution.py:61
  52.8 2.3 %pack.5 = (bf16[2,6,64,128]{3,2,1,0:T(8,128)(2,1)}, bf16[2,6,64,128]{3,2,1,0:T(8,128)(2,1)}, bf16[2,6,64,128]{3,2,1,0:T(8,128)(2,1)}, bf16[2,6,64,128]{3,2,1,0:T(8,128)(2,1)}) custom-call(s32[128]{0:T(128)} %reshape.245.refs_0_, bf16[64,2048]{1,0:T(8,128)(2,1)} %copy-done.3, bf16[64,2048]{1,0:T(8,128)(2,1)} %copy-done.4, bf16[32,2048]{1,0:T(8,128)(2,1)} %copy-done.24, ...), custom_call_target="tpu_custom_call" | custom-call | bytes 3145728 | tf_op jit(solution)/shard_map/pack/pallas_call | solution.py:61
  55.0 2.1 %collective-permute-start.22 = (bf16[2,6,64,128]{3,2,1,0:T(8,128)(2,1)}, bf16[2,6,64,128]{3,2,1,0:T(8,128)(2,1)S(1)}, u32[]{:S(2)}, u32[]{:S(2)}) collective-permute-start(bf16[2,6,64,128]{3,2,1,0:T(8,128)(2,1)} %get-tuple-element.43), channel_id=1, source_target_pairs={{0,192},{4,196},{8,200},{12,204},{16,208},{20,212},{24,216},{28,22... | collective-permute-start | bytes 589832 | tf_op jit(solution)/shard_map/ppermute | solution.py:37
  57.1 1.8 collective-permute-start.21
  59.0 6.1 %collective-permute-start.9 = (bf16[4,6,64,128]{3,2,1,0:T(8,128)(2,1)S(1)}, bf16[4,6,64,128]{3,2,1,0:T(8,128)(2,1)S(1)}, u32[]{:S(2)}, u32[]{:S(2)}) collective-permute-start(bf16[4,6,64,128]{3,2,1,0:T(8,128)(2,1)S(1)} %pad_maximum_fusion), channel_id=1, source_target_pairs={{0,4},{4,0},{8,12},{12,8},{16,20},{20,16},{24,28},{28,24},{32,36},... | collective-permute-start | bytes 1179656 | tf_op jit(solution)/shard_map/ppermute | solution.py:37
  67.0 3.3 %collective-permute-start.13 = (bf16[2,4,64,128]{3,2,1,0:T(8,128)(2,1)S(1)}, bf16[2,4,64,128]{3,2,1,0:T(8,128)(2,1)S(1)}, u32[]{:S(2)}, u32[]{:S(2)}) collective-permute-start(bf16[2,4,64,128]{3,2,1,0:T(8,128)(2,1)S(1)} %copy-done.29), channel_id=1, source_target_pairs={{0,128},{4,132},{8,136},{12,140},{16,144},{20,148},{24,152},{28,15... | collective-permute-start | bytes 393224 | tf_op jit(solution)/shard_map/ppermute | solution.py:37
  70.5 3.2 %collective-permute-start.23 = (bf16[4,6,64,128]{3,2,1,0:T(8,128)(2,1)S(1)}, bf16[4,6,64,128]{3,2,1,0:T(8,128)(2,1)S(1)}, u32[]{:S(2)}, u32[]{:S(2)}) collective-permute-start(bf16[4,6,64,128]{3,2,1,0:T(8,128)(2,1)S(1)} %pad_maximum_fusion.1), channel_id=1, source_target_pairs={{0,4},{4,0},{8,12},{12,8},{16,20},{20,16},{24,28},{28,24},{32,36},... | collective-permute-start | bytes 1179656 | tf_op jit(solution)/shard_map/ppermute | solution.py:37
  73.8 1.6 collective-permute-done.14.refs_8_
  76.3 1.6 collective-permute-start.15
  80.5 4.9 %agg_remote.1.own_ref = bf16[64,2048]{1,0:T(8,128)(2,1)} custom-call(s32[64]{0:T(128)} %copy-done.26, bf16[16,8,128,128]{3,2,1,0:T(8,128)(2,1)} %bitcast.35, f32[64,2048]{1,0:T(8,128)} %agg_local.1.refs_4_.refs_6_.local_ref, bf16[2,6,64,128]{3,2,1,0:T(8,128)(2,1)} %get-tuple-element.32.refs_3_.refs_0_, bf16[2,6,64,128]{3,2,1,0:T(8,128)(2,1)} %copy-done.7, ...), custom_call_target="tpu_custom_call" | custom-call | flops 134217728 | bytes 5242880 | tf_op jit(solution)/shard_map/agg_remote/pallas_call | solution.py:147
  89.8 4.6 %collective-permute-done.24.low_ref = bf16[64,2048]{1,0:T(8,128)(2,1)S(1)} collective-permute-done((bf16[64,2048]{1,0:T(8,128)(2,1)}, bf16[64,2048]{1,0:T(8,128)(2,1)S(1)}, u32[]{:S(2)}, u32[]{:S(2)}) %collective-permute-start.24) | collective-permute-done | bytes 262176 | tf_op jit(solution)/shard_map/ppermute | solution.py:447
  94.4 6.6 %collective-permute-done.26.far_ref = bf16[64,2048]{1,0:T(8,128)(2,1)S(1)} collective-permute-done((bf16[64,2048]{1,0:T(8,128)(2,1)}, bf16[64,2048]{1,0:T(8,128)(2,1)S(1)}, u32[]{:S(2)}, u32[]{:S(2)}) %collective-permute-start.26) | collective-permute-done | bytes 262176 | tf_op jit(solution)/shard_map/ppermute | solution.py:447
  101.7 4.9 %mid.1 = (bf16[64,2048]{1,0:T(8,128)(2,1)}, bf16[64,2048]{1,0:T(8,128)(2,1)}, f32[64,256]{1,0:T(8,128)}, f32[64,128]{1,0:T(8,128)}) custom-call(s32[1]{0:T(128)} %bitcast.me_ref, bf16[64,2048]{1,0:T(8,128)(2,1)} %agg_remote.1.own_ref, bf16[64,2048]{1,0:T(8,128)(2,1)} %copy-done.16, bf16[64,2048]{1,0:T(8,128)(2,1)} %copy-done.17, ...), custom_call_target="tpu_custom_call" | custom-call | flops 402653184 | bytes 3145728 | tf_op jit(solution)/shard_map/mid/pallas_call | solution.py:229
  109.2 7.1 %all-to-all-start = ((f32[64,1,259]{2,1,0:T(1,128)}), f32[64,1,259]{2,1,0:T(1,128)S(1)}, u32[]{:S(2)}, u32[]{:S(2)}) async-start(f32[64,1,259]{2,1,0:T(1,128)} %copy.39), calls=%async_computation | async-start | bytes 196608 | tf_op jit(solution)/shard_map/all_to_all | solution.py:463
  116.4 4.6 %back_remote.1 = bf16[64,136,128]{2,1,0:T(8,128)(2,1)} custom-call(s32[64]{0:T(128)} %copy-done.27, bf16[64,2048]{1,0:T(8,128)(2,1)} %get-tuple-element.47.g_ref, bf16[16,8,128,128]{3,2,1,0:T(8,128)(2,1)} %bitcast.36), custom_call_target="tpu_custom_call" | custom-call | flops 134217728 | bytes 5242880 | tf_op jit(solution)/shard_map/back_remote/pallas_call | solution.py:295
  121.0 5.5 %all-to-all-done = f32[64,1,259]{2,1,0:T(1,128)S(1)} async-done(((f32[64,1,259]{2,1,0:T(1,128)}), f32[64,1,259]{2,1,0:T(1,128)S(1)}, u32[]{:S(2)}, u32[]{:S(2)}) %all-to-all-start) | async-done | bytes 66336 | tf_op jit(solution)/shard_map/all_to_all | solution.py:463
  127.3 4.8 %all-to-all-start.1 = ((bf16[64,136,128]{2,1,0:T(8,128)(2,1)}), bf16[64,136,128]{2,1,0:T(8,128)(2,1)S(1)}, u32[]{:S(2)}, u32[]{:S(2)}) async-start(bf16[64,136,128]{2,1,0:T(8,128)(2,1)} %broadcast_dynamic-update-slice_fusion), calls=%async_computation.1 | async-start | bytes 4456448 | tf_op jit(solution)/shard_map/all_to_all | solution.py:473
  132.2 3.9 %back_local.1.local_ref = f32[64,2048]{1,0:T(8,128)} custom-call(s32[64]{0:T(128)} %reshape.244.cols_ref, bf16[64,2048]{1,0:T(8,128)(2,1)} %get-tuple-element.47.g_ref, bf16[16,8,128,128]{3,2,1,0:T(8,128)(2,1)} %bitcast.37), custom_call_target="tpu_custom_call" | custom-call | flops 134217728 | bytes 3145728 | tf_op jit(solution)/shard_map/back_local/pallas_call | solution.py:333
  136.9 49.1 %all-to-all-done.1.recv_ref = bf16[64,136,128]{2,1,0:T(8,128)(2,1)S(1)} async-done(((bf16[64,136,128]{2,1,0:T(8,128)(2,1)}), bf16[64,136,128]{2,1,0:T(8,128)(2,1)S(1)}, u32[]{:S(2)}, u32[]{:S(2)}) %all-to-all-start.1) | async-done | bytes 2228256 | tf_op jit(solution)/shard_map/all_to_all | solution.py:473
  187.5 3.7 %finish.1 = f32[64,2048]{1,0:T(8,128)} custom-call(s32[128]{0:T(128)} %reshape.247.wanted_ref, bf16[64,136,128]{2,1,0:T(8,128)(2,1)} %copy-done, f32[64,2048]{1,0:T(8,128)} %back_local.1.local_ref), custom_call_target="tpu_custom_call" | custom-call | flops 1114112 | bytes 4194304 | tf_op jit(solution)/shard_map/finish/pallas_call | solution.py:367
  (157 shorter events, 25.6 us)
Async XLA Ops:
  7.2 93.8 %all-gather.2.cloned.1.call-start = ((), (), s32[]{:S(2)}) async-start(), calls=%async_computation.2 | async-start | bytes 1556480 | tf_op jit(solution)/shard_map/all_gather | solution.py:442
  7.2 11.8 %collective-permute-start.4 = (bf16[64,2048]{1,0:T(8,128)(2,1)}, bf16[64,2048]{1,0:T(8,128)(2,1)S(1)}, u32[]{:S(2)}, u32[]{:S(2)}) collective-permute-start(bf16[64,2048]{1,0:T(8,128)(2,1)} %refs_1_.1), channel_id=1, source_target_pairs={{0,56},{4,60},{8,0},{12,4},{16,8},{20,12},{24,16},{28,20},{32,24},... | collective-permute-start | bytes 786440 | tf_op jit(solution)/shard_map/ppermute | solution.py:37
  13.7 8.6 %collective-permute-start.5 = (bf16[64,2048]{1,0:T(8,128)(2,1)}, bf16[64,2048]{1,0:T(8,128)(2,1)S(1)}, u32[]{:S(2)}, u32[]{:S(2)}) collective-permute-start(bf16[64,2048]{1,0:T(8,128)(2,1)} %refs_1_.1), channel_id=1, source_target_pairs={{0,8},{4,12},{8,16},{12,20},{16,24},{20,28},{24,32},{28,36},{32,40... | collective-permute-start | bytes 786440 | tf_op jit(solution)/shard_map/ppermute | solution.py:37
  17.4 32.5 %copy-start.26 = (s32[64]{0:T(128)}, s32[64]{0:T(128)S(1)}, u32[]{:S(2)}) copy-start(s32[64]{0:T(128)S(1)} %get-tuple-element.59.slots_ref) | copy-start | bytes 772
  17.4 32.5 %copy-start.27 = (s32[64]{0:T(128)}, s32[64]{0:T(128)S(1)}, u32[]{:S(2)}) copy-start(s32[64]{0:T(128)S(1)} %get-tuple-element.58.slots_ref) | copy-start | bytes 772
  19.0 7.4 %collective-permute-start.10 = (bf16[64,2048]{1,0:T(8,128)(2,1)S(1)}, bf16[64,2048]{1,0:T(8,128)(2,1)S(1)}, u32[]{:S(2)}, u32[]{:S(2)}) collective-permute-start(bf16[64,2048]{1,0:T(8,128)(2,1)S(1)} %collective-permute-done.4.refs_2_), channel_id=1, source_target_pairs={{0,56},{4,60},{8,0},{12,4},{16,8},{20,12},{24,16},{28,20},{32,24},... | collective-permute-start | bytes 786440 | tf_op jit(solution)/shard_map/ppermute | solution.py:37
  22.3 7.5 %collective-permute-start.11 = (bf16[64,2048]{1,0:T(8,128)(2,1)S(1)}, bf16[64,2048]{1,0:T(8,128)(2,1)S(1)}, u32[]{:S(2)}, u32[]{:S(2)}) collective-permute-start(bf16[64,2048]{1,0:T(8,128)(2,1)S(1)} %collective-permute-done.5.refs_3_), channel_id=1, source_target_pairs={{0,8},{4,12},{8,16},{12,20},{16,24},{20,28},{24,32},{28,36},{32,40... | collective-permute-start | bytes 786440 | tf_op jit(solution)/shard_map/ppermute | solution.py:37
  22.6 7.2 %collective-permute-start = (s32[4,16]{1,0:T(4,128)S(1)}, s32[4,16]{1,0:T(4,128)S(1)}, u32[]{:S(2)}, u32[]{:S(2)}) collective-permute-start(s32[4,16]{1,0:T(4,128)S(1)} %squeeze.12), channel_id=1, source_target_pairs={{0,4},{4,0},{8,12},{12,8},{16,20},{20,16},{24,28},{28,24},{32,36},... | collective-permute-start | bytes 776 | tf_op jit(solution)/shard_map/ppermute | solution.py:37
  26.3 15.5 %collective-permute-start.16 = (bf16[64,2048]{1,0:T(8,128)(2,1)S(1)}, bf16[64,2048]{1,0:T(8,128)(2,1)S(1)}, u32[]{:S(2)}, u32[]{:S(2)}) collective-permute-start(bf16[64,2048]{1,0:T(8,128)(2,1)S(1)} %collective-permute-done.10.refs_1_), channel_id=1, source_target_pairs={{0,56},{4,60},{8,0},{12,4},{16,8},{20,12},{24,16},{28,20},{32,24},... | collective-permute-start | bytes 786440 | tf_op jit(solution)/shard_map/ppermute | solution.py:37
  29.8 12.0 %collective-permute-start.17 = (bf16[64,2048]{1,0:T(8,128)(2,1)S(1)}, bf16[64,2048]{1,0:T(8,128)(2,1)S(1)}, u32[]{:S(2)}, u32[]{:S(2)}) collective-permute-start(bf16[64,2048]{1,0:T(8,128)(2,1)S(1)} %collective-permute-done.11.refs_2_), channel_id=1, source_target_pairs={{0,8},{4,12},{8,16},{12,20},{16,24},{20,28},{24,32},{28,36},{32,40... | collective-permute-start | bytes 786440 | tf_op jit(solution)/shard_map/ppermute | solution.py:37
  29.8 5.1 %collective-permute-start.3 = (s32[2,16]{1,0:T(2,128)S(1)}, s32[2,16]{1,0:T(2,128)S(1)}, u32[]{:S(2)}, u32[]{:S(2)}) collective-permute-start(s32[2,16]{1,0:T(2,128)S(1)} %bitcast.49), channel_id=1, source_target_pairs={{0,64},{4,68},{8,72},{12,76},{16,80},{20,84},{24,88},{28,92},{32,9... | collective-permute-start | bytes 392 | tf_op jit(solution)/shard_map/ppermute | solution.py:37
  31.2 4.0 %collective-permute-start.2 = (s32[2,16]{1,0:T(2,128)S(1)}, s32[2,16]{1,0:T(2,128)S(1)}, u32[]{:S(2)}, u32[]{:S(2)}) collective-permute-start(s32[2,16]{1,0:T(2,128)S(1)} %bitcast.47), channel_id=1, source_target_pairs={{0,128},{4,132},{8,136},{12,140},{16,144},{20,148},{24,152},{28,15... | collective-permute-start | bytes 392 | tf_op jit(solution)/shard_map/ppermute | solution.py:37
  33.8 2.8 %collective-permute-start.1 = (s32[2,16]{1,0:T(2,128)S(1)}, s32[2,16]{1,0:T(2,128)S(1)}, u32[]{:S(2)}, u32[]{:S(2)}) collective-permute-start(s32[2,16]{1,0:T(2,128)S(1)} %bitcast.45), channel_id=1, source_target_pairs={{0,192},{4,196},{8,200},{12,204},{16,208},{20,212},{24,216},{28,22... | collective-permute-start | bytes 392 | tf_op jit(solution)/shard_map/ppermute | solution.py:37
  39.5 19.4 %collective-permute-start.8 = (bf16[2,6,64,128]{3,2,1,0:T(8,128)(2,1)}, bf16[2,6,64,128]{3,2,1,0:T(8,128)(2,1)S(1)}, u32[]{:S(2)}, u32[]{:S(2)}) collective-permute-start(bf16[2,6,64,128]{3,2,1,0:T(8,128)(2,1)} %get-tuple-element.35), channel_id=1, source_target_pairs={{0,192},{4,196},{8,200},{12,204},{16,208},{20,212},{24,216},{28,22... | collective-permute-start | bytes 589832 | tf_op jit(solution)/shard_map/ppermute | solution.py:37
  41.8 10.3 %collective-permute-start.18 = (bf16[32,2048]{1,0:T(8,128)(2,1)S(1)}, bf16[32,2048]{1,0:T(8,128)(2,1)S(1)}, u32[]{:S(2)}, u32[]{:S(2)}) collective-permute-start(bf16[32,2048]{1,0:T(8,128)(2,1)S(1)} %slice.170), channel_id=1, source_target_pairs={{0,8},{4,12},{8,16},{12,20},{16,24},{20,28},{24,32},{28,36},{32,40... | collective-permute-start | bytes 393224 | tf_op jit(solution)/shard_map/ppermute | solution.py:37
  41.9 10.2 %collective-permute-start.19 = (bf16[32,2048]{1,0:T(8,128)(2,1)S(1)}, bf16[32,2048]{1,0:T(8,128)(2,1)S(1)}, u32[]{:S(2)}, u32[]{:S(2)}) collective-permute-start(bf16[32,2048]{1,0:T(8,128)(2,1)S(1)} %slice.171), channel_id=1, source_target_pairs={{0,56},{4,60},{8,0},{12,4},{16,8},{20,12},{24,16},{28,20},{32,24},... | collective-permute-start | bytes 393224 | tf_op jit(solution)/shard_map/ppermute | solution.py:37
  44.6 14.3 %collective-permute-start.7 = (bf16[2,6,64,128]{3,2,1,0:T(8,128)(2,1)}, bf16[2,6,64,128]{3,2,1,0:T(8,128)(2,1)S(1)}, u32[]{:S(2)}, u32[]{:S(2)}) collective-permute-start(bf16[2,6,64,128]{3,2,1,0:T(8,128)(2,1)} %get-tuple-element.34), channel_id=1, source_target_pairs={{0,128},{4,132},{8,136},{12,140},{16,144},{20,148},{24,152},{28,15... | collective-permute-start | bytes 589832 | tf_op jit(solution)/shard_map/ppermute | solution.py:37
  44.6 14.3 %collective-permute-start.6 = (bf16[2,6,64,128]{3,2,1,0:T(8,128)(2,1)}, bf16[2,6,64,128]{3,2,1,0:T(8,128)(2,1)S(1)}, u32[]{:S(2)}, u32[]{:S(2)}) collective-permute-start(bf16[2,6,64,128]{3,2,1,0:T(8,128)(2,1)} %get-tuple-element.33), channel_id=1, source_target_pairs={{0,64},{4,68},{8,72},{12,76},{16,80},{20,84},{24,88},{28,92},{32,9... | collective-permute-start | bytes 589832 | tf_op jit(solution)/shard_map/ppermute | solution.py:37
  55.0 11.9 %collective-permute-start.22 = (bf16[2,6,64,128]{3,2,1,0:T(8,128)(2,1)}, bf16[2,6,64,128]{3,2,1,0:T(8,128)(2,1)S(1)}, u32[]{:S(2)}, u32[]{:S(2)}) collective-permute-start(bf16[2,6,64,128]{3,2,1,0:T(8,128)(2,1)} %get-tuple-element.43), channel_id=1, source_target_pairs={{0,192},{4,196},{8,200},{12,204},{16,208},{20,212},{24,216},{28,22... | collective-permute-start | bytes 589832 | tf_op jit(solution)/shard_map/ppermute | solution.py:37
  57.1 13.2 %collective-permute-start.21 = (bf16[2,6,64,128]{3,2,1,0:T(8,128)(2,1)}, bf16[2,6,64,128]{3,2,1,0:T(8,128)(2,1)S(1)}, u32[]{:S(2)}, u32[]{:S(2)}) collective-permute-start(bf16[2,6,64,128]{3,2,1,0:T(8,128)(2,1)} %get-tuple-element.42), channel_id=1, source_target_pairs={{0,128},{4,132},{8,136},{12,140},{16,144},{20,148},{24,152},{28,15... | collective-permute-start | bytes 589832 | tf_op jit(solution)/shard_map/ppermute | solution.py:37
  58.9 11.6 %collective-permute-start.20 = (bf16[2,6,64,128]{3,2,1,0:T(8,128)(2,1)}, bf16[2,6,64,128]{3,2,1,0:T(8,128)(2,1)S(1)}, u32[]{:S(2)}, u32[]{:S(2)}) collective-permute-start(bf16[2,6,64,128]{3,2,1,0:T(8,128)(2,1)} %get-tuple-element.41), channel_id=1, source_target_pairs={{0,64},{4,68},{8,72},{12,76},{16,80},{20,84},{24,88},{28,92},{32,9... | collective-permute-start | bytes 589832 | tf_op jit(solution)/shard_map/ppermute | solution.py:37
  59.0 18.9 %collective-permute-start.9 = (bf16[4,6,64,128]{3,2,1,0:T(8,128)(2,1)S(1)}, bf16[4,6,64,128]{3,2,1,0:T(8,128)(2,1)S(1)}, u32[]{:S(2)}, u32[]{:S(2)}) collective-permute-start(bf16[4,6,64,128]{3,2,1,0:T(8,128)(2,1)S(1)} %pad_maximum_fusion), channel_id=1, source_target_pairs={{0,4},{4,0},{8,12},{12,8},{16,20},{20,16},{24,28},{28,24},{32,36},... | collective-permute-start | bytes 1179656 | tf_op jit(solution)/shard_map/ppermute | solution.py:37
  65.1 11.1 %collective-permute-start.12 = (bf16[2,4,64,128]{3,2,1,0:T(8,128)(2,1)S(1)}, bf16[2,4,64,128]{3,2,1,0:T(8,128)(2,1)S(1)}, u32[]{:S(2)}, u32[]{:S(2)}) collective-permute-start(bf16[2,4,64,128]{3,2,1,0:T(8,128)(2,1)S(1)} %copy-done.28), channel_id=1, source_target_pairs={{0,64},{4,68},{8,72},{12,76},{16,80},{20,84},{24,88},{28,92},{32,9... | collective-permute-start | bytes 393224 | tf_op jit(solution)/shard_map/ppermute | solution.py:37
  67.0 9.2 %collective-permute-start.13 = (bf16[2,4,64,128]{3,2,1,0:T(8,128)(2,1)S(1)}, bf16[2,4,64,128]{3,2,1,0:T(8,128)(2,1)S(1)}, u32[]{:S(2)}, u32[]{:S(2)}) collective-permute-start(bf16[2,4,64,128]{3,2,1,0:T(8,128)(2,1)S(1)} %copy-done.29), channel_id=1, source_target_pairs={{0,128},{4,132},{8,136},{12,140},{16,144},{20,148},{24,152},{28,15... | collective-permute-start | bytes 393224 | tf_op jit(solution)/shard_map/ppermute | solution.py:37
  70.3 5.0 %collective-permute-start.14 = (bf16[2,4,64,128]{3,2,1,0:T(8,128)(2,1)S(1)}, bf16[2,4,64,128]{3,2,1,0:T(8,128)(2,1)S(1)}, u32[]{:S(2)}, u32[]{:S(2)}) collective-permute-start(bf16[2,4,64,128]{3,2,1,0:T(8,128)(2,1)S(1)} %copy-done.30), channel_id=1, source_target_pairs={{0,192},{4,196},{8,200},{12,204},{16,208},{20,212},{24,216},{28,22... | collective-permute-start | bytes 393224 | tf_op jit(solution)/shard_map/ppermute | solution.py:37
  70.5 8.6 %collective-permute-start.23 = (bf16[4,6,64,128]{3,2,1,0:T(8,128)(2,1)S(1)}, bf16[4,6,64,128]{3,2,1,0:T(8,128)(2,1)S(1)}, u32[]{:S(2)}, u32[]{:S(2)}) collective-permute-start(bf16[4,6,64,128]{3,2,1,0:T(8,128)(2,1)S(1)} %pad_maximum_fusion.1), channel_id=1, source_target_pairs={{0,4},{4,0},{8,12},{12,8},{16,20},{20,16},{24,28},{28,24},{32,36},... | collective-permute-start | bytes 1179656 | tf_op jit(solution)/shard_map/ppermute | solution.py:37
  76.3 2.8 %collective-permute-start.15 = (bf16[4,4,64,128]{3,2,1,0:T(8,128)(2,1)S(1)}, bf16[4,4,64,128]{3,2,1,0:T(8,128)(2,1)S(1)}, u32[]{:S(2)}, u32[]{:S(2)}) collective-permute-start(bf16[4,4,64,128]{3,2,1,0:T(8,128)(2,1)S(1)} %pad_maximum_fusion.2), channel_id=1, source_target_pairs={{0,4},{4,0},{8,12},{12,8},{16,20},{20,16},{24,28},{28,24},{32,36},... | collective-permute-start | bytes 786440 | tf_op jit(solution)/shard_map/ppermute | solution.py:37
  85.4 8.9 %collective-permute-start.24 = (bf16[64,2048]{1,0:T(8,128)(2,1)}, bf16[64,2048]{1,0:T(8,128)(2,1)S(1)}, u32[]{:S(2)}, u32[]{:S(2)}) collective-permute-start(bf16[64,2048]{1,0:T(8,128)(2,1)} %agg_remote.1.own_ref), channel_id=1, source_target_pairs={{0,1},{1,2},{2,3},{3,0},{4,5},{5,6},{6,7},{7,4},{8,9},{9,10},{10,1... | collective-permute-start | bytes 786440 | tf_op jit(solution)/shard_map/ppermute | solution.py:447
  86.6 7.7 %collective-permute-start.25 = (bf16[64,2048]{1,0:T(8,128)(2,1)}, bf16[64,2048]{1,0:T(8,128)(2,1)S(1)}, u32[]{:S(2)}, u32[]{:S(2)}) collective-permute-start(bf16[64,2048]{1,0:T(8,128)(2,1)} %agg_remote.1.own_ref), channel_id=1, source_target_pairs={{0,3},{1,0},{2,1},{3,2},{4,7},{5,4},{6,5},{7,6},{8,11},{9,8},{10,9... | collective-permute-start | bytes 786440 | tf_op jit(solution)/shard_map/ppermute | solution.py:447
  88.1 12.9 %collective-permute-start.26 = (bf16[64,2048]{1,0:T(8,128)(2,1)}, bf16[64,2048]{1,0:T(8,128)(2,1)S(1)}, u32[]{:S(2)}, u32[]{:S(2)}) collective-permute-start(bf16[64,2048]{1,0:T(8,128)(2,1)} %agg_remote.1.own_ref), channel_id=1, source_target_pairs={{0,2},{1,3},{2,0},{3,1},{4,6},{5,7},{6,4},{7,5},{8,10},{9,11},{10,... | collective-permute-start | bytes 786440 | tf_op jit(solution)/shard_map/ppermute | solution.py:447
  109.2 17.3 %all-to-all-start = ((f32[64,1,259]{2,1,0:T(1,128)}), f32[64,1,259]{2,1,0:T(1,128)S(1)}, u32[]{:S(2)}, u32[]{:S(2)}) async-start(f32[64,1,259]{2,1,0:T(1,128)} %copy.39), calls=%async_computation | async-start | bytes 196608 | tf_op jit(solution)/shard_map/all_to_all | solution.py:463
  127.3 58.7 %all-to-all-start.1 = ((bf16[64,136,128]{2,1,0:T(8,128)(2,1)}), bf16[64,136,128]{2,1,0:T(8,128)(2,1)S(1)}, u32[]{:S(2)}, u32[]{:S(2)}) async-start(bf16[64,136,128]{2,1,0:T(8,128)(2,1)} %broadcast_dynamic-update-slice_fusion), calls=%async_computation.1 | async-start | bytes 4456448 | tf_op jit(solution)/shard_map/all_to_all | solution.py:473
  (29 other events, 288.9 us)
Sparse Core Ops, SparseCore 0:
  16.4 25.5 all-gather.1

commit v3 on v2

--- a/solution.py
+++ b/solution.py
@@ -23,46 +23,51 @@
 NY, NZ, NC = 4, 8, 2
 CAP = 2
 ORDER = (0, 1, 7, 2, 6, 3, 5, 4)
-GROUPS = ((0, 3), (3, 5), (5, 8))
+GROUPS = ((0, 5), (5, 8))
+PEERS = NY * NC
 PER = NZ * CAP
 
 
-def shift(x, dy=0, dz=0, dc=0):
+def shift(x, dz):
     pairs = []
     for y in range(NY):
         for z in range(NZ):
             for c in range(NC):
-                to = ((y + dy) % NY * NZ + (z + dz) % NZ) * NC + (c + dc) % NC
-                pairs.append(((y * NZ + z) * NC + c, to))
+                pairs.append(((y * NZ + z) * NC + c, (y * NZ + (z + dz) % NZ) * NC + c))
     return lax.ppermute(x, "rows", pairs)
 
 
+def swap(x):
+    groups = [[(y * NZ + z) * NC + c for y in range(NY) for c in range(NC)] for z in range(NZ)]
+    return lax.all_to_all(
+        x, "rows", split_axis=0, concat_axis=0, tiled=True, axis_index_groups=groups
+    )
+
+
 def pack_kernel(first, count, split, *refs):
-    wanted_ref, sources, outs = refs[0], refs[1 : 1 + count + split], refs[-NY:]
-    width, block = outs[0].shape[2], outs[0].shape[3]
-    for ys in range(NY):
-        for cs in range(NC):
-            for q in range(count * CAP):
-                w = wanted_ref[(ys * NC + cs) * PER + first * CAP + q]
-                where = lanes(jnp.maximum(w, 0), block)
-                j = q // CAP
-                if split and j == count - 1:
-                    outs[ys][cs, q, : width // 2] = sources[j][:, where]
-                    outs[ys][cs, q, width // 2 :] = sources[j + 1][:, where]
-                else:
-                    outs[ys][cs, q] = sources[j][:, where]
+    wanted_ref, sources, out_ref = refs[0], refs[1 : 1 + count + split], refs[-1]
+    width, block = out_ref.shape[2], out_ref.shape[3]
+    for p in range(PEERS):
+        for q in range(count * CAP):
+            w = wanted_ref[p * PER + first * CAP + q]
+            where = lanes(jnp.maximum(w, 0), block)
+            j = q // CAP
+            if split and j == count - 1:
+                out_ref[p, q, : width // 2] = sources[j][:, where]
+                out_ref[p, q, width // 2 :] = sources[j + 1][:, where]
+            else:
+                out_ref[p, q] = sources[j][:, where]
 
 
 def pack(group, wanted, sources, block, after):
     first, last = group
     count = last - first
     width = sources[0].shape[0]
-    shape = jax.ShapeDtypeStruct((NC, count * CAP, width, block), BF)
     return pl.pallas_call(
         functools.partial(pack_kernel, first, count, len(sources) > count),
-        out_shape=[shape] * NY,
+        out_shape=jax.ShapeDtypeStruct((PEERS, count * CAP, width, block), BF),
         in_specs=[SMEM] + [VMEM] * len(sources) + [ANY] * len(after),
-        out_specs=[VMEM] * NY,
+        out_specs=VMEM,
         name="pack",
         cost_estimate=pl.CostEstimate(flops=0, bytes_accessed=3 << 20, transcendentals=0),
     )(wanted, *sources, *after)
@@ -118,13 +123,9 @@
 
     @pl.when(i == 0)
     def _():
-        n = 0
-        for first, last in GROUPS:
-            size = (last - first) * CAP
-            for ys in range(NY):
-                recv_ref[pl.ds(ys * PER + first * CAP, size)] = parts[n + ys][0]
-                recv_ref[pl.ds((NY + ys) * PER + first * CAP, size)] = parts[n + NY][ys]
-            n += NY + 1
+        for part, (first, last) in zip(parts, GROUPS):
+            for p in range(PEERS):
+                recv_ref[pl.ds(p * PER + first * CAP, (last - first) * CAP)] = part[p]
 
     for rr in range(STEP):
         acc = local_ref[:, rr * block : (rr + 1) * block]
@@ -140,10 +141,7 @@
     row_blocks, per_block, block, _ = tiles.shape
     rem = per_block - TL
     width = local.shape[0]
-    specs = []
-    for n, part in enumerate(parts):
-        lead = 1 if n % (NY + 1) < NY else NY
-        specs.append(pl.BlockSpec((lead,) + part.shape[1:], lambda i: (0, 0, 0, 0)))
+    specs = [pl.BlockSpec(part.shape, lambda i: (0, 0, 0, 0)) for part in parts]
     return pl.pallas_call(
         agg_remote_kernel,
         grid=(row_blocks // STEP,),
@@ -155,7 +153,7 @@
         ]
         + specs,
         out_specs=pl.BlockSpec((width, STEP * block), lambda i: (0, i)),
-        scratch_shapes=[pltpu.VMEM((NY * NC * PER, width, block), BF)],
+        scratch_shapes=[pltpu.VMEM((PEERS * PER, width, block), BF)],
         name="agg_remote",
         cost_estimate=pl.CostEstimate(
             flops=2 * width * row_blocks * rem * block * block, bytes_accessed=5 << 20, transcendentals=0
@@ -394,7 +392,7 @@
     per_block = tile_cols.shape[0] // row_blocks
     remote_count = row_blocks * (per_block - TL)
     place = lax.axis_index("rows")
-    y, z, c = place // (NZ * NC), place // NC % NZ, place % NC
+    z = place // NC % NZ
 
     grid = tile_cols.reshape(row_blocks, per_block)
     tiles = tile_values.reshape(row_blocks, per_block, block, block)
@@ -408,38 +406,33 @@
     slots = owner * CAP + rank
     ahead = (owner // NC - z) & (NZ - 1)
     pos = jnp.maximum(jnp.where(ahead <= NZ // 2, 2 * ahead - 1, 2 * (NZ - ahead)), 0)
-    back = (y - owner // (NZ * NC)) & (NY - 1)
-    other = (owner ^ c) & 1
-    near = ((other * NY + back) * NZ + pos) * CAP + rank
+    near = ((owner // (NZ * NC) * NC + owner % NC) * NZ + pos) * CAP + rank
 
     def table(index):
         hit = index[None, :] == jnp.arange(peers * CAP)[:, None]
         return jnp.max(jnp.where(hit, inside[None, :], -1), axis=1)
 
-    asked = table(near).reshape(NC, NY, PER)
-    asked = jnp.stack([asked[0], shift(asked[1], dc=1)], axis=1)
-    wanted = [asked[0]] + [shift(asked[ys], dy=-ys) for ys in range(1, NY)]
-    wanted = jnp.stack(wanted).reshape(-1)
-
-    up, down, parts = [feats], [feats], []
+    wanted = swap(table(near).reshape(PEERS, PER)).reshape(-1)
+
+    up, down = [feats], [feats]
     for k in range(1, NZ // 2):
-        up.append(shift(up[-1], dz=1))
-        down.append(shift(down[-1], dz=-1))
-    far_up = shift(up[-1][: width // 2], dz=1)
-    far_down = shift(down[-1][width // 2 :], dz=-1)
-    groups = ((feats, down[1], up[1]), (down[2], up[2]), (down[3], up[3], far_up, far_down))
-    after = []
-    agg = agg_local(local_cols, feats, tiles)
-    for group, sources in zip(GROUPS, groups):
-        packs = pack(group, wanted, sources, block, after)
-        after = [packs[0], agg]
-        moved = [packs[0]] + [shift(packs[ys], dy=ys) for ys in range(1, NY)]
-        parts += moved
-        parts.append(shift(jnp.concatenate([m[1:] for m in moved]), dc=1))
+        if k == 3:
+            up[2], down[2], wanted = lax.optimization_barrier((up[2], down[2], wanted))
+        up.append(shift(up[-1], 1))
+        down.append(shift(down[-1], -1))
+    far_up = shift(up[-1][: width // 2], 1)
+    far_down = shift(down[-1][width // 2 :], -1)
 
     bias_cols = jnp.pad(jnp.stack(split_bf16(bias, 3), axis=1), ((0, 0), (0, 125)))
     packed = jnp.concatenate([cotangent, weight, bias_cols], axis=1)
     packed = lax.all_gather(packed, "feat", axis=0, tiled=True)
+
+    agg = agg_local(local_cols, feats, tiles)
+    near_sources = (feats, down[1], up[1], down[2], up[2])
+    far_sources = (down[3], up[3], far_up, far_down)
+    first = swap(pack(GROUPS[0], wanted, near_sources, block, []))
+    second = swap(pack(GROUPS[1], wanted, far_sources, block, [first, agg, packed]))
+    parts = [first, second]
 
     agg = agg_remote(near, parts, tiles, agg)
 
@@ -469,9 +462,10 @@
     rider = jnp.concatenate(split_bf16(total, 2) + [jnp.zeros((extra - 2 * span, block), BF)])
 
     send = back_remote(slots, g, tiles, peers, extra)
+    own = back_local(local_cols, g, tiles)
+    own, rider = lax.optimization_barrier((own, rider))
     send = send.at[:, CAP * width :].set(jnp.broadcast_to(rider, (peers, extra, block)))
     recv = lax.all_to_all(send, "rows", split_axis=0, concat_axis=0, tiled=True)
-    own = back_local(local_cols, g, tiles)
     grad_input = finish(holders, recv, own)
     totals = recv[:, CAP * width :].astype(F32)
     totals = (totals[:, :span] + totals[:, span : 2 * span]).reshape(peers, -1)

time: 199 us -> 205 us (1.030)
  blocking collectives: 0 us -> 27.9 us
  starting transfers between devices: 61 us -> 37.7 us
  waiting for transfers between devices: 74.6 us -> 77.8 us
    ppermute x24 -> x8, starting transfers between devices: 44.9 us -> 12.3 us  [shift(): return lax.ppermute(x, 'rows', pairs)]
    all_to_all x0 -> x2, blocking collectives: none -> 27.9 us  [swap(): lax.all_to_all(x, 'rows', split_axis=0, concat_axis=0, tiled=True, axis_i...]
    all_to_all x0 -> x1, starting transfers between devices: none -> 4.29 us  [swap(): lax.all_to_all(x, 'rows', split_axis=0, concat_axis=0, tiled=True, axis_i...]
    all_to_all x1, waiting for transfers between devices: 49.1 us -> 53.1 us  [local(): recv = lax.all_to_all(send, 'rows', split_axis=0, concat_axis=0, tiled=True)]
    all_to_all x1, starting transfers between devices: 4.82 us -> 8.74 us  [local(): recv = lax.all_to_all(send, 'rows', split_axis=0, concat_axis=0, tiled=True)]
    all_to_all x1, waiting for transfers between devices: 5.51 us -> 1.59 us  [local(): sums = lax.all_to_all(sums, 'rows', split_axis=0, concat_axis=0, tiled=True)]
    all_to_all x0 -> x1, waiting for transfers between devices: none -> 3.53 us  [swap(): lax.all_to_all(x, 'rows', split_axis=0, concat_axis=0, tiled=True, axis_i...]
    pallas_call x3 -> x2, Pallas kernels: 6.53 us -> 4.91 us  [pack(): pl.pallas_call(functools.partial(pack_kernel, first, count, len(sources)...]
  transfers between devices with their start and end apart: 30 -> 15, of which waited for: 11 -> 9; matrix products, arithmetic and copies ran while one was open for 4% -> 3% of each run, Pallas kernels for 12% -> 8%
where the time goes in v3:
time: 205 us; the launch traced here: 204 us
  waiting for transfers between devices  77.8 us (38%)
  starting transfers between devices  37.7 us (18%)
  Pallas kernels  30.7 us (15%)
  blocking collectives  27.9 us (14%)
  between operations  14.2 us (7%)
  local copies, waits for them, and re-layouts  9.79 us (5%)
  other arithmetic  5.49 us (3%)
    all_to_all x1, waiting for transfers between devices, local(): recv = lax.all_to_all(send, 'rows', split_axis=0, concat_axis=0, tiled=True)  53.1 us
    all_to_all x2, blocking collectives, swap(): lax.all_to_all(x, 'rows', split_axis=0, concat_axis=0, tiled=True, axis_i...  27.9 us
    ppermute x8, starting transfers between devices, shift(): return lax.ppermute(x, 'rows', pairs)  12.3 us
    ppermute x3, waiting for transfers between devices, local(): lax.ppermute(agg, 'feat', [(k, (k + s) % fpeers) for k in range(fpeers)])  10.6 us
    ppermute x8, waiting for transfers between devices, shift(): return lax.ppermute(x, 'rows', pairs)  8.97 us
    all_to_all x1, starting transfers between devices, local(): recv = lax.all_to_all(send, 'rows', split_axis=0, concat_axis=0, tiled=True)  8.74 us
    all_to_all x1, starting transfers between devices, local(): sums = lax.all_to_all(sums, 'rows', split_axis=0, concat_axis=0, tiled=True)  8.07 us
    pallas_call x2, Pallas kernels, pack(): pl.pallas_call(functools.partial(pack_kernel, first, count, len(sources)...  4.91 us
  transfers between devices with their start and end apart: 15, of which 9 were waited for; matrix products, arithmetic and copies ran while one was open for 3% of the time, Pallas kernels for 8%

profile of v3, /device:TPU:1, one launch (start us, length us, event | category | flops | bytes accessed | tf_op | source)
XLA Modules:
  0.0 203.6 jit_solution(3470023133671236374)
XLA Ops:
  7.2 2.5 %collective-permute-start = (bf16[64,2048]{1,0:T(8,128)(2,1)}, bf16[64,2048]{1,0:T(8,128)(2,1)S(1)}, u32[]{:S(2)}, u32[]{:S(2)}) collective-permute-start(bf16[64,2048]{1,0:T(8,128)(2,1)} %refs_1_.1), channel_id=1, source_target_pairs={{0,8},{4,12},{8,16},{12,20},{16,24},{20,28},{24,32},{28,36},{32,40... | collective-permute-start | bytes 786440 | tf_op jit(solution)/shard_map/ppermute | solution.py:37
  9.8 4.0 %collective-permute-start.2 = (bf16[64,2048]{1,0:T(8,128)(2,1)}, bf16[64,2048]{1,0:T(8,128)(2,1)S(1)}, u32[]{:S(2)}, u32[]{:S(2)}) collective-permute-start(bf16[64,2048]{1,0:T(8,128)(2,1)} %refs_1_.1), channel_id=1, source_target_pairs={{0,56},{4,60},{8,0},{12,4},{16,8},{20,12},{24,16},{28,20},{32,24},... | collective-permute-start | bytes 786440 | tf_op jit(solution)/shard_map/ppermute | solution.py:37
  14.6 1.7 fusion.1
  17.4 2.5 %collective-permute-done.refs_3_ = bf16[64,2048]{1,0:T(8,128)(2,1)S(1)} collective-permute-done((bf16[64,2048]{1,0:T(8,128)(2,1)}, bf16[64,2048]{1,0:T(8,128)(2,1)S(1)}, u32[]{:S(2)}, u32[]{:S(2)}) %collective-permute-start) | collective-permute-done | bytes 262176 | tf_op jit(solution)/shard_map/ppermute | solution.py:37
  20.0 2.7 %collective-permute-start.3 = (bf16[64,2048]{1,0:T(8,128)(2,1)S(1)}, bf16[64,2048]{1,0:T(8,128)(2,1)S(1)}, u32[]{:S(2)}, u32[]{:S(2)}) collective-permute-start(bf16[64,2048]{1,0:T(8,128)(2,1)S(1)} %collective-permute-done.2.refs_2_), channel_id=1, source_target_pairs={{0,56},{4,60},{8,0},{12,4},{16,8},{20,12},{24,16},{28,20},{32,24},... | collective-permute-start | bytes 786440 | tf_op jit(solution)/shard_map/ppermute | solution.py:37
  22.8 10.6 %all_to_all.36 = s32[8,1,16]{2,1,0:T(1,128)S(1)} all-to-all(s32[8,1,16]{2,1,0:T(1,128)S(1)} %bitcast.31), channel_id=1, replica_groups={{0,4,64,68,128,132,192,196},{8,12,72,76,136,140,200,204},{16,20,80,84,1..., dimensions={0} | all-to-all | bytes 1024 | tf_op jit(solution)/shard_map/all_to_all | solution.py:42
  36.6 2.7 %pack.2 = bf16[8,10,64,128]{3,2,1,0:T(8,128)(2,1)} custom-call(s32[128]{0:T(128)} %reshape.236.refs_0_, bf16[64,2048]{1,0:T(8,128)(2,1)} %refs_1_.1, bf16[64,2048]{1,0:T(8,128)(2,1)} %copy-done.8, bf16[64,2048]{1,0:T(8,128)(2,1)} %copy-done.7, bf16[64,2048]{1,0:T(8,128)(2,1)} %copy-done.11, bf16[64,2048]{1,0:T(8,128)(2,1)} %copy-done.9), custom_call_target="tpu_custom_call" | custom-call | bytes 3145728 | tf_op jit(solution)/shard_map/pack/pallas_call | solution.py:66
  39.4 4.3 %all-to-all-start.1 = ((bf16[8,10,64,128]{3,2,1,0:T(8,128)(2,1)}), bf16[8,10,64,128]{3,2,1,0:T(8,128)(2,1)S(1)}, u32[]{:S(2)}, u32[]{:S(2)}) async-start(bf16[8,10,64,128]{3,2,1,0:T(8,128)(2,1)} %pack.2), calls=%async_computation.1 | async-start | bytes 2621440 | tf_op jit(solution)/shard_map/all_to_all | solution.py:42
  43.9 1.2 collective-permute-start.5
  45.1 6.3 %collective-permute-done.4.refs_1_ = bf16[64,2048]{1,0:T(8,128)(2,1)S(1)} collective-permute-done((bf16[64,2048]{1,0:T(8,128)(2,1)S(1)}, bf16[64,2048]{1,0:T(8,128)(2,1)S(1)}, u32[]{:S(2)}, u32[]{:S(2)}) %collective-permute-start.4) | collective-permute-done | bytes 262176 | tf_op jit(solution)/shard_map/ppermute | solution.py:37
  51.4 1.5 collective-permute-start.7
  53.7 4.1 %agg_local.1.refs_6_.local_ref = f32[64,2048]{1,0:T(8,128)} custom-call(s32[64]{0:T(128)} %reshape.235.cols_ref, bf16[64,2048]{1,0:T(8,128)(2,1)} %refs_1_.1, bf16[16,8,128,128]{3,2,1,0:T(8,128)(2,1)} %bitcast.22), custom_call_target="tpu_custom_call" | custom-call | flops 134217728 | bytes 3145728 | tf_op jit(solution)/shard_map/agg_local/pallas_call | solution.py:102
  58.1 3.5 %all-to-all-done.1.refs_5_.refs_0_ = bf16[8,10,64,128]{3,2,1,0:T(8,128)(2,1)S(1)} async-done(((bf16[8,10,64,128]{3,2,1,0:T(8,128)(2,1)}), bf16[8,10,64,128]{3,2,1,0:T(8,128)(2,1)S(1)}, u32[]{:S(2)}, u32[]{:S(2)}) %all-to-all-start.1) | async-done | bytes 1310752 | tf_op jit(solution)/shard_map/all_to_all | solution.py:42
  61.6 1.1 copy-done
  62.7 2.2 %pack.3 = bf16[8,6,64,128]{3,2,1,0:T(8,128)(2,1)} custom-call(s32[128]{0:T(128)} %reshape.236.refs_0_, bf16[64,2048]{1,0:T(8,128)(2,1)} %copy-done.2, bf16[64,2048]{1,0:T(8,128)(2,1)} %copy-done.3, bf16[32,2048]{1,0:T(8,128)(2,1)} %copy-done.14, bf16[32,2048]{1,0:T(8,128)(2,1)} %copy-done.13, bf16[8,10,64,128]{3,2,1,0:T(8,128)(2,1)} %copy-done, ...), custom_call_target="tpu_custom_call" | custom-call | bytes 3145728 | tf_op jit(solution)/shard_map/pack/pallas_call | solution.py:66
  64.9 17.3 %all_to_all.37.refs_1_ = bf16[8,6,64,128]{3,2,1,0:T(8,128)(2,1)} all-to-all(bf16[8,6,64,128]{3,2,1,0:T(8,128)(2,1)} %pack.3), channel_id=1, replica_groups={{0,4,64,68,128,132,192,196},{8,12,72,76,136,140,200,204},{16,20,80,84,1..., dimensions={0} | all-to-all | bytes 1572864 | tf_op jit(solution)/shard_map/all_to_all | solution.py:42
  82.1 4.9 %agg_remote.1.own_ref = bf16[64,2048]{1,0:T(8,128)(2,1)} custom-call(s32[64]{0:T(128)} %copy-done.15, bf16[16,8,128,128]{3,2,1,0:T(8,128)(2,1)} %bitcast.23, f32[64,2048]{1,0:T(8,128)} %agg_local.1.refs_6_.local_ref, bf16[8,10,64,128]{3,2,1,0:T(8,128)(2,1)} %copy-done, bf16[8,6,64,128]{3,2,1,0:T(8,128)(2,1)} %all_to_all.37.refs_1_), custom_call_target="tpu_custom_call" | custom-call | flops 134217728 | bytes 5242880 | tf_op jit(solution)/shard_map/agg_remote/pallas_call | solution.py:145
  87.0 2.8 %collective-permute-start.10 = (bf16[64,2048]{1,0:T(8,128)(2,1)}, bf16[64,2048]{1,0:T(8,128)(2,1)S(1)}, u32[]{:S(2)}, u32[]{:S(2)}) collective-permute-start(bf16[64,2048]{1,0:T(8,128)(2,1)} %agg_remote.1.own_ref), channel_id=1, source_target_pairs={{0,2},{1,3},{2,0},{3,1},{4,6},{5,7},{6,4},{7,5},{8,10},{9,11},{10,... | collective-permute-start | bytes 786440 | tf_op jit(solution)/shard_map/ppermute | solution.py:440
  89.8 0.8 collective-permute-start.9
  91.4 4.1 %collective-permute-done.10.far_ref = bf16[64,2048]{1,0:T(8,128)(2,1)S(1)} collective-permute-done((bf16[64,2048]{1,0:T(8,128)(2,1)}, bf16[64,2048]{1,0:T(8,128)(2,1)S(1)}, u32[]{:S(2)}, u32[]{:S(2)}) %collective-permute-start.10) | collective-permute-done | bytes 262176 | tf_op jit(solution)/shard_map/ppermute | solution.py:440
  95.5 6.2 %collective-permute-done.9.high_ref = bf16[64,2048]{1,0:T(8,128)(2,1)S(1)} collective-permute-done((bf16[64,2048]{1,0:T(8,128)(2,1)}, bf16[64,2048]{1,0:T(8,128)(2,1)S(1)}, u32[]{:S(2)}, u32[]{:S(2)}) %collective-permute-start.9) | collective-permute-done | bytes 262176 | tf_op jit(solution)/shard_map/ppermute | solution.py:440
  102.6 4.9 %mid.1 = (bf16[64,2048]{1,0:T(8,128)(2,1)}, bf16[64,2048]{1,0:T(8,128)(2,1)}, f32[64,256]{1,0:T(8,128)}, f32[64,128]{1,0:T(8,128)}) custom-call(s32[1]{0:T(128)} %bitcast.me_ref, bf16[64,2048]{1,0:T(8,128)(2,1)} %agg_remote.1.own_ref, bf16[64,2048]{1,0:T(8,128)(2,1)} %copy-done.6, bf16[64,2048]{1,0:T(8,128)(2,1)} %copy-done.5, bf16[64,2048]{1,0:T(8,128)(2,1)} %copy-done.4, ...), custom_call_target="tpu_custom_call" | custom-call | flops 402653184 | bytes 3145728 | tf_op jit(solution)/shard_map/mid/pallas_call | solution.py:227
  107.5 0.9 reduce_sum.28
  108.5 0.9 maximum_bitcast_fusion
  110.2 8.1 %all-to-all-start.3 = ((f32[64,1,259]{2,1,0:T(1,128)}), f32[64,1,259]{2,1,0:T(1,128)S(1)}, u32[]{:S(2)}, u32[]{:S(2)}) async-start(f32[64,1,259]{2,1,0:T(1,128)} %copy.25), calls=%async_computation.3 | async-start | bytes 196608 | tf_op jit(solution)/shard_map/all_to_all | solution.py:456
  118.3 3.9 %back_local.1.local_ref = f32[64,2048]{1,0:T(8,128)} custom-call(s32[64]{0:T(128)} %reshape.235.cols_ref, bf16[64,2048]{1,0:T(8,128)(2,1)} %get-tuple-element.31.g_ref, bf16[16,8,128,128]{3,2,1,0:T(8,128)(2,1)} %bitcast.24), custom_call_target="tpu_custom_call" | custom-call | flops 134217728 | bytes 3145728 | tf_op jit(solution)/shard_map/back_local/pallas_call | solution.py:331
  122.2 4.6 %back_remote.1 = bf16[64,136,128]{2,1,0:T(8,128)(2,1)} custom-call(s32[64]{0:T(128)} %copy-done.16, bf16[64,2048]{1,0:T(8,128)(2,1)} %get-tuple-element.31.g_ref, bf16[16,8,128,128]{3,2,1,0:T(8,128)(2,1)} %bitcast.25), custom_call_target="tpu_custom_call" | custom-call | flops 134217728 | bytes 5242880 | tf_op jit(solution)/shard_map/back_remote/pallas_call | solution.py:293
  126.8 1.6 all-to-all-done.3
  129.3 8.7 %all-to-all-start.4 = ((bf16[64,136,128]{2,1,0:T(8,128)(2,1)}), bf16[64,136,128]{2,1,0:T(8,128)(2,1)S(1)}, u32[]{:S(2)}, u32[]{:S(2)}) async-start(bf16[64,136,128]{2,1,0:T(8,128)(2,1)} %broadcast_dynamic-update-slice_fusion), calls=%async_computation.4 | async-start | bytes 4456448 | tf_op jit(solution)/shard_map/all_to_all | solution.py:468
  138.7 53.1 %all-to-all-done.4.recv_ref = bf16[64,136,128]{2,1,0:T(8,128)(2,1)S(1)} async-done(((bf16[64,136,128]{2,1,0:T(8,128)(2,1)}), bf16[64,136,128]{2,1,0:T(8,128)(2,1)S(1)}, u32[]{:S(2)}, u32[]{:S(2)}) %all-to-all-start.4) | async-done | bytes 2228256 | tf_op jit(solution)/shard_map/all_to_all | solution.py:468
  191.9 0.8 slice_reduce_fusion.1
  193.4 3.4 %finish.1 = f32[64,2048]{1,0:T(8,128)} custom-call(s32[128]{0:T(128)} %reshape.238.wanted_ref, bf16[64,136,128]{2,1,0:T(8,128)(2,1)} %copy-done.1, f32[64,2048]{1,0:T(8,128)} %back_local.1.local_ref), custom_call_target="tpu_custom_call" | custom-call | flops 1114112 | bytes 4194304 | tf_op jit(solution)/shard_map/finish/pallas_call | solution.py:365
  (82 shorter events, 11.4 us)
Async XLA Ops:
  7.2 54.4 %all-gather.2.cloned.1.call-start = ((), (), s32[]{:S(2)}) async-start(), calls=%async_computation.5 | async-start | bytes 1556480 | tf_op jit(solution)/shard_map/all_gather | solution.py:428
  7.2 12.7 %collective-permute-start = (bf16[64,2048]{1,0:T(8,128)(2,1)}, bf16[64,2048]{1,0:T(8,128)(2,1)S(1)}, u32[]{:S(2)}, u32[]{:S(2)}) collective-permute-start(bf16[64,2048]{1,0:T(8,128)(2,1)} %refs_1_.1), channel_id=1, source_target_pairs={{0,8},{4,12},{8,16},{12,20},{16,24},{20,28},{24,32},{28,36},{32,40... | collective-permute-start | bytes 786440 | tf_op jit(solution)/shard_map/ppermute | solution.py:37
  9.8 10.2 %collective-permute-start.2 = (bf16[64,2048]{1,0:T(8,128)(2,1)}, bf16[64,2048]{1,0:T(8,128)(2,1)S(1)}, u32[]{:S(2)}, u32[]{:S(2)}) collective-permute-start(bf16[64,2048]{1,0:T(8,128)(2,1)} %refs_1_.1), channel_id=1, source_target_pairs={{0,56},{4,60},{8,0},{12,4},{16,8},{20,12},{24,16},{28,20},{32,24},... | collective-permute-start | bytes 786440 | tf_op jit(solution)/shard_map/ppermute | solution.py:37
  19.9 15.3 %copy-start.7 = (bf16[64,2048]{1,0:T(8,128)(2,1)}, bf16[64,2048]{1,0:T(8,128)(2,1)S(1)}, u32[]{:S(2)}) copy-start(bf16[64,2048]{1,0:T(8,128)(2,1)S(1)} %collective-permute-done.refs_3_) | copy-start | bytes 786436
  19.9 15.3 %collective-permute-start.1 = (bf16[64,2048]{1,0:T(8,128)(2,1)S(1)}, bf16[64,2048]{1,0:T(8,128)(2,1)S(1)}, u32[]{:S(2)}, u32[]{:S(2)}) collective-permute-start(bf16[64,2048]{1,0:T(8,128)(2,1)S(1)} %collective-permute-done.refs_3_), channel_id=1, source_target_pairs={{0,8},{4,12},{8,16},{12,20},{16,24},{20,28},{24,32},{28,36},{32,40... | collective-permute-start | bytes 786440 | tf_op jit(solution)/shard_map/ppermute | solution.py:37
  19.9 15.3 %copy-start.8 = (bf16[64,2048]{1,0:T(8,128)(2,1)}, bf16[64,2048]{1,0:T(8,128)(2,1)S(1)}, u32[]{:S(2)}) copy-start(bf16[64,2048]{1,0:T(8,128)(2,1)S(1)} %collective-permute-done.2.refs_2_) | copy-start | bytes 786436
  20.0 15.3 %collective-permute-start.3 = (bf16[64,2048]{1,0:T(8,128)(2,1)S(1)}, bf16[64,2048]{1,0:T(8,128)(2,1)S(1)}, u32[]{:S(2)}, u32[]{:S(2)}) collective-permute-start(bf16[64,2048]{1,0:T(8,128)(2,1)S(1)} %collective-permute-done.2.refs_2_), channel_id=1, source_target_pairs={{0,56},{4,60},{8,0},{12,4},{16,8},{20,12},{24,16},{28,20},{32,24},... | collective-permute-start | bytes 786440 | tf_op jit(solution)/shard_map/ppermute | solution.py:37
  22.6 16.7 %copy-start.15 = (s32[64]{0:T(128)}, s32[64]{0:T(128)S(1)}, u32[]{:S(2)}) copy-start(s32[64]{0:T(128)S(1)} %get-tuple-element.41.slots_ref) | copy-start | bytes 772
  22.7 16.7 %copy-start.16 = (s32[64]{0:T(128)}, s32[64]{0:T(128)S(1)}, u32[]{:S(2)}) copy-start(s32[64]{0:T(128)S(1)} %get-tuple-element.40.slots_ref) | copy-start | bytes 772
  35.2 0.7 copy-start.9
  35.9 0.7 copy-start.11
  39.3 4.3 %copy-start.12 = (bf16[64,2048]{1,0:T(8,128)(2,1)S(1)}, bf16[64,2048]{1,0:T(8,128)(2,1)}, u32[]{:S(2)}) copy-start(bf16[64,2048]{1,0:T(8,128)(2,1)} %copy-done.11) | copy-start | bytes 786436
  39.3 4.6 %copy-start.10 = (bf16[64,2048]{1,0:T(8,128)(2,1)S(1)}, bf16[64,2048]{1,0:T(8,128)(2,1)}, u32[]{:S(2)}) copy-start(bf16[64,2048]{1,0:T(8,128)(2,1)} %copy-done.9) | copy-start | bytes 786436
  39.4 22.2 %all-to-all-start.1 = ((bf16[8,10,64,128]{3,2,1,0:T(8,128)(2,1)}), bf16[8,10,64,128]{3,2,1,0:T(8,128)(2,1)S(1)}, u32[]{:S(2)}, u32[]{:S(2)}) async-start(bf16[8,10,64,128]{3,2,1,0:T(8,128)(2,1)} %pack.2), calls=%async_computation.1 | async-start | bytes 2621440 | tf_op jit(solution)/shard_map/all_to_all | solution.py:42
  43.7 7.7 %collective-permute-start.4 = (bf16[64,2048]{1,0:T(8,128)(2,1)S(1)}, bf16[64,2048]{1,0:T(8,128)(2,1)S(1)}, u32[]{:S(2)}, u32[]{:S(2)}) collective-permute-start(bf16[64,2048]{1,0:T(8,128)(2,1)S(1)} %copy-done.12), channel_id=1, source_target_pairs={{0,56},{4,60},{8,0},{12,4},{16,8},{20,12},{24,16},{28,20},{32,24},... | collective-permute-start | bytes 786440 | tf_op jit(solution)/shard_map/ppermute | solution.py:37
  43.9 9.0 %collective-permute-start.5 = (bf16[64,2048]{1,0:T(8,128)(2,1)S(1)}, bf16[64,2048]{1,0:T(8,128)(2,1)S(1)}, u32[]{:S(2)}, u32[]{:S(2)}) collective-permute-start(bf16[64,2048]{1,0:T(8,128)(2,1)S(1)} %copy-done.10), channel_id=1, source_target_pairs={{0,8},{4,12},{8,16},{12,20},{16,24},{20,28},{24,32},{28,36},{32,40... | collective-permute-start | bytes 786440 | tf_op jit(solution)/shard_map/ppermute | solution.py:37
  51.4 6.4 %copy-start.2 = (bf16[64,2048]{1,0:T(8,128)(2,1)}, bf16[64,2048]{1,0:T(8,128)(2,1)S(1)}, u32[]{:S(2)}) copy-start(bf16[64,2048]{1,0:T(8,128)(2,1)S(1)} %collective-permute-done.4.refs_1_) | copy-start | bytes 786436
  51.4 6.4 %collective-permute-start.7 = (bf16[32,2048]{1,0:T(8,128)(2,1)S(1)}, bf16[32,2048]{1,0:T(8,128)(2,1)S(1)}, u32[]{:S(2)}, u32[]{:S(2)}) collective-permute-start(bf16[32,2048]{1,0:T(8,128)(2,1)S(1)} %slice.69), channel_id=1, source_target_pairs={{0,56},{4,60},{8,0},{12,4},{16,8},{20,12},{24,16},{28,20},{32,24},... | collective-permute-start | bytes 393224 | tf_op jit(solution)/shard_map/ppermute | solution.py:37
  52.9 4.9 %copy-start.3 = (bf16[64,2048]{1,0:T(8,128)(2,1)}, bf16[64,2048]{1,0:T(8,128)(2,1)S(1)}, u32[]{:S(2)}) copy-start(bf16[64,2048]{1,0:T(8,128)(2,1)S(1)} %collective-permute-done.5.refs_2_) | copy-start | bytes 786436
  52.9 5.1 %collective-permute-start.6 = (bf16[32,2048]{1,0:T(8,128)(2,1)S(1)}, bf16[32,2048]{1,0:T(8,128)(2,1)S(1)}, u32[]{:S(2)}, u32[]{:S(2)}) collective-permute-start(bf16[32,2048]{1,0:T(8,128)(2,1)S(1)} %slice.68), channel_id=1, source_target_pairs={{0,8},{4,12},{8,16},{12,20},{16,24},{20,28},{24,32},{28,36},{32,40... | collective-permute-start | bytes 393224 | tf_op jit(solution)/shard_map/ppermute | solution.py:37
  57.8 3.8 %copy-start.13 = (bf16[32,2048]{1,0:T(8,128)(2,1)}, bf16[32,2048]{1,0:T(8,128)(2,1)S(1)}, u32[]{:S(2)}) copy-start(bf16[32,2048]{1,0:T(8,128)(2,1)S(1)} %collective-permute-done.7.refs_4_) | copy-start | bytes 393220
  58.1 3.5 %copy-start.14 = (bf16[32,2048]{1,0:T(8,128)(2,1)}, bf16[32,2048]{1,0:T(8,128)(2,1)S(1)}, u32[]{:S(2)}) copy-start(bf16[32,2048]{1,0:T(8,128)(2,1)S(1)} %collective-permute-done.6.refs_3_) | copy-start | bytes 393220
  61.6 1.1 copy-start
  87.0 8.5 %collective-permute-start.10 = (bf16[64,2048]{1,0:T(8,128)(2,1)}, bf16[64,2048]{1,0:T(8,128)(2,1)S(1)}, u32[]{:S(2)}, u32[]{:S(2)}) collective-permute-start(bf16[64,2048]{1,0:T(8,128)(2,1)} %agg_remote.1.own_ref), channel_id=1, source_target_pairs={{0,2},{1,3},{2,0},{3,1},{4,6},{5,7},{6,4},{7,5},{8,10},{9,11},{10,... | collective-permute-start | bytes 786440 | tf_op jit(solution)/shard_map/ppermute | solution.py:440
  89.8 12.0 %collective-permute-start.9 = (bf16[64,2048]{1,0:T(8,128)(2,1)}, bf16[64,2048]{1,0:T(8,128)(2,1)S(1)}, u32[]{:S(2)}, u32[]{:S(2)}) collective-permute-start(bf16[64,2048]{1,0:T(8,128)(2,1)} %agg_remote.1.own_ref), channel_id=1, source_target_pairs={{0,3},{1,0},{2,1},{3,2},{4,7},{5,4},{6,5},{7,6},{8,11},{9,8},{10,9... | collective-permute-start | bytes 786440 | tf_op jit(solution)/shard_map/ppermute | solution.py:440
  90.6 11.3 %collective-permute-start.8 = (bf16[64,2048]{1,0:T(8,128)(2,1)}, bf16[64,2048]{1,0:T(8,128)(2,1)S(1)}, u32[]{:S(2)}, u32[]{:S(2)}) collective-permute-start(bf16[64,2048]{1,0:T(8,128)(2,1)} %agg_remote.1.own_ref), channel_id=1, source_target_pairs={{0,1},{1,2},{2,3},{3,0},{4,5},{5,6},{6,7},{7,4},{8,9},{9,10},{10,1... | collective-permute-start | bytes 786440 | tf_op jit(solution)/shard_map/ppermute | solution.py:440
  95.5 6.5 %copy-start.4 = (bf16[64,2048]{1,0:T(8,128)(2,1)}, bf16[64,2048]{1,0:T(8,128)(2,1)S(1)}, u32[]{:S(2)}) copy-start(bf16[64,2048]{1,0:T(8,128)(2,1)S(1)} %collective-permute-done.10.far_ref) | copy-start | bytes 786436
  101.7 0.7 copy-start.5
  101.9 0.7 copy-start.6
  110.2 18.3 %all-to-all-start.3 = ((f32[64,1,259]{2,1,0:T(1,128)}), f32[64,1,259]{2,1,0:T(1,128)S(1)}, u32[]{:S(2)}, u32[]{:S(2)}) async-start(f32[64,1,259]{2,1,0:T(1,128)} %copy.25), calls=%async_computation.3 | async-start | bytes 196608 | tf_op jit(solution)/shard_map/all_to_all | solution.py:456
  129.3 62.6 %all-to-all-start.4 = ((bf16[64,136,128]{2,1,0:T(8,128)(2,1)}), bf16[64,136,128]{2,1,0:T(8,128)(2,1)S(1)}, u32[]{:S(2)}, u32[]{:S(2)}) async-start(bf16[64,136,128]{2,1,0:T(8,128)(2,1)} %broadcast_dynamic-update-slice_fusion), calls=%async_computation.4 | async-start | bytes 4456448 | tf_op jit(solution)/shard_map/all_to_all | solution.py:468
  191.8 1.5 copy-start.1
Sparse Core Ops, SparseCore 0:
  16.4 26.6 all-gather.1

commit v4 on v3

--- a/solution.py
+++ b/solution.py
@@ -22,55 +22,47 @@
 
 NY, NZ, NC = 4, 8, 2
 CAP = 2
-ORDER = (0, 1, 7, 2, 6, 3, 5, 4)
-GROUPS = ((0, 5), (5, 8))
-PEERS = NY * NC
-PER = NZ * CAP
-
-
-def shift(x, dz):
+COLUMN = NZ * NC
+PER = COLUMN * CAP
+
+
+def move(x, dy=0, dc=0, flip=0):
     pairs = []
     for y in range(NY):
         for z in range(NZ):
             for c in range(NC):
-                pairs.append(((y * NZ + z) * NC + c, (y * NZ + (z + dz) % NZ) * NC + c))
+                to = ((y + dy) % NY * NZ + (z ^ flip)) * NC + (c + dc) % NC
+                pairs.append(((y * NZ + z) * NC + c, to))
     return lax.ppermute(x, "rows", pairs)
 
 
-def swap(x):
-    groups = [[(y * NZ + z) * NC + c for y in range(NY) for c in range(NC)] for z in range(NZ)]
-    return lax.all_to_all(
-        x, "rows", split_axis=0, concat_axis=0, tiled=True, axis_index_groups=groups
-    )
-
-
-def pack_kernel(first, count, split, *refs):
-    wanted_ref, sources, out_ref = refs[0], refs[1 : 1 + count + split], refs[-1]
-    width, block = out_ref.shape[2], out_ref.shape[3]
-    for p in range(PEERS):
-        for q in range(count * CAP):
-            w = wanted_ref[p * PER + first * CAP + q]
-            where = lanes(jnp.maximum(w, 0), block)
-            j = q // CAP
-            if split and j == count - 1:
-                out_ref[p, q, : width // 2] = sources[j][:, where]
-                out_ref[p, q, width // 2 :] = sources[j + 1][:, where]
-            else:
-                out_ref[p, q] = sources[j][:, where]
-
-
-def pack(group, wanted, sources, block, after):
-    first, last = group
-    count = last - first
-    width = sources[0].shape[0]
-    return pl.pallas_call(
-        functools.partial(pack_kernel, first, count, len(sources) > count),
-        out_shape=jax.ShapeDtypeStruct((PEERS, count * CAP, width, block), BF),
-        in_specs=[SMEM] + [VMEM] * len(sources) + [ANY] * len(after),
-        out_specs=VMEM,
+def pack_kernel(y_ref, wanted_ref, column_ref, *refs):
+    i = pl.program_id(0)
+    outs = refs[-NY:]
+    block = outs[0].shape[2]
+    slots = outs[0].shape[0]
+    for k in range(NY):
+        base = lax.rem(y_ref[0] + k, NY) * PER + i * slots
+        for q in range(slots):
+            w = jnp.maximum(wanted_ref[base + q], 0)
+            outs[k][q] = column_ref[q // CAP, :, lanes(w, block)]
+
+
+def pack(y, wanted, column, block, after):
+    _, width, nodes = column.shape
+    steps = 4
+    shape = jax.ShapeDtypeStruct((PER, width, block), BF)
+    out = pl.BlockSpec((PER // steps, width, block), lambda i: (i, 0, 0))
+    return pl.pallas_call(
+        pack_kernel,
+        grid=(steps,),
+        out_shape=[shape] * NY,
+        in_specs=[SMEM, SMEM, pl.BlockSpec((COLUMN // steps, width, nodes), lambda i: (i, 0, 0))]
+        + [ANY] * len(after),
+        out_specs=[out] * NY,
         name="pack",
-        cost_estimate=pl.CostEstimate(flops=0, bytes_accessed=3 << 20, transcendentals=0),
-    )(wanted, *sources, *after)
+        cost_estimate=pl.CostEstimate(flops=0, bytes_accessed=6 << 20, transcendentals=0),
+    )(y, wanted, column, *after)
 
 
 def dot(a, b, dims):
@@ -123,9 +115,8 @@
 
     @pl.when(i == 0)
     def _():
-        for part, (first, last) in zip(parts, GROUPS):
-            for p in range(PEERS):
-                recv_ref[pl.ds(p * PER + first * CAP, (last - first) * CAP)] = part[p]
+        for k, part in enumerate(parts):
+            recv_ref[pl.ds(k * PER, PER)] = part[...]
 
     for rr in range(STEP):
         acc = local_ref[:, rr * block : (rr + 1) * block]
@@ -141,7 +132,7 @@
     row_blocks, per_block, block, _ = tiles.shape
     rem = per_block - TL
     width = local.shape[0]
-    specs = [pl.BlockSpec(part.shape, lambda i: (0, 0, 0, 0)) for part in parts]
+    specs = [pl.BlockSpec(part.shape, lambda i: (0, 0, 0)) for part in parts]
     return pl.pallas_call(
         agg_remote_kernel,
         grid=(row_blocks // STEP,),
@@ -153,7 +144,7 @@
         ]
         + specs,
         out_specs=pl.BlockSpec((width, STEP * block), lambda i: (0, i)),
-        scratch_shapes=[pltpu.VMEM((PEERS * PER, width, block), BF)],
+        scratch_shapes=[pltpu.VMEM((NY * PER, width, block), BF)],
         name="agg_remote",
         cost_estimate=pl.CostEstimate(
             flops=2 * width * row_blocks * rem * block * block, bytes_accessed=5 << 20, transcendentals=0
@@ -173,8 +164,7 @@
     wown_ref,
     hid_ref,
     g_ref,
-    gw_ref,
-    gb_ref,
+    sums_ref,
     agg_scr,
     hid_scr,
     wt_scr,
@@ -191,7 +181,7 @@
     @pl.when(i == 0)
     def _():
         wt_scr[...] = w_ref[...].astype(F32).T.astype(BF)
-        gw_ref[...] = jnp.zeros_like(gw_ref)
+        sums_ref[...] = jnp.zeros_like(sums_ref)
         gb_scr[...] = jnp.zeros_like(gb_scr)
 
     agg_scr[rows(3)] = low_ref[...]
@@ -211,11 +201,13 @@
     gb_scr[...] += total
     grad_b = grad_pre.astype(BF)
     g_ref[...] = dot(wown_ref[...], grad_b, (1, 0)).astype(BF)
-    gw_ref[...] += dot(own_ref[...], grad_b, (1, 1))
+    grad_w = dot(own_ref[...], grad_b, (1, 1))
+    for k in range(grad_w.shape[1] // 128):
+        sums_ref[k * width : (k + 1) * width] += grad_w[:, k * 128 : (k + 1) * 128]
 
     @pl.when(i == pl.num_programs(0) - 1)
     def _():
-        gb_ref[...] = gb_scr[rows(0)]
+        sums_ref[-width:] = gb_scr[rows(0)]
 
 
 def mid(me, pieces, packed, w_own):
@@ -230,8 +222,7 @@
         out_shape=(
             jax.ShapeDtypeStruct((width, nodes), BF),
             jax.ShapeDtypeStruct((width, nodes), BF),
-            jax.ShapeDtypeStruct((width, hid_all), F32),
-            jax.ShapeDtypeStruct((width, 128), F32),
+            jax.ShapeDtypeStruct((width * (hid_all // 128 + 1), 128), F32),
         ),
         in_specs=[
             SMEM,
@@ -247,8 +238,7 @@
         out_specs=(
             pl.BlockSpec((width, chunk), col),
             pl.BlockSpec((width, chunk), col),
-            pl.BlockSpec((width, hid_all), lambda i: (0, 0)),
-            pl.BlockSpec((width, 128), lambda i: (0, 0)),
+            pl.BlockSpec((width * (hid_all // 128 + 1), 128), lambda i: (0, 0)),
         ),
         scratch_shapes=[
             pltpu.VMEM((hid_all, chunk), BF),
@@ -286,20 +276,20 @@
                 out_ref[slot // CAP, pl.ds(row, width)] = term[:, k * block : (k + 1) * block]
 
 
-def back_remote(slots, g, tiles, peers, extra):
+def back_remote(slots, g, tiles, peers):
     row_blocks, per_block, block, _ = tiles.shape
     rem = per_block - TL
     width = g.shape[0]
     return pl.pallas_call(
         back_remote_kernel,
         grid=(row_blocks // STEP,),
-        out_shape=jax.ShapeDtypeStruct((peers, CAP * width + extra, block), BF),
+        out_shape=jax.ShapeDtypeStruct((peers, CAP * width, block), BF),
         in_specs=[
             SMEM,
             pl.BlockSpec((width, STEP * block), lambda i: (0, i)),
             pl.BlockSpec((STEP, rem, block, block), lambda i: (i, 1, 0, 0)),
         ],
-        out_specs=pl.BlockSpec((peers, CAP * width + extra, block), lambda i: (0, 0, 0)),
+        out_specs=pl.BlockSpec((peers, CAP * width, block), lambda i: (0, 0, 0)),
         name="back_remote",
         cost_estimate=pl.CostEstimate(
             flops=2 * width * row_blocks * rem * block * block, bytes_accessed=5 << 20, transcendentals=0
@@ -307,7 +297,7 @@
     )(slots, g, tiles)
 
 
-def back_local_kernel(cols_ref, g_ref, tiles_ref, out_ref):
+def back_local_kernel(cols_ref, g_ref, tiles_ref, _, out_ref):
     i = pl.program_id(0)
     count, block = tiles_ref.shape[1], tiles_ref.shape[2]
 
@@ -325,7 +315,7 @@
                 out_ref[:, lanes(cols_ref[base + k], block)] += term[:, k * block : (k + 1) * block]
 
 
-def back_local(cols, g, tiles):
+def back_local(cols, g, tiles, after):
     row_blocks, _, block, _ = tiles.shape
     width = g.shape[0]
     return pl.pallas_call(
@@ -336,13 +326,14 @@
             SMEM,
             pl.BlockSpec((width, STEP * block), lambda i: (0, i)),
             pl.BlockSpec((STEP, TL, block, block), lambda i: (i, 0, 0, 0)),
+            ANY,
         ],
         out_specs=pl.BlockSpec(g.shape, lambda i: (0, 0)),
         name="back_local",
         cost_estimate=pl.CostEstimate(
             flops=2 * width * row_blocks * TL * block * block, bytes_accessed=3 << 20, transcendentals=0
         ),
-    )(cols, g, tiles)
+    )(cols, g, tiles, after)
 
 
 def finish_kernel(wanted_ref, recv_ref, local_ref, out_ref, odd_scr):
@@ -392,7 +383,7 @@
     per_block = tile_cols.shape[0] // row_blocks
     remote_count = row_blocks * (per_block - TL)
     place = lax.axis_index("rows")
-    z = place // NC % NZ
+    y, c = place // COLUMN, place % NC
 
     grid = tile_cols.reshape(row_blocks, per_block)
     tiles = tile_values.reshape(row_blocks, per_block, block, block)
@@ -404,77 +395,64 @@
     earlier = (owner[:, None] == owner[None, :]) & (order[None, :] < order[:, None])
     rank = jnp.sum(earlier.astype(jnp.int32), axis=1)
     slots = owner * CAP + rank
-    ahead = (owner // NC - z) & (NZ - 1)
-    pos = jnp.maximum(jnp.where(ahead <= NZ // 2, 2 * ahead - 1, 2 * (NZ - ahead)), 0)
-    near = ((owner // (NZ * NC) * NC + owner % NC) * NZ + pos) * CAP + rank
-
-    def table(index):
-        hit = index[None, :] == jnp.arange(peers * CAP)[:, None]
-        return jnp.max(jnp.where(hit, inside[None, :], -1), axis=1)
-
-    wanted = swap(table(near).reshape(PEERS, PER)).reshape(-1)
-
-    up, down = [feats], [feats]
-    for k in range(1, NZ // 2):
-        if k == 3:
-            up[2], down[2], wanted = lax.optimization_barrier((up[2], down[2], wanted))
-        up.append(shift(up[-1], 1))
-        down.append(shift(down[-1], -1))
-    far_up = shift(up[-1][: width // 2], 1)
-    far_down = shift(down[-1][width // 2 :], -1)
+    near = ((y - owner // COLUMN) & (NY - 1)) * PER + slots % PER
+
+    hit = slots[None, :] == jnp.arange(peers * CAP)[:, None]
+    request = jnp.max(jnp.where(hit, inside[None, :], -1), axis=1)
+
+    columns = [[y0 * COLUMN + k for k in range(COLUMN)] for y0 in range(NY)]
+    column = lax.all_gather(feats, "rows", axis_index_groups=columns)
+    along_y = [[y0 * COLUMN + k for y0 in range(NY)] for k in range(COLUMN)]
+    wanted = lax.all_to_all(
+        request.reshape(NY, PER), "rows", 0, 0, tiled=True, axis_index_groups=along_y
+    ).reshape(-1)
+    holders = lax.all_to_all(request.reshape(peers, CAP), "rows", 0, 0, tiled=True).reshape(-1)
+    agg = agg_local(local_cols, feats, tiles)
 
     bias_cols = jnp.pad(jnp.stack(split_bf16(bias, 3), axis=1), ((0, 0), (0, 125)))
     packed = jnp.concatenate([cotangent, weight, bias_cols], axis=1)
     packed = lax.all_gather(packed, "feat", axis=0, tiled=True)
 
-    agg = agg_local(local_cols, feats, tiles)
-    near_sources = (feats, down[1], up[1], down[2], up[2])
-    far_sources = (down[3], up[3], far_up, far_down)
-    first = swap(pack(GROUPS[0], wanted, near_sources, block, []))
-    second = swap(pack(GROUPS[1], wanted, far_sources, block, [first, agg, packed]))
-    parts = [first, second]
-
+    packs = pack(y.reshape(1), wanted, column, block, [holders, agg])
+    parts = [packs[0]] + [move(packs[k], dy=k) for k in range(1, NY)]
     agg = agg_remote(near, parts, tiles, agg)
 
     pieces = [agg] + [
         lax.ppermute(agg, "feat", [(k, (k + s) % fpeers) for k in range(fpeers)]) for s in (1, 3, 2)
     ]
     me = lax.axis_index("feat").astype(jnp.int32).reshape(1)
-    hidden_out, g, grad_w, grad_b = mid(me, pieces, packed, weight)
-
-    divisor = math.sqrt(nodes_dev * peers)
-    per = grad_w.size // peers
-    per_b = width // peers
-    sums = jnp.concatenate(
-        [
-            grad_w.reshape(peers, per),
-            jnp.sum(grad_b, axis=1).reshape(peers, per_b),
-            table(slots).reshape(peers, CAP).astype(F32),
-        ],
-        axis=1,
+    hidden_out, g, sums = mid(me, pieces, packed, weight)
+
+    send = back_remote(slots, g, tiles, peers)
+    recv = lax.all_to_all(send, "rows", split_axis=0, concat_axis=0, tiled=True)
+    own = back_local(local_cols, g, tiles, send)
+
+    own, sums = lax.optimization_barrier((own, sums))
+    n_half = sums.shape[0] // NC
+    n = n_half // NY
+
+    def piece(x, index, size):
+        return lax.dynamic_slice_in_dim(x, index * size, size, 0)
+
+    half = piece(sums, c, n_half) + move(piece(sums, 1 - c, n_half), dc=1)
+    part = piece(half, y, n)
+    for k in range(1, NY):
+        part = part + move(piece(half, (y + k) & (NY - 1), n), dy=k)
+    for bit in (1, 2, 4):
+        part = part + move(part, flip=bit)
+    ring = [move(part, dy=k) for k in range(NY - 1, 0, -1)] + [part]
+    half = lax.dynamic_slice_in_dim(jnp.concatenate(ring + ring), ((NY - 1 - y) & (NY - 1)) * n, n_half, 0)
+    other = move(half, dc=1)
+    total = lax.dynamic_slice_in_dim(
+        jnp.concatenate([other, half, other]), (1 - c) * n_half, NC * n_half, 0
+    ) / math.sqrt(nodes_dev * peers)
+    grad_w = jnp.concatenate(
+        [total[k * width : (k + 1) * width] for k in range(hid_all // 128)], axis=1
     )
-    sums = lax.all_to_all(sums, "rows", split_axis=0, concat_axis=0, tiled=True)
-    holders = sums[:, per + per_b :].astype(jnp.int32).reshape(-1)
-    total = jnp.sum(sums[:, : per + per_b], axis=0) / divisor
-    span = -(-total.size // block)
-    total = jnp.pad(total, (0, span * block - total.size)).reshape(span, block)
-    extra = -(-2 * span // 8) * 8
-    rider = jnp.concatenate(split_bf16(total, 2) + [jnp.zeros((extra - 2 * span, block), BF)])
-
-    send = back_remote(slots, g, tiles, peers, extra)
-    own = back_local(local_cols, g, tiles)
-    own, rider = lax.optimization_barrier((own, rider))
-    send = send.at[:, CAP * width :].set(jnp.broadcast_to(rider, (peers, extra, block)))
-    recv = lax.all_to_all(send, "rows", split_axis=0, concat_axis=0, tiled=True)
+    grad_b = jnp.sum(total[-width:], axis=1)
+
     grad_input = finish(holders, recv, own)
-    totals = recv[:, CAP * width :].astype(F32)
-    totals = (totals[:, :span] + totals[:, span : 2 * span]).reshape(peers, -1)
-    return (
-        hidden_out,
-        grad_input,
-        totals[:, :per].reshape(width, hid_all),
-        totals[:, per : per + per_b].reshape(width),
-    )
+    return hidden_out, grad_input, grad_w, grad_b
 
 
 def solution(mesh):

time: 205 us -> 211 us (1.029)
  blocking collectives: 27.9 us -> 0 us
  waiting for transfers between devices: 77.8 us -> 97.9 us
  starting transfers between devices: 37.7 us -> 54.2 us
    ppermute x8 -> x14, waiting for transfers between devices: 8.97 us -> 69 us  [move(): return lax.ppermute(x, 'rows', pairs)]
    all_to_all x1, waiting for transfers between devices: 53.1 us -> 0.01 us  [local(): recv = lax.all_to_all(send, 'rows', split_axis=0, concat_axis=0, tiled=True)]
    all_to_all x2 -> x0, blocking collectives: 27.9 us -> none  [swap(): lax.all_to_all(x, 'rows', split_axis=0, concat_axis=0, tiled=True, axis_i...]
    all_gather x0 -> x1, waiting for transfers between devices: none -> 11.9 us  [local(): column = lax.all_gather(feats, 'rows', axis_index_groups=columns)]
    ppermute x8 -> x14, starting transfers between devices: 12.3 us -> 23.3 us  [move(): return lax.ppermute(x, 'rows', pairs)]
    all_to_all x2, starting transfers between devices: 12.4 us -> 16.7 us  [the longest x1 11.7 us: local(): lax.all_to_all(request.reshape(peers, CAP), 'rows', 0, 0, tiled=True)]
    pallas_call x2 -> x1, Pallas kernels: 4.91 us -> 4.45 us  [pack(): pl.pallas_call(pack_kernel, grid=(steps,), out_shape=[shape] * NY, in_spe...]
  transfers between devices with their start and end apart: 15 -> 22, of which waited for: 9 -> 16; matrix products, arithmetic and copies ran while one was open for 3% -> 4% of each run, Pallas kernels for 8% -> 8%
where the time goes in v4:
time: 211 us; the launch traced here: 210 us
  waiting for transfers between devices  97.9 us (46%)
  starting transfers between devices  54.2 us (26%)
  Pallas kernels  30.3 us (14%)
  between operations  14.2 us (7%)
  local copies, waits for them, and re-layouts  7.85 us (4%)
  other arithmetic  6.06 us (3%)
    ppermute x14, waiting for transfers between devices, move(): return lax.ppermute(x, 'rows', pairs)  69 us
    ppermute x14, starting transfers between devices, move(): return lax.ppermute(x, 'rows', pairs)  23.3 us
    all_gather x1, waiting for transfers between devices, local(): column = lax.all_gather(feats, 'rows', axis_index_groups=columns)  11.9 us
    all_to_all x1, starting transfers between devices, local(): lax.all_to_all(request.reshape(peers, CAP), 'rows', 0, 0, tiled=True)  11.7 us
    ppermute x3, waiting for transfers between devices, local(): lax.ppermute(agg, 'feat', [(k, (k + s) % fpeers) for k in range(fpeers)])  10.3 us
    all_to_all x1, starting transfers between devices, local(): recv = lax.all_to_all(send, 'rows', split_axis=0, concat_axis=0, tiled=True)  9.74 us
    all_to_all x1, starting transfers between devices, local(): lax.all_to_all(request.reshape(NY, PER), 'rows', 0, 0, tiled=True, axis_i...  5.01 us
    pallas_call x1, Pallas kernels, mid(): pl.pallas_call(mid_kernel, grid=(nodes // chunk,), out_shape=(jax.ShapeDt...  4.88 us
  transfers between devices with their start and end apart: 22, of which 16 were waited for; matrix products, arithmetic and copies ran while one was open for 4% of the time, Pallas kernels for 8%

profile of v4, /device:TPU:1, one launch (start us, length us, event | category | flops | bytes accessed | tf_op | source)
XLA Modules:
  0.0 210.5 jit_solution(366996814128075698)
XLA Ops:
  8.7 1.7 fusion.1
  12.9 5.0 %all-to-all-start = ((s32[4,1,32]{2,1,0:T(1,128)}), s32[4,1,32]{2,1,0:T(1,128)S(1)}, u32[]{:S(2)}, u32[]{:S(2)}) async-start(s32[4,1,32]{2,1,0:T(1,128)} %bitcast.3), calls=%async_computation | async-start | bytes 4096 | tf_op jit(solution)/shard_map/all_to_all | solution.py:406
  19.3 2.7 %all-to-all-done = s32[4,1,32]{2,1,0:T(1,128)S(1)} async-done(((s32[4,1,32]{2,1,0:T(1,128)}), s32[4,1,32]{2,1,0:T(1,128)S(1)}, u32[]{:S(2)}, u32[]{:S(2)}) %all-to-all-start) | async-done | bytes 544 | tf_op jit(solution)/shard_map/all_to_all | solution.py:406
  22.0 11.7 %all-to-all-start.1 = ((s32[64,1,2]{2,1,0:T(1,128)}), s32[64,1,2]{2,1,0:T(1,128)S(1)}, u32[]{:S(2)}, u32[]{:S(2)}) async-start(s32[64,1,2]{2,1,0:T(1,128)} %bitcast.5), calls=%async_computation.1 | async-start | bytes 65536 | tf_op jit(solution)/shard_map/all_to_all | solution.py:409
  33.7 4.2 %agg_local.1.refs_1_.local_ref = f32[64,2048]{1,0:T(8,128)} custom-call(s32[64]{0:T(128)} %reshape.136.cols_ref, bf16[64,2048]{1,0:T(8,128)(2,1)} %feats_ref.1, bf16[16,8,128,128]{3,2,1,0:T(8,128)(2,1)} %bitcast.12), custom_call_target="tpu_custom_call" | custom-call | flops 134217728 | bytes 3145728 | tf_op jit(solution)/shard_map/agg_local/pallas_call | solution.py:94
  39.7 3.3 %all-to-all-done.1 = s32[64,1,2]{2,1,0:T(1,128)S(1)} async-done(((s32[64,1,2]{2,1,0:T(1,128)}), s32[64,1,2]{2,1,0:T(1,128)S(1)}, u32[]{:S(2)}, u32[]{:S(2)}) %all-to-all-start.1) | async-done | bytes 544 | tf_op jit(solution)/shard_map/all_to_all | solution.py:409
  44.3 11.9 %all-gather.6.cloned.1.call-done = bf16[1024,2048]{1,0:T(8,128)(2,1)} async-done(((bf16[64,2048]{1,0:T(8,128)(2,1)}), bf16[1024,2048]{1,0:T(8,128)(2,1)}) %all-gather.6.cloned.1.call-update) | async-done | bytes 4194320 | tf_op jit(solution)/shard_map/all_gather | solution.py:404
  56.2 4.5 %pack.1 = (bf16[32,64,128]{2,1,0:T(8,128)(2,1)}, bf16[32,64,128]{2,1,0:T(8,128)(2,1)}, bf16[32,64,128]{2,1,0:T(8,128)(2,1)}, bf16[32,64,128]{2,1,0:T(8,128)(2,1)}) custom-call(s32[1]{0:T(128)} %bitcast.2.y_ref, s32[128]{0:T(128)} %reshape.138.wanted_ref, bf16[16,64,2048]{2,1,0:T(8,128)(2,1)} %bitcast.16, s32[128]{0:T(128)} %reshape.139.refs_0_.wanted_ref, ...), custom_call_target="tpu_custom_call" | custom-call | bytes 6291456 | tf_op jit(solution)/shard_map/pack/pallas_call | solution.py:56
  60.7 1.2 collective-permute-start
  62.0 2.4 %collective-permute-start.1 = (bf16[32,64,128]{2,1,0:T(8,128)(2,1)}, bf16[32,64,128]{2,1,0:T(8,128)(2,1)S(1)}, u32[]{:S(2)}, u32[]{:S(2)}) collective-permute-start(bf16[32,64,128]{2,1,0:T(8,128)(2,1)} %get-tuple-element.15), channel_id=1, source_target_pairs={{0,128},{4,132},{8,136},{12,140},{16,144},{20,148},{24,152},{28,15... | collective-permute-start | bytes 1572872 | tf_op jit(solution)/shard_map/ppermute | solution.py:36
  65.5 10.0 %collective-permute-done.refs_1_ = bf16[32,64,128]{2,1,0:T(8,128)(2,1)S(1)} collective-permute-done((bf16[32,64,128]{2,1,0:T(8,128)(2,1)}, bf16[32,64,128]{2,1,0:T(8,128)(2,1)S(1)}, u32[]{:S(2)}, u32[]{:S(2)}) %collective-permute-start) | collective-permute-done | bytes 524320 | tf_op jit(solution)/shard_map/ppermute | solution.py:36
  75.5 12.1 %collective-permute-done.1.refs_2_ = bf16[32,64,128]{2,1,0:T(8,128)(2,1)S(1)} collective-permute-done((bf16[32,64,128]{2,1,0:T(8,128)(2,1)}, bf16[32,64,128]{2,1,0:T(8,128)(2,1)S(1)}, u32[]{:S(2)}, u32[]{:S(2)}) %collective-permute-start.1) | collective-permute-done | bytes 524320 | tf_op jit(solution)/shard_map/ppermute | solution.py:36
  88.7 4.9 %agg_remote.1.own_ref = bf16[64,2048]{1,0:T(8,128)(2,1)} custom-call(s32[64]{0:T(128)} %get-tuple-element.31.slots_ref, bf16[16,8,128,128]{3,2,1,0:T(8,128)(2,1)} %bitcast.13, f32[64,2048]{1,0:T(8,128)} %agg_local.1.refs_1_.local_ref, bf16[32,64,128]{2,1,0:T(8,128)(2,1)} %get-tuple-element.13.refs_0_, bf16[32,64,128]{2,1,0:T(8,128)(2,1)} %copy-done.1, ...), custom_call_target="tpu_custom_call" | custom-call | flops 134217728 | bytes 5242880 | tf_op jit(solution)/shard_map/agg_remote/pallas_call | solution.py:136
  94.8 1.4 collective-permute-start.4
  96.2 1.6 collective-permute-start.5
  97.8 3.8 %collective-permute-done.3.low_ref = bf16[64,2048]{1,0:T(8,128)(2,1)S(1)} collective-permute-done((bf16[64,2048]{1,0:T(8,128)(2,1)}, bf16[64,2048]{1,0:T(8,128)(2,1)S(1)}, u32[]{:S(2)}, u32[]{:S(2)}) %collective-permute-start.3) | collective-permute-done | bytes 262176 | tf_op jit(solution)/shard_map/ppermute | solution.py:421
  101.7 6.4 %collective-permute-done.5.far_ref = bf16[64,2048]{1,0:T(8,128)(2,1)S(1)} collective-permute-done((bf16[64,2048]{1,0:T(8,128)(2,1)}, bf16[64,2048]{1,0:T(8,128)(2,1)S(1)}, u32[]{:S(2)}, u32[]{:S(2)}) %collective-permute-start.5) | collective-permute-done | bytes 262176 | tf_op jit(solution)/shard_map/ppermute | solution.py:421
  108.8 4.9 %mid.1 = (bf16[64,2048]{1,0:T(8,128)(2,1)}, bf16[64,2048]{1,0:T(8,128)(2,1)}, f32[192,128]{1,0:T(8,128)}) custom-call(s32[1]{0:T(128)} %bitcast.me_ref, bf16[64,2048]{1,0:T(8,128)(2,1)} %agg_remote.1.own_ref, bf16[64,2048]{1,0:T(8,128)(2,1)} %copy-done.4, bf16[64,2048]{1,0:T(8,128)(2,1)} %copy-done.5, bf16[64,2048]{1,0:T(8,128)(2,1)} %copy-done.6, ...), custom_call_target="tpu_custom_call" | custom-call | flops 402653184 | bytes 3145728 | tf_op jit(solution)/shard_map/mid/pallas_call | solution.py:219
  113.7 4.6 %back_remote.1._ = bf16[64,128,128]{2,1,0:T(8,128)(2,1)} custom-call(s32[64]{0:T(128)} %copy-done.8, bf16[64,2048]{1,0:T(8,128)(2,1)} %get-tuple-element.18.g_ref, bf16[16,8,128,128]{3,2,1,0:T(8,128)(2,1)} %bitcast.14), custom_call_target="tpu_custom_call" | custom-call | flops 134217728 | bytes 5242880 | tf_op jit(solution)/shard_map/back_remote/pallas_call | solution.py:283
  118.3 9.7 %all-to-all-start.2 = ((bf16[64,128,128]{2,1,0:T(8,128)(2,1)}), bf16[64,128,128]{2,1,0:T(8,128)(2,1)S(1)}, u32[]{:S(2)}, u32[]{:S(2)}) async-start(bf16[64,128,128]{2,1,0:T(8,128)(2,1)} %back_remote.1._), calls=%async_computation.2 | async-start | bytes 4194304 | tf_op jit(solution)/shard_map/all_to_all | solution.py:427
  128.0 4.0 %back_local.1.local_ref = f32[64,2048]{1,0:T(8,128)} custom-call(s32[64]{0:T(128)} %reshape.136.cols_ref, bf16[64,2048]{1,0:T(8,128)(2,1)} %get-tuple-element.18.g_ref, bf16[16,8,128,128]{3,2,1,0:T(8,128)(2,1)} %bitcast.15, bf16[64,128,128]{2,1,0:T(8,128)(2,1)} %back_remote.1._), custom_call_target="tpu_custom_call" | custom-call | flops 134217728 | bytes 3145728 | tf_op jit(solution)/shard_map/back_local/pallas_call | solution.py:321
  133.4 2.8 %collective-permute-start.9 = (f32[24,128]{1,0:T(8,128)S(1)}, f32[24,128]{1,0:T(8,128)S(1)}, u32[]{:S(2)}, u32[]{:S(2)}) collective-permute-start(f32[24,128]{1,0:T(8,128)S(1)} %get-tuple-element.26), channel_id=1, source_target_pairs={{0,192},{4,196},{8,200},{12,204},{16,208},{20,212},{24,216},{28,22... | collective-permute-start | bytes 36872 | tf_op jit(solution)/shard_map/ppermute | solution.py:36
  137.3 4.0 %collective-permute-done.8 = f32[24,128]{1,0:T(8,128)S(1)} collective-permute-done((f32[24,128]{1,0:T(8,128)S(1)}, f32[24,128]{1,0:T(8,128)S(1)}, u32[]{:S(2)}, u32[]{:S(2)}) %collective-permute-start.8) | collective-permute-done | bytes 12320 | tf_op jit(solution)/shard_map/ppermute | solution.py:36
  142.2 32.7 %collective-permute-done.10 = f32[24,128]{1,0:T(8,128)S(1)} collective-permute-done((f32[24,128]{1,0:T(8,128)S(1)}, f32[24,128]{1,0:T(8,128)S(1)}, u32[]{:S(2)}, u32[]{:S(2)}) %collective-permute-start.10) | collective-permute-done | bytes 12320 | tf_op jit(solution)/shard_map/ppermute | solution.py:36
  175.5 3.1 %collective-permute-done.11 = f32[24,128]{1,0:T(8,128)S(1)} collective-permute-done((f32[24,128]{1,0:T(8,128)S(1)}, f32[24,128]{1,0:T(8,128)S(1)}, u32[]{:S(2)}, u32[]{:S(2)}) %collective-permute-start.11) | collective-permute-done | bytes 12320 | tf_op jit(solution)/shard_map/ppermute | solution.py:36
  178.6 4.4 %collective-permute-start.12 = (f32[24,128]{1,0:T(8,128)S(1)}, f32[24,128]{1,0:T(8,128)S(1)}, u32[]{:S(2)}, u32[]{:S(2)}) collective-permute-start(f32[24,128]{1,0:T(8,128)S(1)} %add.120), channel_id=1, source_target_pairs={{0,32},{4,36},{8,40},{12,44},{16,48},{20,52},{24,56},{28,60},{32,0... | collective-permute-start | bytes 36872 | tf_op jit(solution)/shard_map/ppermute | solution.py:36
  183.0 2.1 collective-permute-done.12
  185.1 2.3 %collective-permute-start.13 = (f32[24,128]{1,0:T(8,128)S(1)}, f32[24,128]{1,0:T(8,128)S(1)}, u32[]{:S(2)}, u32[]{:S(2)}) collective-permute-start(f32[24,128]{1,0:T(8,128)S(1)} %add.121), channel_id=1, source_target_pairs={{0,192},{4,196},{8,200},{12,204},{16,208},{20,212},{24,216},{28,22... | collective-permute-start | bytes 36872 | tf_op jit(solution)/shard_map/ppermute | solution.py:36
  188.5 3.0 %collective-permute-done.14 = f32[24,128]{1,0:T(8,128)S(1)} collective-permute-done((f32[24,128]{1,0:T(8,128)S(1)}, f32[24,128]{1,0:T(8,128)S(1)}, u32[]{:S(2)}, u32[]{:S(2)}) %collective-permute-start.14) | collective-permute-done | bytes 12320 | tf_op jit(solution)/shard_map/ppermute | solution.py:36
  191.7 5.0 %collective-permute-start.16 = (f32[96,128]{1,0:T(8,128)S(1)}, f32[96,128]{1,0:T(8,128)S(1)}, u32[]{:S(2)}, u32[]{:S(2)}) collective-permute-start(f32[96,128]{1,0:T(8,128)S(1)} %constant_dynamic-slice_fusion), channel_id=1, source_target_pairs={{0,4},{4,0},{8,12},{12,8},{16,20},{20,16},{24,28},{28,24},{32,36},... | collective-permute-start | bytes 147464 | tf_op jit(solution)/shard_map/ppermute | solution.py:36
  198.9 1.3 copy-done
  200.3 3.3 %finish.1 = f32[64,2048]{1,0:T(8,128)} custom-call(s32[128]{0:T(128)} %reshape.139.refs_0_.wanted_ref, bf16[64,128,128]{2,1,0:T(8,128)(2,1)} %copy-done, f32[64,2048]{1,0:T(8,128)} %back_local.1.local_ref), custom_call_target="tpu_custom_call" | custom-call | flops 1048576 | bytes 4194304 | tf_op jit(solution)/shard_map/finish/pallas_call | solution.py:356
  (77 shorter events, 20.1 us)
Async XLA Ops:
  7.2 49.1 %all-gather.6.cloned.1.call-start = ((), (), s32[]{:S(2)}) async-start(), calls=%async_computation.4 | async-start | bytes 4456448 | tf_op jit(solution)/shard_map/all_gather | solution.py:404
  7.9 89.9 %all-gather.4.cloned.1.call-start = ((), (), s32[]{:S(2)}) async-start(), calls=%async_computation.3 | async-start | bytes 1556480 | tf_op jit(solution)/shard_map/all_gather | solution.py:414
  12.2 25.8 %copy-start.8 = (s32[64]{0:T(128)}, s32[64]{0:T(128)S(1)}, u32[]{:S(2)}) copy-start(s32[64]{0:T(128)S(1)} %get-tuple-element.30.slots_ref) | copy-start | bytes 772
  12.9 9.0 %all-to-all-start = ((s32[4,1,32]{2,1,0:T(1,128)}), s32[4,1,32]{2,1,0:T(1,128)S(1)}, u32[]{:S(2)}, u32[]{:S(2)}) async-start(s32[4,1,32]{2,1,0:T(1,128)} %bitcast.3), calls=%async_computation | async-start | bytes 4096 | tf_op jit(solution)/shard_map/all_to_all | solution.py:406
  22.0 21.0 %all-to-all-start.1 = ((s32[64,1,2]{2,1,0:T(1,128)}), s32[64,1,2]{2,1,0:T(1,128)S(1)}, u32[]{:S(2)}, u32[]{:S(2)}) async-start(s32[64,1,2]{2,1,0:T(1,128)} %bitcast.5), calls=%async_computation.1 | async-start | bytes 65536 | tf_op jit(solution)/shard_map/all_to_all | solution.py:409
  60.7 14.8 %collective-permute-start = (bf16[32,64,128]{2,1,0:T(8,128)(2,1)}, bf16[32,64,128]{2,1,0:T(8,128)(2,1)S(1)}, u32[]{:S(2)}, u32[]{:S(2)}) collective-permute-start(bf16[32,64,128]{2,1,0:T(8,128)(2,1)} %get-tuple-element.14), channel_id=1, source_target_pairs={{0,64},{4,68},{8,72},{12,76},{16,80},{20,84},{24,88},{28,92},{32,9... | collective-permute-start | bytes 1572872 | tf_op jit(solution)/shard_map/ppermute | solution.py:36
  62.0 25.7 %collective-permute-start.1 = (bf16[32,64,128]{2,1,0:T(8,128)(2,1)}, bf16[32,64,128]{2,1,0:T(8,128)(2,1)S(1)}, u32[]{:S(2)}, u32[]{:S(2)}) collective-permute-start(bf16[32,64,128]{2,1,0:T(8,128)(2,1)} %get-tuple-element.15), channel_id=1, source_target_pairs={{0,128},{4,132},{8,136},{12,140},{16,144},{20,148},{24,152},{28,15... | collective-permute-start | bytes 1572872 | tf_op jit(solution)/shard_map/ppermute | solution.py:36
  64.4 23.3 %collective-permute-start.2 = (bf16[32,64,128]{2,1,0:T(8,128)(2,1)}, bf16[32,64,128]{2,1,0:T(8,128)(2,1)S(1)}, u32[]{:S(2)}, u32[]{:S(2)}) collective-permute-start(bf16[32,64,128]{2,1,0:T(8,128)(2,1)} %get-tuple-element.16), channel_id=1, source_target_pairs={{0,192},{4,196},{8,200},{12,204},{16,208},{20,212},{24,216},{28,22... | collective-permute-start | bytes 1572872 | tf_op jit(solution)/shard_map/ppermute | solution.py:36
  75.5 12.1 %copy-start.1 = (bf16[32,64,128]{2,1,0:T(8,128)(2,1)}, bf16[32,64,128]{2,1,0:T(8,128)(2,1)S(1)}, u32[]{:S(2)}) copy-start(bf16[32,64,128]{2,1,0:T(8,128)(2,1)S(1)} %collective-permute-done.refs_1_) | copy-start | bytes 1572868
  87.6 0.8 copy-start.2
  87.6 1.0 copy-start.3
  93.5 8.2 %collective-permute-start.3 = (bf16[64,2048]{1,0:T(8,128)(2,1)}, bf16[64,2048]{1,0:T(8,128)(2,1)S(1)}, u32[]{:S(2)}, u32[]{:S(2)}) collective-permute-start(bf16[64,2048]{1,0:T(8,128)(2,1)} %agg_remote.1.own_ref), channel_id=1, source_target_pairs={{0,1},{1,2},{2,3},{3,0},{4,5},{5,6},{6,7},{7,4},{8,9},{9,10},{10,1... | collective-permute-start | bytes 786440 | tf_op jit(solution)/shard_map/ppermute | solution.py:421
  94.8 6.9 %collective-permute-start.4 = (bf16[64,2048]{1,0:T(8,128)(2,1)}, bf16[64,2048]{1,0:T(8,128)(2,1)S(1)}, u32[]{:S(2)}, u32[]{:S(2)}) collective-permute-start(bf16[64,2048]{1,0:T(8,128)(2,1)} %agg_remote.1.own_ref), channel_id=1, source_target_pairs={{0,3},{1,0},{2,1},{3,2},{4,7},{5,4},{6,5},{7,6},{8,11},{9,8},{10,9... | collective-permute-start | bytes 786440 | tf_op jit(solution)/shard_map/ppermute | solution.py:421
  96.2 11.9 %collective-permute-start.5 = (bf16[64,2048]{1,0:T(8,128)(2,1)}, bf16[64,2048]{1,0:T(8,128)(2,1)S(1)}, u32[]{:S(2)}, u32[]{:S(2)}) collective-permute-start(bf16[64,2048]{1,0:T(8,128)(2,1)} %agg_remote.1.own_ref), channel_id=1, source_target_pairs={{0,2},{1,3},{2,0},{3,1},{4,6},{5,7},{6,4},{7,5},{8,10},{9,11},{10,... | collective-permute-start | bytes 786440 | tf_op jit(solution)/shard_map/ppermute | solution.py:421
  101.7 6.4 %copy-start.4 = (bf16[64,2048]{1,0:T(8,128)(2,1)}, bf16[64,2048]{1,0:T(8,128)(2,1)S(1)}, u32[]{:S(2)}) copy-start(bf16[64,2048]{1,0:T(8,128)(2,1)S(1)} %collective-permute-done.3.low_ref) | copy-start | bytes 786436
  101.7 6.4 %copy-start.5 = (bf16[64,2048]{1,0:T(8,128)(2,1)}, bf16[64,2048]{1,0:T(8,128)(2,1)S(1)}, u32[]{:S(2)}) copy-start(bf16[64,2048]{1,0:T(8,128)(2,1)S(1)} %collective-permute-done.4.high_ref) | copy-start | bytes 786436
  108.1 0.7 copy-start.6
  118.3 80.7 %all-to-all-start.2 = ((bf16[64,128,128]{2,1,0:T(8,128)(2,1)}), bf16[64,128,128]{2,1,0:T(8,128)(2,1)S(1)}, u32[]{:S(2)}, u32[]{:S(2)}) async-start(bf16[64,128,128]{2,1,0:T(8,128)(2,1)} %back_remote.1._), calls=%async_computation.2 | async-start | bytes 4194304 | tf_op jit(solution)/shard_map/all_to_all | solution.py:427
  128.0 4.0 %copy-start.7 = (f32[192,128]{1,0:T(8,128)S(1)}, f32[192,128]{1,0:T(8,128)}, u32[]{:S(2)}) copy-start(f32[192,128]{1,0:T(8,128)} %get-tuple-element.21) | copy-start | bytes 294916
  132.0 1.4 collective-permute-start.6
  133.4 3.9 %collective-permute-start.9 = (f32[24,128]{1,0:T(8,128)S(1)}, f32[24,128]{1,0:T(8,128)S(1)}, u32[]{:S(2)}, u32[]{:S(2)}) collective-permute-start(f32[24,128]{1,0:T(8,128)S(1)} %get-tuple-element.26), channel_id=1, source_target_pairs={{0,192},{4,196},{8,200},{12,204},{16,208},{20,212},{24,216},{28,22... | collective-permute-start | bytes 36872 | tf_op jit(solution)/shard_map/ppermute | solution.py:36
  136.2 5.0 %collective-permute-start.8 = (f32[24,128]{1,0:T(8,128)S(1)}, f32[24,128]{1,0:T(8,128)S(1)}, u32[]{:S(2)}, u32[]{:S(2)}) collective-permute-start(f32[24,128]{1,0:T(8,128)S(1)} %get-tuple-element.27), channel_id=1, source_target_pairs={{0,128},{4,132},{8,136},{12,140},{16,144},{20,148},{24,152},{28,15... | collective-permute-start | bytes 36872 | tf_op jit(solution)/shard_map/ppermute | solution.py:36
  136.6 4.9 %collective-permute-start.7 = (f32[24,128]{1,0:T(8,128)S(1)}, f32[24,128]{1,0:T(8,128)S(1)}, u32[]{:S(2)}, u32[]{:S(2)}) collective-permute-start(f32[24,128]{1,0:T(8,128)S(1)} %get-tuple-element.25), channel_id=1, source_target_pairs={{0,64},{4,68},{8,72},{12,76},{16,80},{20,84},{24,88},{28,92},{32,9... | collective-permute-start | bytes 36872 | tf_op jit(solution)/shard_map/ppermute | solution.py:36
  141.5 33.3 %collective-permute-start.10 = (f32[24,128]{1,0:T(8,128)S(1)}, f32[24,128]{1,0:T(8,128)S(1)}, u32[]{:S(2)}, u32[]{:S(2)}) collective-permute-start(f32[24,128]{1,0:T(8,128)S(1)} %add_add_fusion), channel_id=1, source_target_pairs={{0,8},{4,12},{8,0},{12,4},{16,24},{20,28},{24,16},{28,20},{32,40},... | collective-permute-start | bytes 36872 | tf_op jit(solution)/shard_map/ppermute | solution.py:36
  174.9 3.8 %collective-permute-start.11 = (f32[24,128]{1,0:T(8,128)S(1)}, f32[24,128]{1,0:T(8,128)S(1)}, u32[]{:S(2)}, u32[]{:S(2)}) collective-permute-start(f32[24,128]{1,0:T(8,128)S(1)} %add.119), channel_id=1, source_target_pairs={{0,16},{4,20},{8,24},{12,28},{16,0},{20,4},{24,8},{28,12},{32,48},... | collective-permute-start | bytes 36872 | tf_op jit(solution)/shard_map/ppermute | solution.py:36
  178.6 6.5 %collective-permute-start.12 = (f32[24,128]{1,0:T(8,128)S(1)}, f32[24,128]{1,0:T(8,128)S(1)}, u32[]{:S(2)}, u32[]{:S(2)}) collective-permute-start(f32[24,128]{1,0:T(8,128)S(1)} %add.120), channel_id=1, source_target_pairs={{0,32},{4,36},{8,40},{12,44},{16,48},{20,52},{24,56},{28,60},{32,0... | collective-permute-start | bytes 36872 | tf_op jit(solution)/shard_map/ppermute | solution.py:36
  185.1 3.4 %collective-permute-start.13 = (f32[24,128]{1,0:T(8,128)S(1)}, f32[24,128]{1,0:T(8,128)S(1)}, u32[]{:S(2)}, u32[]{:S(2)}) collective-permute-start(f32[24,128]{1,0:T(8,128)S(1)} %add.121), channel_id=1, source_target_pairs={{0,192},{4,196},{8,200},{12,204},{16,208},{20,212},{24,216},{28,22... | collective-permute-start | bytes 36872 | tf_op jit(solution)/shard_map/ppermute | solution.py:36
  187.4 4.1 %collective-permute-start.14 = (f32[24,128]{1,0:T(8,128)S(1)}, f32[24,128]{1,0:T(8,128)S(1)}, u32[]{:S(2)}, u32[]{:S(2)}) collective-permute-start(f32[24,128]{1,0:T(8,128)S(1)} %add.121), channel_id=1, source_target_pairs={{0,128},{4,132},{8,136},{12,140},{16,144},{20,148},{24,152},{28,15... | collective-permute-start | bytes 36872 | tf_op jit(solution)/shard_map/ppermute | solution.py:36
  187.8 3.8 %collective-permute-start.15 = (f32[24,128]{1,0:T(8,128)S(1)}, f32[24,128]{1,0:T(8,128)S(1)}, u32[]{:S(2)}, u32[]{:S(2)}) collective-permute-start(f32[24,128]{1,0:T(8,128)S(1)} %add.121), channel_id=1, source_target_pairs={{0,64},{4,68},{8,72},{12,76},{16,80},{20,84},{24,88},{28,92},{32,9... | collective-permute-start | bytes 36872 | tf_op jit(solution)/shard_map/ppermute | solution.py:36
  191.7 5.9 %collective-permute-start.16 = (f32[96,128]{1,0:T(8,128)S(1)}, f32[96,128]{1,0:T(8,128)S(1)}, u32[]{:S(2)}, u32[]{:S(2)}) collective-permute-start(f32[96,128]{1,0:T(8,128)S(1)} %constant_dynamic-slice_fusion), channel_id=1, source_target_pairs={{0,4},{4,0},{8,12},{12,8},{16,20},{20,16},{24,28},{28,24},{32,36},... | collective-permute-start | bytes 147464 | tf_op jit(solution)/shard_map/ppermute | solution.py:36
  198.9 1.3 copy-start
Sparse Core Ops, SparseCore 0:
  9.8 46.3 all-gather.5
  58.1 25.1 all-gather.3

commit v5 on v2

--- a/solution.py
+++ b/solution.py
@@ -23,7 +23,7 @@
 NY, NZ, NC = 4, 8, 2
 CAP = 2
 ORDER = (0, 1, 7, 2, 6, 3, 5, 4)
-GROUPS = ((0, 3), (3, 5), (5, 8))
+GROUPS = ((0, 5), (5, 8))
 PER = NZ * CAP
 
 
@@ -64,7 +64,7 @@
         in_specs=[SMEM] + [VMEM] * len(sources) + [ANY] * len(after),
         out_specs=[VMEM] * NY,
         name="pack",
-        cost_estimate=pl.CostEstimate(flops=0, bytes_accessed=3 << 20, transcendentals=0),
+        cost_estimate=pl.CostEstimate(flops=0, bytes_accessed=12 << 20, transcendentals=0),
     )(wanted, *sources, *after)
 
 
@@ -75,7 +75,7 @@
 STEP = 4
 
 
-def agg_local_kernel(cols_ref, feats_ref, tiles_ref, out_ref):
+def agg_local_kernel(cols_ref, feats_ref, tiles_ref, _, out_ref):
     i = pl.program_id(0)
     count, block = tiles_ref.shape[1], tiles_ref.shape[2]
     for rr in range(STEP):
@@ -91,7 +91,7 @@
         out_ref[:, rr * block : (rr + 1) * block] = acc
 
 
-def agg_local(cols, feats, tiles):
+def agg_local(cols, feats, tiles, after):
     row_blocks, _, block, _ = tiles.shape
     width = feats.shape[0]
     return pl.pallas_call(
@@ -102,13 +102,14 @@
             SMEM,
             pl.BlockSpec(feats.shape, lambda i: (0, 0)),
             pl.BlockSpec((STEP, TL, block, block), lambda i: (i, 0, 0, 0)),
+            ANY,
         ],
         out_specs=pl.BlockSpec((width, STEP * block), lambda i: (0, i)),
         name="agg_local",
         cost_estimate=pl.CostEstimate(
             flops=2 * width * row_blocks * TL * block * block, bytes_accessed=3 << 20, transcendentals=0
         ),
-    )(cols, feats, tiles)
+    )(cols, feats, tiles, after)
 
 
 def agg_remote_kernel(slots_ref, tiles_ref, local_ref, *refs):
@@ -173,14 +174,15 @@
     w_ref,
     bias_ref,
     wown_ref,
+    request_ref,
     hid_ref,
     g_ref,
-    gw_ref,
-    gb_ref,
+    sums_ref,
     agg_scr,
     hid_scr,
     wt_scr,
     gb_scr,
+    gw_scr,
 ):
     i = pl.program_id(0)
     width = own_ref.shape[0]
@@ -193,7 +195,7 @@
     @pl.when(i == 0)
     def _():
         wt_scr[...] = w_ref[...].astype(F32).T.astype(BF)
-        gw_ref[...] = jnp.zeros_like(gw_ref)
+        gw_scr[...] = jnp.zeros_like(gw_scr)
         gb_scr[...] = jnp.zeros_like(gb_scr)
 
     agg_scr[rows(3)] = low_ref[...]
@@ -213,14 +215,17 @@
     gb_scr[...] += total
     grad_b = grad_pre.astype(BF)
     g_ref[...] = dot(wown_ref[...], grad_b, (1, 0)).astype(BF)
-    gw_ref[...] += dot(own_ref[...], grad_b, (1, 1))
+    gw_scr[...] += dot(own_ref[...], grad_b, (1, 1))
 
     @pl.when(i == pl.num_programs(0) - 1)
     def _():
-        gb_ref[...] = gb_scr[rows(0)]
-
-
-def mid(me, pieces, packed, w_own):
+        hid_all = gw_scr.shape[1]
+        sums_ref[:, 0, :hid_all] = gw_scr[...]
+        sums_ref[:, 0, hid_all : hid_all + 128] = gb_scr[rows(0)]
+        sums_ref[:, 0, hid_all + 128 :] = request_ref[...]
+
+
+def mid(me, pieces, packed, w_own, request):
     own, low, high, far = pieces
     width, nodes = own.shape
     hid_all = packed.shape[0]
@@ -232,8 +237,7 @@
         out_shape=(
             jax.ShapeDtypeStruct((width, nodes), BF),
             jax.ShapeDtypeStruct((width, nodes), BF),
-            jax.ShapeDtypeStruct((width, hid_all), F32),
-            jax.ShapeDtypeStruct((width, 128), F32),
+            jax.ShapeDtypeStruct((width, 1, hid_all + 256), F32),
         ),
         in_specs=[
             SMEM,
@@ -245,18 +249,19 @@
             pl.BlockSpec((hid_all, hid_all), lambda i: (0, nodes // hid_all)),
             pl.BlockSpec((hid_all, 128), lambda i: (0, (nodes + hid_all) // 128)),
             pl.BlockSpec((width, hid_all), lambda i: (0, 0)),
+            pl.BlockSpec((width, 128), lambda i: (0, 0)),
         ],
         out_specs=(
             pl.BlockSpec((width, chunk), col),
             pl.BlockSpec((width, chunk), col),
-            pl.BlockSpec((width, hid_all), lambda i: (0, 0)),
-            pl.BlockSpec((width, 128), lambda i: (0, 0)),
+            pl.BlockSpec((width, 1, hid_all + 256), lambda i: (0, 0, 0)),
         ),
         scratch_shapes=[
             pltpu.VMEM((hid_all, chunk), BF),
             pltpu.VMEM((hid_all, chunk), BF),
             pltpu.VMEM((hid_all, hid_all), BF),
             pltpu.VMEM((hid_all, 128), F32),
+            pltpu.VMEM((width, hid_all), F32),
         ],
         name="mid",
         cost_estimate=pl.CostEstimate(
@@ -264,7 +269,7 @@
             bytes_accessed=3 << 20,
             transcendentals=nodes * hid_all,
         ),
-    )(me, own, low, high, far, packed, packed, packed, w_own)
+    )(me, own, low, high, far, packed, packed, packed, w_own, request)
 
 
 def back_remote_kernel(slots_ref, g_ref, tiles_ref, out_ref):
@@ -347,7 +352,39 @@
     )(cols, g, tiles)
 
 
-def finish_kernel(wanted_ref, recv_ref, local_ref, out_ref, odd_scr):
+EXTRA = 8
+
+
+def ride_kernel(divisor, sums_ref, _, send_ref, rider_scr, sem):
+    span = sums_ref.shape[2] // 128 - 1
+    total = jnp.sum(sums_ref[...], axis=0) / divisor
+    rider_scr[...] = jnp.zeros_like(rider_scr)
+    for k in range(span):
+        row = total[:, k * 128 : (k + 1) * 128]
+        high = row.astype(BF)
+        low = (row - high.astype(F32)).astype(BF)
+        peers = rider_scr.shape[0]
+        rider_scr[:, k : k + 1] = jnp.broadcast_to(high[None], (peers, 1, 128))
+        rider_scr[:, span + k : span + k + 1] = jnp.broadcast_to(low[None], (peers, 1, 128))
+    rows = send_ref.shape[1] - EXTRA
+    copy = pltpu.make_async_copy(rider_scr, send_ref.at[:, pl.ds(rows, EXTRA)], sem)
+    copy.start()
+    copy.wait()
+
+
+def ride(divisor, sums, send):
+    return pl.pallas_call(
+        functools.partial(ride_kernel, divisor),
+        out_shape=jax.ShapeDtypeStruct(send.shape, send.dtype),
+        in_specs=[VMEM, ANY],
+        out_specs=ANY,
+        scratch_shapes=[pltpu.VMEM((send.shape[0], EXTRA, 128), BF), pltpu.SemaphoreType.DMA],
+        input_output_aliases={1: 0},
+        name="ride",
+    )(sums, send)
+
+
+def finish_kernel(wanted_ref, recv_ref, local_ref, out_ref, gw_ref, gb_ref, odd_scr):
     width, block = out_ref.shape[0], recv_ref.shape[2]
     out_ref[...] = local_ref[...]
     odd_scr[...] = jnp.zeros_like(odd_scr)
@@ -361,14 +398,24 @@
 
     lax.fori_loop(0, recv_ref.shape[0], body, 0, unroll=4)
     out_ref[...] += odd_scr[...]
-
-
-def finish(wanted, recv, local):
+    rider = recv_ref[:, CAP * width :].astype(F32)
+    span = gw_ref.shape[1] // 128 + 1
+    for k in range(span - 1):
+        gw_ref[:, k * 128 : (k + 1) * 128] = rider[:, k] + rider[:, span + k]
+    gb_ref[...] = rider[:, span - 1] + rider[:, 2 * span - 1]
+
+
+def finish(wanted, recv, local, hid_all):
+    width = local.shape[0]
     return pl.pallas_call(
         finish_kernel,
-        out_shape=jax.ShapeDtypeStruct(local.shape, F32),
+        out_shape=(
+            jax.ShapeDtypeStruct(local.shape, F32),
+            jax.ShapeDtypeStruct((width, hid_all), F32),
+            jax.ShapeDtypeStruct((width, 128), F32),
+        ),
         in_specs=[SMEM, VMEM, VMEM],
-        out_specs=VMEM,
+        out_specs=(VMEM, VMEM, VMEM),
         scratch_shapes=[pltpu.VMEM(local.shape, F32)],
         name="finish",
         cost_estimate=pl.CostEstimate(flops=recv.size, bytes_accessed=4 << 20, transcendentals=0),
@@ -423,64 +470,43 @@
 
     up, down, parts = [feats], [feats], []
     for k in range(1, NZ // 2):
-        up.append(shift(up[-1], dz=1))
-        down.append(shift(down[-1], dz=-1))
+        late = (k == 3) & (wanted[0] > 1 << 20)
+        up.append(shift(jnp.where(late, jnp.zeros_like(feats), up[-1]) if k == 3 else up[-1], dz=1))
+        down.append(shift(jnp.where(late, jnp.zeros_like(feats), down[-1]) if k == 3 else down[-1], dz=-1))
     far_up = shift(up[-1][: width // 2], dz=1)
     far_down = shift(down[-1][width // 2 :], dz=-1)
-    groups = ((feats, down[1], up[1]), (down[2], up[2]), (down[3], up[3], far_up, far_down))
+
+    bias_cols = jnp.pad(jnp.stack(split_bf16(bias, 3), axis=1), ((0, 0), (0, 125)))
+    packed = jnp.concatenate([cotangent, weight, bias_cols], axis=1)
+    packed = lax.all_gather(packed, "feat", axis=0, tiled=True)
+
     after = []
-    agg = agg_local(local_cols, feats, tiles)
+    groups = ((feats, down[1], up[1], down[2], up[2]), (down[3], up[3], far_up, far_down))
     for group, sources in zip(GROUPS, groups):
         packs = pack(group, wanted, sources, block, after)
-        after = [packs[0], agg]
         moved = [packs[0]] + [shift(packs[ys], dy=ys) for ys in range(1, NY)]
         parts += moved
         parts.append(shift(jnp.concatenate([m[1:] for m in moved]), dc=1))
-
-    bias_cols = jnp.pad(jnp.stack(split_bf16(bias, 3), axis=1), ((0, 0), (0, 125)))
-    packed = jnp.concatenate([cotangent, weight, bias_cols], axis=1)
-    packed = lax.all_gather(packed, "feat", axis=0, tiled=True)
-
+        after = [packs[0]]
+    agg = agg_local(local_cols, feats, tiles, after[0])
     agg = agg_remote(near, parts, tiles, agg)
 
     pieces = [agg] + [
         lax.ppermute(agg, "feat", [(k, (k + s) % fpeers) for k in range(fpeers)]) for s in (1, 3, 2)
     ]
     me = lax.axis_index("feat").astype(jnp.int32).reshape(1)
-    hidden_out, g, grad_w, grad_b = mid(me, pieces, packed, weight)
-
-    divisor = math.sqrt(nodes_dev * peers)
-    per = grad_w.size // peers
-    per_b = width // peers
-    sums = jnp.concatenate(
-        [
-            grad_w.reshape(peers, per),
-            jnp.sum(grad_b, axis=1).reshape(peers, per_b),
-            table(slots).reshape(peers, CAP).astype(F32),
-        ],
-        axis=1,
-    )
+    holding = jnp.pad(table(slots).reshape(peers, CAP).astype(F32), ((0, 0), (0, 128 - CAP)))
+    hidden_out, g, sums = mid(me, pieces, packed, weight, holding)
+
     sums = lax.all_to_all(sums, "rows", split_axis=0, concat_axis=0, tiled=True)
-    holders = sums[:, per + per_b :].astype(jnp.int32).reshape(-1)
-    total = jnp.sum(sums[:, : per + per_b], axis=0) / divisor
-    span = -(-total.size // block)
-    total = jnp.pad(total, (0, span * block - total.size)).reshape(span, block)
-    extra = -(-2 * span // 8) * 8
-    rider = jnp.concatenate(split_bf16(total, 2) + [jnp.zeros((extra - 2 * span, block), BF)])
-
-    send = back_remote(slots, g, tiles, peers, extra)
-    send = send.at[:, CAP * width :].set(jnp.broadcast_to(rider, (peers, extra, block)))
+    holders = sums[:, 0, hid_all + 128 : hid_all + 128 + CAP].astype(jnp.int32).reshape(-1)
+    send = back_remote(slots, g, tiles, peers, EXTRA)
+    own = back_local(local_cols, g, tiles)
+    own, sums = lax.optimization_barrier((own, sums))
+    send = ride(math.sqrt(nodes_dev * peers), sums, send)
     recv = lax.all_to_all(send, "rows", split_axis=0, concat_axis=0, tiled=True)
-    own = back_local(local_cols, g, tiles)
-    grad_input = finish(holders, recv, own)
-    totals = recv[:, CAP * width :].astype(F32)
-    totals = (totals[:, :span] + totals[:, span : 2 * span]).reshape(peers, -1)
-    return (
-        hidden_out,
-        grad_input,
-        totals[:, :per].reshape(width, hid_all),
-        totals[:, per : per + per_b].reshape(width),
-    )
+    grad_input, grad_w, grad_b = finish(holders, recv, own, hid_all)
+    return hidden_out, grad_input, grad_w, jnp.sum(grad_b, axis=1)
 
 
 def solution(mesh):

time: 199 us -> 207 us (1.040)
  waiting for transfers between devices: 74.6 us -> 82.5 us
    ppermute x24 -> x20, waiting for transfers between devices: 8.78 us -> 17.3 us  [shift(): return lax.ppermute(x, 'rows', pairs)]
    ppermute x24 -> x20, starting transfers between devices: 44.9 us -> 39.6 us  [shift(): return lax.ppermute(x, 'rows', pairs)]
    all_to_all x1, starting transfers between devices: 4.82 us -> 8.48 us  [local(): recv = lax.all_to_all(send, 'rows', split_axis=0, concat_axis=0, tiled=True)]
    all_to_all x1, waiting for transfers between devices: 5.51 us -> 1.85 us  [local(): sums = lax.all_to_all(sums, 'rows', split_axis=0, concat_axis=0, tiled=True)]
    all_to_all x1, waiting for transfers between devices: 49.1 us -> 52.3 us  [local(): recv = lax.all_to_all(send, 'rows', split_axis=0, concat_axis=0, tiled=True)]
    unnamed x64 -> x48, local copies, waits for them, and re-layouts: 2.85 us -> 5.68 us
    pallas_call x3 -> x2, Pallas kernels: 6.53 us -> 4.89 us  [pack(): pl.pallas_call(functools.partial(pack_kernel, first, count, len(sources)...]
    pallas_call x1 -> x2, Pallas kernels: 3.75 us -> 5.2 us  [the longest x1 3.42 us: finish(): pl.pallas_call(finish_kernel, out_shape=(jax.ShapeDtypeStruct(local.shape...]
  transfers between devices with their start and end apart: 30 -> 26, of which waited for: 11 -> 11; matrix products, arithmetic and copies ran while one was open for 4% -> 5% of each run, Pallas kernels for 12% -> 11%
where the time goes in v5:
time: 207 us; the launch traced here: 206 us
  waiting for transfers between devices  82.5 us (40%)
  starting transfers between devices  59.5 us (29%)
  Pallas kernels  32.5 us (16%)
  between operations  14.5 us (7%)
  local copies, waits for them, and re-layouts  10.9 us (5%)
  other arithmetic  6.14 us (3%)
    all_to_all x1, waiting for transfers between devices, local(): recv = lax.all_to_all(send, 'rows', split_axis=0, concat_axis=0, tiled=True)  52.3 us
    ppermute x20, starting transfers between devices, shift(): return lax.ppermute(x, 'rows', pairs)  39.6 us
    ppermute x20, waiting for transfers between devices, shift(): return lax.ppermute(x, 'rows', pairs)  17.3 us
    ppermute x3, waiting for transfers between devices, local(): lax.ppermute(agg, 'feat', [(k, (k + s) % fpeers) for k in range(fpeers)])  11 us
    all_to_all x1, starting transfers between devices, local(): recv = lax.all_to_all(send, 'rows', split_axis=0, concat_axis=0, tiled=True)  8.48 us
    all_to_all x1, starting transfers between devices, local(): sums = lax.all_to_all(sums, 'rows', split_axis=0, concat_axis=0, tiled=True)  7.1 us
    unnamed x48, local copies, waits for them, and re-layouts  5.68 us
    pallas_call x1, Pallas kernels, mid(): pl.pallas_call(mid_kernel, grid=(nodes // chunk,), out_shape=(jax.ShapeDt...  4.95 us
  transfers between devices with their start and end apart: 26, of which 11 were waited for; matrix products, arithmetic and copies ran while one was open for 5% of the time, Pallas kernels for 11%

profile of v5, /device:TPU:1, one launch (start us, length us, event | category | flops | bytes accessed | tf_op | source)
XLA Modules:
  0.0 206.0 jit_solution(11486292034132351674)
XLA Ops:
  7.2 6.5 %collective-permute-start.4 = (bf16[64,2048]{1,0:T(8,128)(2,1)}, bf16[64,2048]{1,0:T(8,128)(2,1)S(1)}, u32[]{:S(2)}, u32[]{:S(2)}) collective-permute-start(bf16[64,2048]{1,0:T(8,128)(2,1)} %feats_ref.1), channel_id=1, source_target_pairs={{0,56},{4,60},{8,0},{12,4},{16,8},{20,12},{24,16},{28,20},{32,24},... | collective-permute-start | bytes 786440 | tf_op jit(solution)/shard_map/ppermute | solution.py:37
  16.9 5.1 %collective-permute-done.7.refs_3_ = bf16[64,2048]{1,0:T(8,128)(2,1)S(1)} collective-permute-done((bf16[64,2048]{1,0:T(8,128)(2,1)}, bf16[64,2048]{1,0:T(8,128)(2,1)S(1)}, u32[]{:S(2)}, u32[]{:S(2)}) %collective-permute-start.7) | collective-permute-done | bytes 262176 | tf_op jit(solution)/shard_map/ppermute | solution.py:37
  22.0 1.8 fusion.1
  25.3 2.6 %collective-permute-start.2 = (s32[2,16]{1,0:T(2,128)S(1)}, s32[2,16]{1,0:T(2,128)S(1)}, u32[]{:S(2)}, u32[]{:S(2)}) collective-permute-start(s32[2,16]{1,0:T(2,128)S(1)} %bitcast.31), channel_id=1, source_target_pairs={{0,128},{4,132},{8,136},{12,140},{16,144},{20,148},{24,152},{28,15... | collective-permute-start | bytes 392 | tf_op jit(solution)/shard_map/ppermute | solution.py:37
  29.2 1.4 collective-permute-done.1
  30.8 2.6 %collective-permute-start.5 = (bf16[64,2048]{1,0:T(8,128)(2,1)S(1)}, bf16[64,2048]{1,0:T(8,128)(2,1)S(1)}, u32[]{:S(2)}, u32[]{:S(2)}) collective-permute-start(bf16[64,2048]{1,0:T(8,128)(2,1)S(1)} %collective-permute-done.4.refs_2_), channel_id=1, source_target_pairs={{0,56},{4,60},{8,0},{12,4},{16,8},{20,12},{24,16},{28,20},{32,24},... | collective-permute-start | bytes 786440 | tf_op jit(solution)/shard_map/ppermute | solution.py:37
  33.5 3.2 %collective-permute-done.5.refs_4_ = bf16[64,2048]{1,0:T(8,128)(2,1)S(1)} collective-permute-done((bf16[64,2048]{1,0:T(8,128)(2,1)S(1)}, bf16[64,2048]{1,0:T(8,128)(2,1)S(1)}, u32[]{:S(2)}, u32[]{:S(2)}) %collective-permute-start.5) | collective-permute-done | bytes 262176 | tf_op jit(solution)/shard_map/ppermute | solution.py:37
  36.7 3.2 %collective-permute-start.6 = (bf16[64,2048]{1,0:T(8,128)(2,1)S(1)}, bf16[64,2048]{1,0:T(8,128)(2,1)S(1)}, u32[]{:S(2)}, u32[]{:S(2)}) collective-permute-start(bf16[64,2048]{1,0:T(8,128)(2,1)S(1)} %broadcast_select_fusion.1), channel_id=1, source_target_pairs={{0,56},{4,60},{8,0},{12,4},{16,8},{20,12},{24,16},{28,20},{32,24},... | collective-permute-start | bytes 786440 | tf_op jit(solution)/shard_map/ppermute | solution.py:37
  39.9 2.7 %pack.2 = (bf16[2,10,64,128]{3,2,1,0:T(8,128)(2,1)}, bf16[2,10,64,128]{3,2,1,0:T(8,128)(2,1)}, bf16[2,10,64,128]{3,2,1,0:T(8,128)(2,1)}, bf16[2,10,64,128]{3,2,1,0:T(8,128)(2,1)}) custom-call(s32[128]{0:T(128)} %copy-done.21, bf16[64,2048]{1,0:T(8,128)(2,1)} %feats_ref.1, bf16[64,2048]{1,0:T(8,128)(2,1)} %copy-done.14, bf16[64,2048]{1,0:T(8,128)(2,1)} %copy-done.15, ...), custom_call_target="tpu_custom_call" | custom-call | bytes 12582912 | tf_op jit(solution)/shard_map/pack/pallas_call | solution.py:61
  42.6 2.1 %collective-permute-start.14 = (bf16[2,10,64,128]{3,2,1,0:T(8,128)(2,1)}, bf16[2,10,64,128]{3,2,1,0:T(8,128)(2,1)S(1)}, u32[]{:S(2)}, u32[]{:S(2)}) collective-permute-start(bf16[2,10,64,128]{3,2,1,0:T(8,128)(2,1)} %get-tuple-element.24), channel_id=1, source_target_pairs={{0,192},{4,196},{8,200},{12,204},{16,208},{20,212},{24,216},{28,22... | collective-permute-start | bytes 983048 | tf_op jit(solution)/shard_map/ppermute | solution.py:37
  45.4 2.9 %collective-permute-start.11 = (bf16[32,2048]{1,0:T(8,128)(2,1)S(1)}, bf16[32,2048]{1,0:T(8,128)(2,1)S(1)}, u32[]{:S(2)}, u32[]{:S(2)}) collective-permute-start(bf16[32,2048]{1,0:T(8,128)(2,1)S(1)} %slice.107), channel_id=1, source_target_pairs={{0,56},{4,60},{8,0},{12,4},{16,8},{20,12},{24,16},{28,20},{32,24},... | collective-permute-start | bytes 393224 | tf_op jit(solution)/shard_map/ppermute | solution.py:37
  49.2 2.9 %collective-permute-done.14.refs_3_ = bf16[2,10,64,128]{3,2,1,0:T(8,128)(2,1)S(1)} collective-permute-done((bf16[2,10,64,128]{3,2,1,0:T(8,128)(2,1)}, bf16[2,10,64,128]{3,2,1,0:T(8,128)(2,1)S(1)}, u32[]{:S(2)}, u32[]{:S(2)}) %collective-permute-start.14) | collective-permute-done | bytes 327712 | tf_op jit(solution)/shard_map/ppermute | solution.py:37
  52.4 4.3 %collective-permute-done.12.refs_1_ = bf16[2,10,64,128]{3,2,1,0:T(8,128)(2,1)S(1)} collective-permute-done((bf16[2,10,64,128]{3,2,1,0:T(8,128)(2,1)}, bf16[2,10,64,128]{3,2,1,0:T(8,128)(2,1)S(1)}, u32[]{:S(2)}, u32[]{:S(2)}) %collective-permute-start.12) | collective-permute-done | bytes 327712 | tf_op jit(solution)/shard_map/ppermute | solution.py:37
  58.1 2.2 %pack.3 = (bf16[2,6,64,128]{3,2,1,0:T(8,128)(2,1)}, bf16[2,6,64,128]{3,2,1,0:T(8,128)(2,1)}, bf16[2,6,64,128]{3,2,1,0:T(8,128)(2,1)}, bf16[2,6,64,128]{3,2,1,0:T(8,128)(2,1)}) custom-call(s32[128]{0:T(128)} %copy-done.21, bf16[64,2048]{1,0:T(8,128)(2,1)} %copy-done.9, bf16[64,2048]{1,0:T(8,128)(2,1)} %copy-done.8, bf16[32,2048]{1,0:T(8,128)(2,1)} %copy-done.19, ...), custom_call_target="tpu_custom_call" | custom-call | bytes 12582912 | tf_op jit(solution)/shard_map/pack/pallas_call | solution.py:61
  63.1 7.2 %collective-permute-start.15 = (bf16[4,10,64,128]{3,2,1,0:T(8,128)(2,1)S(1)}, bf16[4,10,64,128]{3,2,1,0:T(8,128)(2,1)S(1)}, u32[]{:S(2)}, u32[]{:S(2)}) collective-permute-start(bf16[4,10,64,128]{3,2,1,0:T(8,128)(2,1)S(1)} %pad_maximum_fusion), channel_id=1, source_target_pairs={{0,4},{4,0},{8,12},{12,8},{16,20},{20,16},{24,28},{28,24},{32,36},... | collective-permute-start | bytes 1966088 | tf_op jit(solution)/shard_map/ppermute | solution.py:37
  72.1 5.8 %collective-permute-start.19 = (bf16[4,6,64,128]{3,2,1,0:T(8,128)(2,1)}, bf16[4,6,64,128]{3,2,1,0:T(8,128)(2,1)S(1)}, u32[]{:S(2)}, u32[]{:S(2)}) collective-permute-start(bf16[4,6,64,128]{3,2,1,0:T(8,128)(2,1)} %pad_maximum_fusion.1), channel_id=1, source_target_pairs={{0,4},{4,0},{8,12},{12,8},{16,20},{20,16},{24,28},{28,24},{32,36},... | collective-permute-start | bytes 1179656 | tf_op jit(solution)/shard_map/ppermute | solution.py:37
  78.5 4.1 %agg_local.1.local_ref = f32[64,2048]{1,0:T(8,128)} custom-call(s32[64]{0:T(128)} %reshape.203.cols_ref, bf16[64,2048]{1,0:T(8,128)(2,1)} %feats_ref.1, bf16[16,8,128,128]{3,2,1,0:T(8,128)(2,1)} %bitcast.23, bf16[2,6,64,128]{3,2,1,0:T(8,128)(2,1)} %get-tuple-element.21._.refs_5_), custom_call_target="tpu_custom_call" | custom-call | flops 134217728 | bytes 3145728 | tf_op jit(solution)/shard_map/agg_local/pallas_call | solution.py:97
  84.3 4.8 %agg_remote.1.own_ref = bf16[64,2048]{1,0:T(8,128)(2,1)} custom-call(s32[64]{0:T(128)} %copy-done.22, bf16[16,8,128,128]{3,2,1,0:T(8,128)(2,1)} %bitcast.24, f32[64,2048]{1,0:T(8,128)} %agg_local.1.local_ref, bf16[2,10,64,128]{3,2,1,0:T(8,128)(2,1)} %get-tuple-element.20.refs_5_.refs_0_, bf16[2,10,64,128]{3,2,1,0:T(8,128)(2,1)} %copy-done.5, ...), custom_call_target="tpu_custom_call" | custom-call | flops 134217728 | bytes 5242880 | tf_op jit(solution)/shard_map/agg_remote/pallas_call | solution.py:148
  90.3 1.5 collective-permute-start.21
  91.8 1.5 collective-permute-start.22
  94.1 4.4 %collective-permute-done.20.low_ref = bf16[64,2048]{1,0:T(8,128)(2,1)S(1)} collective-permute-done((bf16[64,2048]{1,0:T(8,128)(2,1)}, bf16[64,2048]{1,0:T(8,128)(2,1)S(1)}, u32[]{:S(2)}, u32[]{:S(2)}) %collective-permute-start.20) | collective-permute-done | bytes 262176 | tf_op jit(solution)/shard_map/ppermute | solution.py:495
  98.5 6.6 %collective-permute-done.22.far_ref = bf16[64,2048]{1,0:T(8,128)(2,1)S(1)} collective-permute-done((bf16[64,2048]{1,0:T(8,128)(2,1)}, bf16[64,2048]{1,0:T(8,128)(2,1)S(1)}, u32[]{:S(2)}, u32[]{:S(2)}) %collective-permute-start.22) | collective-permute-done | bytes 262176 | tf_op jit(solution)/shard_map/ppermute | solution.py:495
  105.8 4.9 %mid.1 = (bf16[64,2048]{1,0:T(8,128)(2,1)}, bf16[64,2048]{1,0:T(8,128)(2,1)}, f32[64,1,512]{2,1,0:T(1,128)}) custom-call(s32[1]{0:T(128)} %bitcast.me_ref, bf16[64,2048]{1,0:T(8,128)(2,1)} %agg_remote.1.own_ref, bf16[64,2048]{1,0:T(8,128)(2,1)} %copy-done.16, bf16[64,2048]{1,0:T(8,128)(2,1)} %copy-done.17, bf16[64,2048]{1,0:T(8,128)(2,1)} %copy-done.18, ...), custom_call_target="tpu_custom_call" | custom-call | flops 402653184 | bytes 3145728 | tf_op jit(solution)/shard_map/mid/pallas_call | solution.py:234
  110.7 7.1 %all-to-all-start = ((f32[64,1,512]{2,1,0:T(1,128)}), f32[64,1,512]{2,1,0:T(1,128)S(1)}, u32[]{:S(2)}, u32[]{:S(2)}) async-start(f32[64,1,512]{2,1,0:T(1,128)} %get-tuple-element.29), calls=%async_computation | async-start | bytes 262144 | tf_op jit(solution)/shard_map/all_to_all | solution.py:501
  117.8 3.9 %back_local.1.local_ref = f32[64,2048]{1,0:T(8,128)} custom-call(s32[64]{0:T(128)} %reshape.203.cols_ref, bf16[64,2048]{1,0:T(8,128)(2,1)} %get-tuple-element.30.g_ref, bf16[16,8,128,128]{3,2,1,0:T(8,128)(2,1)} %bitcast.25), custom_call_target="tpu_custom_call" | custom-call | flops 134217728 | bytes 3145728 | tf_op jit(solution)/shard_map/back_local/pallas_call | solution.py:338
  121.7 4.6 %back_remote.1._ = bf16[64,136,128]{2,1,0:T(8,128)(2,1)} custom-call(s32[64]{0:T(128)} %copy-done.23, bf16[64,2048]{1,0:T(8,128)(2,1)} %get-tuple-element.30.g_ref, bf16[16,8,128,128]{3,2,1,0:T(8,128)(2,1)} %bitcast.26), custom_call_target="tpu_custom_call" | custom-call | flops 134217728 | bytes 5242880 | tf_op jit(solution)/shard_map/back_remote/pallas_call | solution.py:300
  126.3 1.9 all-to-all-done.sums_ref
  128.8 1.8 ride.1
  130.6 8.5 %all-to-all-start.1 = ((bf16[64,136,128]{2,1,0:T(8,128)(2,1)}), bf16[64,136,128]{2,1,0:T(8,128)(2,1)S(1)}, u32[]{:S(2)}, u32[]{:S(2)}) async-start(bf16[64,136,128]{2,1,0:T(8,128)(2,1)} %ride.1), calls=%async_computation.1 | async-start | bytes 4456448 | tf_op jit(solution)/shard_map/all_to_all | solution.py:507
  140.6 52.3 %all-to-all-done.1.recv_ref = bf16[64,136,128]{2,1,0:T(8,128)(2,1)S(1)} async-done(((bf16[64,136,128]{2,1,0:T(8,128)(2,1)}), bf16[64,136,128]{2,1,0:T(8,128)(2,1)S(1)}, u32[]{:S(2)}, u32[]{:S(2)}) %all-to-all-start.1) | async-done | bytes 2228256 | tf_op jit(solution)/shard_map/all_to_all | solution.py:507
  194.3 3.4 %finish.1 = (f32[64,2048]{1,0:T(8,128)}, f32[64,256]{1,0:T(8,128)}, f32[64,128]{1,0:T(8,128)}) custom-call(s32[128]{0:T(128)} %convert_element_type.36.wanted_ref, bf16[64,136,128]{2,1,0:T(8,128)(2,1)} %copy-done, f32[64,2048]{1,0:T(8,128)} %back_local.1.local_ref), custom_call_target="tpu_custom_call" | custom-call | flops 1114112 | bytes 4194304 | tf_op jit(solution)/shard_map/finish/pallas_call | solution.py:410
  197.8 1.4 reduce_sum.19
  (117 shorter events, 22.4 us)
Async XLA Ops:
  7.2 97.9 %all-gather.2.cloned.1.call-start = ((), (), s32[]{:S(2)}) async-start(), calls=%async_computation.2 | async-start | bytes 1556480 | tf_op jit(solution)/shard_map/all_gather | solution.py:481
  7.2 23.6 %collective-permute-start.4 = (bf16[64,2048]{1,0:T(8,128)(2,1)}, bf16[64,2048]{1,0:T(8,128)(2,1)S(1)}, u32[]{:S(2)}, u32[]{:S(2)}) collective-permute-start(bf16[64,2048]{1,0:T(8,128)(2,1)} %feats_ref.1), channel_id=1, source_target_pairs={{0,56},{4,60},{8,0},{12,4},{16,8},{20,12},{24,16},{28,20},{32,24},... | collective-permute-start | bytes 786440 | tf_op jit(solution)/shard_map/ppermute | solution.py:37
  13.7 8.3 %collective-permute-start.7 = (bf16[64,2048]{1,0:T(8,128)(2,1)}, bf16[64,2048]{1,0:T(8,128)(2,1)S(1)}, u32[]{:S(2)}, u32[]{:S(2)}) collective-permute-start(bf16[64,2048]{1,0:T(8,128)(2,1)} %feats_ref.1), channel_id=1, source_target_pairs={{0,8},{4,12},{8,16},{12,20},{16,24},{20,28},{24,32},{28,36},{32,40... | collective-permute-start | bytes 786440 | tf_op jit(solution)/shard_map/ppermute | solution.py:37
  14.9 37.3 %copy-start.22 = (s32[64]{0:T(128)}, s32[64]{0:T(128)S(1)}, u32[]{:S(2)}) copy-start(s32[64]{0:T(128)S(1)} %get-tuple-element.45.slots_ref) | copy-start | bytes 772
  14.9 37.3 %copy-start.23 = (s32[64]{0:T(128)}, s32[64]{0:T(128)S(1)}, u32[]{:S(2)}) copy-start(s32[64]{0:T(128)S(1)} %get-tuple-element.44.slots_ref) | copy-start | bytes 772
  15.1 8.8 %collective-permute-start = (s32[4,16]{1,0:T(4,128)S(1)}, s32[4,16]{1,0:T(4,128)S(1)}, u32[]{:S(2)}, u32[]{:S(2)}) collective-permute-start(s32[4,16]{1,0:T(4,128)S(1)} %squeeze.14), channel_id=1, source_target_pairs={{0,4},{4,0},{8,12},{12,8},{16,20},{20,16},{24,28},{28,24},{32,36},... | collective-permute-start | bytes 776 | tf_op jit(solution)/shard_map/ppermute | solution.py:37
  22.0 17.9 %copy-start.15 = (bf16[64,2048]{1,0:T(8,128)(2,1)}, bf16[64,2048]{1,0:T(8,128)(2,1)S(1)}, u32[]{:S(2)}) copy-start(bf16[64,2048]{1,0:T(8,128)(2,1)S(1)} %collective-permute-done.7.refs_3_) | copy-start | bytes 786436
  22.0 11.4 %collective-permute-start.8 = (bf16[64,2048]{1,0:T(8,128)(2,1)S(1)}, bf16[64,2048]{1,0:T(8,128)(2,1)S(1)}, u32[]{:S(2)}, u32[]{:S(2)}) collective-permute-start(bf16[64,2048]{1,0:T(8,128)(2,1)S(1)} %collective-permute-done.7.refs_3_), channel_id=1, source_target_pairs={{0,8},{4,12},{8,16},{12,20},{16,24},{20,28},{24,32},{28,36},{32,40... | collective-permute-start | bytes 786440 | tf_op jit(solution)/shard_map/ppermute | solution.py:37
  23.9 5.1 %collective-permute-start.3 = (s32[2,16]{1,0:T(2,128)S(1)}, s32[2,16]{1,0:T(2,128)S(1)}, u32[]{:S(2)}, u32[]{:S(2)}) collective-permute-start(s32[2,16]{1,0:T(2,128)S(1)} %bitcast.33), channel_id=1, source_target_pairs={{0,64},{4,68},{8,72},{12,76},{16,80},{20,84},{24,88},{28,92},{32,9... | collective-permute-start | bytes 392 | tf_op jit(solution)/shard_map/ppermute | solution.py:37
  25.3 3.9 %collective-permute-start.2 = (s32[2,16]{1,0:T(2,128)S(1)}, s32[2,16]{1,0:T(2,128)S(1)}, u32[]{:S(2)}, u32[]{:S(2)}) collective-permute-start(s32[2,16]{1,0:T(2,128)S(1)} %bitcast.31), channel_id=1, source_target_pairs={{0,128},{4,132},{8,136},{12,140},{16,144},{20,148},{24,152},{28,15... | collective-permute-start | bytes 392 | tf_op jit(solution)/shard_map/ppermute | solution.py:37
  27.9 2.7 %collective-permute-start.1 = (s32[2,16]{1,0:T(2,128)S(1)}, s32[2,16]{1,0:T(2,128)S(1)}, u32[]{:S(2)}, u32[]{:S(2)}) collective-permute-start(s32[2,16]{1,0:T(2,128)S(1)} %bitcast.29), channel_id=1, source_target_pairs={{0,192},{4,196},{8,200},{12,204},{16,208},{20,212},{24,216},{28,22... | collective-permute-start | bytes 392 | tf_op jit(solution)/shard_map/ppermute | solution.py:37
  30.8 5.9 %collective-permute-start.5 = (bf16[64,2048]{1,0:T(8,128)(2,1)S(1)}, bf16[64,2048]{1,0:T(8,128)(2,1)S(1)}, u32[]{:S(2)}, u32[]{:S(2)}) collective-permute-start(bf16[64,2048]{1,0:T(8,128)(2,1)S(1)} %collective-permute-done.4.refs_2_), channel_id=1, source_target_pairs={{0,56},{4,60},{8,0},{12,4},{16,8},{20,12},{24,16},{28,20},{32,24},... | collective-permute-start | bytes 786440 | tf_op jit(solution)/shard_map/ppermute | solution.py:37
  33.4 11.9 %collective-permute-start.9 = (bf16[64,2048]{1,0:T(8,128)(2,1)S(1)}, bf16[64,2048]{1,0:T(8,128)(2,1)S(1)}, u32[]{:S(2)}, u32[]{:S(2)}) collective-permute-start(bf16[64,2048]{1,0:T(8,128)(2,1)S(1)} %broadcast_select_fusion), channel_id=1, source_target_pairs={{0,8},{4,12},{8,16},{12,20},{16,24},{20,28},{24,32},{28,36},{32,40... | collective-permute-start | bytes 786440 | tf_op jit(solution)/shard_map/ppermute | solution.py:37
  36.7 8.7 %collective-permute-start.6 = (bf16[64,2048]{1,0:T(8,128)(2,1)S(1)}, bf16[64,2048]{1,0:T(8,128)(2,1)S(1)}, u32[]{:S(2)}, u32[]{:S(2)}) collective-permute-start(bf16[64,2048]{1,0:T(8,128)(2,1)S(1)} %broadcast_select_fusion.1), channel_id=1, source_target_pairs={{0,56},{4,60},{8,0},{12,4},{16,8},{20,12},{24,16},{28,20},{32,24},... | collective-permute-start | bytes 786440 | tf_op jit(solution)/shard_map/ppermute | solution.py:37
  42.6 9.5 %collective-permute-start.14 = (bf16[2,10,64,128]{3,2,1,0:T(8,128)(2,1)}, bf16[2,10,64,128]{3,2,1,0:T(8,128)(2,1)S(1)}, u32[]{:S(2)}, u32[]{:S(2)}) collective-permute-start(bf16[2,10,64,128]{3,2,1,0:T(8,128)(2,1)} %get-tuple-element.24), channel_id=1, source_target_pairs={{0,192},{4,196},{8,200},{12,204},{16,208},{20,212},{24,216},{28,22... | collective-permute-start | bytes 983048 | tf_op jit(solution)/shard_map/ppermute | solution.py:37
  44.7 7.7 %collective-permute-start.13 = (bf16[2,10,64,128]{3,2,1,0:T(8,128)(2,1)}, bf16[2,10,64,128]{3,2,1,0:T(8,128)(2,1)S(1)}, u32[]{:S(2)}, u32[]{:S(2)}) collective-permute-start(bf16[2,10,64,128]{3,2,1,0:T(8,128)(2,1)} %get-tuple-element.23), channel_id=1, source_target_pairs={{0,128},{4,132},{8,136},{12,140},{16,144},{20,148},{24,152},{28,15... | collective-permute-start | bytes 983048 | tf_op jit(solution)/shard_map/ppermute | solution.py:37
  44.7 12.0 %collective-permute-start.12 = (bf16[2,10,64,128]{3,2,1,0:T(8,128)(2,1)}, bf16[2,10,64,128]{3,2,1,0:T(8,128)(2,1)S(1)}, u32[]{:S(2)}, u32[]{:S(2)}) collective-permute-start(bf16[2,10,64,128]{3,2,1,0:T(8,128)(2,1)} %get-tuple-element.22), channel_id=1, source_target_pairs={{0,64},{4,68},{8,72},{12,76},{16,80},{20,84},{24,88},{28,92},{32,9... | collective-permute-start | bytes 983048 | tf_op jit(solution)/shard_map/ppermute | solution.py:37
  45.3 11.4 %collective-permute-start.10 = (bf16[32,2048]{1,0:T(8,128)(2,1)S(1)}, bf16[32,2048]{1,0:T(8,128)(2,1)S(1)}, u32[]{:S(2)}, u32[]{:S(2)}) collective-permute-start(bf16[32,2048]{1,0:T(8,128)(2,1)S(1)} %slice.106), channel_id=1, source_target_pairs={{0,8},{4,12},{8,16},{12,20},{16,24},{20,28},{24,32},{28,36},{32,40... | collective-permute-start | bytes 393224 | tf_op jit(solution)/shard_map/ppermute | solution.py:37
  45.4 11.3 %collective-permute-start.11 = (bf16[32,2048]{1,0:T(8,128)(2,1)S(1)}, bf16[32,2048]{1,0:T(8,128)(2,1)S(1)}, u32[]{:S(2)}, u32[]{:S(2)}) collective-permute-start(bf16[32,2048]{1,0:T(8,128)(2,1)S(1)} %slice.107), channel_id=1, source_target_pairs={{0,56},{4,60},{8,0},{12,4},{16,8},{20,12},{24,16},{28,20},{32,24},... | collective-permute-start | bytes 393224 | tf_op jit(solution)/shard_map/ppermute | solution.py:37
  52.1 20.0 %copy-start.3 = (bf16[2,10,64,128]{3,2,1,0:T(8,128)(2,1)}, bf16[2,10,64,128]{3,2,1,0:T(8,128)(2,1)S(1)}, u32[]{:S(2)}) copy-start(bf16[2,10,64,128]{3,2,1,0:T(8,128)(2,1)S(1)} %collective-permute-done.14.refs_3_) | copy-start | bytes 983044
  52.4 19.7 %copy-start.4 = (bf16[2,10,64,128]{3,2,1,0:T(8,128)(2,1)}, bf16[2,10,64,128]{3,2,1,0:T(8,128)(2,1)S(1)}, u32[]{:S(2)}) copy-start(bf16[2,10,64,128]{3,2,1,0:T(8,128)(2,1)S(1)} %collective-permute-done.13.refs_2_) | copy-start | bytes 983044
  56.7 26.0 %copy-start.5 = (bf16[2,10,64,128]{3,2,1,0:T(8,128)(2,1)}, bf16[2,10,64,128]{3,2,1,0:T(8,128)(2,1)S(1)}, u32[]{:S(2)}) copy-start(bf16[2,10,64,128]{3,2,1,0:T(8,128)(2,1)S(1)} %collective-permute-done.12.refs_1_) | copy-start | bytes 983044
  60.3 10.9 %collective-permute-start.16 = (bf16[2,6,64,128]{3,2,1,0:T(8,128)(2,1)}, bf16[2,6,64,128]{3,2,1,0:T(8,128)(2,1)S(1)}, u32[]{:S(2)}, u32[]{:S(2)}) collective-permute-start(bf16[2,6,64,128]{3,2,1,0:T(8,128)(2,1)} %get-tuple-element.25), channel_id=1, source_target_pairs={{0,64},{4,68},{8,72},{12,76},{16,80},{20,84},{24,88},{28,92},{32,9... | collective-permute-start | bytes 589832 | tf_op jit(solution)/shard_map/ppermute | solution.py:37
  60.3 10.9 %collective-permute-start.17 = (bf16[2,6,64,128]{3,2,1,0:T(8,128)(2,1)}, bf16[2,6,64,128]{3,2,1,0:T(8,128)(2,1)S(1)}, u32[]{:S(2)}, u32[]{:S(2)}) collective-permute-start(bf16[2,6,64,128]{3,2,1,0:T(8,128)(2,1)} %get-tuple-element.26), channel_id=1, source_target_pairs={{0,128},{4,132},{8,136},{12,140},{16,144},{20,148},{24,152},{28,15... | collective-permute-start | bytes 589832 | tf_op jit(solution)/shard_map/ppermute | solution.py:37
  61.7 9.5 %collective-permute-start.18 = (bf16[2,6,64,128]{3,2,1,0:T(8,128)(2,1)}, bf16[2,6,64,128]{3,2,1,0:T(8,128)(2,1)S(1)}, u32[]{:S(2)}, u32[]{:S(2)}) collective-permute-start(bf16[2,6,64,128]{3,2,1,0:T(8,128)(2,1)} %get-tuple-element.27), channel_id=1, source_target_pairs={{0,192},{4,196},{8,200},{12,204},{16,208},{20,212},{24,216},{28,22... | collective-permute-start | bytes 589832 | tf_op jit(solution)/shard_map/ppermute | solution.py:37
  63.1 19.6 %collective-permute-start.15 = (bf16[4,10,64,128]{3,2,1,0:T(8,128)(2,1)S(1)}, bf16[4,10,64,128]{3,2,1,0:T(8,128)(2,1)S(1)}, u32[]{:S(2)}, u32[]{:S(2)}) collective-permute-start(bf16[4,10,64,128]{3,2,1,0:T(8,128)(2,1)S(1)} %pad_maximum_fusion), channel_id=1, source_target_pairs={{0,4},{4,0},{8,12},{12,8},{16,20},{20,16},{24,28},{28,24},{32,36},... | collective-permute-start | bytes 1966088 | tf_op jit(solution)/shard_map/ppermute | solution.py:37
  72.1 10.5 %collective-permute-start.19 = (bf16[4,6,64,128]{3,2,1,0:T(8,128)(2,1)}, bf16[4,6,64,128]{3,2,1,0:T(8,128)(2,1)S(1)}, u32[]{:S(2)}, u32[]{:S(2)}) collective-permute-start(bf16[4,6,64,128]{3,2,1,0:T(8,128)(2,1)} %pad_maximum_fusion.1), channel_id=1, source_target_pairs={{0,4},{4,0},{8,12},{12,8},{16,20},{20,16},{24,28},{28,24},{32,36},... | collective-permute-start | bytes 1179656 | tf_op jit(solution)/shard_map/ppermute | solution.py:37
  89.1 9.4 %collective-permute-start.20 = (bf16[64,2048]{1,0:T(8,128)(2,1)}, bf16[64,2048]{1,0:T(8,128)(2,1)S(1)}, u32[]{:S(2)}, u32[]{:S(2)}) collective-permute-start(bf16[64,2048]{1,0:T(8,128)(2,1)} %agg_remote.1.own_ref), channel_id=1, source_target_pairs={{0,1},{1,2},{2,3},{3,0},{4,5},{5,6},{6,7},{7,4},{8,9},{9,10},{10,1... | collective-permute-start | bytes 786440 | tf_op jit(solution)/shard_map/ppermute | solution.py:495
  90.3 8.2 %collective-permute-start.21 = (bf16[64,2048]{1,0:T(8,128)(2,1)}, bf16[64,2048]{1,0:T(8,128)(2,1)S(1)}, u32[]{:S(2)}, u32[]{:S(2)}) collective-permute-start(bf16[64,2048]{1,0:T(8,128)(2,1)} %agg_remote.1.own_ref), channel_id=1, source_target_pairs={{0,3},{1,0},{2,1},{3,2},{4,7},{5,4},{6,5},{7,6},{8,11},{9,8},{10,9... | collective-permute-start | bytes 786440 | tf_op jit(solution)/shard_map/ppermute | solution.py:495
  91.8 13.3 %collective-permute-start.22 = (bf16[64,2048]{1,0:T(8,128)(2,1)}, bf16[64,2048]{1,0:T(8,128)(2,1)S(1)}, u32[]{:S(2)}, u32[]{:S(2)}) collective-permute-start(bf16[64,2048]{1,0:T(8,128)(2,1)} %agg_remote.1.own_ref), channel_id=1, source_target_pairs={{0,2},{1,3},{2,0},{3,1},{4,6},{5,7},{6,4},{7,5},{8,10},{9,11},{10,... | collective-permute-start | bytes 786440 | tf_op jit(solution)/shard_map/ppermute | solution.py:495
  110.7 17.5 %all-to-all-start = ((f32[64,1,512]{2,1,0:T(1,128)}), f32[64,1,512]{2,1,0:T(1,128)S(1)}, u32[]{:S(2)}, u32[]{:S(2)}) async-start(f32[64,1,512]{2,1,0:T(1,128)} %get-tuple-element.29), calls=%async_computation | async-start | bytes 262144 | tf_op jit(solution)/shard_map/all_to_all | solution.py:501
  130.6 62.3 %all-to-all-start.1 = ((bf16[64,136,128]{2,1,0:T(8,128)(2,1)}), bf16[64,136,128]{2,1,0:T(8,128)(2,1)S(1)}, u32[]{:S(2)}, u32[]{:S(2)}) async-start(bf16[64,136,128]{2,1,0:T(8,128)(2,1)} %ride.1), calls=%async_computation.1 | async-start | bytes 4456448 | tf_op jit(solution)/shard_map/all_to_all | solution.py:507
  (18 other events, 104.2 us)
Sparse Core Ops, SparseCore 0:
  23.9 26.2 all-gather.1

commit v6 on v2

--- a/solution.py
+++ b/solution.py
@@ -27,13 +27,13 @@
 PER = NZ * CAP
 
 
-def shift(x, dy=0, dz=0, dc=0):
+def shift(x, dy=0, dz=0, dc=0, flip_y=0, flip_z=0):
     pairs = []
     for y in range(NY):
         for z in range(NZ):
             for c in range(NC):
-                to = ((y + dy) % NY * NZ + (z + dz) % NZ) * NC + (c + dc) % NC
-                pairs.append(((y * NZ + z) * NC + c, to))
+                to_y, to_z = ((y ^ flip_y) + dy) % NY, ((z ^ flip_z) + dz) % NZ
+                pairs.append(((y * NZ + z) * NC + c, (to_y * NZ + to_z) * NC + (c + dc) % NC))
     return lax.ppermute(x, "rows", pairs)
 
 
@@ -165,6 +165,7 @@
 
 def mid_kernel(
     me_ref,
+    _,
     own_ref,
     low_ref,
     high_ref,
@@ -175,12 +176,13 @@
     wown_ref,
     hid_ref,
     g_ref,
-    gw_ref,
-    gb_ref,
+    keep_ref,
+    give_ref,
     agg_scr,
     hid_scr,
     wt_scr,
     gb_scr,
+    sums_scr,
 ):
     i = pl.program_id(0)
     width = own_ref.shape[0]
@@ -193,7 +195,7 @@
     @pl.when(i == 0)
     def _():
         wt_scr[...] = w_ref[...].astype(F32).T.astype(BF)
-        gw_ref[...] = jnp.zeros_like(gw_ref)
+        sums_scr[...] = jnp.zeros_like(sums_scr)
         gb_scr[...] = jnp.zeros_like(gb_scr)
 
     agg_scr[rows(3)] = low_ref[...]
@@ -213,18 +215,24 @@
     gb_scr[...] += total
     grad_b = grad_pre.astype(BF)
     g_ref[...] = dot(wown_ref[...], grad_b, (1, 0)).astype(BF)
-    gw_ref[...] += dot(own_ref[...], grad_b, (1, 1))
+    grad_w = dot(own_ref[...], grad_b, (1, 1))
+    for k in range(grad_w.shape[1] // 128):
+        sums_scr[k * width : (k + 1) * width] += grad_w[:, k * 128 : (k + 1) * 128]
 
     @pl.when(i == pl.num_programs(0) - 1)
     def _():
-        gb_ref[...] = gb_scr[rows(0)]
-
-
-def mid(me, pieces, packed, w_own):
+        half = keep_ref.shape[0]
+        sums_scr[-width:] = gb_scr[rows(0)]
+        keep_ref[...] = sums_scr[pl.ds(pl.multiple_of(me_ref[1] * half, half), half)]
+        give_ref[...] = sums_scr[pl.ds(pl.multiple_of((1 - me_ref[1]) * half, half), half)]
+
+
+def mid(me, pieces, packed, w_own, after):
     own, low, high, far = pieces
     width, nodes = own.shape
     hid_all = packed.shape[0]
     chunk = 512
+    half = width * (hid_all // 128 + 1) // NC
     col = lambda i: (0, i)
     return pl.pallas_call(
         mid_kernel,
@@ -232,11 +240,12 @@
         out_shape=(
             jax.ShapeDtypeStruct((width, nodes), BF),
             jax.ShapeDtypeStruct((width, nodes), BF),
-            jax.ShapeDtypeStruct((width, hid_all), F32),
-            jax.ShapeDtypeStruct((width, 128), F32),
+            jax.ShapeDtypeStruct((half, 128), F32),
+            jax.ShapeDtypeStruct((half, 128), F32),
         ),
         in_specs=[
             SMEM,
+            ANY,
             pl.BlockSpec((width, chunk), col),
             pl.BlockSpec((width, chunk), col),
             pl.BlockSpec((width, chunk), col),
@@ -249,14 +258,15 @@
         out_specs=(
             pl.BlockSpec((width, chunk), col),
             pl.BlockSpec((width, chunk), col),
-            pl.BlockSpec((width, hid_all), lambda i: (0, 0)),
-            pl.BlockSpec((width, 128), lambda i: (0, 0)),
+            pl.BlockSpec((half, 128), lambda i: (0, 0)),
+            pl.BlockSpec((half, 128), lambda i: (0, 0)),
         ),
         scratch_shapes=[
             pltpu.VMEM((hid_all, chunk), BF),
             pltpu.VMEM((hid_all, chunk), BF),
             pltpu.VMEM((hid_all, hid_all), BF),
             pltpu.VMEM((hid_all, 128), F32),
+            pltpu.VMEM((NC * half, 128), F32),
         ],
         name="mid",
         cost_estimate=pl.CostEstimate(
@@ -264,10 +274,10 @@
             bytes_accessed=3 << 20,
             transcendentals=nodes * hid_all,
         ),
-    )(me, own, low, high, far, packed, packed, packed, w_own)
-
-
-def back_remote_kernel(slots_ref, g_ref, tiles_ref, out_ref):
+    )(me, after, own, low, high, far, packed, packed, packed, w_own)
+
+
+def back_remote_kernel(slots_ref, g_ref, tiles_ref, _, out_ref):
     i = pl.program_id(0)
     width = g_ref.shape[0]
     count, block = tiles_ref.shape[1], tiles_ref.shape[2]
@@ -288,28 +298,29 @@
                 out_ref[slot // CAP, pl.ds(row, width)] = term[:, k * block : (k + 1) * block]
 
 
-def back_remote(slots, g, tiles, peers, extra):
+def back_remote(slots, g, tiles, peers, after):
     row_blocks, per_block, block, _ = tiles.shape
     rem = per_block - TL
     width = g.shape[0]
     return pl.pallas_call(
         back_remote_kernel,
         grid=(row_blocks // STEP,),
-        out_shape=jax.ShapeDtypeStruct((peers, CAP * width + extra, block), BF),
+        out_shape=jax.ShapeDtypeStruct((peers, CAP * width, block), BF),
         in_specs=[
             SMEM,
             pl.BlockSpec((width, STEP * block), lambda i: (0, i)),
             pl.BlockSpec((STEP, rem, block, block), lambda i: (i, 1, 0, 0)),
+            ANY,
         ],
-        out_specs=pl.BlockSpec((peers, CAP * width + extra, block), lambda i: (0, 0, 0)),
+        out_specs=pl.BlockSpec((peers, CAP * width, block), lambda i: (0, 0, 0)),
         name="back_remote",
         cost_estimate=pl.CostEstimate(
             flops=2 * width * row_blocks * rem * block * block, bytes_accessed=5 << 20, transcendentals=0
         ),
-    )(slots, g, tiles)
-
-
-def back_local_kernel(cols_ref, g_ref, tiles_ref, out_ref):
+    )(slots, g, tiles, after)
+
+
+def back_local_kernel(cols_ref, g_ref, tiles_ref, _, out_ref):
     i = pl.program_id(0)
     count, block = tiles_ref.shape[1], tiles_ref.shape[2]
 
@@ -327,7 +338,7 @@
                 out_ref[:, lanes(cols_ref[base + k], block)] += term[:, k * block : (k + 1) * block]
 
 
-def back_local(cols, g, tiles):
+def back_local(cols, g, tiles, after):
     row_blocks, _, block, _ = tiles.shape
     width = g.shape[0]
     return pl.pallas_call(
@@ -338,23 +349,26 @@
             SMEM,
             pl.BlockSpec((width, STEP * block), lambda i: (0, i)),
             pl.BlockSpec((STEP, TL, block, block), lambda i: (i, 0, 0, 0)),
+            ANY,
         ],
         out_specs=pl.BlockSpec(g.shape, lambda i: (0, 0)),
         name="back_local",
         cost_estimate=pl.CostEstimate(
             flops=2 * width * row_blocks * TL * block * block, bytes_accessed=3 << 20, transcendentals=0
         ),
-    )(cols, g, tiles)
-
-
-def finish_kernel(wanted_ref, recv_ref, local_ref, out_ref, odd_scr):
+    )(cols, g, tiles, after)
+
+
+def finish_kernel(place_ref, wanted_ref, recv_ref, local_ref, out_ref, odd_scr):
     width, block = out_ref.shape[0], recv_ref.shape[2]
     out_ref[...] = local_ref[...]
     odd_scr[...] = jnp.zeros_like(odd_scr)
 
     def body(p, carry):
-        even = lanes(jnp.maximum(wanted_ref[p * CAP], 0), block)
-        odd = lanes(jnp.maximum(wanted_ref[p * CAP + 1], 0), block)
+        back = (p // (NZ * NC) - place_ref[0]) & (NY - 1)
+        base = ((p // NC % NZ * NY + back) * NC + ((p ^ place_ref[1]) & 1)) * CAP
+        even = lanes(jnp.maximum(wanted_ref[base], 0), block)
+        odd = lanes(jnp.maximum(wanted_ref[base + 1], 0), block)
         out_ref[:, even] += recv_ref[p, :width].astype(F32)
         odd_scr[:, odd] += recv_ref[p, width : 2 * width].astype(F32)
         return carry
@@ -363,16 +377,16 @@
     out_ref[...] += odd_scr[...]
 
 
-def finish(wanted, recv, local):
+def finish(place, wanted, recv, local):
     return pl.pallas_call(
         finish_kernel,
         out_shape=jax.ShapeDtypeStruct(local.shape, F32),
-        in_specs=[SMEM, VMEM, VMEM],
+        in_specs=[SMEM, SMEM, VMEM, VMEM],
         out_specs=VMEM,
         scratch_shapes=[pltpu.VMEM(local.shape, F32)],
         name="finish",
         cost_estimate=pl.CostEstimate(flops=recv.size, bytes_accessed=4 << 20, transcendentals=0),
-    )(wanted, recv, local)
+    )(place, wanted, recv, local)
 
 
 def split_bf16(x, terms):
@@ -407,7 +421,11 @@
     rank = jnp.sum(earlier.astype(jnp.int32), axis=1)
     slots = owner * CAP + rank
     ahead = (owner // NC - z) & (NZ - 1)
-    pos = jnp.maximum(jnp.where(ahead <= NZ // 2, 2 * ahead - 1, 2 * (NZ - ahead)), 0)
+
+    def place_of(ahead):
+        return jnp.maximum(jnp.where(ahead <= NZ // 2, 2 * ahead - 1, 2 * (NZ - ahead)), 0)
+
+    pos = place_of(ahead)
     back = (y - owner // (NZ * NC)) & (NY - 1)
     other = (owner ^ c) & 1
     near = ((other * NY + back) * NZ + pos) * CAP + rank
@@ -446,41 +464,37 @@
     pieces = [agg] + [
         lax.ppermute(agg, "feat", [(k, (k + s) % fpeers) for k in range(fpeers)]) for s in (1, 3, 2)
     ]
-    me = lax.axis_index("feat").astype(jnp.int32).reshape(1)
-    hidden_out, g, grad_w, grad_b = mid(me, pieces, packed, weight)
-
-    divisor = math.sqrt(nodes_dev * peers)
-    per = grad_w.size // peers
-    per_b = width // peers
-    sums = jnp.concatenate(
-        [
-            grad_w.reshape(peers, per),
-            jnp.sum(grad_b, axis=1).reshape(peers, per_b),
-            table(slots).reshape(peers, CAP).astype(F32),
-        ],
-        axis=1,
-    )
-    sums = lax.all_to_all(sums, "rows", split_axis=0, concat_axis=0, tiled=True)
-    holders = sums[:, per + per_b :].astype(jnp.int32).reshape(-1)
-    total = jnp.sum(sums[:, : per + per_b], axis=0) / divisor
-    span = -(-total.size // block)
-    total = jnp.pad(total, (0, span * block - total.size)).reshape(span, block)
-    extra = -(-2 * span // 8) * 8
-    rider = jnp.concatenate(split_bf16(total, 2) + [jnp.zeros((extra - 2 * span, block), BF)])
-
-    send = back_remote(slots, g, tiles, peers, extra)
-    send = send.at[:, CAP * width :].set(jnp.broadcast_to(rider, (peers, extra, block)))
+    by_owner = wanted.reshape(NY * NC, NZ, CAP)
+    steps = (jnp.arange(NZ) - z) & (NZ - 1)
+    match = (place_of(steps)[:, None] == jnp.arange(NZ)[None, :])[:, None, :, None]
+    held = jnp.sum(jnp.where(match, by_owner[None], 0), axis=2).reshape(NZ, NY * NC * CAP)
+    held = jnp.where(agg[0, 0].astype(F32) > jnp.inf, 0, held)
+    along_z = [[(y0 * NZ + z0) * NC + c0 for z0 in range(NZ)] for y0 in range(NY) for c0 in range(NC)]
+    held = lax.all_to_all(held, "rows", 0, 0, tiled=True, axis_index_groups=along_z).reshape(-1)
+
+    me = jnp.stack([lax.axis_index("feat"), c]).astype(jnp.int32)
+    hidden_out, g, keep, give = mid(me, pieces, packed, weight, held)
+
+    part = keep + shift(give, dc=1)
+    part = part + shift(part, flip_z=1)
+    pairs = [part] + [shift(part, flip_z=k) for k in (2, 4, 6)]
+    send = back_remote(slots, g, tiles, peers, part)
+    send, pairs = lax.optimization_barrier((send, pairs))
+    part = (pairs[0] + pairs[1]) + (pairs[2] + pairs[3])
     recv = lax.all_to_all(send, "rows", split_axis=0, concat_axis=0, tiled=True)
-    own = back_local(local_cols, g, tiles)
-    grad_input = finish(holders, recv, own)
-    totals = recv[:, CAP * width :].astype(F32)
-    totals = (totals[:, :span] + totals[:, span : 2 * span]).reshape(peers, -1)
-    return (
-        hidden_out,
-        grad_input,
-        totals[:, :per].reshape(width, hid_all),
-        totals[:, per : per + per_b].reshape(width),
-    )
+    own = back_local(local_cols, g, tiles, send)
+
+    own, part = lax.optimization_barrier((own, part))
+    pairs = [part] + [shift(part, flip_y=k) for k in (1, 2, 3)]
+    part = (pairs[0] + pairs[1]) + (pairs[2] + pairs[3])
+    other = shift(part, dc=1)
+    total = jnp.where(c == 0, jnp.concatenate([part, other]), jnp.concatenate([other, part]))
+    total = total / math.sqrt(nodes_dev * peers)
+    grad_w = jnp.concatenate([total[k * width : (k + 1) * width] for k in range(hid_all // 128)], axis=1)
+    grad_b = jnp.sum(total[-width:], axis=1)
+
+    grad_input = finish(jnp.stack([y, c]).astype(jnp.int32), held, recv, own)
+    return hidden_out, grad_input, grad_w, grad_b
 
 
 def solution(mesh):

time: 199 us -> 200 us (level)
  waiting for transfers between devices: 74.6 us -> 65.9 us
  starting transfers between devices: 61 us -> 67.9 us
  other arithmetic: 4.99 us -> 8.79 us
    ppermute x24 -> x33, waiting for transfers between devices: 8.78 us -> 26.5 us  [shift(): return lax.ppermute(x, 'rows', pairs)]
    all_to_all x1, waiting for transfers between devices: 49.1 us -> 33.6 us  [local(): recv = lax.all_to_all(send, 'rows', split_axis=0, concat_axis=0, tiled=True)]
    ppermute x3, waiting for transfers between devices: 11.2 us -> 0.01 us  [local(): lax.ppermute(agg, 'feat', [(k, (k + s) % fpeers) for k in range(fpeers)])]
    ppermute x24 -> x33, starting transfers between devices: 44.9 us -> 51.7 us  [shift(): return lax.ppermute(x, 'rows', pairs)]
    all_to_all x1, starting transfers between devices: 4.82 us -> 8.73 us  [local(): recv = lax.all_to_all(send, 'rows', split_axis=0, concat_axis=0, tiled=True)]
    all_to_all x1, starting transfers between devices: 7.1 us -> 3.31 us  [local(): lax.all_to_all(held, 'rows', 0, 0, tiled=True, axis_index_groups=along_z)]
  transfers between devices with their start and end apart: 30 -> 39, of which waited for: 11 -> 13; matrix products, arithmetic and copies ran while one was open for 4% -> 7% of each run, Pallas kernels for 12% -> 12%
where the time goes in v6:
time: 200 us; the launch traced here: 199 us
  starting transfers between devices  67.9 us (34%)
  waiting for transfers between devices  65.9 us (33%)
  Pallas kernels  32.7 us (16%)
  between operations  15.2 us (8%)
  local copies, waits for them, and re-layouts  8.83 us (4%)
  other arithmetic  8.79 us (4%)
    ppermute x33, starting transfers between devices, shift(): return lax.ppermute(x, 'rows', pairs)  51.7 us
    all_to_all x1, waiting for transfers between devices, local(): recv = lax.all_to_all(send, 'rows', split_axis=0, concat_axis=0, tiled=True)  33.6 us
    ppermute x33, waiting for transfers between devices, shift(): return lax.ppermute(x, 'rows', pairs)  26.5 us
    all_to_all x1, starting transfers between devices, local(): recv = lax.all_to_all(send, 'rows', split_axis=0, concat_axis=0, tiled=True)  8.73 us
    pallas_call x3, Pallas kernels, pack(): pl.pallas_call(functools.partial(pack_kernel, first, count, len(sources)...  6.49 us
    all_to_all x1, waiting for transfers between devices, local(): lax.all_to_all(held, 'rows', 0, 0, tiled=True, axis_index_groups=along_z)  5.72 us
    pallas_call x1, Pallas kernels, mid(): pl.pallas_call(mid_kernel, grid=(nodes // chunk,), out_shape=(jax.ShapeDt...  4.94 us
    pallas_call x1, Pallas kernels, agg_remote(): pl.pallas_call(agg_remote_kernel, grid=(row_blocks // STEP,), out_shape=j...  4.89 us
  transfers between devices with their start and end apart: 39, of which 13 were waited for; matrix products, arithmetic and copies ran while one was open for 7% of the time, Pallas kernels for 12%

profile of v6, /device:TPU:1, one launch (start us, length us, event | category | flops | bytes accessed | tf_op | source)
XLA Modules:
  0.0 199.4 jit_solution(9991978588519533615)
XLA Ops:
  7.2 6.5 %collective-permute-start.4 = (bf16[64,2048]{1,0:T(8,128)(2,1)}, bf16[64,2048]{1,0:T(8,128)(2,1)S(1)}, u32[]{:S(2)}, u32[]{:S(2)}) collective-permute-start(bf16[64,2048]{1,0:T(8,128)(2,1)} %refs_1_.1), channel_id=1, source_target_pairs={{0,56},{4,60},{8,0},{12,4},{16,8},{20,12},{24,16},{28,20},{32,24},... | collective-permute-start | bytes 786440 | tf_op jit(solution)/shard_map/ppermute | solution.py:37
  17.4 4.6 %collective-permute-done.5.refs_3_ = bf16[64,2048]{1,0:T(8,128)(2,1)S(1)} collective-permute-done((bf16[64,2048]{1,0:T(8,128)(2,1)}, bf16[64,2048]{1,0:T(8,128)(2,1)S(1)}, u32[]{:S(2)}, u32[]{:S(2)}) %collective-permute-start.5) | collective-permute-done | bytes 262176 | tf_op jit(solution)/shard_map/ppermute | solution.py:37
  22.6 2.6 %collective-permute-start.10 = (bf16[64,2048]{1,0:T(8,128)(2,1)S(1)}, bf16[64,2048]{1,0:T(8,128)(2,1)S(1)}, u32[]{:S(2)}, u32[]{:S(2)}) collective-permute-start(bf16[64,2048]{1,0:T(8,128)(2,1)S(1)} %collective-permute-done.4.refs_2_), channel_id=1, source_target_pairs={{0,56},{4,60},{8,0},{12,4},{16,8},{20,12},{24,16},{28,20},{32,24},... | collective-permute-start | bytes 786440 | tf_op jit(solution)/shard_map/ppermute | solution.py:37
  25.4 3.8 %collective-permute-done.11.refs_2_ = bf16[64,2048]{1,0:T(8,128)(2,1)S(1)} collective-permute-done((bf16[64,2048]{1,0:T(8,128)(2,1)S(1)}, bf16[64,2048]{1,0:T(8,128)(2,1)S(1)}, u32[]{:S(2)}, u32[]{:S(2)}) %collective-permute-start.11) | collective-permute-done | bytes 262176 | tf_op jit(solution)/shard_map/ppermute | solution.py:37
  29.3 2.8 %collective-permute-start = (s32[4,16]{1,0:T(4,128)S(1)}, s32[4,16]{1,0:T(4,128)S(1)}, u32[]{:S(2)}, u32[]{:S(2)}) collective-permute-start(s32[4,16]{1,0:T(4,128)S(1)} %squeeze.13), channel_id=1, source_target_pairs={{0,4},{4,0},{8,12},{12,8},{16,20},{20,16},{24,28},{28,24},{32,36},... | collective-permute-start | bytes 776 | tf_op jit(solution)/shard_map/ppermute | solution.py:37
  32.2 3.0 %collective-permute-start.16 = (bf16[64,2048]{1,0:T(8,128)(2,1)S(1)}, bf16[64,2048]{1,0:T(8,128)(2,1)S(1)}, u32[]{:S(2)}, u32[]{:S(2)}) collective-permute-start(bf16[64,2048]{1,0:T(8,128)(2,1)S(1)} %collective-permute-done.10.refs_1_), channel_id=1, source_target_pairs={{0,56},{4,60},{8,0},{12,4},{16,8},{20,12},{24,16},{28,20},{32,24},... | collective-permute-start | bytes 786440 | tf_op jit(solution)/shard_map/ppermute | solution.py:37
  39.7 2.3 %collective-permute-done.2 = s32[2,16]{1,0:T(2,128)S(1)} collective-permute-done((s32[2,16]{1,0:T(2,128)S(1)}, s32[2,16]{1,0:T(2,128)S(1)}, u32[]{:S(2)}, u32[]{:S(2)}) %collective-permute-start.2) | collective-permute-done | bytes 160 | tf_op jit(solution)/shard_map/ppermute | solution.py:37
  42.7 2.3 %pack.3 = (bf16[2,6,64,128]{3,2,1,0:T(8,128)(2,1)}, bf16[2,6,64,128]{3,2,1,0:T(8,128)(2,1)}, bf16[2,6,64,128]{3,2,1,0:T(8,128)(2,1)}, bf16[2,6,64,128]{3,2,1,0:T(8,128)(2,1)}) custom-call(s32[128]{0:T(128)} %reshape.236.refs_0_, bf16[64,2048]{1,0:T(8,128)(2,1)} %refs_1_.1, bf16[64,2048]{1,0:T(8,128)(2,1)} %copy-done.19, bf16[64,2048]{1,0:T(8,128)(2,1)} %copy-done.20), custom_call_target="tpu_custom_call" | custom-call | bytes 3145728 | tf_op jit(solution)/shard_map/pack/pallas_call | solution.py:61
  45.2 2.2 %collective-permute-start.7 = (bf16[2,6,64,128]{3,2,1,0:T(8,128)(2,1)}, bf16[2,6,64,128]{3,2,1,0:T(8,128)(2,1)S(1)}, u32[]{:S(2)}, u32[]{:S(2)}) collective-permute-start(bf16[2,6,64,128]{3,2,1,0:T(8,128)(2,1)} %get-tuple-element.29), channel_id=1, source_target_pairs={{0,128},{4,132},{8,136},{12,140},{16,144},{20,148},{24,152},{28,15... | collective-permute-start | bytes 589832 | tf_op jit(solution)/shard_map/ppermute | solution.py:37
  50.2 4.1 %agg_local.1.refs_4_.refs_6_.local_ref = f32[64,2048]{1,0:T(8,128)} custom-call(s32[64]{0:T(128)} %reshape.235.cols_ref, bf16[64,2048]{1,0:T(8,128)(2,1)} %refs_1_.1, bf16[16,8,128,128]{3,2,1,0:T(8,128)(2,1)} %bitcast.25), custom_call_target="tpu_custom_call" | custom-call | flops 134217728 | bytes 3145728 | tf_op jit(solution)/shard_map/agg_local/pallas_call | solution.py:97
  54.4 2.0 %pack.4 = (bf16[2,4,64,128]{3,2,1,0:T(8,128)(2,1)}, bf16[2,4,64,128]{3,2,1,0:T(8,128)(2,1)}, bf16[2,4,64,128]{3,2,1,0:T(8,128)(2,1)}, bf16[2,4,64,128]{3,2,1,0:T(8,128)(2,1)}) custom-call(s32[128]{0:T(128)} %reshape.236.refs_0_, bf16[64,2048]{1,0:T(8,128)(2,1)} %copy-done.22, bf16[64,2048]{1,0:T(8,128)(2,1)} %copy-done.21, ...), custom_call_target="tpu_custom_call" | custom-call | bytes 3145728 | tf_op jit(solution)/shard_map/pack/pallas_call | solution.py:61
  57.9 2.2 %pack.5 = (bf16[2,6,64,128]{3,2,1,0:T(8,128)(2,1)}, bf16[2,6,64,128]{3,2,1,0:T(8,128)(2,1)}, bf16[2,6,64,128]{3,2,1,0:T(8,128)(2,1)}, bf16[2,6,64,128]{3,2,1,0:T(8,128)(2,1)}) custom-call(s32[128]{0:T(128)} %reshape.236.refs_0_, bf16[64,2048]{1,0:T(8,128)(2,1)} %copy-done.4, bf16[64,2048]{1,0:T(8,128)(2,1)} %copy-done.3, bf16[32,2048]{1,0:T(8,128)(2,1)} %copy-done.26, ...), custom_call_target="tpu_custom_call" | custom-call | bytes 3145728 | tf_op jit(solution)/shard_map/pack/pallas_call | solution.py:61
  60.1 2.2 %collective-permute-start.14 = (bf16[2,4,64,128]{3,2,1,0:T(8,128)(2,1)}, bf16[2,4,64,128]{3,2,1,0:T(8,128)(2,1)S(1)}, u32[]{:S(2)}, u32[]{:S(2)}) collective-permute-start(bf16[2,4,64,128]{3,2,1,0:T(8,128)(2,1)} %get-tuple-element.34), channel_id=1, source_target_pairs={{0,192},{4,196},{8,200},{12,204},{16,208},{20,212},{24,216},{28,22... | collective-permute-start | bytes 393224 | tf_op jit(solution)/shard_map/ppermute | solution.py:37
  66.3 4.5 %collective-permute-start.9 = (bf16[4,6,64,128]{3,2,1,0:T(8,128)(2,1)S(1)}, bf16[4,6,64,128]{3,2,1,0:T(8,128)(2,1)S(1)}, u32[]{:S(2)}, u32[]{:S(2)}) collective-permute-start(bf16[4,6,64,128]{3,2,1,0:T(8,128)(2,1)S(1)} %pad_maximum_fusion), channel_id=1, source_target_pairs={{0,4},{4,0},{8,12},{12,8},{16,20},{20,16},{24,28},{28,24},{32,36},... | collective-permute-start | bytes 1179656 | tf_op jit(solution)/shard_map/ppermute | solution.py:37
  71.5 3.2 %collective-permute-done.22.refs_13_ = bf16[2,6,64,128]{3,2,1,0:T(8,128)(2,1)S(1)} collective-permute-done((bf16[2,6,64,128]{3,2,1,0:T(8,128)(2,1)}, bf16[2,6,64,128]{3,2,1,0:T(8,128)(2,1)S(1)}, u32[]{:S(2)}, u32[]{:S(2)}) %collective-permute-start.22) | collective-permute-done | bytes 196640 | tf_op jit(solution)/shard_map/ppermute | solution.py:37
  74.8 2.6 %collective-permute-start.23 = (bf16[4,6,64,128]{3,2,1,0:T(8,128)(2,1)S(1)}, bf16[4,6,64,128]{3,2,1,0:T(8,128)(2,1)S(1)}, u32[]{:S(2)}, u32[]{:S(2)}) collective-permute-start(bf16[4,6,64,128]{3,2,1,0:T(8,128)(2,1)S(1)} %pad_maximum_fusion.1), channel_id=1, source_target_pairs={{0,4},{4,0},{8,12},{12,8},{16,20},{20,16},{24,28},{28,24},{32,36},... | collective-permute-start | bytes 1179656 | tf_op jit(solution)/shard_map/ppermute | solution.py:37
  80.9 4.9 %agg_remote.1.own_ref = bf16[64,2048]{1,0:T(8,128)(2,1)} custom-call(s32[64]{0:T(128)} %copy-done.28, bf16[16,8,128,128]{3,2,1,0:T(8,128)(2,1)} %bitcast.26, f32[64,2048]{1,0:T(8,128)} %agg_local.1.refs_4_.refs_6_.local_ref, bf16[2,6,64,128]{3,2,1,0:T(8,128)(2,1)} %get-tuple-element.27.refs_3_.refs_0_, bf16[2,6,64,128]{3,2,1,0:T(8,128)(2,1)} %copy-done.7, ...), custom_call_target="tpu_custom_call" | custom-call | flops 134217728 | bytes 5242880 | tf_op jit(solution)/shard_map/agg_remote/pallas_call | solution.py:147
  92.6 3.3 %all-to-all-start = ((s32[8,1,16]{2,1,0:T(1,128)}), s32[8,1,16]{2,1,0:T(1,128)S(1)}, u32[]{:S(2)}, u32[]{:S(2)}) async-start(s32[8,1,16]{2,1,0:T(1,128)} %copy.42), calls=%async_computation | async-start | bytes 8192 | tf_op jit(solution)/shard_map/all_to_all | solution.py:473
  96.6 5.7 %all-to-all-done = s32[8,1,16]{2,1,0:T(1,128)S(1)} async-done(((s32[8,1,16]{2,1,0:T(1,128)}), s32[8,1,16]{2,1,0:T(1,128)S(1)}, u32[]{:S(2)}, u32[]{:S(2)}) %all-to-all-start) | async-done | bytes 544 | tf_op jit(solution)/shard_map/all_to_all | solution.py:473
  105.0 4.9 %mid.1 = (bf16[64,2048]{1,0:T(8,128)(2,1)}, bf16[64,2048]{1,0:T(8,128)(2,1)}, f32[96,128]{1,0:T(8,128)}, f32[96,128]{1,0:T(8,128)}) custom-call(s32[2]{0:T(128)} %pad_add_fusion.2.me_ref, s32[128]{0:T(128)} %reshape.237._.wanted_ref, bf16[64,2048]{1,0:T(8,128)(2,1)} %agg_remote.1.own_ref, bf16[64,2048]{1,0:T(8,128)(2,1)} %copy-done.23, ...), custom_call_target="tpu_custom_call" | custom-call | flops 402653184 | bytes 3145728 | tf_op jit(solution)/shard_map/mid/pallas_call | solution.py:237
  110.0 2.2 %collective-permute-start.27 = (f32[96,128]{1,0:T(8,128)}, f32[96,128]{1,0:T(8,128)S(1)}, u32[]{:S(2)}, u32[]{:S(2)}) collective-permute-start(f32[96,128]{1,0:T(8,128)} %get-tuple-element.42), channel_id=1, source_target_pairs={{0,4},{4,0},{8,12},{12,8},{16,20},{20,16},{24,28},{28,24},{32,36},... | collective-permute-start | bytes 147464 | tf_op jit(solution)/shard_map/ppermute | solution.py:37
  114.4 2.7 %collective-permute-done.28 = f32[96,128]{1,0:T(8,128)S(1)} collective-permute-done((f32[96,128]{1,0:T(8,128)S(1)}, f32[96,128]{1,0:T(8,128)S(1)}, u32[]{:S(2)}, u32[]{:S(2)}) %collective-permute-start.28) | collective-permute-done | bytes 49184 | tf_op jit(solution)/shard_map/ppermute | solution.py:37
  117.4 2.1 %collective-permute-start.30 = (f32[96,128]{1,0:T(8,128)S(1)}, f32[96,128]{1,0:T(8,128)S(1)}, u32[]{:S(2)}, u32[]{:S(2)}) collective-permute-start(f32[96,128]{1,0:T(8,128)S(1)} %add.112._), channel_id=1, source_target_pairs={{0,32},{4,36},{8,40},{12,44},{16,48},{20,52},{24,56},{28,60},{32,0... | collective-permute-start | bytes 147464 | tf_op jit(solution)/shard_map/ppermute | solution.py:37
  119.5 3.3 %collective-permute-start.31 = (f32[96,128]{1,0:T(8,128)S(1)}, f32[96,128]{1,0:T(8,128)S(1)}, u32[]{:S(2)}, u32[]{:S(2)}) collective-permute-start(f32[96,128]{1,0:T(8,128)S(1)} %add.112._), channel_id=1, source_target_pairs={{0,48},{4,52},{8,56},{12,60},{16,32},{20,36},{24,40},{28,44},{32,1... | collective-permute-start | bytes 147464 | tf_op jit(solution)/shard_map/ppermute | solution.py:37
  122.8 4.5 %back_remote.1._ = bf16[64,128,128]{2,1,0:T(8,128)(2,1)} custom-call(s32[64]{0:T(128)} %get-tuple-element.59.slots_ref, bf16[64,2048]{1,0:T(8,128)(2,1)} %get-tuple-element.40.g_ref, bf16[16,8,128,128]{3,2,1,0:T(8,128)(2,1)} %bitcast.27, f32[96,128]{1,0:T(8,128)} %copy-done.5), custom_call_target="tpu_custom_call" | custom-call | flops 134217728 | bytes 5242880 | tf_op jit(solution)/shard_map/back_remote/pallas_call | solution.py:305
  127.3 8.7 %all-to-all-start.1 = ((bf16[64,128,128]{2,1,0:T(8,128)(2,1)}), bf16[64,128,128]{2,1,0:T(8,128)(2,1)S(1)}, u32[]{:S(2)}, u32[]{:S(2)}) async-start(bf16[64,128,128]{2,1,0:T(8,128)(2,1)} %back_remote.1._), calls=%async_computation.1 | async-start | bytes 4194304 | tf_op jit(solution)/shard_map/all_to_all | solution.py:484
  136.1 3.9 %back_local.1.local_ref = f32[64,2048]{1,0:T(8,128)} custom-call(s32[64]{0:T(128)} %reshape.235.cols_ref, bf16[64,2048]{1,0:T(8,128)(2,1)} %get-tuple-element.40.g_ref, bf16[16,8,128,128]{3,2,1,0:T(8,128)(2,1)} %bitcast.28, bf16[64,128,128]{2,1,0:T(8,128)(2,1)} %back_remote.1._), custom_call_target="tpu_custom_call" | custom-call | flops 134217728 | bytes 3145728 | tf_op jit(solution)/shard_map/back_local/pallas_call | solution.py:344
  141.5 2.6 %collective-permute-start.33 = (f32[96,128]{1,0:T(8,128)S(1)}, f32[96,128]{1,0:T(8,128)S(1)}, u32[]{:S(2)}, u32[]{:S(2)}) collective-permute-start(f32[96,128]{1,0:T(8,128)S(1)} %add_add_fusion.1), channel_id=1, source_target_pairs={{0,128},{4,132},{8,136},{12,140},{16,144},{20,148},{24,152},{28,15... | collective-permute-start | bytes 147464 | tf_op jit(solution)/shard_map/ppermute | solution.py:37
  144.1 4.1 %collective-permute-done.33 = f32[96,128]{1,0:T(8,128)S(1)} collective-permute-done((f32[96,128]{1,0:T(8,128)S(1)}, f32[96,128]{1,0:T(8,128)S(1)}, u32[]{:S(2)}, u32[]{:S(2)}) %collective-permute-start.33) | collective-permute-done | bytes 49184 | tf_op jit(solution)/shard_map/ppermute | solution.py:37
  148.2 2.8 %collective-permute-done.34 = f32[96,128]{1,0:T(8,128)S(1)} collective-permute-done((f32[96,128]{1,0:T(8,128)S(1)}, f32[96,128]{1,0:T(8,128)S(1)}, u32[]{:S(2)}, u32[]{:S(2)}) %collective-permute-start.34) | collective-permute-done | bytes 49184 | tf_op jit(solution)/shard_map/ppermute | solution.py:37
  153.7 33.6 %all-to-all-done.1.recv_ref = bf16[64,128,128]{2,1,0:T(8,128)(2,1)S(1)} async-done(((bf16[64,128,128]{2,1,0:T(8,128)(2,1)}), bf16[64,128,128]{2,1,0:T(8,128)(2,1)S(1)}, u32[]{:S(2)}, u32[]{:S(2)}) %all-to-all-start.1) | async-done | bytes 2097184 | tf_op jit(solution)/shard_map/all_to_all | solution.py:484
  188.7 3.9 %finish.1 = f32[64,2048]{1,0:T(8,128)} custom-call(s32[2]{0:T(128)} %pad_add_fusion.3.place_ref, s32[128]{0:T(128)} %reshape.237._.wanted_ref, bf16[64,128,128]{2,1,0:T(8,128)(2,1)} %copy-done, f32[64,2048]{1,0:T(8,128)} %back_local.1.local_ref), custom_call_target="tpu_custom_call" | custom-call | flops 1048576 | bytes 4194304 | tf_op jit(solution)/shard_map/finish/pallas_call | solution.py:381
  (171 shorter events, 39.9 us)
Async XLA Ops:
  7.2 97.0 %all-gather.2.cloned.1.call-start = ((), (), s32[]{:S(2)}) async-start(), calls=%async_computation.2 | async-start | bytes 1556480 | tf_op jit(solution)/shard_map/all_gather | solution.py:460
  7.2 15.4 %collective-permute-start.4 = (bf16[64,2048]{1,0:T(8,128)(2,1)}, bf16[64,2048]{1,0:T(8,128)(2,1)S(1)}, u32[]{:S(2)}, u32[]{:S(2)}) collective-permute-start(bf16[64,2048]{1,0:T(8,128)(2,1)} %refs_1_.1), channel_id=1, source_target_pairs={{0,56},{4,60},{8,0},{12,4},{16,8},{20,12},{24,16},{28,20},{32,24},... | collective-permute-start | bytes 786440 | tf_op jit(solution)/shard_map/ppermute | solution.py:37
  13.7 8.3 %collective-permute-start.5 = (bf16[64,2048]{1,0:T(8,128)(2,1)}, bf16[64,2048]{1,0:T(8,128)(2,1)S(1)}, u32[]{:S(2)}, u32[]{:S(2)}) collective-permute-start(bf16[64,2048]{1,0:T(8,128)(2,1)} %refs_1_.1), channel_id=1, source_target_pairs={{0,8},{4,12},{8,16},{12,20},{16,24},{20,28},{24,32},{28,36},{32,40... | collective-permute-start | bytes 786440 | tf_op jit(solution)/shard_map/ppermute | solution.py:37
  22.0 7.1 %collective-permute-start.11 = (bf16[64,2048]{1,0:T(8,128)(2,1)S(1)}, bf16[64,2048]{1,0:T(8,128)(2,1)S(1)}, u32[]{:S(2)}, u32[]{:S(2)}) collective-permute-start(bf16[64,2048]{1,0:T(8,128)(2,1)S(1)} %collective-permute-done.5.refs_3_), channel_id=1, source_target_pairs={{0,8},{4,12},{8,16},{12,20},{16,24},{20,28},{24,32},{28,36},{32,40... | collective-permute-start | bytes 786440 | tf_op jit(solution)/shard_map/ppermute | solution.py:37
  22.6 9.5 %collective-permute-start.10 = (bf16[64,2048]{1,0:T(8,128)(2,1)S(1)}, bf16[64,2048]{1,0:T(8,128)(2,1)S(1)}, u32[]{:S(2)}, u32[]{:S(2)}) collective-permute-start(bf16[64,2048]{1,0:T(8,128)(2,1)S(1)} %collective-permute-done.4.refs_2_), channel_id=1, source_target_pairs={{0,56},{4,60},{8,0},{12,4},{16,8},{20,12},{24,16},{28,20},{32,24},... | collective-permute-start | bytes 786440 | tf_op jit(solution)/shard_map/ppermute | solution.py:37
  29.1 10.5 %collective-permute-start.17 = (bf16[64,2048]{1,0:T(8,128)(2,1)S(1)}, bf16[64,2048]{1,0:T(8,128)(2,1)S(1)}, u32[]{:S(2)}, u32[]{:S(2)}) collective-permute-start(bf16[64,2048]{1,0:T(8,128)(2,1)S(1)} %collective-permute-done.11.refs_2_), channel_id=1, source_target_pairs={{0,8},{4,12},{8,16},{12,20},{16,24},{20,28},{24,32},{28,36},{32,40... | collective-permute-start | bytes 786440 | tf_op jit(solution)/shard_map/ppermute | solution.py:37
  29.3 5.9 %collective-permute-start = (s32[4,16]{1,0:T(4,128)S(1)}, s32[4,16]{1,0:T(4,128)S(1)}, u32[]{:S(2)}, u32[]{:S(2)}) collective-permute-start(s32[4,16]{1,0:T(4,128)S(1)} %squeeze.13), channel_id=1, source_target_pairs={{0,4},{4,0},{8,12},{12,8},{16,20},{20,16},{24,28},{28,24},{32,36},... | collective-permute-start | bytes 776 | tf_op jit(solution)/shard_map/ppermute | solution.py:37
  32.2 17.3 %collective-permute-start.16 = (bf16[64,2048]{1,0:T(8,128)(2,1)S(1)}, bf16[64,2048]{1,0:T(8,128)(2,1)S(1)}, u32[]{:S(2)}, u32[]{:S(2)}) collective-permute-start(bf16[64,2048]{1,0:T(8,128)(2,1)S(1)} %collective-permute-done.10.refs_1_), channel_id=1, source_target_pairs={{0,56},{4,60},{8,0},{12,4},{16,8},{20,12},{24,16},{28,20},{32,24},... | collective-permute-start | bytes 786440 | tf_op jit(solution)/shard_map/ppermute | solution.py:37
  35.2 4.6 %collective-permute-start.3 = (s32[2,16]{1,0:T(2,128)S(1)}, s32[2,16]{1,0:T(2,128)S(1)}, u32[]{:S(2)}, u32[]{:S(2)}) collective-permute-start(s32[2,16]{1,0:T(2,128)S(1)} %bitcast.35), channel_id=1, source_target_pairs={{0,64},{4,68},{8,72},{12,76},{16,80},{20,84},{24,88},{28,92},{32,9... | collective-permute-start | bytes 392 | tf_op jit(solution)/shard_map/ppermute | solution.py:37
  39.6 16.8 %collective-permute-start.18 = (bf16[32,2048]{1,0:T(8,128)(2,1)S(1)}, bf16[32,2048]{1,0:T(8,128)(2,1)S(1)}, u32[]{:S(2)}, u32[]{:S(2)}) collective-permute-start(bf16[32,2048]{1,0:T(8,128)(2,1)S(1)} %slice.136), channel_id=1, source_target_pairs={{0,8},{4,12},{8,16},{12,20},{16,24},{20,28},{24,32},{28,36},{32,40... | collective-permute-start | bytes 393224 | tf_op jit(solution)/shard_map/ppermute | solution.py:37
  44.9 15.2 %collective-permute-start.6 = (bf16[2,6,64,128]{3,2,1,0:T(8,128)(2,1)}, bf16[2,6,64,128]{3,2,1,0:T(8,128)(2,1)S(1)}, u32[]{:S(2)}, u32[]{:S(2)}) collective-permute-start(bf16[2,6,64,128]{3,2,1,0:T(8,128)(2,1)} %get-tuple-element.28), channel_id=1, source_target_pairs={{0,64},{4,68},{8,72},{12,76},{16,80},{20,84},{24,88},{28,92},{32,9... | collective-permute-start | bytes 589832 | tf_op jit(solution)/shard_map/ppermute | solution.py:37
  45.2 17.1 %collective-permute-start.7 = (bf16[2,6,64,128]{3,2,1,0:T(8,128)(2,1)}, bf16[2,6,64,128]{3,2,1,0:T(8,128)(2,1)S(1)}, u32[]{:S(2)}, u32[]{:S(2)}) collective-permute-start(bf16[2,6,64,128]{3,2,1,0:T(8,128)(2,1)} %get-tuple-element.29), channel_id=1, source_target_pairs={{0,128},{4,132},{8,136},{12,140},{16,144},{20,148},{24,152},{28,15... | collective-permute-start | bytes 589832 | tf_op jit(solution)/shard_map/ppermute | solution.py:37
  47.4 14.9 %collective-permute-start.8 = (bf16[2,6,64,128]{3,2,1,0:T(8,128)(2,1)}, bf16[2,6,64,128]{3,2,1,0:T(8,128)(2,1)S(1)}, u32[]{:S(2)}, u32[]{:S(2)}) collective-permute-start(bf16[2,6,64,128]{3,2,1,0:T(8,128)(2,1)} %get-tuple-element.30), channel_id=1, source_target_pairs={{0,192},{4,196},{8,200},{12,204},{16,208},{20,212},{24,216},{28,22... | collective-permute-start | bytes 589832 | tf_op jit(solution)/shard_map/ppermute | solution.py:37
  49.5 7.2 %collective-permute-start.19 = (bf16[32,2048]{1,0:T(8,128)(2,1)S(1)}, bf16[32,2048]{1,0:T(8,128)(2,1)S(1)}, u32[]{:S(2)}, u32[]{:S(2)}) collective-permute-start(bf16[32,2048]{1,0:T(8,128)(2,1)S(1)} %slice.137), channel_id=1, source_target_pairs={{0,56},{4,60},{8,0},{12,4},{16,8},{20,12},{24,16},{28,20},{32,24},... | collective-permute-start | bytes 393224 | tf_op jit(solution)/shard_map/ppermute | solution.py:37
  56.4 7.7 %collective-permute-start.12 = (bf16[2,4,64,128]{3,2,1,0:T(8,128)(2,1)}, bf16[2,4,64,128]{3,2,1,0:T(8,128)(2,1)S(1)}, u32[]{:S(2)}, u32[]{:S(2)}) collective-permute-start(bf16[2,4,64,128]{3,2,1,0:T(8,128)(2,1)} %get-tuple-element.32), channel_id=1, source_target_pairs={{0,64},{4,68},{8,72},{12,76},{16,80},{20,84},{24,88},{28,92},{32,9... | collective-permute-start | bytes 393224 | tf_op jit(solution)/shard_map/ppermute | solution.py:37
  56.7 9.6 %collective-permute-start.13 = (bf16[2,4,64,128]{3,2,1,0:T(8,128)(2,1)}, bf16[2,4,64,128]{3,2,1,0:T(8,128)(2,1)S(1)}, u32[]{:S(2)}, u32[]{:S(2)}) collective-permute-start(bf16[2,4,64,128]{3,2,1,0:T(8,128)(2,1)} %get-tuple-element.33), channel_id=1, source_target_pairs={{0,128},{4,132},{8,136},{12,140},{16,144},{20,148},{24,152},{28,15... | collective-permute-start | bytes 393224 | tf_op jit(solution)/shard_map/ppermute | solution.py:37
  60.1 10.8 %collective-permute-start.14 = (bf16[2,4,64,128]{3,2,1,0:T(8,128)(2,1)}, bf16[2,4,64,128]{3,2,1,0:T(8,128)(2,1)S(1)}, u32[]{:S(2)}, u32[]{:S(2)}) collective-permute-start(bf16[2,4,64,128]{3,2,1,0:T(8,128)(2,1)} %get-tuple-element.34), channel_id=1, source_target_pairs={{0,192},{4,196},{8,200},{12,204},{16,208},{20,212},{24,216},{28,22... | collective-permute-start | bytes 393224 | tf_op jit(solution)/shard_map/ppermute | solution.py:37
  62.3 8.6 %collective-permute-start.20 = (bf16[2,6,64,128]{3,2,1,0:T(8,128)(2,1)}, bf16[2,6,64,128]{3,2,1,0:T(8,128)(2,1)S(1)}, u32[]{:S(2)}, u32[]{:S(2)}) collective-permute-start(bf16[2,6,64,128]{3,2,1,0:T(8,128)(2,1)} %get-tuple-element.36), channel_id=1, source_target_pairs={{0,64},{4,68},{8,72},{12,76},{16,80},{20,84},{24,88},{28,92},{32,9... | collective-permute-start | bytes 589832 | tf_op jit(solution)/shard_map/ppermute | solution.py:37
  62.4 9.2 %collective-permute-start.21 = (bf16[2,6,64,128]{3,2,1,0:T(8,128)(2,1)}, bf16[2,6,64,128]{3,2,1,0:T(8,128)(2,1)S(1)}, u32[]{:S(2)}, u32[]{:S(2)}) collective-permute-start(bf16[2,6,64,128]{3,2,1,0:T(8,128)(2,1)} %get-tuple-element.37), channel_id=1, source_target_pairs={{0,128},{4,132},{8,136},{12,140},{16,144},{20,148},{24,152},{28,15... | collective-permute-start | bytes 589832 | tf_op jit(solution)/shard_map/ppermute | solution.py:37
  64.2 10.6 %collective-permute-start.22 = (bf16[2,6,64,128]{3,2,1,0:T(8,128)(2,1)}, bf16[2,6,64,128]{3,2,1,0:T(8,128)(2,1)S(1)}, u32[]{:S(2)}, u32[]{:S(2)}) collective-permute-start(bf16[2,6,64,128]{3,2,1,0:T(8,128)(2,1)} %get-tuple-element.38), channel_id=1, source_target_pairs={{0,192},{4,196},{8,200},{12,204},{16,208},{20,212},{24,216},{28,22... | collective-permute-start | bytes 589832 | tf_op jit(solution)/shard_map/ppermute | solution.py:37
  66.3 12.6 %collective-permute-start.9 = (bf16[4,6,64,128]{3,2,1,0:T(8,128)(2,1)S(1)}, bf16[4,6,64,128]{3,2,1,0:T(8,128)(2,1)S(1)}, u32[]{:S(2)}, u32[]{:S(2)}) collective-permute-start(bf16[4,6,64,128]{3,2,1,0:T(8,128)(2,1)S(1)} %pad_maximum_fusion), channel_id=1, source_target_pairs={{0,4},{4,0},{8,12},{12,8},{16,20},{20,16},{24,28},{28,24},{32,36},... | collective-permute-start | bytes 1179656 | tf_op jit(solution)/shard_map/ppermute | solution.py:37
  74.8 5.3 %collective-permute-start.23 = (bf16[4,6,64,128]{3,2,1,0:T(8,128)(2,1)S(1)}, bf16[4,6,64,128]{3,2,1,0:T(8,128)(2,1)S(1)}, u32[]{:S(2)}, u32[]{:S(2)}) collective-permute-start(bf16[4,6,64,128]{3,2,1,0:T(8,128)(2,1)S(1)} %pad_maximum_fusion.1), channel_id=1, source_target_pairs={{0,4},{4,0},{8,12},{12,8},{16,20},{20,16},{24,28},{28,24},{32,36},... | collective-permute-start | bytes 1179656 | tf_op jit(solution)/shard_map/ppermute | solution.py:37
  85.8 18.3 %collective-permute-start.24 = (bf16[64,2048]{1,0:T(8,128)(2,1)}, bf16[64,2048]{1,0:T(8,128)(2,1)S(1)}, u32[]{:S(2)}, u32[]{:S(2)}) collective-permute-start(bf16[64,2048]{1,0:T(8,128)(2,1)} %agg_remote.1.own_ref), channel_id=1, source_target_pairs={{0,1},{1,2},{2,3},{3,0},{4,5},{5,6},{6,7},{7,4},{8,9},{9,10},{10,1... | collective-permute-start | bytes 786440 | tf_op jit(solution)/shard_map/ppermute | solution.py:465
  86.9 17.2 %collective-permute-start.25 = (bf16[64,2048]{1,0:T(8,128)(2,1)}, bf16[64,2048]{1,0:T(8,128)(2,1)S(1)}, u32[]{:S(2)}, u32[]{:S(2)}) collective-permute-start(bf16[64,2048]{1,0:T(8,128)(2,1)} %agg_remote.1.own_ref), channel_id=1, source_target_pairs={{0,3},{1,0},{2,1},{3,2},{4,7},{5,4},{6,5},{7,6},{8,11},{9,8},{10,9... | collective-permute-start | bytes 786440 | tf_op jit(solution)/shard_map/ppermute | solution.py:465
  88.5 15.6 %collective-permute-start.26 = (bf16[64,2048]{1,0:T(8,128)(2,1)}, bf16[64,2048]{1,0:T(8,128)(2,1)S(1)}, u32[]{:S(2)}, u32[]{:S(2)}) collective-permute-start(bf16[64,2048]{1,0:T(8,128)(2,1)} %agg_remote.1.own_ref), channel_id=1, source_target_pairs={{0,2},{1,3},{2,0},{3,1},{4,6},{5,7},{6,4},{7,5},{8,10},{9,11},{10,... | collective-permute-start | bytes 786440 | tf_op jit(solution)/shard_map/ppermute | solution.py:465
  92.6 9.7 %all-to-all-start = ((s32[8,1,16]{2,1,0:T(1,128)}), s32[8,1,16]{2,1,0:T(1,128)S(1)}, u32[]{:S(2)}, u32[]{:S(2)}) async-start(s32[8,1,16]{2,1,0:T(1,128)} %copy.42), calls=%async_computation | async-start | bytes 8192 | tf_op jit(solution)/shard_map/all_to_all | solution.py:473
  117.0 10.3 %collective-permute-start.29 = (f32[96,128]{1,0:T(8,128)S(1)}, f32[96,128]{1,0:T(8,128)S(1)}, u32[]{:S(2)}, u32[]{:S(2)}) collective-permute-start(f32[96,128]{1,0:T(8,128)S(1)} %add.112._), channel_id=1, source_target_pairs={{0,16},{4,20},{8,24},{12,28},{16,0},{20,4},{24,8},{28,12},{32,48},... | collective-permute-start | bytes 147464 | tf_op jit(solution)/shard_map/ppermute | solution.py:37
  117.4 9.9 %collective-permute-start.30 = (f32[96,128]{1,0:T(8,128)S(1)}, f32[96,128]{1,0:T(8,128)S(1)}, u32[]{:S(2)}, u32[]{:S(2)}) collective-permute-start(f32[96,128]{1,0:T(8,128)S(1)} %add.112._), channel_id=1, source_target_pairs={{0,32},{4,36},{8,40},{12,44},{16,48},{20,52},{24,56},{28,60},{32,0... | collective-permute-start | bytes 147464 | tf_op jit(solution)/shard_map/ppermute | solution.py:37
  119.5 7.8 %collective-permute-start.31 = (f32[96,128]{1,0:T(8,128)S(1)}, f32[96,128]{1,0:T(8,128)S(1)}, u32[]{:S(2)}, u32[]{:S(2)}) collective-permute-start(f32[96,128]{1,0:T(8,128)S(1)} %add.112._), channel_id=1, source_target_pairs={{0,48},{4,52},{8,56},{12,60},{16,32},{20,36},{24,40},{28,44},{32,1... | collective-permute-start | bytes 147464 | tf_op jit(solution)/shard_map/ppermute | solution.py:37
  127.3 60.0 %all-to-all-start.1 = ((bf16[64,128,128]{2,1,0:T(8,128)(2,1)}), bf16[64,128,128]{2,1,0:T(8,128)(2,1)S(1)}, u32[]{:S(2)}, u32[]{:S(2)}) async-start(bf16[64,128,128]{2,1,0:T(8,128)(2,1)} %back_remote.1._), calls=%async_computation.1 | async-start | bytes 4194304 | tf_op jit(solution)/shard_map/all_to_all | solution.py:484
  141.5 6.7 %collective-permute-start.33 = (f32[96,128]{1,0:T(8,128)S(1)}, f32[96,128]{1,0:T(8,128)S(1)}, u32[]{:S(2)}, u32[]{:S(2)}) collective-permute-start(f32[96,128]{1,0:T(8,128)S(1)} %add_add_fusion.1), channel_id=1, source_target_pairs={{0,128},{4,132},{8,136},{12,140},{16,144},{20,148},{24,152},{28,15... | collective-permute-start | bytes 147464 | tf_op jit(solution)/shard_map/ppermute | solution.py:37
  144.1 6.9 %collective-permute-start.34 = (f32[96,128]{1,0:T(8,128)S(1)}, f32[96,128]{1,0:T(8,128)S(1)}, u32[]{:S(2)}, u32[]{:S(2)}) collective-permute-start(f32[96,128]{1,0:T(8,128)S(1)} %add_add_fusion.1), channel_id=1, source_target_pairs={{0,192},{4,196},{8,200},{12,204},{16,208},{20,212},{24,216},{28,22... | collective-permute-start | bytes 147464 | tf_op jit(solution)/shard_map/ppermute | solution.py:37
  (36 other events, 320.8 us)
Sparse Core Ops, SparseCore 0:
  16.3 25.5 all-gather.1

commit v7 on v6

--- a/solution.py
+++ b/solution.py
@@ -22,9 +22,8 @@
 
 NY, NZ, NC = 4, 8, 2
 CAP = 2
-ORDER = (0, 1, 7, 2, 6, 3, 5, 4)
-GROUPS = ((0, 3), (3, 5), (5, 8))
-PER = NZ * CAP
+COLUMN = NZ * NC
+PER = COLUMN * CAP
 
 
 def shift(x, dy=0, dz=0, dc=0, flip_y=0, flip_z=0):
@@ -37,35 +36,29 @@
     return lax.ppermute(x, "rows", pairs)
 
 
-def pack_kernel(first, count, split, *refs):
-    wanted_ref, sources, outs = refs[0], refs[1 : 1 + count + split], refs[-NY:]
-    width, block = outs[0].shape[2], outs[0].shape[3]
-    for ys in range(NY):
-        for cs in range(NC):
-            for q in range(count * CAP):
-                w = wanted_ref[(ys * NC + cs) * PER + first * CAP + q]
-                where = lanes(jnp.maximum(w, 0), block)
-                j = q // CAP
-                if split and j == count - 1:
-                    outs[ys][cs, q, : width // 2] = sources[j][:, where]
-                    outs[ys][cs, q, width // 2 :] = sources[j + 1][:, where]
-                else:
-                    outs[ys][cs, q] = sources[j][:, where]
-
-
-def pack(group, wanted, sources, block, after):
-    first, last = group
-    count = last - first
-    width = sources[0].shape[0]
-    shape = jax.ShapeDtypeStruct((NC, count * CAP, width, block), BF)
-    return pl.pallas_call(
-        functools.partial(pack_kernel, first, count, len(sources) > count),
-        out_shape=[shape] * NY,
-        in_specs=[SMEM] + [VMEM] * len(sources) + [ANY] * len(after),
-        out_specs=[VMEM] * NY,
+def pack_kernel(ks, wanted_ref, column_ref, *refs):
+    outs = refs[-len(ks) :]
+    slots, _, block = outs[0].shape
+    for k, out_ref in zip(ks, outs):
+        base = k * PER + pl.program_id(0) * slots
+        for q in range(slots):
+            w = jnp.maximum(wanted_ref[base + q], 0)
+            out_ref[q] = column_ref[q // CAP, :, lanes(w, block)]
+
+
+def pack(ks, wanted, column, block, after):
+    _, width, nodes = column.shape
+    steps = 4
+    return pl.pallas_call(
+        functools.partial(pack_kernel, ks),
+        grid=(steps,),
+        out_shape=[jax.ShapeDtypeStruct((PER, width, block), BF)] * len(ks),
+        in_specs=[SMEM, pl.BlockSpec((COLUMN // steps, width, nodes), lambda i: (i, 0, 0))]
+        + [ANY] * len(after),
+        out_specs=[pl.BlockSpec((PER // steps, width, block), lambda i: (i, 0, 0))] * len(ks),
         name="pack",
-        cost_estimate=pl.CostEstimate(flops=0, bytes_accessed=3 << 20, transcendentals=0),
-    )(wanted, *sources, *after)
+        cost_estimate=pl.CostEstimate(flops=0, bytes_accessed=5 << 20, transcendentals=0),
+    )(wanted, column, *after)
 
 
 def dot(a, b, dims):
@@ -118,13 +111,8 @@
 
     @pl.when(i == 0)
     def _():
-        n = 0
-        for first, last in GROUPS:
-            size = (last - first) * CAP
-            for ys in range(NY):
-                recv_ref[pl.ds(ys * PER + first * CAP, size)] = parts[n + ys][0]
-                recv_ref[pl.ds((NY + ys) * PER + first * CAP, size)] = parts[n + NY][ys]
-            n += NY + 1
+        for k, part in enumerate(parts):
+            recv_ref[pl.ds(k * PER, PER)] = part[...]
 
     for rr in range(STEP):
         acc = local_ref[:, rr * block : (rr + 1) * block]
@@ -140,10 +128,7 @@
     row_blocks, per_block, block, _ = tiles.shape
     rem = per_block - TL
     width = local.shape[0]
-    specs = []
-    for n, part in enumerate(parts):
-        lead = 1 if n % (NY + 1) < NY else NY
-        specs.append(pl.BlockSpec((lead,) + part.shape[1:], lambda i: (0, 0, 0, 0)))
+    specs = [pl.BlockSpec(part.shape, lambda i: (0, 0, 0)) for part in parts]
     return pl.pallas_call(
         agg_remote_kernel,
         grid=(row_blocks // STEP,),
@@ -155,7 +140,7 @@
         ]
         + specs,
         out_specs=pl.BlockSpec((width, STEP * block), lambda i: (0, i)),
-        scratch_shapes=[pltpu.VMEM((NY * NC * PER, width, block), BF)],
+        scratch_shapes=[pltpu.VMEM((NY * PER, width, block), BF)],
         name="agg_remote",
         cost_estimate=pl.CostEstimate(
             flops=2 * width * row_blocks * rem * block * block, bytes_accessed=5 << 20, transcendentals=0
@@ -365,8 +350,8 @@
     odd_scr[...] = jnp.zeros_like(odd_scr)
 
     def body(p, carry):
-        back = (p // (NZ * NC) - place_ref[0]) & (NY - 1)
-        base = ((p // NC % NZ * NY + back) * NC + ((p ^ place_ref[1]) & 1)) * CAP
+        back = (p // COLUMN - place_ref[0]) & (NY - 1)
+        base = (p % COLUMN * NY + back) * CAP
         even = lanes(jnp.maximum(wanted_ref[base], 0), block)
         odd = lanes(jnp.maximum(wanted_ref[base + 1], 0), block)
         out_ref[:, even] += recv_ref[p, :width].astype(F32)
@@ -387,6 +372,21 @@
         name="finish",
         cost_estimate=pl.CostEstimate(flops=recv.size, bytes_accessed=4 << 20, transcendentals=0),
     )(place, wanted, recv, local)
+
+
+def join_kernel(a_ref, b_ref, _, out_ref):
+    out_ref[...] = a_ref[...] + b_ref[...]
+
+
+def join(a, b, after):
+    return pl.pallas_call(
+        join_kernel,
+        out_shape=jax.ShapeDtypeStruct(a.shape, a.dtype),
+        in_specs=[VMEM, VMEM, ANY],
+        out_specs=VMEM,
+        name="join",
+        cost_estimate=pl.CostEstimate(flops=a.size, bytes_accessed=1 << 17, transcendentals=0),
+    )(a, b, after)
 
 
 def split_bf16(x, terms):
@@ -408,7 +408,7 @@
     per_block = tile_cols.shape[0] // row_blocks
     remote_count = row_blocks * (per_block - TL)
     place = lax.axis_index("rows")
-    y, z, c = place // (NZ * NC), place // NC % NZ, place % NC
+    y, c = place // COLUMN, place % NC
 
     grid = tile_cols.reshape(row_blocks, per_block)
     tiles = tile_values.reshape(row_blocks, per_block, block, block)
@@ -420,72 +420,43 @@
     earlier = (owner[:, None] == owner[None, :]) & (order[None, :] < order[:, None])
     rank = jnp.sum(earlier.astype(jnp.int32), axis=1)
     slots = owner * CAP + rank
-    ahead = (owner // NC - z) & (NZ - 1)
-
-    def place_of(ahead):
-        return jnp.maximum(jnp.where(ahead <= NZ // 2, 2 * ahead - 1, 2 * (NZ - ahead)), 0)
-
-    pos = place_of(ahead)
-    back = (y - owner // (NZ * NC)) & (NY - 1)
-    other = (owner ^ c) & 1
-    near = ((other * NY + back) * NZ + pos) * CAP + rank
-
-    def table(index):
-        hit = index[None, :] == jnp.arange(peers * CAP)[:, None]
-        return jnp.max(jnp.where(hit, inside[None, :], -1), axis=1)
-
-    asked = table(near).reshape(NC, NY, PER)
-    asked = jnp.stack([asked[0], shift(asked[1], dc=1)], axis=1)
-    wanted = [asked[0]] + [shift(asked[ys], dy=-ys) for ys in range(1, NY)]
-    wanted = jnp.stack(wanted).reshape(-1)
-
-    up, down, parts = [feats], [feats], []
-    for k in range(1, NZ // 2):
-        up.append(shift(up[-1], dz=1))
-        down.append(shift(down[-1], dz=-1))
-    far_up = shift(up[-1][: width // 2], dz=1)
-    far_down = shift(down[-1][width // 2 :], dz=-1)
-    groups = ((feats, down[1], up[1]), (down[2], up[2]), (down[3], up[3], far_up, far_down))
-    after = []
+    near = ((y - owner // COLUMN) & (NY - 1)) * PER + slots % PER
+    hit = near[None, :] == jnp.arange(NY * PER)[:, None]
+    asked = jnp.max(jnp.where(hit, inside[None, :], -1), axis=1).reshape(NY, PER)
+
+    columns = [[y0 * COLUMN + k for k in range(COLUMN)] for y0 in range(NY)]
+    column = lax.all_gather(feats, "rows", axis_index_groups=columns)
+    wanted = jnp.stack([asked[0]] + [shift(asked[k], dy=-k) for k in range(1, NY)])
+    held = wanted.reshape(NY, COLUMN, CAP).transpose(1, 0, 2).reshape(COLUMN, 1, NY * CAP)
+    held = lax.all_to_all(held, "rows", 0, 0, tiled=True, axis_index_groups=columns)
+    wanted = wanted.reshape(-1)
     agg = agg_local(local_cols, feats, tiles)
-    for group, sources in zip(GROUPS, groups):
-        packs = pack(group, wanted, sources, block, after)
-        after = [packs[0], agg]
-        moved = [packs[0]] + [shift(packs[ys], dy=ys) for ys in range(1, NY)]
-        parts += moved
-        parts.append(shift(jnp.concatenate([m[1:] for m in moved]), dc=1))
 
     bias_cols = jnp.pad(jnp.stack(split_bf16(bias, 3), axis=1), ((0, 0), (0, 125)))
     packed = jnp.concatenate([cotangent, weight, bias_cols], axis=1)
     packed = lax.all_gather(packed, "feat", axis=0, tiled=True)
 
+    away = pack(range(1, NY), wanted, column, block, [held, agg])
+    parts = pack((0,), wanted, column, block, [away[0]])
+    parts = list(parts) + [shift(blocks, dy=k) for k, blocks in enumerate(away, 1)]
     agg = agg_remote(near, parts, tiles, agg)
 
     pieces = [agg] + [
         lax.ppermute(agg, "feat", [(k, (k + s) % fpeers) for k in range(fpeers)]) for s in (1, 3, 2)
     ]
-    by_owner = wanted.reshape(NY * NC, NZ, CAP)
-    steps = (jnp.arange(NZ) - z) & (NZ - 1)
-    match = (place_of(steps)[:, None] == jnp.arange(NZ)[None, :])[:, None, :, None]
-    held = jnp.sum(jnp.where(match, by_owner[None], 0), axis=2).reshape(NZ, NY * NC * CAP)
-    held = jnp.where(agg[0, 0].astype(F32) > jnp.inf, 0, held)
-    along_z = [[(y0 * NZ + z0) * NC + c0 for z0 in range(NZ)] for y0 in range(NY) for c0 in range(NC)]
-    held = lax.all_to_all(held, "rows", 0, 0, tiled=True, axis_index_groups=along_z).reshape(-1)
-
     me = jnp.stack([lax.axis_index("feat"), c]).astype(jnp.int32)
     hidden_out, g, keep, give = mid(me, pieces, packed, weight, held)
 
-    part = keep + shift(give, dc=1)
-    part = part + shift(part, flip_z=1)
-    pairs = [part] + [shift(part, flip_z=k) for k in (2, 4, 6)]
-    send = back_remote(slots, g, tiles, peers, part)
-    send, pairs = lax.optimization_barrier((send, pairs))
-    part = (pairs[0] + pairs[1]) + (pairs[2] + pairs[3])
+    send = back_remote(slots, g, tiles, peers, keep)
     recv = lax.all_to_all(send, "rows", split_axis=0, concat_axis=0, tiled=True)
     own = back_local(local_cols, g, tiles, send)
 
-    own, part = lax.optimization_barrier((own, part))
+    own, keep, give = lax.optimization_barrier((own, keep, give))
+    part = keep + shift(give, dc=1)
     pairs = [part] + [shift(part, flip_y=k) for k in (1, 2, 3)]
+    part = (pairs[0] + pairs[1]) + (pairs[2] + pairs[3])
+    part = join(part, shift(part, flip_z=1), recv)
+    pairs = [part] + [shift(part, flip_z=k) for k in (2, 4, 6)]
     part = (pairs[0] + pairs[1]) + (pairs[2] + pairs[3])
     other = shift(part, dc=1)
     total = jnp.where(c == 0, jnp.concatenate([part, other]), jnp.concatenate([other, part]))
@@ -493,7 +464,7 @@
     grad_w = jnp.concatenate([total[k * width : (k + 1) * width] for k in range(hid_all // 128)], axis=1)
     grad_b = jnp.sum(total[-width:], axis=1)
 
-    grad_input = finish(jnp.stack([y, c]).astype(jnp.int32), held, recv, own)
+    grad_input = finish(y.reshape(1), held.reshape(-1), recv, own)
     return hidden_out, grad_input, grad_w, grad_b
 
 

time: 200 us -> 207 us (1.035)
  waiting for transfers between devices: 65.9 us -> 94.5 us
  starting transfers between devices: 67.9 us -> 46.7 us
  Pallas kernels: 32.7 us -> 35.9 us
    ppermute x33 -> x15, waiting for transfers between devices: 26.5 us -> 59.3 us  [shift(): return lax.ppermute(x, 'rows', pairs)]
    all_to_all x1, waiting for transfers between devices: 33.6 us -> 3.47 us  [local(): recv = lax.all_to_all(send, 'rows', split_axis=0, concat_axis=0, tiled=True)]
    ppermute x33 -> x15, starting transfers between devices: 51.7 us -> 23.9 us  [shift(): return lax.ppermute(x, 'rows', pairs)]
    all_gather x0 -> x1, waiting for transfers between devices: none -> 14.7 us  [local(): column = lax.all_gather(feats, 'rows', axis_index_groups=columns)]
    ppermute x3, waiting for transfers between devices: 0.01 us -> 9.95 us  [local(): lax.ppermute(agg, 'feat', [(k, (k + s) % fpeers) for k in range(fpeers)])]
    all_to_all x1, starting transfers between devices: 3.31 us -> 9.99 us  [local(): lax.all_to_all(held, 'rows', 0, 0, tiled=True, axis_index_groups=columns)]
    pallas_call x3, Pallas kernels: 6.49 us -> 9.77 us  [the longest x2 8.33 us: pack(): pl.pallas_call(functools.partial(pack_kernel, ks), grid=(steps,), out_sha...]
  transfers between devices with their start and end apart: 39 -> 22, of which waited for: 13 -> 13; matrix products, arithmetic and copies ran while one was open for 7% -> 5% of each run, Pallas kernels for 12% -> 12%
where the time goes in v7:
time: 207 us
  waiting for transfers between devices  94.5 us (46%)
  starting transfers between devices  46.7 us (23%)
  Pallas kernels  35.9 us (17%)
  between operations  14.2 us (7%)
  local copies, waits for them, and re-layouts  8.45 us (4%)
  other arithmetic  6.76 us (3%)
    ppermute x15, waiting for transfers between devices, shift(): return lax.ppermute(x, 'rows', pairs)  59.3 us
    ppermute x15, starting transfers between devices, shift(): return lax.ppermute(x, 'rows', pairs)  23.9 us
    all_gather x1, waiting for transfers between devices, local(): column = lax.all_gather(feats, 'rows', axis_index_groups=columns)  14.7 us
    all_to_all x1, starting transfers between devices, local(): lax.all_to_all(held, 'rows', 0, 0, tiled=True, axis_index_groups=columns)  9.99 us
    ppermute x3, waiting for transfers between devices, local(): lax.ppermute(agg, 'feat', [(k, (k + s) % fpeers) for k in range(fpeers)])  9.95 us
    all_to_all x1, starting transfers between devices, local(): recv = lax.all_to_all(send, 'rows', split_axis=0, concat_axis=0, tiled=True)  8.52 us
    pallas_call x2, Pallas kernels, pack(): pl.pallas_call(functools.partial(pack_kernel, ks), grid=(steps,), out_sha...  8.33 us
    all_to_all x1, waiting for transfers between devices, local(): lax.all_to_all(held, 'rows', 0, 0, tiled=True, axis_index_groups=columns)  6.42 us
  transfers between devices with their start and end apart: 22, of which 13 were waited for; matrix products, arithmetic and copies ran while one was open for 5% of the time, Pallas kernels for 12%

profile of v7, /device:TPU:1, one launch (start us, length us, event | category | flops | bytes accessed | tf_op | source)
XLA Modules:
  0.0 206.6 jit_solution(12810606871644980847)
XLA Ops:
  8.7 1.8 fusion.1
  12.4 2.1 %collective-permute-start.2 = (s32[32]{0:T(128)S(1)}, s32[32]{0:T(128)S(1)}, u32[]{:S(2)}, u32[]{:S(2)}) collective-permute-start(s32[32]{0:T(128)S(1)} %get-tuple-element.35), channel_id=1, source_target_pairs={{0,64},{4,68},{8,72},{12,76},{16,80},{20,84},{24,88},{28,92},{32,9... | collective-permute-start | bytes 392 | tf_op jit(solution)/shard_map/ppermute | solution.py:36
  14.5 2.6 %collective-permute-start.1 = (s32[32]{0:T(128)S(1)}, s32[32]{0:T(128)S(1)}, u32[]{:S(2)}, u32[]{:S(2)}) collective-permute-start(s32[32]{0:T(128)S(1)} %get-tuple-element.36), channel_id=1, source_target_pairs={{0,128},{4,132},{8,136},{12,140},{16,144},{20,148},{24,152},{28,15... | collective-permute-start | bytes 392 | tf_op jit(solution)/shard_map/ppermute | solution.py:36
  18.9 4.1 %agg_local.1.refs_1_.local_ref = f32[64,2048]{1,0:T(8,128)} custom-call(s32[64]{0:T(128)} %reshape.179.cols_ref, bf16[64,2048]{1,0:T(8,128)(2,1)} %feats_ref.1, bf16[16,8,128,128]{3,2,1,0:T(8,128)(2,1)} %bitcast.19), custom_call_target="tpu_custom_call" | custom-call | flops 134217728 | bytes 3145728 | tf_op jit(solution)/shard_map/agg_local/pallas_call | solution.py:90
  24.4 10.0 %all-to-all-start = ((s32[16,1,8]{2,1,0:T(1,128)}), s32[16,1,8]{2,1,0:T(1,128)S(1)}, u32[]{:S(2)}, u32[]{:S(2)}) async-start(s32[16,1,8]{2,1,0:T(1,128)} %copy.32), calls=%async_computation | async-start | bytes 16384 | tf_op jit(solution)/shard_map/all_to_all | solution.py:431
  35.0 6.4 %all-to-all-done.refs_0_._ = s32[16,1,8]{2,1,0:T(1,128)S(1)} async-done(((s32[16,1,8]{2,1,0:T(1,128)}), s32[16,1,8]{2,1,0:T(1,128)S(1)}, u32[]{:S(2)}, u32[]{:S(2)}) %all-to-all-start) | async-done | bytes 544 | tf_op jit(solution)/shard_map/all_to_all | solution.py:431
  41.4 14.7 %all-gather.6.cloned.1.call-done = bf16[1024,2048]{1,0:T(8,128)(2,1)} async-done(((bf16[64,2048]{1,0:T(8,128)(2,1)}), bf16[1024,2048]{1,0:T(8,128)(2,1)}) %all-gather.6.cloned.1.call-update) | async-done | bytes 4194320 | tf_op jit(solution)/shard_map/all_gather | solution.py:428
  56.2 4.3 %pack.2 = (bf16[32,64,128]{2,1,0:T(8,128)(2,1)}, bf16[32,64,128]{2,1,0:T(8,128)(2,1)}, bf16[32,64,128]{2,1,0:T(8,128)(2,1)}) custom-call(s32[128]{0:T(128)} %reshape.180.wanted_ref, bf16[16,64,2048]{2,1,0:T(8,128)(2,1)} %bitcast.23, s32[16,1,8]{2,1,0:T(1,128)} %copy-done.9, f32[64,2048]{1,0:T(8,128)} %agg_local.1.refs_1_.local_ref), custom_call_target="tpu_custom_call" | custom-call | bytes 5242880 | tf_op jit(solution)/shard_map/pack/pallas_call | solution.py:52
  60.5 1.7 collective-permute-start.3
  62.2 2.1 collective-permute-start.4
  65.4 4.0 %pack.3.refs_0_ = bf16[32,64,128]{2,1,0:T(8,128)(2,1)} custom-call(s32[128]{0:T(128)} %reshape.180.wanted_ref, bf16[16,64,2048]{2,1,0:T(8,128)(2,1)} %bitcast.24, bf16[32,64,128]{2,1,0:T(8,128)(2,1)} %get-tuple-element.14.refs_0_), custom_call_target="tpu_custom_call" | custom-call | bytes 5242880 | tf_op jit(solution)/shard_map/pack/pallas_call | solution.py:52
  69.4 5.8 %collective-permute-done.3.refs_1_ = bf16[32,64,128]{2,1,0:T(8,128)(2,1)S(1)} collective-permute-done((bf16[32,64,128]{2,1,0:T(8,128)(2,1)}, bf16[32,64,128]{2,1,0:T(8,128)(2,1)S(1)}, u32[]{:S(2)}, u32[]{:S(2)}) %collective-permute-start.3) | collective-permute-done | bytes 524320 | tf_op jit(solution)/shard_map/ppermute | solution.py:36
  75.3 12.2 %collective-permute-done.4.refs_2_ = bf16[32,64,128]{2,1,0:T(8,128)(2,1)S(1)} collective-permute-done((bf16[32,64,128]{2,1,0:T(8,128)(2,1)}, bf16[32,64,128]{2,1,0:T(8,128)(2,1)S(1)}, u32[]{:S(2)}, u32[]{:S(2)}) %collective-permute-start.4) | collective-permute-done | bytes 524320 | tf_op jit(solution)/shard_map/ppermute | solution.py:36
  89.1 4.9 %agg_remote.1.own_ref = bf16[64,2048]{1,0:T(8,128)(2,1)} custom-call(s32[64]{0:T(128)} %copy-done.12, bf16[16,8,128,128]{3,2,1,0:T(8,128)(2,1)} %bitcast.20, f32[64,2048]{1,0:T(8,128)} %agg_local.1.refs_1_.local_ref, bf16[32,64,128]{2,1,0:T(8,128)(2,1)} %pack.3.refs_0_, bf16[32,64,128]{2,1,0:T(8,128)(2,1)} %copy-done.1, bf16[32,64,128]{2,1,0:T(8,128)(2,1)} %copy-done.2, ...), custom_call_target="tpu_custom_call" | custom-call | flops 134217728 | bytes 5242880 | tf_op jit(solution)/shard_map/agg_remote/pallas_call | solution.py:132
  95.2 1.4 collective-permute-start.7
  96.6 1.5 collective-permute-start.8
  98.7 3.3 %collective-permute-done.6.low_ref = bf16[64,2048]{1,0:T(8,128)(2,1)S(1)} collective-permute-done((bf16[64,2048]{1,0:T(8,128)(2,1)}, bf16[64,2048]{1,0:T(8,128)(2,1)S(1)}, u32[]{:S(2)}, u32[]{:S(2)}) %collective-permute-start.6) | collective-permute-done | bytes 262176 | tf_op jit(solution)/shard_map/ppermute | solution.py:445
  102.1 6.6 %collective-permute-done.8.far_ref = bf16[64,2048]{1,0:T(8,128)(2,1)S(1)} collective-permute-done((bf16[64,2048]{1,0:T(8,128)(2,1)}, bf16[64,2048]{1,0:T(8,128)(2,1)S(1)}, u32[]{:S(2)}, u32[]{:S(2)}) %collective-permute-start.8) | collective-permute-done | bytes 262176 | tf_op jit(solution)/shard_map/ppermute | solution.py:445
  109.4 4.9 %mid.1 = (bf16[64,2048]{1,0:T(8,128)(2,1)}, bf16[64,2048]{1,0:T(8,128)(2,1)}, f32[96,128]{1,0:T(8,128)}, f32[96,128]{1,0:T(8,128)}) custom-call(s32[2]{0:T(128)} %pad_add_fusion.1.me_ref, s32[16,1,8]{2,1,0:T(1,128)} %copy-done.9, bf16[64,2048]{1,0:T(8,128)(2,1)} %agg_remote.1.own_ref, bf16[64,2048]{1,0:T(8,128)(2,1)} %copy-done.4, ...), custom_call_target="tpu_custom_call" | custom-call | flops 402653184 | bytes 3145728 | tf_op jit(solution)/shard_map/mid/pallas_call | solution.py:222
  114.3 4.6 %back_remote.1._ = bf16[64,128,128]{2,1,0:T(8,128)(2,1)} custom-call(s32[64]{0:T(128)} %get-tuple-element.29.slots_ref, bf16[64,2048]{1,0:T(8,128)(2,1)} %get-tuple-element.18.g_ref, bf16[16,8,128,128]{3,2,1,0:T(8,128)(2,1)} %bitcast.21, f32[96,128]{1,0:T(8,128)} %get-tuple-element.22._), custom_call_target="tpu_custom_call" | custom-call | flops 134217728 | bytes 5242880 | tf_op jit(solution)/shard_map/back_remote/pallas_call | solution.py:290
  118.9 8.5 %all-to-all-start.1 = ((bf16[64,128,128]{2,1,0:T(8,128)(2,1)}), bf16[64,128,128]{2,1,0:T(8,128)(2,1)S(1)}, u32[]{:S(2)}, u32[]{:S(2)}) async-start(bf16[64,128,128]{2,1,0:T(8,128)(2,1)} %back_remote.1._), calls=%async_computation.1 | async-start | bytes 4194304 | tf_op jit(solution)/shard_map/all_to_all | solution.py:451
  127.5 3.9 %back_local.1.local_ref = f32[64,2048]{1,0:T(8,128)} custom-call(s32[64]{0:T(128)} %reshape.179.cols_ref, bf16[64,2048]{1,0:T(8,128)(2,1)} %get-tuple-element.18.g_ref, bf16[16,8,128,128]{3,2,1,0:T(8,128)(2,1)} %bitcast.22, bf16[64,128,128]{2,1,0:T(8,128)(2,1)} %back_remote.1._), custom_call_target="tpu_custom_call" | custom-call | flops 134217728 | bytes 3145728 | tf_op jit(solution)/shard_map/back_local/pallas_call | solution.py:329
  132.8 3.0 %collective-permute-start.11 = (f32[96,128]{1,0:T(8,128)S(1)}, f32[96,128]{1,0:T(8,128)S(1)}, u32[]{:S(2)}, u32[]{:S(2)}) collective-permute-start(f32[96,128]{1,0:T(8,128)S(1)} %add.81), channel_id=1, source_target_pairs={{0,128},{4,132},{8,136},{12,140},{16,144},{20,148},{24,152},{28,15... | collective-permute-start | bytes 147464 | tf_op jit(solution)/shard_map/ppermute | solution.py:36
  136.5 1.8 collective-permute-done.11
  138.3 3.3 %collective-permute-done.12 = f32[96,128]{1,0:T(8,128)S(1)} collective-permute-done((f32[96,128]{1,0:T(8,128)S(1)}, f32[96,128]{1,0:T(8,128)S(1)}, u32[]{:S(2)}, u32[]{:S(2)}) %collective-permute-start.12) | collective-permute-done | bytes 49184 | tf_op jit(solution)/shard_map/ppermute | solution.py:36
  142.3 32.9 %collective-permute-done.13.b_ref = f32[96,128]{1,0:T(8,128)S(1)} collective-permute-done((f32[96,128]{1,0:T(8,128)S(1)}, f32[96,128]{1,0:T(8,128)S(1)}, u32[]{:S(2)}, u32[]{:S(2)}) %collective-permute-start.13) | collective-permute-done | bytes 49184 | tf_op jit(solution)/shard_map/ppermute | solution.py:36
  175.2 3.5 %all-to-all-done.1.recv_ref._ = bf16[64,128,128]{2,1,0:T(8,128)(2,1)S(1)} async-done(((bf16[64,128,128]{2,1,0:T(8,128)(2,1)}), bf16[64,128,128]{2,1,0:T(8,128)(2,1)S(1)}, u32[]{:S(2)}, u32[]{:S(2)}) %all-to-all-start.1) | async-done | bytes 2097184 | tf_op jit(solution)/shard_map/all_to_all | solution.py:451
  181.5 2.3 %collective-permute-start.15 = (f32[96,128]{1,0:T(8,128)}, f32[96,128]{1,0:T(8,128)S(1)}, u32[]{:S(2)}, u32[]{:S(2)}) collective-permute-start(f32[96,128]{1,0:T(8,128)} %join.1), channel_id=1, source_target_pairs={{0,32},{4,36},{8,40},{12,44},{16,48},{20,52},{24,56},{28,60},{32,0... | collective-permute-start | bytes 147464 | tf_op jit(solution)/shard_map/ppermute | solution.py:36
  184.9 2.3 %collective-permute-start.14 = (f32[96,128]{1,0:T(8,128)}, f32[96,128]{1,0:T(8,128)S(1)}, u32[]{:S(2)}, u32[]{:S(2)}) collective-permute-start(f32[96,128]{1,0:T(8,128)} %join.1), channel_id=1, source_target_pairs={{0,16},{4,20},{8,24},{12,28},{16,0},{20,4},{24,8},{28,12},{32,48},... | collective-permute-start | bytes 147464 | tf_op jit(solution)/shard_map/ppermute | solution.py:36
  187.2 1.5 collective-permute-done.15
  190.3 2.6 %collective-permute-start.17 = (f32[96,128]{1,0:T(8,128)S(1)}, f32[96,128]{1,0:T(8,128)S(1)}, u32[]{:S(2)}, u32[]{:S(2)}) collective-permute-start(f32[96,128]{1,0:T(8,128)S(1)} %add_add_fusion), channel_id=1, source_target_pairs={{0,4},{4,0},{8,12},{12,8},{16,20},{20,16},{24,28},{28,24},{32,36},... | collective-permute-start | bytes 147464 | tf_op jit(solution)/shard_map/ppermute | solution.py:36
  194.8 3.7 %finish.1 = f32[64,2048]{1,0:T(8,128)} custom-call(s32[1]{0:T(128)} %bitcast.13.place_ref, s32[128]{0:T(128)} %reshape.182.wanted_ref, bf16[64,128,128]{2,1,0:T(8,128)(2,1)} %copy-done, f32[64,2048]{1,0:T(8,128)} %back_local.1.local_ref), custom_call_target="tpu_custom_call" | custom-call | flops 1048576 | bytes 4194304 | tf_op jit(solution)/shard_map/finish/pallas_call | solution.py:366
  (87 shorter events, 23.9 us)
Async XLA Ops:
  7.2 49.0 %all-gather.6.cloned.1.call-start = ((), (), s32[]{:S(2)}) async-start(), calls=%async_computation.3 | async-start | bytes 4456448 | tf_op jit(solution)/shard_map/all_gather | solution.py:428
  7.9 90.8 %all-gather.4.cloned.1.call-start = ((), (), s32[]{:S(2)}) async-start(), calls=%async_computation.2 | async-start | bytes 1556480 | tf_op jit(solution)/shard_map/all_gather | solution.py:437
  12.2 10.8 %copy-start.12 = (s32[64]{0:T(128)}, s32[64]{0:T(128)S(1)}, u32[]{:S(2)}) copy-start(s32[64]{0:T(128)S(1)} %get-tuple-element.30.slots_ref) | copy-start | bytes 772
  12.4 10.8 %collective-permute-start.2 = (s32[32]{0:T(128)S(1)}, s32[32]{0:T(128)S(1)}, u32[]{:S(2)}, u32[]{:S(2)}) collective-permute-start(s32[32]{0:T(128)S(1)} %get-tuple-element.35), channel_id=1, source_target_pairs={{0,64},{4,68},{8,72},{12,76},{16,80},{20,84},{24,88},{28,92},{32,9... | collective-permute-start | bytes 392 | tf_op jit(solution)/shard_map/ppermute | solution.py:36
  14.5 8.8 %collective-permute-start.1 = (s32[32]{0:T(128)S(1)}, s32[32]{0:T(128)S(1)}, u32[]{:S(2)}, u32[]{:S(2)}) collective-permute-start(s32[32]{0:T(128)S(1)} %get-tuple-element.36), channel_id=1, source_target_pairs={{0,128},{4,132},{8,136},{12,140},{16,144},{20,148},{24,152},{28,15... | collective-permute-start | bytes 392 | tf_op jit(solution)/shard_map/ppermute | solution.py:36
  17.2 6.4 %collective-permute-start = (s32[32]{0:T(128)S(1)}, s32[32]{0:T(128)S(1)}, u32[]{:S(2)}, u32[]{:S(2)}) collective-permute-start(s32[32]{0:T(128)S(1)} %get-tuple-element.37), channel_id=1, source_target_pairs={{0,192},{4,196},{8,200},{12,204},{16,208},{20,212},{24,216},{28,22... | collective-permute-start | bytes 392 | tf_op jit(solution)/shard_map/ppermute | solution.py:36
  24.4 17.0 %all-to-all-start = ((s32[16,1,8]{2,1,0:T(1,128)}), s32[16,1,8]{2,1,0:T(1,128)S(1)}, u32[]{:S(2)}, u32[]{:S(2)}) async-start(s32[16,1,8]{2,1,0:T(1,128)} %copy.32), calls=%async_computation | async-start | bytes 16384 | tf_op jit(solution)/shard_map/all_to_all | solution.py:431
  41.4 14.7 %copy-start.9 = (s32[16,1,8]{2,1,0:T(1,128)}, s32[16,1,8]{2,1,0:T(1,128)S(1)}, u32[]{:S(2)}) copy-start(s32[16,1,8]{2,1,0:T(1,128)S(1)} %all-to-all-done.refs_0_._) | copy-start | bytes 1540
  60.5 14.8 %collective-permute-start.3 = (bf16[32,64,128]{2,1,0:T(8,128)(2,1)}, bf16[32,64,128]{2,1,0:T(8,128)(2,1)S(1)}, u32[]{:S(2)}, u32[]{:S(2)}) collective-permute-start(bf16[32,64,128]{2,1,0:T(8,128)(2,1)} %get-tuple-element.14.refs_0_), channel_id=1, source_target_pairs={{0,64},{4,68},{8,72},{12,76},{16,80},{20,84},{24,88},{28,92},{32,9... | collective-permute-start | bytes 1572872 | tf_op jit(solution)/shard_map/ppermute | solution.py:36
  62.2 25.3 %collective-permute-start.4 = (bf16[32,64,128]{2,1,0:T(8,128)(2,1)}, bf16[32,64,128]{2,1,0:T(8,128)(2,1)S(1)}, u32[]{:S(2)}, u32[]{:S(2)}) collective-permute-start(bf16[32,64,128]{2,1,0:T(8,128)(2,1)} %get-tuple-element.15), channel_id=1, source_target_pairs={{0,128},{4,132},{8,136},{12,140},{16,144},{20,148},{24,152},{28,15... | collective-permute-start | bytes 1572872 | tf_op jit(solution)/shard_map/ppermute | solution.py:36
  64.2 23.3 %collective-permute-start.5 = (bf16[32,64,128]{2,1,0:T(8,128)(2,1)}, bf16[32,64,128]{2,1,0:T(8,128)(2,1)S(1)}, u32[]{:S(2)}, u32[]{:S(2)}) collective-permute-start(bf16[32,64,128]{2,1,0:T(8,128)(2,1)} %get-tuple-element.16), channel_id=1, source_target_pairs={{0,192},{4,196},{8,200},{12,204},{16,208},{20,212},{24,216},{28,22... | collective-permute-start | bytes 1572872 | tf_op jit(solution)/shard_map/ppermute | solution.py:36
  75.3 12.2 %copy-start.1 = (bf16[32,64,128]{2,1,0:T(8,128)(2,1)}, bf16[32,64,128]{2,1,0:T(8,128)(2,1)S(1)}, u32[]{:S(2)}) copy-start(bf16[32,64,128]{2,1,0:T(8,128)(2,1)S(1)} %collective-permute-done.3.refs_1_) | copy-start | bytes 1572868
  93.9 8.2 %collective-permute-start.6 = (bf16[64,2048]{1,0:T(8,128)(2,1)}, bf16[64,2048]{1,0:T(8,128)(2,1)S(1)}, u32[]{:S(2)}, u32[]{:S(2)}) collective-permute-start(bf16[64,2048]{1,0:T(8,128)(2,1)} %agg_remote.1.own_ref), channel_id=1, source_target_pairs={{0,1},{1,2},{2,3},{3,0},{4,5},{5,6},{6,7},{7,4},{8,9},{9,10},{10,1... | collective-permute-start | bytes 786440 | tf_op jit(solution)/shard_map/ppermute | solution.py:445
  95.2 6.9 %collective-permute-start.7 = (bf16[64,2048]{1,0:T(8,128)(2,1)}, bf16[64,2048]{1,0:T(8,128)(2,1)S(1)}, u32[]{:S(2)}, u32[]{:S(2)}) collective-permute-start(bf16[64,2048]{1,0:T(8,128)(2,1)} %agg_remote.1.own_ref), channel_id=1, source_target_pairs={{0,3},{1,0},{2,1},{3,2},{4,7},{5,4},{6,5},{7,6},{8,11},{9,8},{10,9... | collective-permute-start | bytes 786440 | tf_op jit(solution)/shard_map/ppermute | solution.py:445
  96.6 12.1 %collective-permute-start.8 = (bf16[64,2048]{1,0:T(8,128)(2,1)}, bf16[64,2048]{1,0:T(8,128)(2,1)S(1)}, u32[]{:S(2)}, u32[]{:S(2)}) collective-permute-start(bf16[64,2048]{1,0:T(8,128)(2,1)} %agg_remote.1.own_ref), channel_id=1, source_target_pairs={{0,2},{1,3},{2,0},{3,1},{4,6},{5,7},{6,4},{7,5},{8,10},{9,11},{10,... | collective-permute-start | bytes 786440 | tf_op jit(solution)/shard_map/ppermute | solution.py:445
  102.1 6.6 %copy-start.4 = (bf16[64,2048]{1,0:T(8,128)(2,1)}, bf16[64,2048]{1,0:T(8,128)(2,1)S(1)}, u32[]{:S(2)}) copy-start(bf16[64,2048]{1,0:T(8,128)(2,1)S(1)} %collective-permute-done.6.low_ref) | copy-start | bytes 786436
  102.1 6.6 %copy-start.5 = (bf16[64,2048]{1,0:T(8,128)(2,1)}, bf16[64,2048]{1,0:T(8,128)(2,1)S(1)}, u32[]{:S(2)}) copy-start(bf16[64,2048]{1,0:T(8,128)(2,1)S(1)} %collective-permute-done.7.high_ref) | copy-start | bytes 786436
  118.9 59.8 %all-to-all-start.1 = ((bf16[64,128,128]{2,1,0:T(8,128)(2,1)}), bf16[64,128,128]{2,1,0:T(8,128)(2,1)S(1)}, u32[]{:S(2)}, u32[]{:S(2)}) async-start(bf16[64,128,128]{2,1,0:T(8,128)(2,1)} %back_remote.1._), calls=%async_computation.1 | async-start | bytes 4194304 | tf_op jit(solution)/shard_map/all_to_all | solution.py:451
  127.5 4.0 %copy-start.13 = (f32[96,128]{1,0:T(8,128)S(1)}, f32[96,128]{1,0:T(8,128)}, u32[]{:S(2)}) copy-start(f32[96,128]{1,0:T(8,128)} %get-tuple-element.23) | copy-start | bytes 147460
  127.5 5.3 %copy-start.7 = (f32[96,128]{1,0:T(8,128)S(1)}, f32[96,128]{1,0:T(8,128)}, u32[]{:S(2)}) copy-start(f32[96,128]{1,0:T(8,128)} %get-tuple-element.22._) | copy-start | bytes 147460
  131.4 62.1 %copy-start.10 = (s32[16,1,8]{2,1,0:T(1,128)S(1)}, s32[16,1,8]{2,1,0:T(1,128)}, u32[]{:S(2)}) copy-start(s32[16,1,8]{2,1,0:T(1,128)} %copy-done.9) | copy-start | bytes 1540
  131.4 1.3 collective-permute-start.9
  132.8 5.6 %collective-permute-start.11 = (f32[96,128]{1,0:T(8,128)S(1)}, f32[96,128]{1,0:T(8,128)S(1)}, u32[]{:S(2)}, u32[]{:S(2)}) collective-permute-start(f32[96,128]{1,0:T(8,128)S(1)} %add.81), channel_id=1, source_target_pairs={{0,128},{4,132},{8,136},{12,140},{16,144},{20,148},{24,152},{28,15... | collective-permute-start | bytes 147464 | tf_op jit(solution)/shard_map/ppermute | solution.py:36
  135.7 5.9 %collective-permute-start.12 = (f32[96,128]{1,0:T(8,128)S(1)}, f32[96,128]{1,0:T(8,128)S(1)}, u32[]{:S(2)}, u32[]{:S(2)}) collective-permute-start(f32[96,128]{1,0:T(8,128)S(1)} %add.81), channel_id=1, source_target_pairs={{0,192},{4,196},{8,200},{12,204},{16,208},{20,212},{24,216},{28,22... | collective-permute-start | bytes 147464 | tf_op jit(solution)/shard_map/ppermute | solution.py:36
  136.5 5.1 %collective-permute-start.10 = (f32[96,128]{1,0:T(8,128)S(1)}, f32[96,128]{1,0:T(8,128)S(1)}, u32[]{:S(2)}, u32[]{:S(2)}) collective-permute-start(f32[96,128]{1,0:T(8,128)S(1)} %add.81), channel_id=1, source_target_pairs={{0,64},{4,68},{8,72},{12,76},{16,80},{20,84},{24,88},{28,92},{32,9... | collective-permute-start | bytes 147464 | tf_op jit(solution)/shard_map/ppermute | solution.py:36
  141.7 37.0 %copy-start.8 = (f32[96,128]{1,0:T(8,128)}, f32[96,128]{1,0:T(8,128)S(1)}, u32[]{:S(2)}) copy-start(f32[96,128]{1,0:T(8,128)S(1)} %add_add_fusion.1.a_ref) | copy-start | bytes 147460
  141.7 33.5 %collective-permute-start.13 = (f32[96,128]{1,0:T(8,128)S(1)}, f32[96,128]{1,0:T(8,128)S(1)}, u32[]{:S(2)}, u32[]{:S(2)}) collective-permute-start(f32[96,128]{1,0:T(8,128)S(1)} %add_add_fusion.1.a_ref), channel_id=1, source_target_pairs={{0,8},{4,12},{8,0},{12,4},{16,24},{20,28},{24,16},{28,20},{32,40},... | collective-permute-start | bytes 147464 | tf_op jit(solution)/shard_map/ppermute | solution.py:36
  175.2 3.5 %copy-start.11 = (f32[96,128]{1,0:T(8,128)}, f32[96,128]{1,0:T(8,128)S(1)}, u32[]{:S(2)}) copy-start(f32[96,128]{1,0:T(8,128)S(1)} %collective-permute-done.13.b_ref) | copy-start | bytes 147460
  181.5 7.2 %collective-permute-start.15 = (f32[96,128]{1,0:T(8,128)}, f32[96,128]{1,0:T(8,128)S(1)}, u32[]{:S(2)}, u32[]{:S(2)}) collective-permute-start(f32[96,128]{1,0:T(8,128)} %join.1), channel_id=1, source_target_pairs={{0,32},{4,36},{8,40},{12,44},{16,48},{20,52},{24,56},{28,60},{32,0... | collective-permute-start | bytes 147464 | tf_op jit(solution)/shard_map/ppermute | solution.py:36
  183.8 5.7 %collective-permute-start.16 = (f32[96,128]{1,0:T(8,128)}, f32[96,128]{1,0:T(8,128)S(1)}, u32[]{:S(2)}, u32[]{:S(2)}) collective-permute-start(f32[96,128]{1,0:T(8,128)} %join.1), channel_id=1, source_target_pairs={{0,48},{4,52},{8,56},{12,60},{16,32},{20,36},{24,40},{28,44},{32,1... | collective-permute-start | bytes 147464 | tf_op jit(solution)/shard_map/ppermute | solution.py:36
  184.9 4.7 %collective-permute-start.14 = (f32[96,128]{1,0:T(8,128)}, f32[96,128]{1,0:T(8,128)S(1)}, u32[]{:S(2)}, u32[]{:S(2)}) collective-permute-start(f32[96,128]{1,0:T(8,128)} %join.1), channel_id=1, source_target_pairs={{0,16},{4,20},{8,24},{12,28},{16,0},{20,4},{24,8},{28,12},{32,48},... | collective-permute-start | bytes 147464 | tf_op jit(solution)/shard_map/ppermute | solution.py:36
  190.3 8.1 %collective-permute-start.17 = (f32[96,128]{1,0:T(8,128)S(1)}, f32[96,128]{1,0:T(8,128)S(1)}, u32[]{:S(2)}, u32[]{:S(2)}) collective-permute-start(f32[96,128]{1,0:T(8,128)S(1)} %add_add_fusion), channel_id=1, source_target_pairs={{0,4},{4,0},{8,12},{12,8},{16,20},{20,16},{24,28},{28,24},{32,36},... | collective-permute-start | bytes 147464 | tf_op jit(solution)/shard_map/ppermute | solution.py:36
  (4 other events, 3.7 us)
Sparse Core Ops, SparseCore 0:
  9.8 46.2 all-gather.5
  58.0 24.3 all-gather.3

commit v8 on v6

--- a/solution.py
+++ b/solution.py
@@ -22,6 +22,7 @@
 
 NY, NZ, NC = 4, 8, 2
 CAP = 2
+TAIL = 16
 ORDER = (0, 1, 7, 2, 6, 3, 5, 4)
 GROUPS = ((0, 3), (3, 5), (5, 8))
 PER = NZ * CAP
@@ -111,13 +112,14 @@
     )(cols, feats, tiles)
 
 
-def agg_remote_kernel(slots_ref, tiles_ref, local_ref, *refs):
-    parts, out_ref, recv_ref = refs[:-2], refs[-2], refs[-1]
+def agg_remote_kernel(slots_ref, held_ref, tiles_ref, local_ref, *refs):
+    parts, out_ref, held_out_ref, recv_ref = refs[:-3], refs[-3], refs[-2], refs[-1]
     i = pl.program_id(0)
     count, block = tiles_ref.shape[1], tiles_ref.shape[2]
 
     @pl.when(i == 0)
     def _():
+        held_out_ref[...] = held_ref[...]
         n = 0
         for first, last in GROUPS:
             size = (last - first) * CAP
@@ -136,7 +138,7 @@
         out_ref[:, rr * block : (rr + 1) * block] = acc.astype(out_ref.dtype)
 
 
-def agg_remote(slots, parts, tiles, local):
+def agg_remote(slots, held, parts, tiles, local):
     row_blocks, per_block, block, _ = tiles.shape
     rem = per_block - TL
     width = local.shape[0]
@@ -147,20 +149,24 @@
     return pl.pallas_call(
         agg_remote_kernel,
         grid=(row_blocks // STEP,),
-        out_shape=jax.ShapeDtypeStruct(local.shape, BF),
+        out_shape=(jax.ShapeDtypeStruct(local.shape, BF), jax.ShapeDtypeStruct(held.shape, held.dtype)),
         in_specs=[
             SMEM,
+            pl.BlockSpec(held.shape, lambda i: (0, 0, 0)),
             pl.BlockSpec((STEP, rem, block, block), lambda i: (i, 1, 0, 0)),
             pl.BlockSpec((width, STEP * block), lambda i: (0, i)),
         ]
         + specs,
-        out_specs=pl.BlockSpec((width, STEP * block), lambda i: (0, i)),
+        out_specs=(
+            pl.BlockSpec((width, STEP * block), lambda i: (0, i)),
+            pl.BlockSpec(held.shape, lambda i: (0, 0, 0)),
+        ),
         scratch_shapes=[pltpu.VMEM((NY * NC * PER, width, block), BF)],
         name="agg_remote",
         cost_estimate=pl.CostEstimate(
             flops=2 * width * row_blocks * rem * block * block, bytes_accessed=5 << 20, transcendentals=0
         ),
-    )(slots, tiles, local, *parts)
+    )(slots, held, tiles, local, *parts)
 
 
 def mid_kernel(
@@ -222,7 +228,8 @@
     @pl.when(i == pl.num_programs(0) - 1)
     def _():
         half = keep_ref.shape[0]
-        sums_scr[-width:] = gb_scr[rows(0)]
+        own = gb_scr[rows(0)]
+        sums_scr[2 * half - TAIL : 2 * half - TAIL + 1, :width] = jnp.sum(own.T, axis=0, keepdims=True)
         keep_ref[...] = sums_scr[pl.ds(pl.multiple_of(me_ref[1] * half, half), half)]
         give_ref[...] = sums_scr[pl.ds(pl.multiple_of((1 - me_ref[1]) * half, half), half)]
 
@@ -232,7 +239,7 @@
     width, nodes = own.shape
     hid_all = packed.shape[0]
     chunk = 512
-    half = width * (hid_all // 128 + 1) // NC
+    half = (width * (hid_all // 128) + TAIL) // NC
     col = lambda i: (0, i)
     return pl.pallas_call(
         mid_kernel,
@@ -359,34 +366,53 @@
     )(cols, g, tiles, after)
 
 
-def finish_kernel(place_ref, wanted_ref, recv_ref, local_ref, out_ref, odd_scr):
-    width, block = out_ref.shape[0], recv_ref.shape[2]
+STREAMS = 4
+
+
+def finish_kernel(place_ref, held_ref, recv_ref, local_ref, out_ref, odd_scr, recv_scr, sems):
+    width, block = out_ref.shape[0], recv_scr.shape[2]
+    count = recv_scr.shape[0] // STREAMS
+
+    def stream(n):
+        part = pl.ds(n * count, count)
+        return pltpu.make_async_copy(recv_ref.at[part], recv_scr.at[part], sems.at[n])
+
+    for n in range(STREAMS):
+        stream(n).start()
     out_ref[...] = local_ref[...]
     odd_scr[...] = jnp.zeros_like(odd_scr)
-
-    def body(p, carry):
-        back = (p // (NZ * NC) - place_ref[0]) & (NY - 1)
-        base = ((p // NC % NZ * NY + back) * NC + ((p ^ place_ref[1]) & 1)) * CAP
-        even = lanes(jnp.maximum(wanted_ref[base], 0), block)
-        odd = lanes(jnp.maximum(wanted_ref[base + 1], 0), block)
-        out_ref[:, even] += recv_ref[p, :width].astype(F32)
-        odd_scr[:, odd] += recv_ref[p, width : 2 * width].astype(F32)
-        return carry
-
-    lax.fori_loop(0, recv_ref.shape[0], body, 0, unroll=4)
+    for n in range(STREAMS):
+        stream(n).wait()
+
+        def body(p, carry):
+            back = (p // (NZ * NC) - place_ref[0]) & (NY - 1)
+            base = (back * NC + ((p ^ place_ref[1]) & 1)) * CAP
+            z = p // NC % NZ
+            even = lanes(jnp.maximum(held_ref[z, 0, base], 0), block)
+            odd = lanes(jnp.maximum(held_ref[z, 0, base + 1], 0), block)
+            out_ref[:, even] += recv_scr[p, :width].astype(F32)
+            odd_scr[:, odd] += recv_scr[p, width : 2 * width].astype(F32)
+            return carry
+
+        lax.fori_loop(n * count, (n + 1) * count, body, 0, unroll=4)
     out_ref[...] += odd_scr[...]
 
 
-def finish(place, wanted, recv, local):
+def finish(place, held, recv, local):
     return pl.pallas_call(
         finish_kernel,
         out_shape=jax.ShapeDtypeStruct(local.shape, F32),
-        in_specs=[SMEM, SMEM, VMEM, VMEM],
+        in_specs=[SMEM, SMEM, ANY, VMEM],
         out_specs=VMEM,
-        scratch_shapes=[pltpu.VMEM(local.shape, F32)],
+        scratch_shapes=[
+            pltpu.VMEM(local.shape, F32),
+            pltpu.VMEM(recv.shape, recv.dtype),
+            pltpu.SemaphoreType.DMA((STREAMS,)),
+        ],
         name="finish",
+        compiler_params=pltpu.CompilerParams(vmem_limit_bytes=16 << 20),
         cost_estimate=pl.CostEstimate(flops=recv.size, bytes_accessed=4 << 20, transcendentals=0),
-    )(place, wanted, recv, local)
+    )(place, held, recv, local)
 
 
 def split_bf16(x, terms):
@@ -459,39 +485,38 @@
     packed = jnp.concatenate([cotangent, weight, bias_cols], axis=1)
     packed = lax.all_gather(packed, "feat", axis=0, tiled=True)
 
-    agg = agg_remote(near, parts, tiles, agg)
+    by_owner = wanted.reshape(NY * NC, NZ, CAP)
+    steps = (jnp.arange(NZ) - z) & (NZ - 1)
+    match = (place_of(steps)[:, None] == jnp.arange(NZ)[None, :])[:, None, :, None]
+    held = jnp.sum(jnp.where(match, by_owner[None], 0), axis=2).reshape(NZ, 1, NY * NC * CAP)
+    agg, held = agg_remote(near, held, parts, tiles, agg)
 
     pieces = [agg] + [
         lax.ppermute(agg, "feat", [(k, (k + s) % fpeers) for k in range(fpeers)]) for s in (1, 3, 2)
     ]
-    by_owner = wanted.reshape(NY * NC, NZ, CAP)
-    steps = (jnp.arange(NZ) - z) & (NZ - 1)
-    match = (place_of(steps)[:, None] == jnp.arange(NZ)[None, :])[:, None, :, None]
-    held = jnp.sum(jnp.where(match, by_owner[None], 0), axis=2).reshape(NZ, NY * NC * CAP)
-    held = jnp.where(agg[0, 0].astype(F32) > jnp.inf, 0, held)
     along_z = [[(y0 * NZ + z0) * NC + c0 for z0 in range(NZ)] for y0 in range(NY) for c0 in range(NC)]
-    held = lax.all_to_all(held, "rows", 0, 0, tiled=True, axis_index_groups=along_z).reshape(-1)
+    held = lax.all_to_all(held, "rows", 0, 0, tiled=True, axis_index_groups=along_z)
 
     me = jnp.stack([lax.axis_index("feat"), c]).astype(jnp.int32)
     hidden_out, g, keep, give = mid(me, pieces, packed, weight, held)
 
     part = keep + shift(give, dc=1)
-    part = part + shift(part, flip_z=1)
-    pairs = [part] + [shift(part, flip_z=k) for k in (2, 4, 6)]
+    twin = shift(part, flip_z=1)
     send = back_remote(slots, g, tiles, peers, part)
-    send, pairs = lax.optimization_barrier((send, pairs))
-    part = (pairs[0] + pairs[1]) + (pairs[2] + pairs[3])
+    send, twin = lax.optimization_barrier((send, twin))
     recv = lax.all_to_all(send, "rows", split_axis=0, concat_axis=0, tiled=True)
     own = back_local(local_cols, g, tiles, send)
-
-    own, part = lax.optimization_barrier((own, part))
+    own, part, twin = lax.optimization_barrier((own, part, twin))
+    part = part + twin
     pairs = [part] + [shift(part, flip_y=k) for k in (1, 2, 3)]
+    part = (pairs[0] + pairs[1]) + (pairs[2] + pairs[3])
+    pairs = [part] + [shift(part, flip_z=k) for k in (2, 4, 6)]
     part = (pairs[0] + pairs[1]) + (pairs[2] + pairs[3])
     other = shift(part, dc=1)
     total = jnp.where(c == 0, jnp.concatenate([part, other]), jnp.concatenate([other, part]))
     total = total / math.sqrt(nodes_dev * peers)
     grad_w = jnp.concatenate([total[k * width : (k + 1) * width] for k in range(hid_all // 128)], axis=1)
-    grad_b = jnp.sum(total[-width:], axis=1)
+    grad_b = total[width * (hid_all // 128), :width]
 
     grad_input = finish(jnp.stack([y, c]).astype(jnp.int32), held, recv, own)
     return hidden_out, grad_input, grad_w, grad_b

time: 200 us -> 192 us (0.960)
  local copies, waits for them, and re-layouts: 8.83 us -> 6.82 us
    all_to_all x1, waiting for transfers between devices: 33.6 us -> 0.01 us  [local(): recv = lax.all_to_all(send, 'rows', split_axis=0, concat_axis=0, tiled=True)]
    ppermute x33, waiting for transfers between devices: 26.5 us -> 57.3 us  [shift(): return lax.ppermute(x, 'rows', pairs)]
  transfers between devices with their start and end apart: 39 -> 39, of which waited for: 13 -> 14; matrix products, arithmetic and copies ran while one was open for 7% -> 5% of each run, Pallas kernels for 12% -> 13%
where the time goes in v8:
time: 192 us; the launch traced here: 191 us
  starting transfers between devices  66 us (34%)
  waiting for transfers between devices  64.7 us (34%)
  Pallas kernels  32 us (17%)
  between operations  14.5 us (8%)
  other arithmetic  6.88 us (4%)
  local copies, waits for them, and re-layouts  6.82 us (4%)
    ppermute x33, waiting for transfers between devices, shift(): return lax.ppermute(x, 'rows', pairs)  57.3 us
    ppermute x33, starting transfers between devices, shift(): return lax.ppermute(x, 'rows', pairs)  51.5 us
    all_to_all x1, starting transfers between devices, local(): recv = lax.all_to_all(send, 'rows', split_axis=0, concat_axis=0, tiled=True)  6.9 us
    pallas_call x3, Pallas kernels, pack(): pl.pallas_call(functools.partial(pack_kernel, first, count, len(sources)...  6.52 us
    all_to_all x1, waiting for transfers between devices, local(): lax.all_to_all(held, 'rows', 0, 0, tiled=True, axis_index_groups=along_z)  5.71 us
    pallas_call x1, Pallas kernels, mid(): pl.pallas_call(mid_kernel, grid=(nodes // chunk,), out_shape=(jax.ShapeDt...  4.99 us
    pallas_call x1, Pallas kernels, agg_remote(): pl.pallas_call(agg_remote_kernel, grid=(row_blocks // STEP,), out_shape=(...  4.89 us
    pallas_call x1, Pallas kernels, back_remote(): pl.pallas_call(back_remote_kernel, grid=(row_blocks // STEP,), out_shape=...  4.51 us
  transfers between devices with their start and end apart: 39, of which 14 were waited for; matrix products, arithmetic and copies ran while one was open for 5% of the time, Pallas kernels for 13%

profile of v8, /device:TPU:1, one launch (start us, length us, event | category | flops | bytes accessed | tf_op | source)
XLA Modules:
  0.0 190.9 jit_solution(5493532676305394612)
XLA Ops:
  7.2 6.5 %collective-permute-start.4 = (bf16[64,2048]{1,0:T(8,128)(2,1)}, bf16[64,2048]{1,0:T(8,128)(2,1)S(1)}, u32[]{:S(2)}, u32[]{:S(2)}) collective-permute-start(bf16[64,2048]{1,0:T(8,128)(2,1)} %refs_1_.1), channel_id=1, source_target_pairs={{0,56},{4,60},{8,0},{12,4},{16,8},{20,12},{24,16},{28,20},{32,24},... | collective-permute-start | bytes 786440 | tf_op jit(solution)/shard_map/ppermute | solution.py:38
  17.4 4.6 %collective-permute-done.5.refs_3_ = bf16[64,2048]{1,0:T(8,128)(2,1)S(1)} collective-permute-done((bf16[64,2048]{1,0:T(8,128)(2,1)}, bf16[64,2048]{1,0:T(8,128)(2,1)S(1)}, u32[]{:S(2)}, u32[]{:S(2)}) %collective-permute-start.5) | collective-permute-done | bytes 262176 | tf_op jit(solution)/shard_map/ppermute | solution.py:38
  22.6 2.6 %collective-permute-start.10 = (bf16[64,2048]{1,0:T(8,128)(2,1)S(1)}, bf16[64,2048]{1,0:T(8,128)(2,1)S(1)}, u32[]{:S(2)}, u32[]{:S(2)}) collective-permute-start(bf16[64,2048]{1,0:T(8,128)(2,1)S(1)} %collective-permute-done.4.refs_2_), channel_id=1, source_target_pairs={{0,56},{4,60},{8,0},{12,4},{16,8},{20,12},{24,16},{28,20},{32,24},... | collective-permute-start | bytes 786440 | tf_op jit(solution)/shard_map/ppermute | solution.py:38
  25.3 3.8 %collective-permute-done.11.refs_2_ = bf16[64,2048]{1,0:T(8,128)(2,1)S(1)} collective-permute-done((bf16[64,2048]{1,0:T(8,128)(2,1)S(1)}, bf16[64,2048]{1,0:T(8,128)(2,1)S(1)}, u32[]{:S(2)}, u32[]{:S(2)}) %collective-permute-start.11) | collective-permute-done | bytes 262176 | tf_op jit(solution)/shard_map/ppermute | solution.py:38
  29.3 2.8 %collective-permute-start = (s32[4,16]{1,0:T(4,128)S(1)}, s32[4,16]{1,0:T(4,128)S(1)}, u32[]{:S(2)}, u32[]{:S(2)}) collective-permute-start(s32[4,16]{1,0:T(4,128)S(1)} %squeeze.15), channel_id=1, source_target_pairs={{0,4},{4,0},{8,12},{12,8},{16,20},{20,16},{24,28},{28,24},{32,36},... | collective-permute-start | bytes 776 | tf_op jit(solution)/shard_map/ppermute | solution.py:38
  32.2 3.0 %collective-permute-start.16 = (bf16[64,2048]{1,0:T(8,128)(2,1)S(1)}, bf16[64,2048]{1,0:T(8,128)(2,1)S(1)}, u32[]{:S(2)}, u32[]{:S(2)}) collective-permute-start(bf16[64,2048]{1,0:T(8,128)(2,1)S(1)} %collective-permute-done.10.refs_1_), channel_id=1, source_target_pairs={{0,56},{4,60},{8,0},{12,4},{16,8},{20,12},{24,16},{28,20},{32,24},... | collective-permute-start | bytes 786440 | tf_op jit(solution)/shard_map/ppermute | solution.py:38
  39.7 2.3 %collective-permute-done.2 = s32[2,16]{1,0:T(2,128)S(1)} collective-permute-done((s32[2,16]{1,0:T(2,128)S(1)}, s32[2,16]{1,0:T(2,128)S(1)}, u32[]{:S(2)}, u32[]{:S(2)}) %collective-permute-start.2) | collective-permute-done | bytes 160 | tf_op jit(solution)/shard_map/ppermute | solution.py:38
  42.7 2.2 %pack.3 = (bf16[2,6,64,128]{3,2,1,0:T(8,128)(2,1)}, bf16[2,6,64,128]{3,2,1,0:T(8,128)(2,1)}, bf16[2,6,64,128]{3,2,1,0:T(8,128)(2,1)}, bf16[2,6,64,128]{3,2,1,0:T(8,128)(2,1)}) custom-call(s32[128]{0:T(128)} %reshape.217.refs_0_, bf16[64,2048]{1,0:T(8,128)(2,1)} %refs_1_.1, bf16[64,2048]{1,0:T(8,128)(2,1)} %copy-done.24, bf16[64,2048]{1,0:T(8,128)(2,1)} %copy-done.25), custom_call_target="tpu_custom_call" | custom-call | bytes 3145728 | tf_op jit(solution)/shard_map/pack/pallas_call | solution.py:62
  45.2 2.2 %collective-permute-start.7 = (bf16[2,6,64,128]{3,2,1,0:T(8,128)(2,1)}, bf16[2,6,64,128]{3,2,1,0:T(8,128)(2,1)S(1)}, u32[]{:S(2)}, u32[]{:S(2)}) collective-permute-start(bf16[2,6,64,128]{3,2,1,0:T(8,128)(2,1)} %get-tuple-element.29), channel_id=1, source_target_pairs={{0,128},{4,132},{8,136},{12,140},{16,144},{20,148},{24,152},{28,15... | collective-permute-start | bytes 589832 | tf_op jit(solution)/shard_map/ppermute | solution.py:38
  50.2 4.1 %agg_local.1.refs_4_.refs_6_.local_ref = f32[64,2048]{1,0:T(8,128)} custom-call(s32[64]{0:T(128)} %reshape.216.cols_ref, bf16[64,2048]{1,0:T(8,128)(2,1)} %refs_1_.1, bf16[16,8,128,128]{3,2,1,0:T(8,128)(2,1)} %bitcast.26), custom_call_target="tpu_custom_call" | custom-call | flops 134217728 | bytes 3145728 | tf_op jit(solution)/shard_map/agg_local/pallas_call | solution.py:98
  54.3 2.0 %pack.4 = (bf16[2,4,64,128]{3,2,1,0:T(8,128)(2,1)}, bf16[2,4,64,128]{3,2,1,0:T(8,128)(2,1)}, bf16[2,4,64,128]{3,2,1,0:T(8,128)(2,1)}, bf16[2,4,64,128]{3,2,1,0:T(8,128)(2,1)}) custom-call(s32[128]{0:T(128)} %reshape.217.refs_0_, bf16[64,2048]{1,0:T(8,128)(2,1)} %copy-done.27, bf16[64,2048]{1,0:T(8,128)(2,1)} %copy-done.26, ...), custom_call_target="tpu_custom_call" | custom-call | bytes 3145728 | tf_op jit(solution)/shard_map/pack/pallas_call | solution.py:62
  57.8 2.3 %pack.5 = (bf16[2,6,64,128]{3,2,1,0:T(8,128)(2,1)}, bf16[2,6,64,128]{3,2,1,0:T(8,128)(2,1)}, bf16[2,6,64,128]{3,2,1,0:T(8,128)(2,1)}, bf16[2,6,64,128]{3,2,1,0:T(8,128)(2,1)}) custom-call(s32[128]{0:T(128)} %reshape.217.refs_0_, bf16[64,2048]{1,0:T(8,128)(2,1)} %copy-done.6, bf16[64,2048]{1,0:T(8,128)(2,1)} %copy-done.5, bf16[32,2048]{1,0:T(8,128)(2,1)} %copy-done.28, ...), custom_call_target="tpu_custom_call" | custom-call | bytes 3145728 | tf_op jit(solution)/shard_map/pack/pallas_call | solution.py:62
  60.1 2.2 %collective-permute-start.14 = (bf16[2,4,64,128]{3,2,1,0:T(8,128)(2,1)}, bf16[2,4,64,128]{3,2,1,0:T(8,128)(2,1)S(1)}, u32[]{:S(2)}, u32[]{:S(2)}) collective-permute-start(bf16[2,4,64,128]{3,2,1,0:T(8,128)(2,1)} %get-tuple-element.34), channel_id=1, source_target_pairs={{0,192},{4,196},{8,200},{12,204},{16,208},{20,212},{24,216},{28,22... | collective-permute-start | bytes 393224 | tf_op jit(solution)/shard_map/ppermute | solution.py:38
  64.2 2.0 %collective-permute-start.22 = (bf16[2,6,64,128]{3,2,1,0:T(8,128)(2,1)}, bf16[2,6,64,128]{3,2,1,0:T(8,128)(2,1)S(1)}, u32[]{:S(2)}, u32[]{:S(2)}) collective-permute-start(bf16[2,6,64,128]{3,2,1,0:T(8,128)(2,1)} %get-tuple-element.38), channel_id=1, source_target_pairs={{0,192},{4,196},{8,200},{12,204},{16,208},{20,212},{24,216},{28,22... | collective-permute-start | bytes 589832 | tf_op jit(solution)/shard_map/ppermute | solution.py:38
  66.3 4.5 %collective-permute-start.9 = (bf16[4,6,64,128]{3,2,1,0:T(8,128)(2,1)S(1)}, bf16[4,6,64,128]{3,2,1,0:T(8,128)(2,1)S(1)}, u32[]{:S(2)}, u32[]{:S(2)}) collective-permute-start(bf16[4,6,64,128]{3,2,1,0:T(8,128)(2,1)S(1)} %pad_maximum_fusion), channel_id=1, source_target_pairs={{0,4},{4,0},{8,12},{12,8},{16,20},{20,16},{24,28},{28,24},{32,36},... | collective-permute-start | bytes 1179656 | tf_op jit(solution)/shard_map/ppermute | solution.py:38
  71.5 3.3 %collective-permute-done.22.refs_13_ = bf16[2,6,64,128]{3,2,1,0:T(8,128)(2,1)S(1)} collective-permute-done((bf16[2,6,64,128]{3,2,1,0:T(8,128)(2,1)}, bf16[2,6,64,128]{3,2,1,0:T(8,128)(2,1)S(1)}, u32[]{:S(2)}, u32[]{:S(2)}) %collective-permute-start.22) | collective-permute-done | bytes 196640 | tf_op jit(solution)/shard_map/ppermute | solution.py:38
  74.8 2.6 %collective-permute-start.23 = (bf16[4,6,64,128]{3,2,1,0:T(8,128)(2,1)S(1)}, bf16[4,6,64,128]{3,2,1,0:T(8,128)(2,1)S(1)}, u32[]{:S(2)}, u32[]{:S(2)}) collective-permute-start(bf16[4,6,64,128]{3,2,1,0:T(8,128)(2,1)S(1)} %pad_maximum_fusion.1), channel_id=1, source_target_pairs={{0,4},{4,0},{8,12},{12,8},{16,20},{20,16},{24,28},{28,24},{32,36},... | collective-permute-start | bytes 1179656 | tf_op jit(solution)/shard_map/ppermute | solution.py:38
  81.2 4.9 %agg_remote.1 = (bf16[64,2048]{1,0:T(8,128)(2,1)}, s32[8,1,16]{2,1,0:T(1,128)}) custom-call(s32[64]{0:T(128)} %copy-done.30, s32[8,1,16]{2,1,0:T(1,128)} %copy.42.held_ref, bf16[16,8,128,128]{3,2,1,0:T(8,128)(2,1)} %bitcast.27, f32[64,2048]{1,0:T(8,128)} %agg_local.1.refs_4_.refs_6_.local_ref, bf16[2,6,64,128]{3,2,1,0:T(8,128)(2,1)} %get-tuple-element.27.refs_3_.refs_0_, ...), custom_call_target="tpu_custom_call" | custom-call | flops 134217728 | bytes 5242880 | tf_op jit(solution)/shard_map/agg_remote/pallas_call | solution.py:149
  90.3 3.3 %all-to-all-start = ((s32[8,1,16]{2,1,0:T(1,128)}), s32[8,1,16]{2,1,0:T(1,128)S(1)}, u32[]{:S(2)}, u32[]{:S(2)}) async-start(s32[8,1,16]{2,1,0:T(1,128)} %get-tuple-element.39), calls=%async_computation | async-start | bytes 8192 | tf_op jit(solution)/shard_map/all_to_all | solution.py:498
  94.3 5.7 %all-to-all-done._.held_ref = s32[8,1,16]{2,1,0:T(1,128)S(1)} async-done(((s32[8,1,16]{2,1,0:T(1,128)}), s32[8,1,16]{2,1,0:T(1,128)S(1)}, u32[]{:S(2)}, u32[]{:S(2)}) %all-to-all-start) | async-done | bytes 544 | tf_op jit(solution)/shard_map/all_to_all | solution.py:498
  102.3 5.0 %mid.1 = (bf16[64,2048]{1,0:T(8,128)(2,1)}, bf16[64,2048]{1,0:T(8,128)(2,1)}, f32[72,128]{1,0:T(8,128)}, f32[72,128]{1,0:T(8,128)}) custom-call(s32[2]{0:T(128)} %pad_add_fusion.2.me_ref, s32[8,1,16]{2,1,0:T(1,128)} %copy-done.1, bf16[64,2048]{1,0:T(8,128)(2,1)} %get-tuple-element.40.own_ref, bf16[64,2048]{1,0:T(8,128)(2,1)} %copy-done.21, ...), custom_call_target="tpu_custom_call" | custom-call | flops 402653184 | bytes 3145728 | tf_op jit(solution)/shard_map/mid/pallas_call | solution.py:244
  111.4 4.5 %back_remote.1._ = bf16[64,128,128]{2,1,0:T(8,128)(2,1)} custom-call(s32[64]{0:T(128)} %get-tuple-element.58.slots_ref, bf16[64,2048]{1,0:T(8,128)(2,1)} %get-tuple-element.42.g_ref, bf16[16,8,128,128]{3,2,1,0:T(8,128)(2,1)} %bitcast.28, f32[72,128]{1,0:T(8,128)} %copy-done.16), custom_call_target="tpu_custom_call" | custom-call | flops 134217728 | bytes 5242880 | tf_op jit(solution)/shard_map/back_remote/pallas_call | solution.py:312
  116.0 6.9 %all-to-all-start.1 = ((bf16[64,128,128]{2,1,0:T(8,128)(2,1)}), bf16[64,128,128]{2,1,0:T(8,128)(2,1)S(1)}, u32[]{:S(2)}, u32[]{:S(2)}) async-start(bf16[64,128,128]{2,1,0:T(8,128)(2,1)} %back_remote.1._), calls=%async_computation.1 | async-start | bytes 4194304 | tf_op jit(solution)/shard_map/all_to_all | solution.py:507
  122.9 3.9 %back_local.1.local_ref = f32[64,2048]{1,0:T(8,128)} custom-call(s32[64]{0:T(128)} %reshape.216.cols_ref, bf16[64,2048]{1,0:T(8,128)(2,1)} %get-tuple-element.42.g_ref, bf16[16,8,128,128]{3,2,1,0:T(8,128)(2,1)} %bitcast.29, bf16[64,128,128]{2,1,0:T(8,128)(2,1)} %back_remote.1._), custom_call_target="tpu_custom_call" | custom-call | flops 134217728 | bytes 3145728 | tf_op jit(solution)/shard_map/back_local/pallas_call | solution.py:351
  128.3 2.6 %collective-permute-start.30 = (f32[72,128]{1,0:T(8,128)S(1)}, f32[72,128]{1,0:T(8,128)S(1)}, u32[]{:S(2)}, u32[]{:S(2)}) collective-permute-start(f32[72,128]{1,0:T(8,128)S(1)} %add.112), channel_id=1, source_target_pairs={{0,128},{4,132},{8,136},{12,140},{16,144},{20,148},{24,152},{28,15... | collective-permute-start | bytes 110600 | tf_op jit(solution)/shard_map/ppermute | solution.py:38
  130.9 3.4 %collective-permute-done.30 = f32[72,128]{1,0:T(8,128)S(1)} collective-permute-done((f32[72,128]{1,0:T(8,128)S(1)}, f32[72,128]{1,0:T(8,128)S(1)}, u32[]{:S(2)}, u32[]{:S(2)}) %collective-permute-start.30) | collective-permute-done | bytes 36896 | tf_op jit(solution)/shard_map/ppermute | solution.py:38
  134.3 2.4 %collective-permute-done.31 = f32[72,128]{1,0:T(8,128)S(1)} collective-permute-done((f32[72,128]{1,0:T(8,128)S(1)}, f32[72,128]{1,0:T(8,128)S(1)}, u32[]{:S(2)}, u32[]{:S(2)}) %collective-permute-start.31) | collective-permute-done | bytes 36896 | tf_op jit(solution)/shard_map/ppermute | solution.py:38
  136.8 1.8 collective-permute-start.32
  138.6 2.7 %collective-permute-start.33 = (f32[72,128]{1,0:T(8,128)S(1)}, f32[72,128]{1,0:T(8,128)S(1)}, u32[]{:S(2)}, u32[]{:S(2)}) collective-permute-start(f32[72,128]{1,0:T(8,128)S(1)} %add_add_fusion.1), channel_id=1, source_target_pairs={{0,32},{4,36},{8,40},{12,44},{16,48},{20,52},{24,56},{28,60},{32,0... | collective-permute-start | bytes 110600 | tf_op jit(solution)/shard_map/ppermute | solution.py:38
  142.5 29.9 %collective-permute-done.32 = f32[72,128]{1,0:T(8,128)S(1)} collective-permute-done((f32[72,128]{1,0:T(8,128)S(1)}, f32[72,128]{1,0:T(8,128)S(1)}, u32[]{:S(2)}, u32[]{:S(2)}) %collective-permute-start.32) | collective-permute-done | bytes 36896 | tf_op jit(solution)/shard_map/ppermute | solution.py:38
  172.4 4.8 %collective-permute-done.33 = f32[72,128]{1,0:T(8,128)S(1)} collective-permute-done((f32[72,128]{1,0:T(8,128)S(1)}, f32[72,128]{1,0:T(8,128)S(1)}, u32[]{:S(2)}, u32[]{:S(2)}) %collective-permute-start.33) | collective-permute-done | bytes 36896 | tf_op jit(solution)/shard_map/ppermute | solution.py:38
  180.9 3.1 %finish.1 = f32[64,2048]{1,0:T(8,128)} custom-call(s32[2]{0:T(128)S(1)} %pad_add_fusion.3.place_ref, s32[8,1,16]{2,1,0:T(1,128)S(1)} %copy-done.2, bf16[64,128,128]{2,1,0:T(8,128)(2,1)S(1)} %all-to-all-done.1.recv_ref, f32[64,2048]{1,0:T(8,128)S(1)} %copy-done), custom_call_target="tpu_custom_call" | custom-call | flops 1048576 | bytes 4194304 | tf_op jit(solution)/shard_map/finish/pallas_call | solution.py:402
  (171 shorter events, 38.4 us)
Async XLA Ops:
  7.2 94.4 %all-gather.2.cloned.1.call-start = ((), (), s32[]{:S(2)}) async-start(), calls=%async_computation.2 | async-start | bytes 1556480 | tf_op jit(solution)/shard_map/all_gather | solution.py:486
  7.2 15.4 %collective-permute-start.4 = (bf16[64,2048]{1,0:T(8,128)(2,1)}, bf16[64,2048]{1,0:T(8,128)(2,1)S(1)}, u32[]{:S(2)}, u32[]{:S(2)}) collective-permute-start(bf16[64,2048]{1,0:T(8,128)(2,1)} %refs_1_.1), channel_id=1, source_target_pairs={{0,56},{4,60},{8,0},{12,4},{16,8},{20,12},{24,16},{28,20},{32,24},... | collective-permute-start | bytes 786440 | tf_op jit(solution)/shard_map/ppermute | solution.py:38
  13.7 8.3 %collective-permute-start.5 = (bf16[64,2048]{1,0:T(8,128)(2,1)}, bf16[64,2048]{1,0:T(8,128)(2,1)S(1)}, u32[]{:S(2)}, u32[]{:S(2)}) collective-permute-start(bf16[64,2048]{1,0:T(8,128)(2,1)} %refs_1_.1), channel_id=1, source_target_pairs={{0,8},{4,12},{8,16},{12,20},{16,24},{20,28},{24,32},{28,36},{32,40... | collective-permute-start | bytes 786440 | tf_op jit(solution)/shard_map/ppermute | solution.py:38
  22.0 7.1 %collective-permute-start.11 = (bf16[64,2048]{1,0:T(8,128)(2,1)S(1)}, bf16[64,2048]{1,0:T(8,128)(2,1)S(1)}, u32[]{:S(2)}, u32[]{:S(2)}) collective-permute-start(bf16[64,2048]{1,0:T(8,128)(2,1)S(1)} %collective-permute-done.5.refs_3_), channel_id=1, source_target_pairs={{0,8},{4,12},{8,16},{12,20},{16,24},{20,28},{24,32},{28,36},{32,40... | collective-permute-start | bytes 786440 | tf_op jit(solution)/shard_map/ppermute | solution.py:38
  22.6 9.5 %collective-permute-start.10 = (bf16[64,2048]{1,0:T(8,128)(2,1)S(1)}, bf16[64,2048]{1,0:T(8,128)(2,1)S(1)}, u32[]{:S(2)}, u32[]{:S(2)}) collective-permute-start(bf16[64,2048]{1,0:T(8,128)(2,1)S(1)} %collective-permute-done.4.refs_2_), channel_id=1, source_target_pairs={{0,56},{4,60},{8,0},{12,4},{16,8},{20,12},{24,16},{28,20},{32,24},... | collective-permute-start | bytes 786440 | tf_op jit(solution)/shard_map/ppermute | solution.py:38
  29.1 10.5 %collective-permute-start.17 = (bf16[64,2048]{1,0:T(8,128)(2,1)S(1)}, bf16[64,2048]{1,0:T(8,128)(2,1)S(1)}, u32[]{:S(2)}, u32[]{:S(2)}) collective-permute-start(bf16[64,2048]{1,0:T(8,128)(2,1)S(1)} %collective-permute-done.11.refs_2_), channel_id=1, source_target_pairs={{0,8},{4,12},{8,16},{12,20},{16,24},{20,28},{24,32},{28,36},{32,40... | collective-permute-start | bytes 786440 | tf_op jit(solution)/shard_map/ppermute | solution.py:38
  29.3 5.9 %collective-permute-start = (s32[4,16]{1,0:T(4,128)S(1)}, s32[4,16]{1,0:T(4,128)S(1)}, u32[]{:S(2)}, u32[]{:S(2)}) collective-permute-start(s32[4,16]{1,0:T(4,128)S(1)} %squeeze.15), channel_id=1, source_target_pairs={{0,4},{4,0},{8,12},{12,8},{16,20},{20,16},{24,28},{28,24},{32,36},... | collective-permute-start | bytes 776 | tf_op jit(solution)/shard_map/ppermute | solution.py:38
  32.2 17.3 %collective-permute-start.16 = (bf16[64,2048]{1,0:T(8,128)(2,1)S(1)}, bf16[64,2048]{1,0:T(8,128)(2,1)S(1)}, u32[]{:S(2)}, u32[]{:S(2)}) collective-permute-start(bf16[64,2048]{1,0:T(8,128)(2,1)S(1)} %collective-permute-done.10.refs_1_), channel_id=1, source_target_pairs={{0,56},{4,60},{8,0},{12,4},{16,8},{20,12},{24,16},{28,20},{32,24},... | collective-permute-start | bytes 786440 | tf_op jit(solution)/shard_map/ppermute | solution.py:38
  39.6 16.7 %collective-permute-start.18 = (bf16[32,2048]{1,0:T(8,128)(2,1)S(1)}, bf16[32,2048]{1,0:T(8,128)(2,1)S(1)}, u32[]{:S(2)}, u32[]{:S(2)}) collective-permute-start(bf16[32,2048]{1,0:T(8,128)(2,1)S(1)} %slice.132), channel_id=1, source_target_pairs={{0,8},{4,12},{8,16},{12,20},{16,24},{20,28},{24,32},{28,36},{32,40... | collective-permute-start | bytes 393224 | tf_op jit(solution)/shard_map/ppermute | solution.py:38
  44.9 15.2 %collective-permute-start.6 = (bf16[2,6,64,128]{3,2,1,0:T(8,128)(2,1)}, bf16[2,6,64,128]{3,2,1,0:T(8,128)(2,1)S(1)}, u32[]{:S(2)}, u32[]{:S(2)}) collective-permute-start(bf16[2,6,64,128]{3,2,1,0:T(8,128)(2,1)} %get-tuple-element.28), channel_id=1, source_target_pairs={{0,64},{4,68},{8,72},{12,76},{16,80},{20,84},{24,88},{28,92},{32,9... | collective-permute-start | bytes 589832 | tf_op jit(solution)/shard_map/ppermute | solution.py:38
  45.2 17.2 %collective-permute-start.7 = (bf16[2,6,64,128]{3,2,1,0:T(8,128)(2,1)}, bf16[2,6,64,128]{3,2,1,0:T(8,128)(2,1)S(1)}, u32[]{:S(2)}, u32[]{:S(2)}) collective-permute-start(bf16[2,6,64,128]{3,2,1,0:T(8,128)(2,1)} %get-tuple-element.29), channel_id=1, source_target_pairs={{0,128},{4,132},{8,136},{12,140},{16,144},{20,148},{24,152},{28,15... | collective-permute-start | bytes 589832 | tf_op jit(solution)/shard_map/ppermute | solution.py:38
  47.4 15.0 %collective-permute-start.8 = (bf16[2,6,64,128]{3,2,1,0:T(8,128)(2,1)}, bf16[2,6,64,128]{3,2,1,0:T(8,128)(2,1)S(1)}, u32[]{:S(2)}, u32[]{:S(2)}) collective-permute-start(bf16[2,6,64,128]{3,2,1,0:T(8,128)(2,1)} %get-tuple-element.30), channel_id=1, source_target_pairs={{0,192},{4,196},{8,200},{12,204},{16,208},{20,212},{24,216},{28,22... | collective-permute-start | bytes 589832 | tf_op jit(solution)/shard_map/ppermute | solution.py:38
  49.5 7.2 %collective-permute-start.19 = (bf16[32,2048]{1,0:T(8,128)(2,1)S(1)}, bf16[32,2048]{1,0:T(8,128)(2,1)S(1)}, u32[]{:S(2)}, u32[]{:S(2)}) collective-permute-start(bf16[32,2048]{1,0:T(8,128)(2,1)S(1)} %slice.133), channel_id=1, source_target_pairs={{0,56},{4,60},{8,0},{12,4},{16,8},{20,12},{24,16},{28,20},{32,24},... | collective-permute-start | bytes 393224 | tf_op jit(solution)/shard_map/ppermute | solution.py:38
  56.4 7.8 %collective-permute-start.12 = (bf16[2,4,64,128]{3,2,1,0:T(8,128)(2,1)}, bf16[2,4,64,128]{3,2,1,0:T(8,128)(2,1)S(1)}, u32[]{:S(2)}, u32[]{:S(2)}) collective-permute-start(bf16[2,4,64,128]{3,2,1,0:T(8,128)(2,1)} %get-tuple-element.32), channel_id=1, source_target_pairs={{0,64},{4,68},{8,72},{12,76},{16,80},{20,84},{24,88},{28,92},{32,9... | collective-permute-start | bytes 393224 | tf_op jit(solution)/shard_map/ppermute | solution.py:38
  56.7 9.6 %collective-permute-start.13 = (bf16[2,4,64,128]{3,2,1,0:T(8,128)(2,1)}, bf16[2,4,64,128]{3,2,1,0:T(8,128)(2,1)S(1)}, u32[]{:S(2)}, u32[]{:S(2)}) collective-permute-start(bf16[2,4,64,128]{3,2,1,0:T(8,128)(2,1)} %get-tuple-element.33), channel_id=1, source_target_pairs={{0,128},{4,132},{8,136},{12,140},{16,144},{20,148},{24,152},{28,15... | collective-permute-start | bytes 393224 | tf_op jit(solution)/shard_map/ppermute | solution.py:38
  60.1 10.8 %collective-permute-start.14 = (bf16[2,4,64,128]{3,2,1,0:T(8,128)(2,1)}, bf16[2,4,64,128]{3,2,1,0:T(8,128)(2,1)S(1)}, u32[]{:S(2)}, u32[]{:S(2)}) collective-permute-start(bf16[2,4,64,128]{3,2,1,0:T(8,128)(2,1)} %get-tuple-element.34), channel_id=1, source_target_pairs={{0,192},{4,196},{8,200},{12,204},{16,208},{20,212},{24,216},{28,22... | collective-permute-start | bytes 393224 | tf_op jit(solution)/shard_map/ppermute | solution.py:38
  62.4 8.6 %collective-permute-start.20 = (bf16[2,6,64,128]{3,2,1,0:T(8,128)(2,1)}, bf16[2,6,64,128]{3,2,1,0:T(8,128)(2,1)S(1)}, u32[]{:S(2)}, u32[]{:S(2)}) collective-permute-start(bf16[2,6,64,128]{3,2,1,0:T(8,128)(2,1)} %get-tuple-element.36), channel_id=1, source_target_pairs={{0,64},{4,68},{8,72},{12,76},{16,80},{20,84},{24,88},{28,92},{32,9... | collective-permute-start | bytes 589832 | tf_op jit(solution)/shard_map/ppermute | solution.py:38
  62.4 9.1 %collective-permute-start.21 = (bf16[2,6,64,128]{3,2,1,0:T(8,128)(2,1)}, bf16[2,6,64,128]{3,2,1,0:T(8,128)(2,1)S(1)}, u32[]{:S(2)}, u32[]{:S(2)}) collective-permute-start(bf16[2,6,64,128]{3,2,1,0:T(8,128)(2,1)} %get-tuple-element.37), channel_id=1, source_target_pairs={{0,128},{4,132},{8,136},{12,140},{16,144},{20,148},{24,152},{28,15... | collective-permute-start | bytes 589832 | tf_op jit(solution)/shard_map/ppermute | solution.py:38
  64.2 10.6 %collective-permute-start.22 = (bf16[2,6,64,128]{3,2,1,0:T(8,128)(2,1)}, bf16[2,6,64,128]{3,2,1,0:T(8,128)(2,1)S(1)}, u32[]{:S(2)}, u32[]{:S(2)}) collective-permute-start(bf16[2,6,64,128]{3,2,1,0:T(8,128)(2,1)} %get-tuple-element.38), channel_id=1, source_target_pairs={{0,192},{4,196},{8,200},{12,204},{16,208},{20,212},{24,216},{28,22... | collective-permute-start | bytes 589832 | tf_op jit(solution)/shard_map/ppermute | solution.py:38
  66.3 13.4 %collective-permute-start.9 = (bf16[4,6,64,128]{3,2,1,0:T(8,128)(2,1)S(1)}, bf16[4,6,64,128]{3,2,1,0:T(8,128)(2,1)S(1)}, u32[]{:S(2)}, u32[]{:S(2)}) collective-permute-start(bf16[4,6,64,128]{3,2,1,0:T(8,128)(2,1)S(1)} %pad_maximum_fusion), channel_id=1, source_target_pairs={{0,4},{4,0},{8,12},{12,8},{16,20},{20,16},{24,28},{28,24},{32,36},... | collective-permute-start | bytes 1179656 | tf_op jit(solution)/shard_map/ppermute | solution.py:38
  74.8 5.3 %collective-permute-start.23 = (bf16[4,6,64,128]{3,2,1,0:T(8,128)(2,1)S(1)}, bf16[4,6,64,128]{3,2,1,0:T(8,128)(2,1)S(1)}, u32[]{:S(2)}, u32[]{:S(2)}) collective-permute-start(bf16[4,6,64,128]{3,2,1,0:T(8,128)(2,1)S(1)} %pad_maximum_fusion.1), channel_id=1, source_target_pairs={{0,4},{4,0},{8,12},{12,8},{16,20},{20,16},{24,28},{28,24},{32,36},... | collective-permute-start | bytes 1179656 | tf_op jit(solution)/shard_map/ppermute | solution.py:38
  86.1 13.9 %collective-permute-start.24 = (bf16[64,2048]{1,0:T(8,128)(2,1)}, bf16[64,2048]{1,0:T(8,128)(2,1)S(1)}, u32[]{:S(2)}, u32[]{:S(2)}) collective-permute-start(bf16[64,2048]{1,0:T(8,128)(2,1)} %get-tuple-element.40.own_ref), channel_id=1, source_target_pairs={{0,1},{1,2},{2,3},{3,0},{4,5},{5,6},{6,7},{7,4},{8,9},{9,10},{10,1... | collective-permute-start | bytes 786440 | tf_op jit(solution)/shard_map/ppermute | solution.py:495
  87.3 12.7 %collective-permute-start.25 = (bf16[64,2048]{1,0:T(8,128)(2,1)}, bf16[64,2048]{1,0:T(8,128)(2,1)S(1)}, u32[]{:S(2)}, u32[]{:S(2)}) collective-permute-start(bf16[64,2048]{1,0:T(8,128)(2,1)} %get-tuple-element.40.own_ref), channel_id=1, source_target_pairs={{0,3},{1,0},{2,1},{3,2},{4,7},{5,4},{6,5},{7,6},{8,11},{9,8},{10,9... | collective-permute-start | bytes 786440 | tf_op jit(solution)/shard_map/ppermute | solution.py:495
  88.9 12.7 %collective-permute-start.26 = (bf16[64,2048]{1,0:T(8,128)(2,1)}, bf16[64,2048]{1,0:T(8,128)(2,1)S(1)}, u32[]{:S(2)}, u32[]{:S(2)}) collective-permute-start(bf16[64,2048]{1,0:T(8,128)(2,1)} %get-tuple-element.40.own_ref), channel_id=1, source_target_pairs={{0,2},{1,3},{2,0},{3,1},{4,6},{5,7},{6,4},{7,5},{8,10},{9,11},{10,... | collective-permute-start | bytes 786440 | tf_op jit(solution)/shard_map/ppermute | solution.py:495
  90.3 9.7 %all-to-all-start = ((s32[8,1,16]{2,1,0:T(1,128)}), s32[8,1,16]{2,1,0:T(1,128)S(1)}, u32[]{:S(2)}, u32[]{:S(2)}) async-start(s32[8,1,16]{2,1,0:T(1,128)} %get-tuple-element.39), calls=%async_computation | async-start | bytes 8192 | tf_op jit(solution)/shard_map/all_to_all | solution.py:498
  110.6 5.4 %collective-permute-start.28 = (f32[72,128]{1,0:T(8,128)S(1)}, f32[72,128]{1,0:T(8,128)S(1)}, u32[]{:S(2)}, u32[]{:S(2)}) collective-permute-start(f32[72,128]{1,0:T(8,128)S(1)} %add.111._), channel_id=1, source_target_pairs={{0,8},{4,12},{8,0},{12,4},{16,24},{20,28},{24,16},{28,20},{32,40},... | collective-permute-start | bytes 110600 | tf_op jit(solution)/shard_map/ppermute | solution.py:38
  116.0 63.9 %all-to-all-start.1 = ((bf16[64,128,128]{2,1,0:T(8,128)(2,1)}), bf16[64,128,128]{2,1,0:T(8,128)(2,1)S(1)}, u32[]{:S(2)}, u32[]{:S(2)}) async-start(bf16[64,128,128]{2,1,0:T(8,128)(2,1)} %back_remote.1._), calls=%async_computation.1 | async-start | bytes 4194304 | tf_op jit(solution)/shard_map/all_to_all | solution.py:507
  128.3 6.0 %collective-permute-start.30 = (f32[72,128]{1,0:T(8,128)S(1)}, f32[72,128]{1,0:T(8,128)S(1)}, u32[]{:S(2)}, u32[]{:S(2)}) collective-permute-start(f32[72,128]{1,0:T(8,128)S(1)} %add.112), channel_id=1, source_target_pairs={{0,128},{4,132},{8,136},{12,140},{16,144},{20,148},{24,152},{28,15... | collective-permute-start | bytes 110600 | tf_op jit(solution)/shard_map/ppermute | solution.py:38
  130.9 5.9 %collective-permute-start.31 = (f32[72,128]{1,0:T(8,128)S(1)}, f32[72,128]{1,0:T(8,128)S(1)}, u32[]{:S(2)}, u32[]{:S(2)}) collective-permute-start(f32[72,128]{1,0:T(8,128)S(1)} %add.112), channel_id=1, source_target_pairs={{0,192},{4,196},{8,200},{12,204},{16,208},{20,212},{24,216},{28,22... | collective-permute-start | bytes 110600 | tf_op jit(solution)/shard_map/ppermute | solution.py:38
  136.8 35.7 %collective-permute-start.32 = (f32[72,128]{1,0:T(8,128)S(1)}, f32[72,128]{1,0:T(8,128)S(1)}, u32[]{:S(2)}, u32[]{:S(2)}) collective-permute-start(f32[72,128]{1,0:T(8,128)S(1)} %add_add_fusion.1), channel_id=1, source_target_pairs={{0,16},{4,20},{8,24},{12,28},{16,0},{20,4},{24,8},{28,12},{32,48},... | collective-permute-start | bytes 110600 | tf_op jit(solution)/shard_map/ppermute | solution.py:38
  138.6 38.6 %collective-permute-start.33 = (f32[72,128]{1,0:T(8,128)S(1)}, f32[72,128]{1,0:T(8,128)S(1)}, u32[]{:S(2)}, u32[]{:S(2)}) collective-permute-start(f32[72,128]{1,0:T(8,128)S(1)} %add_add_fusion.1), channel_id=1, source_target_pairs={{0,32},{4,36},{8,40},{12,44},{16,48},{20,52},{24,56},{28,60},{32,0... | collective-permute-start | bytes 110600 | tf_op jit(solution)/shard_map/ppermute | solution.py:38
  141.3 35.9 %collective-permute-start.34 = (f32[72,128]{1,0:T(8,128)S(1)}, f32[72,128]{1,0:T(8,128)S(1)}, u32[]{:S(2)}, u32[]{:S(2)}) collective-permute-start(f32[72,128]{1,0:T(8,128)S(1)} %add_add_fusion.1), channel_id=1, source_target_pairs={{0,48},{4,52},{8,56},{12,60},{16,32},{20,36},{24,40},{28,44},{32,1... | collective-permute-start | bytes 110600 | tf_op jit(solution)/shard_map/ppermute | solution.py:38
  (38 other events, 376.5 us)
Sparse Core Ops, SparseCore 0:
  16.3 25.5 all-gather.1

commit v9 on v8

--- a/solution.py
+++ b/solution.py
@@ -76,9 +76,11 @@
 STEP = 4
 
 
-def agg_local_kernel(cols_ref, feats_ref, tiles_ref, out_ref):
+def agg_local_kernel(cols_ref, asked_ref, feats_ref, tiles_ref, out_ref, own_ref, other_ref):
     i = pl.program_id(0)
     count, block = tiles_ref.shape[1], tiles_ref.shape[2]
+    own_ref[...] = asked_ref[0]
+    other_ref[...] = asked_ref[1]
     for rr in range(STEP):
         acc = None
         for t in range(0, count, 2):
@@ -92,41 +94,55 @@
         out_ref[:, rr * block : (rr + 1) * block] = acc
 
 
-def agg_local(cols, feats, tiles):
+def agg_local(cols, asked, feats, tiles):
     row_blocks, _, block, _ = tiles.shape
     width = feats.shape[0]
     return pl.pallas_call(
         agg_local_kernel,
         grid=(row_blocks // STEP,),
-        out_shape=jax.ShapeDtypeStruct((width, row_blocks * block), F32),
+        out_shape=(
+            jax.ShapeDtypeStruct((width, row_blocks * block), F32),
+            jax.ShapeDtypeStruct(asked.shape[1:], asked.dtype),
+            jax.ShapeDtypeStruct(asked.shape[1:], asked.dtype),
+        ),
         in_specs=[
             SMEM,
+            pl.BlockSpec(asked.shape, lambda i: (0, 0, 0)),
             pl.BlockSpec(feats.shape, lambda i: (0, 0)),
             pl.BlockSpec((STEP, TL, block, block), lambda i: (i, 0, 0, 0)),
         ],
-        out_specs=pl.BlockSpec((width, STEP * block), lambda i: (0, i)),
+        out_specs=(
+            pl.BlockSpec((width, STEP * block), lambda i: (0, i)),
+            pl.BlockSpec(asked.shape[1:], lambda i: (0, 0)),
+            pl.BlockSpec(asked.shape[1:], lambda i: (0, 0)),
+        ),
         name="agg_local",
         cost_estimate=pl.CostEstimate(
             flops=2 * width * row_blocks * TL * block * block, bytes_accessed=3 << 20, transcendentals=0
         ),
-    )(cols, feats, tiles)
+    )(cols, asked, feats, tiles)
 
 
 def agg_remote_kernel(slots_ref, held_ref, tiles_ref, local_ref, *refs):
-    parts, out_ref, held_out_ref, recv_ref = refs[:-3], refs[-3], refs[-2], refs[-1]
+    parts, out_ref, held_out_ref, recv_ref, sems = refs[:-4], refs[-4], refs[-3], refs[-2], refs[-1]
     i = pl.program_id(0)
     count, block = tiles_ref.shape[1], tiles_ref.shape[2]
 
     @pl.when(i == 0)
     def _():
+        copies = []
+        for g, (first, last) in enumerate(GROUPS):
+            size = (last - first) * CAP
+            own, other = parts[g * (NY + 1) : g * (NY + 1) + NY], parts[g * (NY + 1) + NY]
+            sources = [ref.at[0] for ref in own] + [other.at[ys] for ys in range(NY)]
+            for k, source in enumerate(sources):
+                target = recv_ref.at[pl.ds(k * PER + first * CAP, size)]
+                copies.append(pltpu.make_async_copy(source, target, sems.at[len(copies)]))
+        for copy in copies:
+            copy.start()
         held_out_ref[...] = held_ref[...]
-        n = 0
-        for first, last in GROUPS:
-            size = (last - first) * CAP
-            for ys in range(NY):
-                recv_ref[pl.ds(ys * PER + first * CAP, size)] = parts[n + ys][0]
-                recv_ref[pl.ds((NY + ys) * PER + first * CAP, size)] = parts[n + NY][ys]
-            n += NY + 1
+        for copy in copies:
+            copy.wait()
 
     for rr in range(STEP):
         acc = local_ref[:, rr * block : (rr + 1) * block]
@@ -142,10 +158,6 @@
     row_blocks, per_block, block, _ = tiles.shape
     rem = per_block - TL
     width = local.shape[0]
-    specs = []
-    for n, part in enumerate(parts):
-        lead = 1 if n % (NY + 1) < NY else NY
-        specs.append(pl.BlockSpec((lead,) + part.shape[1:], lambda i: (0, 0, 0, 0)))
     return pl.pallas_call(
         agg_remote_kernel,
         grid=(row_blocks // STEP,),
@@ -156,13 +168,17 @@
             pl.BlockSpec((STEP, rem, block, block), lambda i: (i, 1, 0, 0)),
             pl.BlockSpec((width, STEP * block), lambda i: (0, i)),
         ]
-        + specs,
+        + [ANY] * len(parts),
         out_specs=(
             pl.BlockSpec((width, STEP * block), lambda i: (0, i)),
             pl.BlockSpec(held.shape, lambda i: (0, 0, 0)),
         ),
-        scratch_shapes=[pltpu.VMEM((NY * NC * PER, width, block), BF)],
+        scratch_shapes=[
+            pltpu.VMEM((NY * NC * PER, width, block), BF),
+            pltpu.SemaphoreType.DMA((len(GROUPS) * NY * NC,)),
+        ],
         name="agg_remote",
+        compiler_params=pltpu.CompilerParams(vmem_limit_bytes=49 << 20),
         cost_estimate=pl.CostEstimate(
             flops=2 * width * row_blocks * rem * block * block, bytes_accessed=5 << 20, transcendentals=0
         ),
@@ -415,6 +431,20 @@
     )(place, held, recv, local)
 
 
+def join_kernel(a_ref, b_ref, c_ref, d_ref, _, out_ref):
+    out_ref[...] = (a_ref[...] + b_ref[...]) + (c_ref[...] + d_ref[...])
+
+
+def join(terms, after):
+    return pl.pallas_call(
+        join_kernel,
+        out_shape=jax.ShapeDtypeStruct(terms[0].shape, terms[0].dtype),
+        in_specs=[VMEM] * 4 + [ANY],
+        out_specs=VMEM,
+        name="join",
+    )(*terms, after)
+
+
 def split_bf16(x, terms):
     parts = []
     for _ in range(terms):
@@ -461,7 +491,8 @@
         return jnp.max(jnp.where(hit, inside[None, :], -1), axis=1)
 
     asked = table(near).reshape(NC, NY, PER)
-    asked = jnp.stack([asked[0], shift(asked[1], dc=1)], axis=1)
+    agg, asked_own, asked_other = agg_local(local_cols, asked, feats, tiles)
+    asked = jnp.stack([asked_own, shift(asked_other, dc=1)], axis=1)
     wanted = [asked[0]] + [shift(asked[ys], dy=-ys) for ys in range(1, NY)]
     wanted = jnp.stack(wanted).reshape(-1)
 
@@ -473,10 +504,9 @@
     far_down = shift(down[-1][width // 2 :], dz=-1)
     groups = ((feats, down[1], up[1]), (down[2], up[2]), (down[3], up[3], far_up, far_down))
     after = []
-    agg = agg_local(local_cols, feats, tiles)
     for group, sources in zip(GROUPS, groups):
         packs = pack(group, wanted, sources, block, after)
-        after = [packs[0], agg]
+        after = [packs[0]]
         moved = [packs[0]] + [shift(packs[ys], dy=ys) for ys in range(1, NY)]
         parts += moved
         parts.append(shift(jnp.concatenate([m[1:] for m in moved]), dc=1))
@@ -511,14 +541,14 @@
     pairs = [part] + [shift(part, flip_y=k) for k in (1, 2, 3)]
     part = (pairs[0] + pairs[1]) + (pairs[2] + pairs[3])
     pairs = [part] + [shift(part, flip_z=k) for k in (2, 4, 6)]
-    part = (pairs[0] + pairs[1]) + (pairs[2] + pairs[3])
+    grad_input = finish(jnp.stack([y, c]).astype(jnp.int32), held, recv, own)
+    part = join(pairs, grad_input)
     other = shift(part, dc=1)
     total = jnp.where(c == 0, jnp.concatenate([part, other]), jnp.concatenate([other, part]))
     total = total / math.sqrt(nodes_dev * peers)
     grad_w = jnp.concatenate([total[k * width : (k + 1) * width] for k in range(hid_all // 128)], axis=1)
     grad_b = total[width * (hid_all // 128), :width]
 
-    grad_input = finish(jnp.stack([y, c]).astype(jnp.int32), held, recv, own)
     return hidden_out, grad_input, grad_w, grad_b
 
 

time: 192 us -> 198 us (1.031)
  waiting for transfers between devices: 64.7 us -> 59.8 us
  Pallas kernels: 32 us -> 35.5 us
  other arithmetic: 6.88 us -> 9.89 us
  starting transfers between devices: 66 us -> 69 us
    ppermute x33, waiting for transfers between devices: 57.3 us -> 20.6 us  [shift(): return lax.ppermute(x, 'rows', pairs)]
    all_to_all x1, waiting for transfers between devices: 0.01 us -> 32 us  [local(): recv = lax.all_to_all(send, 'rows', split_axis=0, concat_axis=0, tiled=True)]
    pallas_call x1, Pallas kernels: 4.89 us -> 6.95 us  [agg_remote(): pl.pallas_call(agg_remote_kernel, grid=(row_blocks // STEP,), out_shape=(...]
    pallas_call x1 -> x2, Pallas kernels: 4.12 us -> 5.58 us  [the longest x1 4.15 us: agg_local(): pl.pallas_call(agg_local_kernel, grid=(row_blocks // STEP,), out_shape=(j...]
  transfers between devices with their start and end apart: 39 -> 39, of which waited for: 14 -> 12; matrix products, arithmetic and copies ran while one was open for 5% -> 6% of each run, Pallas kernels for 13% -> 15%
where the time goes in v9:
time: 198 us; the launch traced here: 197 us
  starting transfers between devices  69 us (35%)
  waiting for transfers between devices  59.8 us (30%)
  Pallas kernels  35.5 us (18%)
  between operations  14.5 us (7%)
  other arithmetic  9.89 us (5%)
  local copies, waits for them, and re-layouts  8.31 us (4%)
    ppermute x33, starting transfers between devices, shift(): return lax.ppermute(x, 'rows', pairs)  53.5 us
    all_to_all x1, waiting for transfers between devices, local(): recv = lax.all_to_all(send, 'rows', split_axis=0, concat_axis=0, tiled=True)  32 us
    ppermute x33, waiting for transfers between devices, shift(): return lax.ppermute(x, 'rows', pairs)  20.6 us
    all_to_all x1, starting transfers between devices, local(): recv = lax.all_to_all(send, 'rows', split_axis=0, concat_axis=0, tiled=True)  7.36 us
    pallas_call x1, Pallas kernels, agg_remote(): pl.pallas_call(agg_remote_kernel, grid=(row_blocks // STEP,), out_shape=(...  6.95 us
    pallas_call x3, Pallas kernels, pack(): pl.pallas_call(functools.partial(pack_kernel, first, count, len(sources)...  6.43 us
    all_to_all x1, waiting for transfers between devices, local(): lax.all_to_all(held, 'rows', 0, 0, tiled=True, axis_index_groups=along_z)  5.86 us
    pallas_call x1, Pallas kernels, mid(): pl.pallas_call(mid_kernel, grid=(nodes // chunk,), out_shape=(jax.ShapeDt...  4.99 us
  transfers between devices with their start and end apart: 39, of which 12 were waited for; matrix products, arithmetic and copies ran while one was open for 6% of the time, Pallas kernels for 15%

profile of v9, /device:TPU:1, one launch (start us, length us, event | category | flops | bytes accessed | tf_op | source)
XLA Modules:
  0.0 197.0 jit_solution(4901816045419814659)
XLA Ops:
  7.2 6.5 %collective-permute-start.4 = (bf16[64,2048]{1,0:T(8,128)(2,1)}, bf16[64,2048]{1,0:T(8,128)(2,1)S(1)}, u32[]{:S(2)}, u32[]{:S(2)}) collective-permute-start(bf16[64,2048]{1,0:T(8,128)(2,1)} %refs_1_.1), channel_id=1, source_target_pairs={{0,56},{4,60},{8,0},{12,4},{16,8},{20,12},{24,16},{28,20},{32,24},... | collective-permute-start | bytes 786440 | tf_op jit(solution)/shard_map/ppermute | solution.py:38
  14.5 1.7 fusion.1
  17.1 4.8 %collective-permute-done.5.refs_3_ = bf16[64,2048]{1,0:T(8,128)(2,1)S(1)} collective-permute-done((bf16[64,2048]{1,0:T(8,128)(2,1)}, bf16[64,2048]{1,0:T(8,128)(2,1)S(1)}, u32[]{:S(2)}, u32[]{:S(2)}) %collective-permute-start.5) | collective-permute-done | bytes 262176 | tf_op jit(solution)/shard_map/ppermute | solution.py:38
  22.2 2.7 %collective-permute-start.10 = (bf16[64,2048]{1,0:T(8,128)(2,1)S(1)}, bf16[64,2048]{1,0:T(8,128)(2,1)S(1)}, u32[]{:S(2)}, u32[]{:S(2)}) collective-permute-start(bf16[64,2048]{1,0:T(8,128)(2,1)S(1)} %collective-permute-done.4.refs_2_), channel_id=1, source_target_pairs={{0,56},{4,60},{8,0},{12,4},{16,8},{20,12},{24,16},{28,20},{32,24},... | collective-permute-start | bytes 786440 | tf_op jit(solution)/shard_map/ppermute | solution.py:38
  25.0 4.1 %collective-permute-done.11.refs_2_ = bf16[64,2048]{1,0:T(8,128)(2,1)S(1)} collective-permute-done((bf16[64,2048]{1,0:T(8,128)(2,1)S(1)}, bf16[64,2048]{1,0:T(8,128)(2,1)S(1)}, u32[]{:S(2)}, u32[]{:S(2)}) %collective-permute-start.11) | collective-permute-done | bytes 262176 | tf_op jit(solution)/shard_map/ppermute | solution.py:38
  31.1 4.2 %agg_local.1 = (f32[64,2048]{1,0:T(8,128)}, s32[4,16]{1,0:T(4,128)}, s32[4,16]{1,0:T(4,128)}) custom-call(s32[64]{0:T(128)} %reshape.196.cols_ref, s32[2,4,16]{2,1,0:T(4,128)} %reshape.197.asked_ref, bf16[64,2048]{1,0:T(8,128)(2,1)} %refs_1_.1, bf16[16,8,128,128]{3,2,1,0:T(8,128)(2,1)} %bitcast.27), custom_call_target="tpu_custom_call" | custom-call | flops 134217728 | bytes 3145728 | tf_op jit(solution)/shard_map/agg_local/pallas_call | solution.py:100
  35.3 2.9 %collective-permute-start = (s32[4,16]{1,0:T(4,128)}, s32[4,16]{1,0:T(4,128)S(1)}, u32[]{:S(2)}, u32[]{:S(2)}) collective-permute-start(s32[4,16]{1,0:T(4,128)} %get-tuple-element.31), channel_id=1, source_target_pairs={{0,4},{4,0},{8,12},{12,8},{16,20},{20,16},{24,28},{28,24},{32,36},... | collective-permute-start | bytes 776 | tf_op jit(solution)/shard_map/ppermute | solution.py:38
  38.2 2.9 %collective-permute-start.16 = (bf16[64,2048]{1,0:T(8,128)(2,1)S(1)}, bf16[64,2048]{1,0:T(8,128)(2,1)S(1)}, u32[]{:S(2)}, u32[]{:S(2)}) collective-permute-start(bf16[64,2048]{1,0:T(8,128)(2,1)S(1)} %collective-permute-done.10.refs_1_), channel_id=1, source_target_pairs={{0,56},{4,60},{8,0},{12,4},{16,8},{20,12},{24,16},{28,20},{32,24},... | collective-permute-start | bytes 786440 | tf_op jit(solution)/shard_map/ppermute | solution.py:38
  41.9 3.0 %collective-permute-start.2 = (s32[2,16]{1,0:T(2,128)S(1)}, s32[2,16]{1,0:T(2,128)S(1)}, u32[]{:S(2)}, u32[]{:S(2)}) collective-permute-start(s32[2,16]{1,0:T(2,128)S(1)} %bitcast.38), channel_id=1, source_target_pairs={{0,128},{4,132},{8,136},{12,140},{16,144},{20,148},{24,152},{28,15... | collective-permute-start | bytes 392 | tf_op jit(solution)/shard_map/ppermute | solution.py:38
  45.3 2.3 %collective-permute-start.1 = (s32[2,16]{1,0:T(2,128)S(1)}, s32[2,16]{1,0:T(2,128)S(1)}, u32[]{:S(2)}, u32[]{:S(2)}) collective-permute-start(s32[2,16]{1,0:T(2,128)S(1)} %bitcast.34), channel_id=1, source_target_pairs={{0,192},{4,196},{8,200},{12,204},{16,208},{20,212},{24,216},{28,22... | collective-permute-start | bytes 392 | tf_op jit(solution)/shard_map/ppermute | solution.py:38
  49.2 2.2 %pack.3 = (bf16[2,6,64,128]{3,2,1,0:T(8,128)(2,1)}, bf16[2,6,64,128]{3,2,1,0:T(8,128)(2,1)}, bf16[2,6,64,128]{3,2,1,0:T(8,128)(2,1)}, bf16[2,6,64,128]{3,2,1,0:T(8,128)(2,1)}) custom-call(s32[128]{0:T(128)} %reshape.200.refs_0_, bf16[64,2048]{1,0:T(8,128)(2,1)} %refs_1_.1, bf16[64,2048]{1,0:T(8,128)(2,1)} %copy-done.16, bf16[64,2048]{1,0:T(8,128)(2,1)} %copy-done.17), custom_call_target="tpu_custom_call" | custom-call | bytes 3145728 | tf_op jit(solution)/shard_map/pack/pallas_call | solution.py:62
  51.4 3.9 %collective-permute-start.7 = (bf16[2,6,64,128]{3,2,1,0:T(8,128)(2,1)}, bf16[2,6,64,128]{3,2,1,0:T(8,128)(2,1)S(1)}, u32[]{:S(2)}, u32[]{:S(2)}) collective-permute-start(bf16[2,6,64,128]{3,2,1,0:T(8,128)(2,1)} %get-tuple-element.35), channel_id=1, source_target_pairs={{0,128},{4,132},{8,136},{12,140},{16,144},{20,148},{24,152},{28,15... | collective-permute-start | bytes 589832 | tf_op jit(solution)/shard_map/ppermute | solution.py:38
  56.6 2.0 pack.4
  58.6 1.7 collective-permute-start.12
  61.0 2.2 %pack.5 = (bf16[2,6,64,128]{3,2,1,0:T(8,128)(2,1)}, bf16[2,6,64,128]{3,2,1,0:T(8,128)(2,1)}, bf16[2,6,64,128]{3,2,1,0:T(8,128)(2,1)}, bf16[2,6,64,128]{3,2,1,0:T(8,128)(2,1)}) custom-call(s32[128]{0:T(128)} %reshape.200.refs_0_, bf16[64,2048]{1,0:T(8,128)(2,1)} %copy-done.8, bf16[64,2048]{1,0:T(8,128)(2,1)} %copy-done.7, bf16[32,2048]{1,0:T(8,128)(2,1)} %copy-done.19, ...), custom_call_target="tpu_custom_call" | custom-call | bytes 3145728 | tf_op jit(solution)/shard_map/pack/pallas_call | solution.py:62
  63.2 2.4 %collective-permute-start.14 = (bf16[2,4,64,128]{3,2,1,0:T(8,128)(2,1)}, bf16[2,4,64,128]{3,2,1,0:T(8,128)(2,1)S(1)}, u32[]{:S(2)}, u32[]{:S(2)}) collective-permute-start(bf16[2,4,64,128]{3,2,1,0:T(8,128)(2,1)} %get-tuple-element.40), channel_id=1, source_target_pairs={{0,192},{4,196},{8,200},{12,204},{16,208},{20,212},{24,216},{28,22... | collective-permute-start | bytes 393224 | tf_op jit(solution)/shard_map/ppermute | solution.py:38
  70.2 5.0 %collective-permute-start.9 = (bf16[4,6,64,128]{3,2,1,0:T(8,128)(2,1)}, bf16[4,6,64,128]{3,2,1,0:T(8,128)(2,1)S(1)}, u32[]{:S(2)}, u32[]{:S(2)}) collective-permute-start(bf16[4,6,64,128]{3,2,1,0:T(8,128)(2,1)} %pad_maximum_fusion), channel_id=1, source_target_pairs={{0,4},{4,0},{8,12},{12,8},{16,20},{20,16},{24,28},{28,24},{32,36},... | collective-permute-start | bytes 1179656 | tf_op jit(solution)/shard_map/ppermute | solution.py:38
  77.5 3.7 %collective-permute-start.23 = (bf16[4,6,64,128]{3,2,1,0:T(8,128)(2,1)}, bf16[4,6,64,128]{3,2,1,0:T(8,128)(2,1)S(1)}, u32[]{:S(2)}, u32[]{:S(2)}) collective-permute-start(bf16[4,6,64,128]{3,2,1,0:T(8,128)(2,1)} %pad_maximum_fusion.1), channel_id=1, source_target_pairs={{0,4},{4,0},{8,12},{12,8},{16,20},{20,16},{24,28},{28,24},{32,36},... | collective-permute-start | bytes 1179656 | tf_op jit(solution)/shard_map/ppermute | solution.py:38
  83.8 6.9 %agg_remote.1 = (bf16[64,2048]{1,0:T(8,128)(2,1)}, s32[8,1,16]{2,1,0:T(1,128)}) custom-call(s32[64]{0:T(128)S(1)} %get-tuple-element.65.slots_ref, s32[8,1,16]{2,1,0:T(1,128)S(1)} %copy.42.held_ref, bf16[16,8,128,128]{3,2,1,0:T(8,128)(2,1)} %bitcast.28, f32[64,2048]{1,0:T(8,128)S(1)} %copy-done.3, bf16[2,6,64,128]{3,2,1,0:T(8,128)(2,1)S(1)} %copy-done.1, ...), custom_call_target="tpu_custom_call" | custom-call | flops 134217728 | bytes 5242880 | tf_op jit(solution)/shard_map/agg_remote/pallas_call | solution.py:161
  95.1 3.8 %all-to-all-start = ((s32[8,1,16]{2,1,0:T(1,128)}), s32[8,1,16]{2,1,0:T(1,128)S(1)}, u32[]{:S(2)}, u32[]{:S(2)}) async-start(s32[8,1,16]{2,1,0:T(1,128)} %get-tuple-element.45), calls=%async_computation | async-start | bytes 8192 | tf_op jit(solution)/shard_map/all_to_all | solution.py:528
  99.5 5.9 %all-to-all-done._.held_ref = s32[8,1,16]{2,1,0:T(1,128)S(1)} async-done(((s32[8,1,16]{2,1,0:T(1,128)}), s32[8,1,16]{2,1,0:T(1,128)S(1)}, u32[]{:S(2)}, u32[]{:S(2)}) %all-to-all-start) | async-done | bytes 544 | tf_op jit(solution)/shard_map/all_to_all | solution.py:528
  107.4 5.0 %mid.1 = (bf16[64,2048]{1,0:T(8,128)(2,1)}, bf16[64,2048]{1,0:T(8,128)(2,1)}, f32[72,128]{1,0:T(8,128)}, f32[72,128]{1,0:T(8,128)}) custom-call(s32[2]{0:T(128)} %pad_add_fusion.2.me_ref, s32[8,1,16]{2,1,0:T(1,128)} %copy-done.5, bf16[64,2048]{1,0:T(8,128)(2,1)} %get-tuple-element.46.own_ref, bf16[64,2048]{1,0:T(8,128)(2,1)} %copy-done.11, ...), custom_call_target="tpu_custom_call" | custom-call | flops 402653184 | bytes 3145728 | tf_op jit(solution)/shard_map/mid/pallas_call | solution.py:260
  116.3 4.5 %back_remote.1._ = bf16[64,128,128]{2,1,0:T(8,128)(2,1)} custom-call(s32[64]{0:T(128)} %get-tuple-element.64.slots_ref, bf16[64,2048]{1,0:T(8,128)(2,1)} %get-tuple-element.48.g_ref, bf16[16,8,128,128]{3,2,1,0:T(8,128)(2,1)} %bitcast.29, f32[72,128]{1,0:T(8,128)} %copy-done.9), custom_call_target="tpu_custom_call" | custom-call | flops 134217728 | bytes 5242880 | tf_op jit(solution)/shard_map/back_remote/pallas_call | solution.py:328
  120.8 7.4 %all-to-all-start.1 = ((bf16[64,128,128]{2,1,0:T(8,128)(2,1)}), bf16[64,128,128]{2,1,0:T(8,128)(2,1)S(1)}, u32[]{:S(2)}, u32[]{:S(2)}) async-start(bf16[64,128,128]{2,1,0:T(8,128)(2,1)} %back_remote.1._), calls=%async_computation.1 | async-start | bytes 4194304 | tf_op jit(solution)/shard_map/all_to_all | solution.py:537
  128.2 3.9 %back_local.1.local_ref = f32[64,2048]{1,0:T(8,128)} custom-call(s32[64]{0:T(128)} %reshape.196.cols_ref, bf16[64,2048]{1,0:T(8,128)(2,1)} %get-tuple-element.48.g_ref, bf16[16,8,128,128]{3,2,1,0:T(8,128)(2,1)} %bitcast.30, bf16[64,128,128]{2,1,0:T(8,128)(2,1)} %back_remote.1._), custom_call_target="tpu_custom_call" | custom-call | flops 134217728 | bytes 3145728 | tf_op jit(solution)/shard_map/back_local/pallas_call | solution.py:367
  133.6 2.6 %collective-permute-start.30 = (f32[72,128]{1,0:T(8,128)S(1)}, f32[72,128]{1,0:T(8,128)S(1)}, u32[]{:S(2)}, u32[]{:S(2)}) collective-permute-start(f32[72,128]{1,0:T(8,128)S(1)} %add.103), channel_id=1, source_target_pairs={{0,128},{4,132},{8,136},{12,140},{16,144},{20,148},{24,152},{28,15... | collective-permute-start | bytes 110600 | tf_op jit(solution)/shard_map/ppermute | solution.py:38
  136.2 3.4 %collective-permute-done.30 = f32[72,128]{1,0:T(8,128)S(1)} collective-permute-done((f32[72,128]{1,0:T(8,128)S(1)}, f32[72,128]{1,0:T(8,128)S(1)}, u32[]{:S(2)}, u32[]{:S(2)}) %collective-permute-start.30) | collective-permute-done | bytes 36896 | tf_op jit(solution)/shard_map/ppermute | solution.py:38
  139.6 2.4 %collective-permute-done.31 = f32[72,128]{1,0:T(8,128)S(1)} collective-permute-done((f32[72,128]{1,0:T(8,128)S(1)}, f32[72,128]{1,0:T(8,128)S(1)}, u32[]{:S(2)}, u32[]{:S(2)}) %collective-permute-start.31) | collective-permute-done | bytes 36896 | tf_op jit(solution)/shard_map/ppermute | solution.py:38
  142.1 1.9 collective-permute-start.32
  143.9 2.7 %collective-permute-start.33 = (f32[72,128]{1,0:T(8,128)S(1)}, f32[72,128]{1,0:T(8,128)S(1)}, u32[]{:S(2)}, u32[]{:S(2)}) collective-permute-start(f32[72,128]{1,0:T(8,128)S(1)} %add_add_fusion.a_ref), channel_id=1, source_target_pairs={{0,32},{4,36},{8,40},{12,44},{16,48},{20,52},{24,56},{28,60},{32,0... | collective-permute-start | bytes 110600 | tf_op jit(solution)/shard_map/ppermute | solution.py:38
  147.9 32.0 %all-to-all-done.1.recv_ref = bf16[64,128,128]{2,1,0:T(8,128)(2,1)S(1)} async-done(((bf16[64,128,128]{2,1,0:T(8,128)(2,1)}), bf16[64,128,128]{2,1,0:T(8,128)(2,1)S(1)}, u32[]{:S(2)}, u32[]{:S(2)}) %all-to-all-start.1) | async-done | bytes 2097184 | tf_op jit(solution)/shard_map/all_to_all | solution.py:537
  180.9 3.1 %finish.1._ = f32[64,2048]{1,0:T(8,128)} custom-call(s32[2]{0:T(128)S(1)} %pad_add_fusion.3.place_ref, s32[8,1,16]{2,1,0:T(1,128)S(1)} %copy-done.6, bf16[64,128,128]{2,1,0:T(8,128)(2,1)S(1)} %all-to-all-done.1.recv_ref, f32[64,2048]{1,0:T(8,128)S(1)} %copy-done), custom_call_target="tpu_custom_call" | custom-call | flops 1048576 | bytes 4194304 | tf_op jit(solution)/shard_map/finish/pallas_call | solution.py:418
  (155 shorter events, 38.8 us)
Async XLA Ops:
  7.2 99.5 %all-gather.2.cloned.1.call-start = ((), (), s32[]{:S(2)}) async-start(), calls=%async_computation.2 | async-start | bytes 1556480 | tf_op jit(solution)/shard_map/all_gather | solution.py:516
  7.2 15.0 %collective-permute-start.4 = (bf16[64,2048]{1,0:T(8,128)(2,1)}, bf16[64,2048]{1,0:T(8,128)(2,1)S(1)}, u32[]{:S(2)}, u32[]{:S(2)}) collective-permute-start(bf16[64,2048]{1,0:T(8,128)(2,1)} %refs_1_.1), channel_id=1, source_target_pairs={{0,56},{4,60},{8,0},{12,4},{16,8},{20,12},{24,16},{28,20},{32,24},... | collective-permute-start | bytes 786440 | tf_op jit(solution)/shard_map/ppermute | solution.py:38
  13.7 8.3 %collective-permute-start.5 = (bf16[64,2048]{1,0:T(8,128)(2,1)}, bf16[64,2048]{1,0:T(8,128)(2,1)S(1)}, u32[]{:S(2)}, u32[]{:S(2)}) collective-permute-start(bf16[64,2048]{1,0:T(8,128)(2,1)} %refs_1_.1), channel_id=1, source_target_pairs={{0,8},{4,12},{8,16},{12,20},{16,24},{20,28},{24,32},{28,36},{32,40... | collective-permute-start | bytes 786440 | tf_op jit(solution)/shard_map/ppermute | solution.py:38
  22.0 7.1 %collective-permute-start.11 = (bf16[64,2048]{1,0:T(8,128)(2,1)S(1)}, bf16[64,2048]{1,0:T(8,128)(2,1)S(1)}, u32[]{:S(2)}, u32[]{:S(2)}) collective-permute-start(bf16[64,2048]{1,0:T(8,128)(2,1)S(1)} %collective-permute-done.5.refs_3_), channel_id=1, source_target_pairs={{0,8},{4,12},{8,16},{12,20},{16,24},{20,28},{24,32},{28,36},{32,40... | collective-permute-start | bytes 786440 | tf_op jit(solution)/shard_map/ppermute | solution.py:38
  22.2 15.9 %collective-permute-start.10 = (bf16[64,2048]{1,0:T(8,128)(2,1)S(1)}, bf16[64,2048]{1,0:T(8,128)(2,1)S(1)}, u32[]{:S(2)}, u32[]{:S(2)}) collective-permute-start(bf16[64,2048]{1,0:T(8,128)(2,1)S(1)} %collective-permute-done.4.refs_2_), channel_id=1, source_target_pairs={{0,56},{4,60},{8,0},{12,4},{16,8},{20,12},{24,16},{28,20},{32,24},... | collective-permute-start | bytes 786440 | tf_op jit(solution)/shard_map/ppermute | solution.py:38
  29.1 18.5 %collective-permute-start.17 = (bf16[64,2048]{1,0:T(8,128)(2,1)S(1)}, bf16[64,2048]{1,0:T(8,128)(2,1)S(1)}, u32[]{:S(2)}, u32[]{:S(2)}) collective-permute-start(bf16[64,2048]{1,0:T(8,128)(2,1)S(1)} %collective-permute-done.11.refs_2_), channel_id=1, source_target_pairs={{0,8},{4,12},{8,16},{12,20},{16,24},{20,28},{24,32},{28,36},{32,40... | collective-permute-start | bytes 786440 | tf_op jit(solution)/shard_map/ppermute | solution.py:38
  35.3 5.8 %collective-permute-start = (s32[4,16]{1,0:T(4,128)}, s32[4,16]{1,0:T(4,128)S(1)}, u32[]{:S(2)}, u32[]{:S(2)}) collective-permute-start(s32[4,16]{1,0:T(4,128)} %get-tuple-element.31), channel_id=1, source_target_pairs={{0,4},{4,0},{8,12},{12,8},{16,20},{20,16},{24,28},{28,24},{32,36},... | collective-permute-start | bytes 776 | tf_op jit(solution)/shard_map/ppermute | solution.py:38
  38.2 17.1 %collective-permute-start.16 = (bf16[64,2048]{1,0:T(8,128)(2,1)S(1)}, bf16[64,2048]{1,0:T(8,128)(2,1)S(1)}, u32[]{:S(2)}, u32[]{:S(2)}) collective-permute-start(bf16[64,2048]{1,0:T(8,128)(2,1)S(1)} %collective-permute-done.10.refs_1_), channel_id=1, source_target_pairs={{0,56},{4,60},{8,0},{12,4},{16,8},{20,12},{24,16},{28,20},{32,24},... | collective-permute-start | bytes 786440 | tf_op jit(solution)/shard_map/ppermute | solution.py:38
  41.9 5.8 %collective-permute-start.2 = (s32[2,16]{1,0:T(2,128)S(1)}, s32[2,16]{1,0:T(2,128)S(1)}, u32[]{:S(2)}, u32[]{:S(2)}) collective-permute-start(s32[2,16]{1,0:T(2,128)S(1)} %bitcast.38), channel_id=1, source_target_pairs={{0,128},{4,132},{8,136},{12,140},{16,144},{20,148},{24,152},{28,15... | collective-permute-start | bytes 392 | tf_op jit(solution)/shard_map/ppermute | solution.py:38
  47.6 11.0 %collective-permute-start.18 = (bf16[32,2048]{1,0:T(8,128)(2,1)S(1)}, bf16[32,2048]{1,0:T(8,128)(2,1)S(1)}, u32[]{:S(2)}, u32[]{:S(2)}) collective-permute-start(bf16[32,2048]{1,0:T(8,128)(2,1)S(1)} %slice.106), channel_id=1, source_target_pairs={{0,8},{4,12},{8,16},{12,20},{16,24},{20,28},{24,32},{28,36},{32,40... | collective-permute-start | bytes 393224 | tf_op jit(solution)/shard_map/ppermute | solution.py:38
  51.4 11.8 %collective-permute-start.6 = (bf16[2,6,64,128]{3,2,1,0:T(8,128)(2,1)}, bf16[2,6,64,128]{3,2,1,0:T(8,128)(2,1)S(1)}, u32[]{:S(2)}, u32[]{:S(2)}) collective-permute-start(bf16[2,6,64,128]{3,2,1,0:T(8,128)(2,1)} %get-tuple-element.34), channel_id=1, source_target_pairs={{0,64},{4,68},{8,72},{12,76},{16,80},{20,84},{24,88},{28,92},{32,9... | collective-permute-start | bytes 589832 | tf_op jit(solution)/shard_map/ppermute | solution.py:38
  51.4 14.3 %collective-permute-start.7 = (bf16[2,6,64,128]{3,2,1,0:T(8,128)(2,1)}, bf16[2,6,64,128]{3,2,1,0:T(8,128)(2,1)S(1)}, u32[]{:S(2)}, u32[]{:S(2)}) collective-permute-start(bf16[2,6,64,128]{3,2,1,0:T(8,128)(2,1)} %get-tuple-element.35), channel_id=1, source_target_pairs={{0,128},{4,132},{8,136},{12,140},{16,144},{20,148},{24,152},{28,15... | collective-permute-start | bytes 589832 | tf_op jit(solution)/shard_map/ppermute | solution.py:38
  55.2 10.4 %collective-permute-start.8 = (bf16[2,6,64,128]{3,2,1,0:T(8,128)(2,1)}, bf16[2,6,64,128]{3,2,1,0:T(8,128)(2,1)S(1)}, u32[]{:S(2)}, u32[]{:S(2)}) collective-permute-start(bf16[2,6,64,128]{3,2,1,0:T(8,128)(2,1)} %get-tuple-element.36), channel_id=1, source_target_pairs={{0,192},{4,196},{8,200},{12,204},{16,208},{20,212},{24,216},{28,22... | collective-permute-start | bytes 589832 | tf_op jit(solution)/shard_map/ppermute | solution.py:38
  58.6 8.5 %collective-permute-start.12 = (bf16[2,4,64,128]{3,2,1,0:T(8,128)(2,1)}, bf16[2,4,64,128]{3,2,1,0:T(8,128)(2,1)S(1)}, u32[]{:S(2)}, u32[]{:S(2)}) collective-permute-start(bf16[2,4,64,128]{3,2,1,0:T(8,128)(2,1)} %get-tuple-element.38), channel_id=1, source_target_pairs={{0,64},{4,68},{8,72},{12,76},{16,80},{20,84},{24,88},{28,92},{32,9... | collective-permute-start | bytes 393224 | tf_op jit(solution)/shard_map/ppermute | solution.py:38
  60.3 9.9 %collective-permute-start.13 = (bf16[2,4,64,128]{3,2,1,0:T(8,128)(2,1)}, bf16[2,4,64,128]{3,2,1,0:T(8,128)(2,1)S(1)}, u32[]{:S(2)}, u32[]{:S(2)}) collective-permute-start(bf16[2,4,64,128]{3,2,1,0:T(8,128)(2,1)} %get-tuple-element.39), channel_id=1, source_target_pairs={{0,128},{4,132},{8,136},{12,140},{16,144},{20,148},{24,152},{28,15... | collective-permute-start | bytes 393224 | tf_op jit(solution)/shard_map/ppermute | solution.py:38
  63.2 12.0 %collective-permute-start.14 = (bf16[2,4,64,128]{3,2,1,0:T(8,128)(2,1)}, bf16[2,4,64,128]{3,2,1,0:T(8,128)(2,1)S(1)}, u32[]{:S(2)}, u32[]{:S(2)}) collective-permute-start(bf16[2,4,64,128]{3,2,1,0:T(8,128)(2,1)} %get-tuple-element.40), channel_id=1, source_target_pairs={{0,192},{4,196},{8,200},{12,204},{16,208},{20,212},{24,216},{28,22... | collective-permute-start | bytes 393224 | tf_op jit(solution)/shard_map/ppermute | solution.py:38
  65.6 9.6 %collective-permute-start.20 = (bf16[2,6,64,128]{3,2,1,0:T(8,128)(2,1)}, bf16[2,6,64,128]{3,2,1,0:T(8,128)(2,1)S(1)}, u32[]{:S(2)}, u32[]{:S(2)}) collective-permute-start(bf16[2,6,64,128]{3,2,1,0:T(8,128)(2,1)} %get-tuple-element.42), channel_id=1, source_target_pairs={{0,64},{4,68},{8,72},{12,76},{16,80},{20,84},{24,88},{28,92},{32,9... | collective-permute-start | bytes 589832 | tf_op jit(solution)/shard_map/ppermute | solution.py:38
  65.7 11.0 %collective-permute-start.21 = (bf16[2,6,64,128]{3,2,1,0:T(8,128)(2,1)}, bf16[2,6,64,128]{3,2,1,0:T(8,128)(2,1)S(1)}, u32[]{:S(2)}, u32[]{:S(2)}) collective-permute-start(bf16[2,6,64,128]{3,2,1,0:T(8,128)(2,1)} %get-tuple-element.43), channel_id=1, source_target_pairs={{0,128},{4,132},{8,136},{12,140},{16,144},{20,148},{24,152},{28,15... | collective-permute-start | bytes 589832 | tf_op jit(solution)/shard_map/ppermute | solution.py:38
  67.1 9.5 %collective-permute-start.22 = (bf16[2,6,64,128]{3,2,1,0:T(8,128)(2,1)}, bf16[2,6,64,128]{3,2,1,0:T(8,128)(2,1)S(1)}, u32[]{:S(2)}, u32[]{:S(2)}) collective-permute-start(bf16[2,6,64,128]{3,2,1,0:T(8,128)(2,1)} %get-tuple-element.44), channel_id=1, source_target_pairs={{0,192},{4,196},{8,200},{12,204},{16,208},{20,212},{24,216},{28,22... | collective-permute-start | bytes 589832 | tf_op jit(solution)/shard_map/ppermute | solution.py:38
  70.2 12.5 %collective-permute-start.9 = (bf16[4,6,64,128]{3,2,1,0:T(8,128)(2,1)}, bf16[4,6,64,128]{3,2,1,0:T(8,128)(2,1)S(1)}, u32[]{:S(2)}, u32[]{:S(2)}) collective-permute-start(bf16[4,6,64,128]{3,2,1,0:T(8,128)(2,1)} %pad_maximum_fusion), channel_id=1, source_target_pairs={{0,4},{4,0},{8,12},{12,8},{16,20},{20,16},{24,28},{28,24},{32,36},... | collective-permute-start | bytes 1179656 | tf_op jit(solution)/shard_map/ppermute | solution.py:38
  77.5 6.4 %collective-permute-start.23 = (bf16[4,6,64,128]{3,2,1,0:T(8,128)(2,1)}, bf16[4,6,64,128]{3,2,1,0:T(8,128)(2,1)S(1)}, u32[]{:S(2)}, u32[]{:S(2)}) collective-permute-start(bf16[4,6,64,128]{3,2,1,0:T(8,128)(2,1)} %pad_maximum_fusion.1), channel_id=1, source_target_pairs={{0,4},{4,0},{8,12},{12,8},{16,20},{20,16},{24,28},{28,24},{32,36},... | collective-permute-start | bytes 1179656 | tf_op jit(solution)/shard_map/ppermute | solution.py:38
  90.8 14.6 %collective-permute-start.24 = (bf16[64,2048]{1,0:T(8,128)(2,1)}, bf16[64,2048]{1,0:T(8,128)(2,1)S(1)}, u32[]{:S(2)}, u32[]{:S(2)}) collective-permute-start(bf16[64,2048]{1,0:T(8,128)(2,1)} %get-tuple-element.46.own_ref), channel_id=1, source_target_pairs={{0,1},{1,2},{2,3},{3,0},{4,5},{5,6},{6,7},{7,4},{8,9},{9,10},{10,1... | collective-permute-start | bytes 786440 | tf_op jit(solution)/shard_map/ppermute | solution.py:525
  92.1 13.3 %collective-permute-start.25 = (bf16[64,2048]{1,0:T(8,128)(2,1)}, bf16[64,2048]{1,0:T(8,128)(2,1)S(1)}, u32[]{:S(2)}, u32[]{:S(2)}) collective-permute-start(bf16[64,2048]{1,0:T(8,128)(2,1)} %get-tuple-element.46.own_ref), channel_id=1, source_target_pairs={{0,3},{1,0},{2,1},{3,2},{4,7},{5,4},{6,5},{7,6},{8,11},{9,8},{10,9... | collective-permute-start | bytes 786440 | tf_op jit(solution)/shard_map/ppermute | solution.py:525
  93.6 13.1 %collective-permute-start.26 = (bf16[64,2048]{1,0:T(8,128)(2,1)}, bf16[64,2048]{1,0:T(8,128)(2,1)S(1)}, u32[]{:S(2)}, u32[]{:S(2)}) collective-permute-start(bf16[64,2048]{1,0:T(8,128)(2,1)} %get-tuple-element.46.own_ref), channel_id=1, source_target_pairs={{0,2},{1,3},{2,0},{3,1},{4,6},{5,7},{6,4},{7,5},{8,10},{9,11},{10,... | collective-permute-start | bytes 786440 | tf_op jit(solution)/shard_map/ppermute | solution.py:525
  95.1 10.3 %all-to-all-start = ((s32[8,1,16]{2,1,0:T(1,128)}), s32[8,1,16]{2,1,0:T(1,128)S(1)}, u32[]{:S(2)}, u32[]{:S(2)}) async-start(s32[8,1,16]{2,1,0:T(1,128)} %get-tuple-element.45), calls=%async_computation | async-start | bytes 8192 | tf_op jit(solution)/shard_map/all_to_all | solution.py:528
  115.6 5.1 %collective-permute-start.28 = (f32[72,128]{1,0:T(8,128)S(1)}, f32[72,128]{1,0:T(8,128)S(1)}, u32[]{:S(2)}, u32[]{:S(2)}) collective-permute-start(f32[72,128]{1,0:T(8,128)S(1)} %add.102._), channel_id=1, source_target_pairs={{0,8},{4,12},{8,0},{12,4},{16,24},{20,28},{24,16},{28,20},{32,40},... | collective-permute-start | bytes 110600 | tf_op jit(solution)/shard_map/ppermute | solution.py:38
  120.8 59.1 %all-to-all-start.1 = ((bf16[64,128,128]{2,1,0:T(8,128)(2,1)}), bf16[64,128,128]{2,1,0:T(8,128)(2,1)S(1)}, u32[]{:S(2)}, u32[]{:S(2)}) async-start(bf16[64,128,128]{2,1,0:T(8,128)(2,1)} %back_remote.1._), calls=%async_computation.1 | async-start | bytes 4194304 | tf_op jit(solution)/shard_map/all_to_all | solution.py:537
  133.6 6.0 %collective-permute-start.30 = (f32[72,128]{1,0:T(8,128)S(1)}, f32[72,128]{1,0:T(8,128)S(1)}, u32[]{:S(2)}, u32[]{:S(2)}) collective-permute-start(f32[72,128]{1,0:T(8,128)S(1)} %add.103), channel_id=1, source_target_pairs={{0,128},{4,132},{8,136},{12,140},{16,144},{20,148},{24,152},{28,15... | collective-permute-start | bytes 110600 | tf_op jit(solution)/shard_map/ppermute | solution.py:38
  136.2 5.9 %collective-permute-start.31 = (f32[72,128]{1,0:T(8,128)S(1)}, f32[72,128]{1,0:T(8,128)S(1)}, u32[]{:S(2)}, u32[]{:S(2)}) collective-permute-start(f32[72,128]{1,0:T(8,128)S(1)} %add.103), channel_id=1, source_target_pairs={{0,192},{4,196},{8,200},{12,204},{16,208},{20,212},{24,216},{28,22... | collective-permute-start | bytes 110600 | tf_op jit(solution)/shard_map/ppermute | solution.py:38
  142.1 42.0 %collective-permute-start.32 = (f32[72,128]{1,0:T(8,128)S(1)}, f32[72,128]{1,0:T(8,128)S(1)}, u32[]{:S(2)}, u32[]{:S(2)}) collective-permute-start(f32[72,128]{1,0:T(8,128)S(1)} %add_add_fusion.a_ref), channel_id=1, source_target_pairs={{0,16},{4,20},{8,24},{12,28},{16,0},{20,4},{24,8},{28,12},{32,48},... | collective-permute-start | bytes 110600 | tf_op jit(solution)/shard_map/ppermute | solution.py:38
  143.9 40.1 %collective-permute-start.33 = (f32[72,128]{1,0:T(8,128)S(1)}, f32[72,128]{1,0:T(8,128)S(1)}, u32[]{:S(2)}, u32[]{:S(2)}) collective-permute-start(f32[72,128]{1,0:T(8,128)S(1)} %add_add_fusion.a_ref), channel_id=1, source_target_pairs={{0,32},{4,36},{8,40},{12,44},{16,48},{20,52},{24,56},{28,60},{32,0... | collective-permute-start | bytes 110600 | tf_op jit(solution)/shard_map/ppermute | solution.py:38
  146.6 37.5 %collective-permute-start.34 = (f32[72,128]{1,0:T(8,128)S(1)}, f32[72,128]{1,0:T(8,128)S(1)}, u32[]{:S(2)}, u32[]{:S(2)}) collective-permute-start(f32[72,128]{1,0:T(8,128)S(1)} %add_add_fusion.a_ref), channel_id=1, source_target_pairs={{0,48},{4,52},{8,56},{12,60},{16,32},{20,36},{24,40},{28,44},{32,1... | collective-permute-start | bytes 110600 | tf_op jit(solution)/shard_map/ppermute | solution.py:38
  (31 other events, 252.6 us)
Sparse Core Ops, SparseCore 0:
  16.3 25.8 all-gather.1

commit v10 on v8

--- a/solution.py
+++ b/solution.py
@@ -476,7 +476,7 @@
     agg = agg_local(local_cols, feats, tiles)
     for group, sources in zip(GROUPS, groups):
         packs = pack(group, wanted, sources, block, after)
-        after = [packs[0], agg]
+        after = [packs[0]] if group == GROUPS[0] else [packs[0], agg]
         moved = [packs[0]] + [shift(packs[ys], dy=ys) for ys in range(1, NY)]
         parts += moved
         parts.append(shift(jnp.concatenate([m[1:] for m in moved]), dc=1))
@@ -491,9 +491,10 @@
     held = jnp.sum(jnp.where(match, by_owner[None], 0), axis=2).reshape(NZ, 1, NY * NC * CAP)
     agg, held = agg_remote(near, held, parts, tiles, agg)
 
-    pieces = [agg] + [
-        lax.ppermute(agg, "feat", [(k, (k + s) % fpeers) for k in range(fpeers)]) for s in (1, 3, 2)
+    ahead = [
+        lax.ppermute(agg, "feat", [(k, (k + s) % fpeers) for k in range(fpeers)]) for s in (2, 1, 3)
     ]
+    pieces = [agg, ahead[1], ahead[2], ahead[0]]
     along_z = [[(y0 * NZ + z0) * NC + c0 for z0 in range(NZ)] for y0 in range(NY) for c0 in range(NC)]
     held = lax.all_to_all(held, "rows", 0, 0, tiled=True, axis_index_groups=along_z)
 

time: 192 us -> 192 us (level)
  no operation moved by 1% of the time
where the time goes in v10:
time: 192 us; the launch traced here: 191 us
  starting transfers between devices  66 us (34%)
  waiting for transfers between devices  64.7 us (34%)
  Pallas kernels  32 us (17%)
  between operations  14.5 us (8%)
  local copies, waits for them, and re-layouts  6.88 us (4%)
  other arithmetic  6.82 us (4%)
    ppermute x33, waiting for transfers between devices, shift(): return lax.ppermute(x, 'rows', pairs)  57.4 us
    ppermute x33, starting transfers between devices, shift(): return lax.ppermute(x, 'rows', pairs)  51.5 us
    all_to_all x1, starting transfers between devices, local(): recv = lax.all_to_all(send, 'rows', split_axis=0, concat_axis=0, tiled=True)  6.9 us
    pallas_call x3, Pallas kernels, pack(): pl.pallas_call(functools.partial(pack_kernel, first, count, len(sources)...  6.43 us
    all_to_all x1, waiting for transfers between devices, local(): lax.all_to_all(held, 'rows', 0, 0, tiled=True, axis_index_groups=along_z)  5.7 us
    pallas_call x1, Pallas kernels, mid(): pl.pallas_call(mid_kernel, grid=(nodes // chunk,), out_shape=(jax.ShapeDt...  4.99 us
    pallas_call x1, Pallas kernels, agg_remote(): pl.pallas_call(agg_remote_kernel, grid=(row_blocks // STEP,), out_shape=(...  4.9 us
    pallas_call x1, Pallas kernels, back_remote(): pl.pallas_call(back_remote_kernel, grid=(row_blocks // STEP,), out_shape=...  4.51 us
  transfers between devices with their start and end apart: 39, of which 14 were waited for; matrix products, arithmetic and copies ran while one was open for 5% of the time, Pallas kernels for 13%

profile of v10, /device:TPU:1, one launch (start us, length us, event | category | flops | bytes accessed | tf_op | source)
XLA Modules:
  0.0 190.9 jit_solution(741410351352899483)
XLA Ops:
  7.2 6.5 %collective-permute-start.4 = (bf16[64,2048]{1,0:T(8,128)(2,1)}, bf16[64,2048]{1,0:T(8,128)(2,1)S(1)}, u32[]{:S(2)}, u32[]{:S(2)}) collective-permute-start(bf16[64,2048]{1,0:T(8,128)(2,1)} %refs_1_.1), channel_id=1, source_target_pairs={{0,56},{4,60},{8,0},{12,4},{16,8},{20,12},{24,16},{28,20},{32,24},... | collective-permute-start | bytes 786440 | tf_op jit(solution)/shard_map/ppermute | solution.py:38
  17.4 4.6 %collective-permute-done.5.refs_3_ = bf16[64,2048]{1,0:T(8,128)(2,1)S(1)} collective-permute-done((bf16[64,2048]{1,0:T(8,128)(2,1)}, bf16[64,2048]{1,0:T(8,128)(2,1)S(1)}, u32[]{:S(2)}, u32[]{:S(2)}) %collective-permute-start.5) | collective-permute-done | bytes 262176 | tf_op jit(solution)/shard_map/ppermute | solution.py:38
  22.6 2.6 %collective-permute-start.10 = (bf16[64,2048]{1,0:T(8,128)(2,1)S(1)}, bf16[64,2048]{1,0:T(8,128)(2,1)S(1)}, u32[]{:S(2)}, u32[]{:S(2)}) collective-permute-start(bf16[64,2048]{1,0:T(8,128)(2,1)S(1)} %collective-permute-done.4.refs_2_), channel_id=1, source_target_pairs={{0,56},{4,60},{8,0},{12,4},{16,8},{20,12},{24,16},{28,20},{32,24},... | collective-permute-start | bytes 786440 | tf_op jit(solution)/shard_map/ppermute | solution.py:38
  25.3 3.8 %collective-permute-done.11.refs_2_ = bf16[64,2048]{1,0:T(8,128)(2,1)S(1)} collective-permute-done((bf16[64,2048]{1,0:T(8,128)(2,1)S(1)}, bf16[64,2048]{1,0:T(8,128)(2,1)S(1)}, u32[]{:S(2)}, u32[]{:S(2)}) %collective-permute-start.11) | collective-permute-done | bytes 262176 | tf_op jit(solution)/shard_map/ppermute | solution.py:38
  29.3 2.8 %collective-permute-start = (s32[4,16]{1,0:T(4,128)S(1)}, s32[4,16]{1,0:T(4,128)S(1)}, u32[]{:S(2)}, u32[]{:S(2)}) collective-permute-start(s32[4,16]{1,0:T(4,128)S(1)} %squeeze.15), channel_id=1, source_target_pairs={{0,4},{4,0},{8,12},{12,8},{16,20},{20,16},{24,28},{28,24},{32,36},... | collective-permute-start | bytes 776 | tf_op jit(solution)/shard_map/ppermute | solution.py:38
  32.2 3.0 %collective-permute-start.16 = (bf16[64,2048]{1,0:T(8,128)(2,1)S(1)}, bf16[64,2048]{1,0:T(8,128)(2,1)S(1)}, u32[]{:S(2)}, u32[]{:S(2)}) collective-permute-start(bf16[64,2048]{1,0:T(8,128)(2,1)S(1)} %collective-permute-done.10.refs_1_), channel_id=1, source_target_pairs={{0,56},{4,60},{8,0},{12,4},{16,8},{20,12},{24,16},{28,20},{32,24},... | collective-permute-start | bytes 786440 | tf_op jit(solution)/shard_map/ppermute | solution.py:38
  39.7 2.3 %collective-permute-done.2 = s32[2,16]{1,0:T(2,128)S(1)} collective-permute-done((s32[2,16]{1,0:T(2,128)S(1)}, s32[2,16]{1,0:T(2,128)S(1)}, u32[]{:S(2)}, u32[]{:S(2)}) %collective-permute-start.2) | collective-permute-done | bytes 160 | tf_op jit(solution)/shard_map/ppermute | solution.py:38
  42.7 2.2 %pack.3 = (bf16[2,6,64,128]{3,2,1,0:T(8,128)(2,1)}, bf16[2,6,64,128]{3,2,1,0:T(8,128)(2,1)}, bf16[2,6,64,128]{3,2,1,0:T(8,128)(2,1)}, bf16[2,6,64,128]{3,2,1,0:T(8,128)(2,1)}) custom-call(s32[128]{0:T(128)} %reshape.217.refs_0_, bf16[64,2048]{1,0:T(8,128)(2,1)} %refs_1_.1, bf16[64,2048]{1,0:T(8,128)(2,1)} %copy-done.26, bf16[64,2048]{1,0:T(8,128)(2,1)} %copy-done.27), custom_call_target="tpu_custom_call" | custom-call | bytes 3145728 | tf_op jit(solution)/shard_map/pack/pallas_call | solution.py:62
  45.2 2.2 %collective-permute-start.7 = (bf16[2,6,64,128]{3,2,1,0:T(8,128)(2,1)}, bf16[2,6,64,128]{3,2,1,0:T(8,128)(2,1)S(1)}, u32[]{:S(2)}, u32[]{:S(2)}) collective-permute-start(bf16[2,6,64,128]{3,2,1,0:T(8,128)(2,1)} %get-tuple-element.29), channel_id=1, source_target_pairs={{0,128},{4,132},{8,136},{12,140},{16,144},{20,148},{24,152},{28,15... | collective-permute-start | bytes 589832 | tf_op jit(solution)/shard_map/ppermute | solution.py:38
  49.6 2.0 %pack.4 = (bf16[2,4,64,128]{3,2,1,0:T(8,128)(2,1)}, bf16[2,4,64,128]{3,2,1,0:T(8,128)(2,1)}, bf16[2,4,64,128]{3,2,1,0:T(8,128)(2,1)}, bf16[2,4,64,128]{3,2,1,0:T(8,128)(2,1)}) custom-call(s32[128]{0:T(128)} %reshape.217.refs_0_, bf16[64,2048]{1,0:T(8,128)(2,1)} %copy-done.25, bf16[64,2048]{1,0:T(8,128)(2,1)} %copy-done.24, ...), custom_call_target="tpu_custom_call" | custom-call | bytes 3145728 | tf_op jit(solution)/shard_map/pack/pallas_call | solution.py:62
  52.5 4.2 %agg_local.1.refs_6_.local_ref = f32[64,2048]{1,0:T(8,128)} custom-call(s32[64]{0:T(128)} %reshape.216.cols_ref, bf16[64,2048]{1,0:T(8,128)(2,1)} %refs_1_.1, bf16[16,8,128,128]{3,2,1,0:T(8,128)(2,1)} %bitcast.26), custom_call_target="tpu_custom_call" | custom-call | flops 134217728 | bytes 3145728 | tf_op jit(solution)/shard_map/agg_local/pallas_call | solution.py:98
  58.0 2.2 %pack.5 = (bf16[2,6,64,128]{3,2,1,0:T(8,128)(2,1)}, bf16[2,6,64,128]{3,2,1,0:T(8,128)(2,1)}, bf16[2,6,64,128]{3,2,1,0:T(8,128)(2,1)}, bf16[2,6,64,128]{3,2,1,0:T(8,128)(2,1)}) custom-call(s32[128]{0:T(128)} %reshape.217.refs_0_, bf16[64,2048]{1,0:T(8,128)(2,1)} %copy-done.6, bf16[64,2048]{1,0:T(8,128)(2,1)} %copy-done.5, bf16[32,2048]{1,0:T(8,128)(2,1)} %copy-done.28, ...), custom_call_target="tpu_custom_call" | custom-call | bytes 3145728 | tf_op jit(solution)/shard_map/pack/pallas_call | solution.py:62
  60.3 2.1 %collective-permute-start.14 = (bf16[2,4,64,128]{3,2,1,0:T(8,128)(2,1)S(1)}, bf16[2,4,64,128]{3,2,1,0:T(8,128)(2,1)S(1)}, u32[]{:S(2)}, u32[]{:S(2)}) collective-permute-start(bf16[2,4,64,128]{3,2,1,0:T(8,128)(2,1)S(1)} %copy-done.31), channel_id=1, source_target_pairs={{0,192},{4,196},{8,200},{12,204},{16,208},{20,212},{24,216},{28,22... | collective-permute-start | bytes 393224 | tf_op jit(solution)/shard_map/ppermute | solution.py:38
  64.3 2.0 %collective-permute-start.22 = (bf16[2,6,64,128]{3,2,1,0:T(8,128)(2,1)}, bf16[2,6,64,128]{3,2,1,0:T(8,128)(2,1)S(1)}, u32[]{:S(2)}, u32[]{:S(2)}) collective-permute-start(bf16[2,6,64,128]{3,2,1,0:T(8,128)(2,1)} %get-tuple-element.38), channel_id=1, source_target_pairs={{0,192},{4,196},{8,200},{12,204},{16,208},{20,212},{24,216},{28,22... | collective-permute-start | bytes 589832 | tf_op jit(solution)/shard_map/ppermute | solution.py:38
  66.5 4.5 %collective-permute-start.9 = (bf16[4,6,64,128]{3,2,1,0:T(8,128)(2,1)S(1)}, bf16[4,6,64,128]{3,2,1,0:T(8,128)(2,1)S(1)}, u32[]{:S(2)}, u32[]{:S(2)}) collective-permute-start(bf16[4,6,64,128]{3,2,1,0:T(8,128)(2,1)S(1)} %pad_maximum_fusion), channel_id=1, source_target_pairs={{0,4},{4,0},{8,12},{12,8},{16,20},{20,16},{24,28},{28,24},{32,36},... | collective-permute-start | bytes 1179656 | tf_op jit(solution)/shard_map/ppermute | solution.py:38
  71.3 3.6 %collective-permute-done.22.refs_13_ = bf16[2,6,64,128]{3,2,1,0:T(8,128)(2,1)S(1)} collective-permute-done((bf16[2,6,64,128]{3,2,1,0:T(8,128)(2,1)}, bf16[2,6,64,128]{3,2,1,0:T(8,128)(2,1)S(1)}, u32[]{:S(2)}, u32[]{:S(2)}) %collective-permute-start.22) | collective-permute-done | bytes 196640 | tf_op jit(solution)/shard_map/ppermute | solution.py:38
  75.0 2.5 %collective-permute-start.23 = (bf16[4,6,64,128]{3,2,1,0:T(8,128)(2,1)S(1)}, bf16[4,6,64,128]{3,2,1,0:T(8,128)(2,1)S(1)}, u32[]{:S(2)}, u32[]{:S(2)}) collective-permute-start(bf16[4,6,64,128]{3,2,1,0:T(8,128)(2,1)S(1)} %pad_maximum_fusion.1), channel_id=1, source_target_pairs={{0,4},{4,0},{8,12},{12,8},{16,20},{20,16},{24,28},{28,24},{32,36},... | collective-permute-start | bytes 1179656 | tf_op jit(solution)/shard_map/ppermute | solution.py:38
  81.2 4.9 %agg_remote.1 = (bf16[64,2048]{1,0:T(8,128)(2,1)}, s32[8,1,16]{2,1,0:T(1,128)}) custom-call(s32[64]{0:T(128)} %copy-done.30, s32[8,1,16]{2,1,0:T(1,128)} %copy.42.held_ref, bf16[16,8,128,128]{3,2,1,0:T(8,128)(2,1)} %bitcast.27, f32[64,2048]{1,0:T(8,128)} %agg_local.1.refs_6_.local_ref, bf16[2,6,64,128]{3,2,1,0:T(8,128)(2,1)} %get-tuple-element.27.refs_3_.refs_0_, ...), custom_call_target="tpu_custom_call" | custom-call | flops 134217728 | bytes 5242880 | tf_op jit(solution)/shard_map/agg_remote/pallas_call | solution.py:149
  90.4 3.3 %all-to-all-start = ((s32[8,1,16]{2,1,0:T(1,128)}), s32[8,1,16]{2,1,0:T(1,128)S(1)}, u32[]{:S(2)}, u32[]{:S(2)}) async-start(s32[8,1,16]{2,1,0:T(1,128)} %get-tuple-element.39), calls=%async_computation | async-start | bytes 8192 | tf_op jit(solution)/shard_map/all_to_all | solution.py:499
  94.4 5.7 %all-to-all-done._.held_ref = s32[8,1,16]{2,1,0:T(1,128)S(1)} async-done(((s32[8,1,16]{2,1,0:T(1,128)}), s32[8,1,16]{2,1,0:T(1,128)S(1)}, u32[]{:S(2)}, u32[]{:S(2)}) %all-to-all-start) | async-done | bytes 544 | tf_op jit(solution)/shard_map/all_to_all | solution.py:499
  102.3 5.0 %mid.1 = (bf16[64,2048]{1,0:T(8,128)(2,1)}, bf16[64,2048]{1,0:T(8,128)(2,1)}, f32[72,128]{1,0:T(8,128)}, f32[72,128]{1,0:T(8,128)}) custom-call(s32[2]{0:T(128)} %pad_add_fusion.2.me_ref, s32[8,1,16]{2,1,0:T(1,128)} %copy-done.1, bf16[64,2048]{1,0:T(8,128)(2,1)} %get-tuple-element.40.own_ref, bf16[64,2048]{1,0:T(8,128)(2,1)} %copy-done.21, ...), custom_call_target="tpu_custom_call" | custom-call | flops 402653184 | bytes 3145728 | tf_op jit(solution)/shard_map/mid/pallas_call | solution.py:244
  111.5 4.5 %back_remote.1._ = bf16[64,128,128]{2,1,0:T(8,128)(2,1)} custom-call(s32[64]{0:T(128)} %get-tuple-element.58.slots_ref, bf16[64,2048]{1,0:T(8,128)(2,1)} %get-tuple-element.42.g_ref, bf16[16,8,128,128]{3,2,1,0:T(8,128)(2,1)} %bitcast.28, f32[72,128]{1,0:T(8,128)} %copy-done.16), custom_call_target="tpu_custom_call" | custom-call | flops 134217728 | bytes 5242880 | tf_op jit(solution)/shard_map/back_remote/pallas_call | solution.py:312
  116.0 6.9 %all-to-all-start.1 = ((bf16[64,128,128]{2,1,0:T(8,128)(2,1)}), bf16[64,128,128]{2,1,0:T(8,128)(2,1)S(1)}, u32[]{:S(2)}, u32[]{:S(2)}) async-start(bf16[64,128,128]{2,1,0:T(8,128)(2,1)} %back_remote.1._), calls=%async_computation.1 | async-start | bytes 4194304 | tf_op jit(solution)/shard_map/all_to_all | solution.py:508
  122.9 3.9 %back_local.1.local_ref = f32[64,2048]{1,0:T(8,128)} custom-call(s32[64]{0:T(128)} %reshape.216.cols_ref, bf16[64,2048]{1,0:T(8,128)(2,1)} %get-tuple-element.42.g_ref, bf16[16,8,128,128]{3,2,1,0:T(8,128)(2,1)} %bitcast.29, bf16[64,128,128]{2,1,0:T(8,128)(2,1)} %back_remote.1._), custom_call_target="tpu_custom_call" | custom-call | flops 134217728 | bytes 3145728 | tf_op jit(solution)/shard_map/back_local/pallas_call | solution.py:351
  128.3 2.6 %collective-permute-start.30 = (f32[72,128]{1,0:T(8,128)S(1)}, f32[72,128]{1,0:T(8,128)S(1)}, u32[]{:S(2)}, u32[]{:S(2)}) collective-permute-start(f32[72,128]{1,0:T(8,128)S(1)} %add.112), channel_id=1, source_target_pairs={{0,128},{4,132},{8,136},{12,140},{16,144},{20,148},{24,152},{28,15... | collective-permute-start | bytes 110600 | tf_op jit(solution)/shard_map/ppermute | solution.py:38
  130.9 3.4 %collective-permute-done.30 = f32[72,128]{1,0:T(8,128)S(1)} collective-permute-done((f32[72,128]{1,0:T(8,128)S(1)}, f32[72,128]{1,0:T(8,128)S(1)}, u32[]{:S(2)}, u32[]{:S(2)}) %collective-permute-start.30) | collective-permute-done | bytes 36896 | tf_op jit(solution)/shard_map/ppermute | solution.py:38
  134.3 2.4 %collective-permute-done.31 = f32[72,128]{1,0:T(8,128)S(1)} collective-permute-done((f32[72,128]{1,0:T(8,128)S(1)}, f32[72,128]{1,0:T(8,128)S(1)}, u32[]{:S(2)}, u32[]{:S(2)}) %collective-permute-start.31) | collective-permute-done | bytes 36896 | tf_op jit(solution)/shard_map/ppermute | solution.py:38
  136.8 1.8 collective-permute-start.32
  138.6 2.7 %collective-permute-start.33 = (f32[72,128]{1,0:T(8,128)S(1)}, f32[72,128]{1,0:T(8,128)S(1)}, u32[]{:S(2)}, u32[]{:S(2)}) collective-permute-start(f32[72,128]{1,0:T(8,128)S(1)} %add_add_fusion.1), channel_id=1, source_target_pairs={{0,32},{4,36},{8,40},{12,44},{16,48},{20,52},{24,56},{28,60},{32,0... | collective-permute-start | bytes 110600 | tf_op jit(solution)/shard_map/ppermute | solution.py:38
  142.5 29.9 %collective-permute-done.32 = f32[72,128]{1,0:T(8,128)S(1)} collective-permute-done((f32[72,128]{1,0:T(8,128)S(1)}, f32[72,128]{1,0:T(8,128)S(1)}, u32[]{:S(2)}, u32[]{:S(2)}) %collective-permute-start.32) | collective-permute-done | bytes 36896 | tf_op jit(solution)/shard_map/ppermute | solution.py:38
  172.4 4.8 %collective-permute-done.33 = f32[72,128]{1,0:T(8,128)S(1)} collective-permute-done((f32[72,128]{1,0:T(8,128)S(1)}, f32[72,128]{1,0:T(8,128)S(1)}, u32[]{:S(2)}, u32[]{:S(2)}) %collective-permute-start.33) | collective-permute-done | bytes 36896 | tf_op jit(solution)/shard_map/ppermute | solution.py:38
  181.0 3.1 %finish.1 = f32[64,2048]{1,0:T(8,128)} custom-call(s32[2]{0:T(128)S(1)} %pad_add_fusion.3.place_ref, s32[8,1,16]{2,1,0:T(1,128)S(1)} %copy-done.2, bf16[64,128,128]{2,1,0:T(8,128)(2,1)S(1)} %all-to-all-done.1.recv_ref, f32[64,2048]{1,0:T(8,128)S(1)} %copy-done), custom_call_target="tpu_custom_call" | custom-call | flops 1048576 | bytes 4194304 | tf_op jit(solution)/shard_map/finish/pallas_call | solution.py:402
  (175 shorter events, 38.3 us)
Async XLA Ops:
  7.2 94.5 %all-gather.2.cloned.1.call-start = ((), (), s32[]{:S(2)}) async-start(), calls=%async_computation.2 | async-start | bytes 1556480 | tf_op jit(solution)/shard_map/all_gather | solution.py:486
  7.2 15.3 %collective-permute-start.4 = (bf16[64,2048]{1,0:T(8,128)(2,1)}, bf16[64,2048]{1,0:T(8,128)(2,1)S(1)}, u32[]{:S(2)}, u32[]{:S(2)}) collective-permute-start(bf16[64,2048]{1,0:T(8,128)(2,1)} %refs_1_.1), channel_id=1, source_target_pairs={{0,56},{4,60},{8,0},{12,4},{16,8},{20,12},{24,16},{28,20},{32,24},... | collective-permute-start | bytes 786440 | tf_op jit(solution)/shard_map/ppermute | solution.py:38
  13.7 8.3 %collective-permute-start.5 = (bf16[64,2048]{1,0:T(8,128)(2,1)}, bf16[64,2048]{1,0:T(8,128)(2,1)S(1)}, u32[]{:S(2)}, u32[]{:S(2)}) collective-permute-start(bf16[64,2048]{1,0:T(8,128)(2,1)} %refs_1_.1), channel_id=1, source_target_pairs={{0,8},{4,12},{8,16},{12,20},{16,24},{20,28},{24,32},{28,36},{32,40... | collective-permute-start | bytes 786440 | tf_op jit(solution)/shard_map/ppermute | solution.py:38
  22.0 7.1 %collective-permute-start.11 = (bf16[64,2048]{1,0:T(8,128)(2,1)S(1)}, bf16[64,2048]{1,0:T(8,128)(2,1)S(1)}, u32[]{:S(2)}, u32[]{:S(2)}) collective-permute-start(bf16[64,2048]{1,0:T(8,128)(2,1)S(1)} %collective-permute-done.5.refs_3_), channel_id=1, source_target_pairs={{0,8},{4,12},{8,16},{12,20},{16,24},{20,28},{24,32},{28,36},{32,40... | collective-permute-start | bytes 786440 | tf_op jit(solution)/shard_map/ppermute | solution.py:38
  22.6 9.6 %collective-permute-start.10 = (bf16[64,2048]{1,0:T(8,128)(2,1)S(1)}, bf16[64,2048]{1,0:T(8,128)(2,1)S(1)}, u32[]{:S(2)}, u32[]{:S(2)}) collective-permute-start(bf16[64,2048]{1,0:T(8,128)(2,1)S(1)} %collective-permute-done.4.refs_2_), channel_id=1, source_target_pairs={{0,56},{4,60},{8,0},{12,4},{16,8},{20,12},{24,16},{28,20},{32,24},... | collective-permute-start | bytes 786440 | tf_op jit(solution)/shard_map/ppermute | solution.py:38
  29.1 10.5 %collective-permute-start.17 = (bf16[64,2048]{1,0:T(8,128)(2,1)S(1)}, bf16[64,2048]{1,0:T(8,128)(2,1)S(1)}, u32[]{:S(2)}, u32[]{:S(2)}) collective-permute-start(bf16[64,2048]{1,0:T(8,128)(2,1)S(1)} %collective-permute-done.11.refs_2_), channel_id=1, source_target_pairs={{0,8},{4,12},{8,16},{12,20},{16,24},{20,28},{24,32},{28,36},{32,40... | collective-permute-start | bytes 786440 | tf_op jit(solution)/shard_map/ppermute | solution.py:38
  29.3 5.9 %collective-permute-start = (s32[4,16]{1,0:T(4,128)S(1)}, s32[4,16]{1,0:T(4,128)S(1)}, u32[]{:S(2)}, u32[]{:S(2)}) collective-permute-start(s32[4,16]{1,0:T(4,128)S(1)} %squeeze.15), channel_id=1, source_target_pairs={{0,4},{4,0},{8,12},{12,8},{16,20},{20,16},{24,28},{28,24},{32,36},... | collective-permute-start | bytes 776 | tf_op jit(solution)/shard_map/ppermute | solution.py:38
  32.2 16.7 %collective-permute-start.16 = (bf16[64,2048]{1,0:T(8,128)(2,1)S(1)}, bf16[64,2048]{1,0:T(8,128)(2,1)S(1)}, u32[]{:S(2)}, u32[]{:S(2)}) collective-permute-start(bf16[64,2048]{1,0:T(8,128)(2,1)S(1)} %collective-permute-done.10.refs_1_), channel_id=1, source_target_pairs={{0,56},{4,60},{8,0},{12,4},{16,8},{20,12},{24,16},{28,20},{32,24},... | collective-permute-start | bytes 786440 | tf_op jit(solution)/shard_map/ppermute | solution.py:38
  39.6 11.9 %collective-permute-start.18 = (bf16[32,2048]{1,0:T(8,128)(2,1)S(1)}, bf16[32,2048]{1,0:T(8,128)(2,1)S(1)}, u32[]{:S(2)}, u32[]{:S(2)}) collective-permute-start(bf16[32,2048]{1,0:T(8,128)(2,1)S(1)} %slice.132), channel_id=1, source_target_pairs={{0,8},{4,12},{8,16},{12,20},{16,24},{20,28},{24,32},{28,36},{32,40... | collective-permute-start | bytes 393224 | tf_op jit(solution)/shard_map/ppermute | solution.py:38
  44.9 15.4 %collective-permute-start.6 = (bf16[2,6,64,128]{3,2,1,0:T(8,128)(2,1)}, bf16[2,6,64,128]{3,2,1,0:T(8,128)(2,1)S(1)}, u32[]{:S(2)}, u32[]{:S(2)}) collective-permute-start(bf16[2,6,64,128]{3,2,1,0:T(8,128)(2,1)} %get-tuple-element.28), channel_id=1, source_target_pairs={{0,64},{4,68},{8,72},{12,76},{16,80},{20,84},{24,88},{28,92},{32,9... | collective-permute-start | bytes 589832 | tf_op jit(solution)/shard_map/ppermute | solution.py:38
  45.2 17.2 %collective-permute-start.7 = (bf16[2,6,64,128]{3,2,1,0:T(8,128)(2,1)}, bf16[2,6,64,128]{3,2,1,0:T(8,128)(2,1)S(1)}, u32[]{:S(2)}, u32[]{:S(2)}) collective-permute-start(bf16[2,6,64,128]{3,2,1,0:T(8,128)(2,1)} %get-tuple-element.29), channel_id=1, source_target_pairs={{0,128},{4,132},{8,136},{12,140},{16,144},{20,148},{24,152},{28,15... | collective-permute-start | bytes 589832 | tf_op jit(solution)/shard_map/ppermute | solution.py:38
  47.4 15.2 %collective-permute-start.8 = (bf16[2,6,64,128]{3,2,1,0:T(8,128)(2,1)}, bf16[2,6,64,128]{3,2,1,0:T(8,128)(2,1)S(1)}, u32[]{:S(2)}, u32[]{:S(2)}) collective-permute-start(bf16[2,6,64,128]{3,2,1,0:T(8,128)(2,1)} %get-tuple-element.30), channel_id=1, source_target_pairs={{0,192},{4,196},{8,200},{12,204},{16,208},{20,212},{24,216},{28,22... | collective-permute-start | bytes 589832 | tf_op jit(solution)/shard_map/ppermute | solution.py:38
  48.9 7.9 %collective-permute-start.19 = (bf16[32,2048]{1,0:T(8,128)(2,1)S(1)}, bf16[32,2048]{1,0:T(8,128)(2,1)S(1)}, u32[]{:S(2)}, u32[]{:S(2)}) collective-permute-start(bf16[32,2048]{1,0:T(8,128)(2,1)S(1)} %slice.133), channel_id=1, source_target_pairs={{0,56},{4,60},{8,0},{12,4},{16,8},{20,12},{24,16},{28,20},{32,24},... | collective-permute-start | bytes 393224 | tf_op jit(solution)/shard_map/ppermute | solution.py:38
  51.6 12.8 %collective-permute-start.12 = (bf16[2,4,64,128]{3,2,1,0:T(8,128)(2,1)}, bf16[2,4,64,128]{3,2,1,0:T(8,128)(2,1)S(1)}, u32[]{:S(2)}, u32[]{:S(2)}) collective-permute-start(bf16[2,4,64,128]{3,2,1,0:T(8,128)(2,1)} %get-tuple-element.32), channel_id=1, source_target_pairs={{0,64},{4,68},{8,72},{12,76},{16,80},{20,84},{24,88},{28,92},{32,9... | collective-permute-start | bytes 393224 | tf_op jit(solution)/shard_map/ppermute | solution.py:38
  56.8 9.7 %collective-permute-start.13 = (bf16[2,4,64,128]{3,2,1,0:T(8,128)(2,1)S(1)}, bf16[2,4,64,128]{3,2,1,0:T(8,128)(2,1)S(1)}, u32[]{:S(2)}, u32[]{:S(2)}) collective-permute-start(bf16[2,4,64,128]{3,2,1,0:T(8,128)(2,1)S(1)} %copy-done.32), channel_id=1, source_target_pairs={{0,128},{4,132},{8,136},{12,140},{16,144},{20,148},{24,152},{28,15... | collective-permute-start | bytes 393224 | tf_op jit(solution)/shard_map/ppermute | solution.py:38
  60.3 10.7 %collective-permute-start.14 = (bf16[2,4,64,128]{3,2,1,0:T(8,128)(2,1)S(1)}, bf16[2,4,64,128]{3,2,1,0:T(8,128)(2,1)S(1)}, u32[]{:S(2)}, u32[]{:S(2)}) collective-permute-start(bf16[2,4,64,128]{3,2,1,0:T(8,128)(2,1)S(1)} %copy-done.31), channel_id=1, source_target_pairs={{0,192},{4,196},{8,200},{12,204},{16,208},{20,212},{24,216},{28,22... | collective-permute-start | bytes 393224 | tf_op jit(solution)/shard_map/ppermute | solution.py:38
  62.4 8.7 %collective-permute-start.20 = (bf16[2,6,64,128]{3,2,1,0:T(8,128)(2,1)}, bf16[2,6,64,128]{3,2,1,0:T(8,128)(2,1)S(1)}, u32[]{:S(2)}, u32[]{:S(2)}) collective-permute-start(bf16[2,6,64,128]{3,2,1,0:T(8,128)(2,1)} %get-tuple-element.36), channel_id=1, source_target_pairs={{0,64},{4,68},{8,72},{12,76},{16,80},{20,84},{24,88},{28,92},{32,9... | collective-permute-start | bytes 589832 | tf_op jit(solution)/shard_map/ppermute | solution.py:38
  62.5 8.8 %collective-permute-start.21 = (bf16[2,6,64,128]{3,2,1,0:T(8,128)(2,1)}, bf16[2,6,64,128]{3,2,1,0:T(8,128)(2,1)S(1)}, u32[]{:S(2)}, u32[]{:S(2)}) collective-permute-start(bf16[2,6,64,128]{3,2,1,0:T(8,128)(2,1)} %get-tuple-element.37), channel_id=1, source_target_pairs={{0,128},{4,132},{8,136},{12,140},{16,144},{20,148},{24,152},{28,15... | collective-permute-start | bytes 589832 | tf_op jit(solution)/shard_map/ppermute | solution.py:38
  64.3 10.6 %collective-permute-start.22 = (bf16[2,6,64,128]{3,2,1,0:T(8,128)(2,1)}, bf16[2,6,64,128]{3,2,1,0:T(8,128)(2,1)S(1)}, u32[]{:S(2)}, u32[]{:S(2)}) collective-permute-start(bf16[2,6,64,128]{3,2,1,0:T(8,128)(2,1)} %get-tuple-element.38), channel_id=1, source_target_pairs={{0,192},{4,196},{8,200},{12,204},{16,208},{20,212},{24,216},{28,22... | collective-permute-start | bytes 589832 | tf_op jit(solution)/shard_map/ppermute | solution.py:38
  66.5 13.3 %collective-permute-start.9 = (bf16[4,6,64,128]{3,2,1,0:T(8,128)(2,1)S(1)}, bf16[4,6,64,128]{3,2,1,0:T(8,128)(2,1)S(1)}, u32[]{:S(2)}, u32[]{:S(2)}) collective-permute-start(bf16[4,6,64,128]{3,2,1,0:T(8,128)(2,1)S(1)} %pad_maximum_fusion), channel_id=1, source_target_pairs={{0,4},{4,0},{8,12},{12,8},{16,20},{20,16},{24,28},{28,24},{32,36},... | collective-permute-start | bytes 1179656 | tf_op jit(solution)/shard_map/ppermute | solution.py:38
  75.0 5.2 %collective-permute-start.23 = (bf16[4,6,64,128]{3,2,1,0:T(8,128)(2,1)S(1)}, bf16[4,6,64,128]{3,2,1,0:T(8,128)(2,1)S(1)}, u32[]{:S(2)}, u32[]{:S(2)}) collective-permute-start(bf16[4,6,64,128]{3,2,1,0:T(8,128)(2,1)S(1)} %pad_maximum_fusion.1), channel_id=1, source_target_pairs={{0,4},{4,0},{8,12},{12,8},{16,20},{20,16},{24,28},{28,24},{32,36},... | collective-permute-start | bytes 1179656 | tf_op jit(solution)/shard_map/ppermute | solution.py:38
  86.2 13.9 %collective-permute-start.24 = (bf16[64,2048]{1,0:T(8,128)(2,1)}, bf16[64,2048]{1,0:T(8,128)(2,1)S(1)}, u32[]{:S(2)}, u32[]{:S(2)}) collective-permute-start(bf16[64,2048]{1,0:T(8,128)(2,1)} %get-tuple-element.40.own_ref), channel_id=1, source_target_pairs={{0,1},{1,2},{2,3},{3,0},{4,5},{5,6},{6,7},{7,4},{8,9},{9,10},{10,1... | collective-permute-start | bytes 786440 | tf_op jit(solution)/shard_map/ppermute | solution.py:495
  87.4 12.7 %collective-permute-start.25 = (bf16[64,2048]{1,0:T(8,128)(2,1)}, bf16[64,2048]{1,0:T(8,128)(2,1)S(1)}, u32[]{:S(2)}, u32[]{:S(2)}) collective-permute-start(bf16[64,2048]{1,0:T(8,128)(2,1)} %get-tuple-element.40.own_ref), channel_id=1, source_target_pairs={{0,3},{1,0},{2,1},{3,2},{4,7},{5,4},{6,5},{7,6},{8,11},{9,8},{10,9... | collective-permute-start | bytes 786440 | tf_op jit(solution)/shard_map/ppermute | solution.py:495
  88.9 12.7 %collective-permute-start.26 = (bf16[64,2048]{1,0:T(8,128)(2,1)}, bf16[64,2048]{1,0:T(8,128)(2,1)S(1)}, u32[]{:S(2)}, u32[]{:S(2)}) collective-permute-start(bf16[64,2048]{1,0:T(8,128)(2,1)} %get-tuple-element.40.own_ref), channel_id=1, source_target_pairs={{0,2},{1,3},{2,0},{3,1},{4,6},{5,7},{6,4},{7,5},{8,10},{9,11},{10,... | collective-permute-start | bytes 786440 | tf_op jit(solution)/shard_map/ppermute | solution.py:495
  90.4 9.7 %all-to-all-start = ((s32[8,1,16]{2,1,0:T(1,128)}), s32[8,1,16]{2,1,0:T(1,128)S(1)}, u32[]{:S(2)}, u32[]{:S(2)}) async-start(s32[8,1,16]{2,1,0:T(1,128)} %get-tuple-element.39), calls=%async_computation | async-start | bytes 8192 | tf_op jit(solution)/shard_map/all_to_all | solution.py:499
  110.6 5.4 %collective-permute-start.28 = (f32[72,128]{1,0:T(8,128)S(1)}, f32[72,128]{1,0:T(8,128)S(1)}, u32[]{:S(2)}, u32[]{:S(2)}) collective-permute-start(f32[72,128]{1,0:T(8,128)S(1)} %add.111._), channel_id=1, source_target_pairs={{0,8},{4,12},{8,0},{12,4},{16,24},{20,28},{24,16},{28,20},{32,40},... | collective-permute-start | bytes 110600 | tf_op jit(solution)/shard_map/ppermute | solution.py:38
  116.0 63.9 %all-to-all-start.1 = ((bf16[64,128,128]{2,1,0:T(8,128)(2,1)}), bf16[64,128,128]{2,1,0:T(8,128)(2,1)S(1)}, u32[]{:S(2)}, u32[]{:S(2)}) async-start(bf16[64,128,128]{2,1,0:T(8,128)(2,1)} %back_remote.1._), calls=%async_computation.1 | async-start | bytes 4194304 | tf_op jit(solution)/shard_map/all_to_all | solution.py:508
  128.3 6.0 %collective-permute-start.30 = (f32[72,128]{1,0:T(8,128)S(1)}, f32[72,128]{1,0:T(8,128)S(1)}, u32[]{:S(2)}, u32[]{:S(2)}) collective-permute-start(f32[72,128]{1,0:T(8,128)S(1)} %add.112), channel_id=1, source_target_pairs={{0,128},{4,132},{8,136},{12,140},{16,144},{20,148},{24,152},{28,15... | collective-permute-start | bytes 110600 | tf_op jit(solution)/shard_map/ppermute | solution.py:38
  130.9 5.9 %collective-permute-start.31 = (f32[72,128]{1,0:T(8,128)S(1)}, f32[72,128]{1,0:T(8,128)S(1)}, u32[]{:S(2)}, u32[]{:S(2)}) collective-permute-start(f32[72,128]{1,0:T(8,128)S(1)} %add.112), channel_id=1, source_target_pairs={{0,192},{4,196},{8,200},{12,204},{16,208},{20,212},{24,216},{28,22... | collective-permute-start | bytes 110600 | tf_op jit(solution)/shard_map/ppermute | solution.py:38
  136.8 35.7 %collective-permute-start.32 = (f32[72,128]{1,0:T(8,128)S(1)}, f32[72,128]{1,0:T(8,128)S(1)}, u32[]{:S(2)}, u32[]{:S(2)}) collective-permute-start(f32[72,128]{1,0:T(8,128)S(1)} %add_add_fusion.1), channel_id=1, source_target_pairs={{0,16},{4,20},{8,24},{12,28},{16,0},{20,4},{24,8},{28,12},{32,48},... | collective-permute-start | bytes 110600 | tf_op jit(solution)/shard_map/ppermute | solution.py:38
  138.6 38.6 %collective-permute-start.33 = (f32[72,128]{1,0:T(8,128)S(1)}, f32[72,128]{1,0:T(8,128)S(1)}, u32[]{:S(2)}, u32[]{:S(2)}) collective-permute-start(f32[72,128]{1,0:T(8,128)S(1)} %add_add_fusion.1), channel_id=1, source_target_pairs={{0,32},{4,36},{8,40},{12,44},{16,48},{20,52},{24,56},{28,60},{32,0... | collective-permute-start | bytes 110600 | tf_op jit(solution)/shard_map/ppermute | solution.py:38
  141.3 35.9 %collective-permute-start.34 = (f32[72,128]{1,0:T(8,128)S(1)}, f32[72,128]{1,0:T(8,128)S(1)}, u32[]{:S(2)}, u32[]{:S(2)}) collective-permute-start(f32[72,128]{1,0:T(8,128)S(1)} %add_add_fusion.1), channel_id=1, source_target_pairs={{0,48},{4,52},{8,56},{12,60},{16,32},{20,36},{24,40},{28,44},{32,1... | collective-permute-start | bytes 110600 | tf_op jit(solution)/shard_map/ppermute | solution.py:38
  (40 other events, 391.7 us)
Sparse Core Ops, SparseCore 0:
  16.3 25.5 all-gather.1

commit v11 on v10

--- a/solution.py
+++ b/solution.py
@@ -477,7 +477,8 @@
     for group, sources in zip(GROUPS, groups):
         packs = pack(group, wanted, sources, block, after)
         after = [packs[0]] if group == GROUPS[0] else [packs[0], agg]
-        moved = [packs[0]] + [shift(packs[ys], dy=ys) for ys in range(1, NY)]
+        two, one, three = (shift(packs[ys], dy=ys) for ys in (2, 1, 3))
+        moved = [packs[0], one, two, three]
         parts += moved
         parts.append(shift(jnp.concatenate([m[1:] for m in moved]), dc=1))
 
@@ -512,6 +513,8 @@
     pairs = [part] + [shift(part, flip_y=k) for k in (1, 2, 3)]
     part = (pairs[0] + pairs[1]) + (pairs[2] + pairs[3])
     pairs = [part] + [shift(part, flip_z=k) for k in (2, 4, 6)]
+    grad_input = finish(jnp.stack([y, c]).astype(jnp.int32), held, recv, own)
+    grad_input, pairs = lax.optimization_barrier((grad_input, pairs))
     part = (pairs[0] + pairs[1]) + (pairs[2] + pairs[3])
     other = shift(part, dc=1)
     total = jnp.where(c == 0, jnp.concatenate([part, other]), jnp.concatenate([other, part]))
@@ -519,7 +522,6 @@
     grad_w = jnp.concatenate([total[k * width : (k + 1) * width] for k in range(hid_all // 128)], axis=1)
     grad_b = total[width * (hid_all // 128), :width]
 
-    grad_input = finish(jnp.stack([y, c]).astype(jnp.int32), held, recv, own)
     return hidden_out, grad_input, grad_w, grad_b
 
 

time: 192 us -> 189 us (0.984)
  waiting for transfers between devices: 64.7 us -> 62.4 us
    ppermute x33, waiting for transfers between devices: 57.4 us -> 23.1 us  [shift(): return lax.ppermute(x, 'rows', pairs)]
    all_to_all x1, waiting for transfers between devices: 0.01 us -> 32 us  [local(): recv = lax.all_to_all(send, 'rows', split_axis=0, concat_axis=0, tiled=True)]
  transfers between devices with their start and end apart: 39 -> 39, of which waited for: 14 -> 13; matrix products, arithmetic and copies ran while one was open for 5% -> 5% of each run, Pallas kernels for 13% -> 14%
where the time goes in v11:
time: 189 us; the launch traced here: 188 us
  starting transfers between devices  65.5 us (35%)
  waiting for transfers between devices  62.4 us (33%)
  Pallas kernels  32 us (17%)
  between operations  14.6 us (8%)
  local copies, waits for them, and re-layouts  6.88 us (4%)
  other arithmetic  6.82 us (4%)
    ppermute x33, starting transfers between devices, shift(): return lax.ppermute(x, 'rows', pairs)  51 us
    all_to_all x1, waiting for transfers between devices, local(): recv = lax.all_to_all(send, 'rows', split_axis=0, concat_axis=0, tiled=True)  32 us
    ppermute x33, waiting for transfers between devices, shift(): return lax.ppermute(x, 'rows', pairs)  23.1 us
    all_to_all x1, starting transfers between devices, local(): recv = lax.all_to_all(send, 'rows', split_axis=0, concat_axis=0, tiled=True)  6.9 us
    pallas_call x3, Pallas kernels, pack(): pl.pallas_call(functools.partial(pack_kernel, first, count, len(sources)...  6.43 us
    all_to_all x1, waiting for transfers between devices, local(): lax.all_to_all(held, 'rows', 0, 0, tiled=True, axis_index_groups=along_z)  5.7 us
    pallas_call x1, Pallas kernels, mid(): pl.pallas_call(mid_kernel, grid=(nodes // chunk,), out_shape=(jax.ShapeDt...  4.99 us
    pallas_call x1, Pallas kernels, agg_remote(): pl.pallas_call(agg_remote_kernel, grid=(row_blocks // STEP,), out_shape=(...  4.9 us
  transfers between devices with their start and end apart: 39, of which 13 were waited for; matrix products, arithmetic and copies ran while one was open for 5% of the time, Pallas kernels for 14%

profile of v11, /device:TPU:1, one launch (start us, length us, event | category | flops | bytes accessed | tf_op | source)
XLA Modules:
  0.0 188.1 jit_solution(7631475147121380438)
XLA Ops:
  7.2 6.5 %collective-permute-start.4 = (bf16[64,2048]{1,0:T(8,128)(2,1)}, bf16[64,2048]{1,0:T(8,128)(2,1)S(1)}, u32[]{:S(2)}, u32[]{:S(2)}) collective-permute-start(bf16[64,2048]{1,0:T(8,128)(2,1)} %refs_1_.1), channel_id=1, source_target_pairs={{0,56},{4,60},{8,0},{12,4},{16,8},{20,12},{24,16},{28,20},{32,24},... | collective-permute-start | bytes 786440 | tf_op jit(solution)/shard_map/ppermute | solution.py:38
  17.4 4.6 %collective-permute-done.5.refs_3_ = bf16[64,2048]{1,0:T(8,128)(2,1)S(1)} collective-permute-done((bf16[64,2048]{1,0:T(8,128)(2,1)}, bf16[64,2048]{1,0:T(8,128)(2,1)S(1)}, u32[]{:S(2)}, u32[]{:S(2)}) %collective-permute-start.5) | collective-permute-done | bytes 262176 | tf_op jit(solution)/shard_map/ppermute | solution.py:38
  22.6 2.6 %collective-permute-start.10 = (bf16[64,2048]{1,0:T(8,128)(2,1)S(1)}, bf16[64,2048]{1,0:T(8,128)(2,1)S(1)}, u32[]{:S(2)}, u32[]{:S(2)}) collective-permute-start(bf16[64,2048]{1,0:T(8,128)(2,1)S(1)} %collective-permute-done.4.refs_2_), channel_id=1, source_target_pairs={{0,56},{4,60},{8,0},{12,4},{16,8},{20,12},{24,16},{28,20},{32,24},... | collective-permute-start | bytes 786440 | tf_op jit(solution)/shard_map/ppermute | solution.py:38
  25.3 3.8 %collective-permute-done.11.refs_2_ = bf16[64,2048]{1,0:T(8,128)(2,1)S(1)} collective-permute-done((bf16[64,2048]{1,0:T(8,128)(2,1)S(1)}, bf16[64,2048]{1,0:T(8,128)(2,1)S(1)}, u32[]{:S(2)}, u32[]{:S(2)}) %collective-permute-start.11) | collective-permute-done | bytes 262176 | tf_op jit(solution)/shard_map/ppermute | solution.py:38
  29.3 2.8 %collective-permute-start = (s32[4,16]{1,0:T(4,128)S(1)}, s32[4,16]{1,0:T(4,128)S(1)}, u32[]{:S(2)}, u32[]{:S(2)}) collective-permute-start(s32[4,16]{1,0:T(4,128)S(1)} %squeeze.15), channel_id=1, source_target_pairs={{0,4},{4,0},{8,12},{12,8},{16,20},{20,16},{24,28},{28,24},{32,36},... | collective-permute-start | bytes 776 | tf_op jit(solution)/shard_map/ppermute | solution.py:38
  32.2 3.0 %collective-permute-start.16 = (bf16[64,2048]{1,0:T(8,128)(2,1)S(1)}, bf16[64,2048]{1,0:T(8,128)(2,1)S(1)}, u32[]{:S(2)}, u32[]{:S(2)}) collective-permute-start(bf16[64,2048]{1,0:T(8,128)(2,1)S(1)} %collective-permute-done.10.refs_1_), channel_id=1, source_target_pairs={{0,56},{4,60},{8,0},{12,4},{16,8},{20,12},{24,16},{28,20},{32,24},... | collective-permute-start | bytes 786440 | tf_op jit(solution)/shard_map/ppermute | solution.py:38
  39.7 2.3 %collective-permute-done.2 = s32[2,16]{1,0:T(2,128)S(1)} collective-permute-done((s32[2,16]{1,0:T(2,128)S(1)}, s32[2,16]{1,0:T(2,128)S(1)}, u32[]{:S(2)}, u32[]{:S(2)}) %collective-permute-start.2) | collective-permute-done | bytes 160 | tf_op jit(solution)/shard_map/ppermute | solution.py:38
  42.7 2.2 %pack.3 = (bf16[2,6,64,128]{3,2,1,0:T(8,128)(2,1)}, bf16[2,6,64,128]{3,2,1,0:T(8,128)(2,1)}, bf16[2,6,64,128]{3,2,1,0:T(8,128)(2,1)}, bf16[2,6,64,128]{3,2,1,0:T(8,128)(2,1)}) custom-call(s32[128]{0:T(128)} %reshape.217.refs_0_, bf16[64,2048]{1,0:T(8,128)(2,1)} %refs_1_.1, bf16[64,2048]{1,0:T(8,128)(2,1)} %copy-done.26, bf16[64,2048]{1,0:T(8,128)(2,1)} %copy-done.27), custom_call_target="tpu_custom_call" | custom-call | bytes 3145728 | tf_op jit(solution)/shard_map/pack/pallas_call | solution.py:62
  45.2 2.2 %collective-permute-start.7 = (bf16[2,6,64,128]{3,2,1,0:T(8,128)(2,1)}, bf16[2,6,64,128]{3,2,1,0:T(8,128)(2,1)S(1)}, u32[]{:S(2)}, u32[]{:S(2)}) collective-permute-start(bf16[2,6,64,128]{3,2,1,0:T(8,128)(2,1)} %get-tuple-element.34), channel_id=1, source_target_pairs={{0,128},{4,132},{8,136},{12,140},{16,144},{20,148},{24,152},{28,15... | collective-permute-start | bytes 589832 | tf_op jit(solution)/shard_map/ppermute | solution.py:38
  49.6 2.0 %pack.4 = (bf16[2,4,64,128]{3,2,1,0:T(8,128)(2,1)}, bf16[2,4,64,128]{3,2,1,0:T(8,128)(2,1)}, bf16[2,4,64,128]{3,2,1,0:T(8,128)(2,1)}, bf16[2,4,64,128]{3,2,1,0:T(8,128)(2,1)}) custom-call(s32[128]{0:T(128)} %reshape.217.refs_0_, bf16[64,2048]{1,0:T(8,128)(2,1)} %copy-done.25, bf16[64,2048]{1,0:T(8,128)(2,1)} %copy-done.24, ...), custom_call_target="tpu_custom_call" | custom-call | bytes 3145728 | tf_op jit(solution)/shard_map/pack/pallas_call | solution.py:62
  52.5 4.2 %agg_local.1.refs_6_.local_ref = f32[64,2048]{1,0:T(8,128)} custom-call(s32[64]{0:T(128)} %reshape.216.cols_ref, bf16[64,2048]{1,0:T(8,128)(2,1)} %refs_1_.1, bf16[16,8,128,128]{3,2,1,0:T(8,128)(2,1)} %bitcast.26), custom_call_target="tpu_custom_call" | custom-call | flops 134217728 | bytes 3145728 | tf_op jit(solution)/shard_map/agg_local/pallas_call | solution.py:98
  58.0 2.2 %pack.5 = (bf16[2,6,64,128]{3,2,1,0:T(8,128)(2,1)}, bf16[2,6,64,128]{3,2,1,0:T(8,128)(2,1)}, bf16[2,6,64,128]{3,2,1,0:T(8,128)(2,1)}, bf16[2,6,64,128]{3,2,1,0:T(8,128)(2,1)}) custom-call(s32[128]{0:T(128)} %reshape.217.refs_0_, bf16[64,2048]{1,0:T(8,128)(2,1)} %copy-done.6, bf16[64,2048]{1,0:T(8,128)(2,1)} %copy-done.5, bf16[32,2048]{1,0:T(8,128)(2,1)} %copy-done.28, ...), custom_call_target="tpu_custom_call" | custom-call | bytes 3145728 | tf_op jit(solution)/shard_map/pack/pallas_call | solution.py:62
  60.3 2.1 %collective-permute-start.14 = (bf16[2,4,64,128]{3,2,1,0:T(8,128)(2,1)S(1)}, bf16[2,4,64,128]{3,2,1,0:T(8,128)(2,1)S(1)}, u32[]{:S(2)}, u32[]{:S(2)}) collective-permute-start(bf16[2,4,64,128]{3,2,1,0:T(8,128)(2,1)S(1)} %copy-done.31), channel_id=1, source_target_pairs={{0,192},{4,196},{8,200},{12,204},{16,208},{20,212},{24,216},{28,22... | collective-permute-start | bytes 393224 | tf_op jit(solution)/shard_map/ppermute | solution.py:38
  62.5 1.8 collective-permute-start.21
  64.3 2.0 %collective-permute-start.22 = (bf16[2,6,64,128]{3,2,1,0:T(8,128)(2,1)}, bf16[2,6,64,128]{3,2,1,0:T(8,128)(2,1)S(1)}, u32[]{:S(2)}, u32[]{:S(2)}) collective-permute-start(bf16[2,6,64,128]{3,2,1,0:T(8,128)(2,1)} %get-tuple-element.43), channel_id=1, source_target_pairs={{0,192},{4,196},{8,200},{12,204},{16,208},{20,212},{24,216},{28,22... | collective-permute-start | bytes 589832 | tf_op jit(solution)/shard_map/ppermute | solution.py:38
  66.5 4.5 %collective-permute-start.9 = (bf16[4,6,64,128]{3,2,1,0:T(8,128)(2,1)S(1)}, bf16[4,6,64,128]{3,2,1,0:T(8,128)(2,1)S(1)}, u32[]{:S(2)}, u32[]{:S(2)}) collective-permute-start(bf16[4,6,64,128]{3,2,1,0:T(8,128)(2,1)S(1)} %pad_maximum_fusion), channel_id=1, source_target_pairs={{0,4},{4,0},{8,12},{12,8},{16,20},{20,16},{24,28},{28,24},{32,36},... | collective-permute-start | bytes 1179656 | tf_op jit(solution)/shard_map/ppermute | solution.py:38
  71.3 3.6 %collective-permute-done.22.refs_13_ = bf16[2,6,64,128]{3,2,1,0:T(8,128)(2,1)S(1)} collective-permute-done((bf16[2,6,64,128]{3,2,1,0:T(8,128)(2,1)}, bf16[2,6,64,128]{3,2,1,0:T(8,128)(2,1)S(1)}, u32[]{:S(2)}, u32[]{:S(2)}) %collective-permute-start.22) | collective-permute-done | bytes 196640 | tf_op jit(solution)/shard_map/ppermute | solution.py:38
  75.0 2.5 %collective-permute-start.23 = (bf16[4,6,64,128]{3,2,1,0:T(8,128)(2,1)S(1)}, bf16[4,6,64,128]{3,2,1,0:T(8,128)(2,1)S(1)}, u32[]{:S(2)}, u32[]{:S(2)}) collective-permute-start(bf16[4,6,64,128]{3,2,1,0:T(8,128)(2,1)S(1)} %pad_maximum_fusion.1), channel_id=1, source_target_pairs={{0,4},{4,0},{8,12},{12,8},{16,20},{20,16},{24,28},{28,24},{32,36},... | collective-permute-start | bytes 1179656 | tf_op jit(solution)/shard_map/ppermute | solution.py:38
  81.2 4.9 %agg_remote.1 = (bf16[64,2048]{1,0:T(8,128)(2,1)}, s32[8,1,16]{2,1,0:T(1,128)}) custom-call(s32[64]{0:T(128)} %copy-done.30, s32[8,1,16]{2,1,0:T(1,128)} %copy.42.held_ref, bf16[16,8,128,128]{3,2,1,0:T(8,128)(2,1)} %bitcast.27, f32[64,2048]{1,0:T(8,128)} %agg_local.1.refs_6_.local_ref, bf16[2,6,64,128]{3,2,1,0:T(8,128)(2,1)} %get-tuple-element.32.refs_3_.refs_0_, ...), custom_call_target="tpu_custom_call" | custom-call | flops 134217728 | bytes 5242880 | tf_op jit(solution)/shard_map/agg_remote/pallas_call | solution.py:149
  90.4 3.3 %all-to-all-start = ((s32[8,1,16]{2,1,0:T(1,128)}), s32[8,1,16]{2,1,0:T(1,128)S(1)}, u32[]{:S(2)}, u32[]{:S(2)}) async-start(s32[8,1,16]{2,1,0:T(1,128)} %get-tuple-element.44), calls=%async_computation | async-start | bytes 8192 | tf_op jit(solution)/shard_map/all_to_all | solution.py:500
  94.4 5.7 %all-to-all-done._.held_ref = s32[8,1,16]{2,1,0:T(1,128)S(1)} async-done(((s32[8,1,16]{2,1,0:T(1,128)}), s32[8,1,16]{2,1,0:T(1,128)S(1)}, u32[]{:S(2)}, u32[]{:S(2)}) %all-to-all-start) | async-done | bytes 544 | tf_op jit(solution)/shard_map/all_to_all | solution.py:500
  102.3 5.0 %mid.1 = (bf16[64,2048]{1,0:T(8,128)(2,1)}, bf16[64,2048]{1,0:T(8,128)(2,1)}, f32[72,128]{1,0:T(8,128)}, f32[72,128]{1,0:T(8,128)}) custom-call(s32[2]{0:T(128)} %pad_add_fusion.2.me_ref, s32[8,1,16]{2,1,0:T(1,128)} %copy-done.1, bf16[64,2048]{1,0:T(8,128)(2,1)} %get-tuple-element.45.own_ref, bf16[64,2048]{1,0:T(8,128)(2,1)} %copy-done.21, ...), custom_call_target="tpu_custom_call" | custom-call | flops 402653184 | bytes 3145728 | tf_op jit(solution)/shard_map/mid/pallas_call | solution.py:244
  111.5 4.5 %back_remote.1._ = bf16[64,128,128]{2,1,0:T(8,128)(2,1)} custom-call(s32[64]{0:T(128)} %get-tuple-element.68.slots_ref, bf16[64,2048]{1,0:T(8,128)(2,1)} %get-tuple-element.47.g_ref, bf16[16,8,128,128]{3,2,1,0:T(8,128)(2,1)} %bitcast.28, f32[72,128]{1,0:T(8,128)} %copy-done.16), custom_call_target="tpu_custom_call" | custom-call | flops 134217728 | bytes 5242880 | tf_op jit(solution)/shard_map/back_remote/pallas_call | solution.py:312
  116.0 6.9 %all-to-all-start.1 = ((bf16[64,128,128]{2,1,0:T(8,128)(2,1)}), bf16[64,128,128]{2,1,0:T(8,128)(2,1)S(1)}, u32[]{:S(2)}, u32[]{:S(2)}) async-start(bf16[64,128,128]{2,1,0:T(8,128)(2,1)} %back_remote.1._), calls=%async_computation.1 | async-start | bytes 4194304 | tf_op jit(solution)/shard_map/all_to_all | solution.py:509
  122.9 3.9 %back_local.1.local_ref = f32[64,2048]{1,0:T(8,128)} custom-call(s32[64]{0:T(128)} %reshape.216.cols_ref, bf16[64,2048]{1,0:T(8,128)(2,1)} %get-tuple-element.47.g_ref, bf16[16,8,128,128]{3,2,1,0:T(8,128)(2,1)} %bitcast.29, bf16[64,128,128]{2,1,0:T(8,128)(2,1)} %back_remote.1._), custom_call_target="tpu_custom_call" | custom-call | flops 134217728 | bytes 3145728 | tf_op jit(solution)/shard_map/back_local/pallas_call | solution.py:351
  128.3 2.6 %collective-permute-start.30 = (f32[72,128]{1,0:T(8,128)S(1)}, f32[72,128]{1,0:T(8,128)S(1)}, u32[]{:S(2)}, u32[]{:S(2)}) collective-permute-start(f32[72,128]{1,0:T(8,128)S(1)} %add.112), channel_id=1, source_target_pairs={{0,128},{4,132},{8,136},{12,140},{16,144},{20,148},{24,152},{28,15... | collective-permute-start | bytes 110600 | tf_op jit(solution)/shard_map/ppermute | solution.py:38
  130.9 3.4 %collective-permute-done.30 = f32[72,128]{1,0:T(8,128)S(1)} collective-permute-done((f32[72,128]{1,0:T(8,128)S(1)}, f32[72,128]{1,0:T(8,128)S(1)}, u32[]{:S(2)}, u32[]{:S(2)}) %collective-permute-start.30) | collective-permute-done | bytes 36896 | tf_op jit(solution)/shard_map/ppermute | solution.py:38
  134.4 2.4 %collective-permute-done.31 = f32[72,128]{1,0:T(8,128)S(1)} collective-permute-done((f32[72,128]{1,0:T(8,128)S(1)}, f32[72,128]{1,0:T(8,128)S(1)}, u32[]{:S(2)}, u32[]{:S(2)}) %collective-permute-start.31) | collective-permute-done | bytes 36896 | tf_op jit(solution)/shard_map/ppermute | solution.py:38
  136.8 1.8 collective-permute-start.32
  138.6 2.7 %collective-permute-start.33 = (f32[72,128]{1,0:T(8,128)S(1)}, f32[72,128]{1,0:T(8,128)S(1)}, u32[]{:S(2)}, u32[]{:S(2)}) collective-permute-start(f32[72,128]{1,0:T(8,128)S(1)} %add_add_fusion.1), channel_id=1, source_target_pairs={{0,32},{4,36},{8,40},{12,44},{16,48},{20,52},{24,56},{28,60},{32,0... | collective-permute-start | bytes 110600 | tf_op jit(solution)/shard_map/ppermute | solution.py:38
  142.6 32.0 %all-to-all-done.1.recv_ref = bf16[64,128,128]{2,1,0:T(8,128)(2,1)S(1)} async-done(((bf16[64,128,128]{2,1,0:T(8,128)(2,1)}), bf16[64,128,128]{2,1,0:T(8,128)(2,1)S(1)}, u32[]{:S(2)}, u32[]{:S(2)}) %all-to-all-start.1) | async-done | bytes 2097184 | tf_op jit(solution)/shard_map/all_to_all | solution.py:509
  175.7 3.1 %finish.1 = f32[64,2048]{1,0:T(8,128)} custom-call(s32[2]{0:T(128)S(1)} %pad_add_fusion.3.place_ref, s32[8,1,16]{2,1,0:T(1,128)S(1)} %copy-done.2, bf16[64,128,128]{2,1,0:T(8,128)(2,1)S(1)} %all-to-all-done.1.recv_ref, f32[64,2048]{1,0:T(8,128)S(1)} %copy-done), custom_call_target="tpu_custom_call" | custom-call | flops 1048576 | bytes 4194304 | tf_op jit(solution)/shard_map/finish/pallas_call | solution.py:402
  (175 shorter events, 36.4 us)
Async XLA Ops:
  7.2 94.5 %all-gather.2.cloned.1.call-start = ((), (), s32[]{:S(2)}) async-start(), calls=%async_computation.2 | async-start | bytes 1556480 | tf_op jit(solution)/shard_map/all_gather | solution.py:487
  7.2 15.3 %collective-permute-start.4 = (bf16[64,2048]{1,0:T(8,128)(2,1)}, bf16[64,2048]{1,0:T(8,128)(2,1)S(1)}, u32[]{:S(2)}, u32[]{:S(2)}) collective-permute-start(bf16[64,2048]{1,0:T(8,128)(2,1)} %refs_1_.1), channel_id=1, source_target_pairs={{0,56},{4,60},{8,0},{12,4},{16,8},{20,12},{24,16},{28,20},{32,24},... | collective-permute-start | bytes 786440 | tf_op jit(solution)/shard_map/ppermute | solution.py:38
  13.7 8.3 %collective-permute-start.5 = (bf16[64,2048]{1,0:T(8,128)(2,1)}, bf16[64,2048]{1,0:T(8,128)(2,1)S(1)}, u32[]{:S(2)}, u32[]{:S(2)}) collective-permute-start(bf16[64,2048]{1,0:T(8,128)(2,1)} %refs_1_.1), channel_id=1, source_target_pairs={{0,8},{4,12},{8,16},{12,20},{16,24},{20,28},{24,32},{28,36},{32,40... | collective-permute-start | bytes 786440 | tf_op jit(solution)/shard_map/ppermute | solution.py:38
  22.0 7.1 %collective-permute-start.11 = (bf16[64,2048]{1,0:T(8,128)(2,1)S(1)}, bf16[64,2048]{1,0:T(8,128)(2,1)S(1)}, u32[]{:S(2)}, u32[]{:S(2)}) collective-permute-start(bf16[64,2048]{1,0:T(8,128)(2,1)S(1)} %collective-permute-done.5.refs_3_), channel_id=1, source_target_pairs={{0,8},{4,12},{8,16},{12,20},{16,24},{20,28},{24,32},{28,36},{32,40... | collective-permute-start | bytes 786440 | tf_op jit(solution)/shard_map/ppermute | solution.py:38
  22.6 9.6 %collective-permute-start.10 = (bf16[64,2048]{1,0:T(8,128)(2,1)S(1)}, bf16[64,2048]{1,0:T(8,128)(2,1)S(1)}, u32[]{:S(2)}, u32[]{:S(2)}) collective-permute-start(bf16[64,2048]{1,0:T(8,128)(2,1)S(1)} %collective-permute-done.4.refs_2_), channel_id=1, source_target_pairs={{0,56},{4,60},{8,0},{12,4},{16,8},{20,12},{24,16},{28,20},{32,24},... | collective-permute-start | bytes 786440 | tf_op jit(solution)/shard_map/ppermute | solution.py:38
  29.1 10.5 %collective-permute-start.17 = (bf16[64,2048]{1,0:T(8,128)(2,1)S(1)}, bf16[64,2048]{1,0:T(8,128)(2,1)S(1)}, u32[]{:S(2)}, u32[]{:S(2)}) collective-permute-start(bf16[64,2048]{1,0:T(8,128)(2,1)S(1)} %collective-permute-done.11.refs_2_), channel_id=1, source_target_pairs={{0,8},{4,12},{8,16},{12,20},{16,24},{20,28},{24,32},{28,36},{32,40... | collective-permute-start | bytes 786440 | tf_op jit(solution)/shard_map/ppermute | solution.py:38
  29.3 5.9 %collective-permute-start = (s32[4,16]{1,0:T(4,128)S(1)}, s32[4,16]{1,0:T(4,128)S(1)}, u32[]{:S(2)}, u32[]{:S(2)}) collective-permute-start(s32[4,16]{1,0:T(4,128)S(1)} %squeeze.15), channel_id=1, source_target_pairs={{0,4},{4,0},{8,12},{12,8},{16,20},{20,16},{24,28},{28,24},{32,36},... | collective-permute-start | bytes 776 | tf_op jit(solution)/shard_map/ppermute | solution.py:38
  32.2 16.7 %collective-permute-start.16 = (bf16[64,2048]{1,0:T(8,128)(2,1)S(1)}, bf16[64,2048]{1,0:T(8,128)(2,1)S(1)}, u32[]{:S(2)}, u32[]{:S(2)}) collective-permute-start(bf16[64,2048]{1,0:T(8,128)(2,1)S(1)} %collective-permute-done.10.refs_1_), channel_id=1, source_target_pairs={{0,56},{4,60},{8,0},{12,4},{16,8},{20,12},{24,16},{28,20},{32,24},... | collective-permute-start | bytes 786440 | tf_op jit(solution)/shard_map/ppermute | solution.py:38
  39.6 11.9 %collective-permute-start.18 = (bf16[32,2048]{1,0:T(8,128)(2,1)S(1)}, bf16[32,2048]{1,0:T(8,128)(2,1)S(1)}, u32[]{:S(2)}, u32[]{:S(2)}) collective-permute-start(bf16[32,2048]{1,0:T(8,128)(2,1)S(1)} %slice.132), channel_id=1, source_target_pairs={{0,8},{4,12},{8,16},{12,20},{16,24},{20,28},{24,32},{28,36},{32,40... | collective-permute-start | bytes 393224 | tf_op jit(solution)/shard_map/ppermute | solution.py:38
  44.9 15.4 %collective-permute-start.6 = (bf16[2,6,64,128]{3,2,1,0:T(8,128)(2,1)}, bf16[2,6,64,128]{3,2,1,0:T(8,128)(2,1)S(1)}, u32[]{:S(2)}, u32[]{:S(2)}) collective-permute-start(bf16[2,6,64,128]{3,2,1,0:T(8,128)(2,1)} %get-tuple-element.33), channel_id=1, source_target_pairs={{0,64},{4,68},{8,72},{12,76},{16,80},{20,84},{24,88},{28,92},{32,9... | collective-permute-start | bytes 589832 | tf_op jit(solution)/shard_map/ppermute | solution.py:38
  45.2 17.2 %collective-permute-start.7 = (bf16[2,6,64,128]{3,2,1,0:T(8,128)(2,1)}, bf16[2,6,64,128]{3,2,1,0:T(8,128)(2,1)S(1)}, u32[]{:S(2)}, u32[]{:S(2)}) collective-permute-start(bf16[2,6,64,128]{3,2,1,0:T(8,128)(2,1)} %get-tuple-element.34), channel_id=1, source_target_pairs={{0,128},{4,132},{8,136},{12,140},{16,144},{20,148},{24,152},{28,15... | collective-permute-start | bytes 589832 | tf_op jit(solution)/shard_map/ppermute | solution.py:38
  47.4 15.1 %collective-permute-start.8 = (bf16[2,6,64,128]{3,2,1,0:T(8,128)(2,1)}, bf16[2,6,64,128]{3,2,1,0:T(8,128)(2,1)S(1)}, u32[]{:S(2)}, u32[]{:S(2)}) collective-permute-start(bf16[2,6,64,128]{3,2,1,0:T(8,128)(2,1)} %get-tuple-element.35), channel_id=1, source_target_pairs={{0,192},{4,196},{8,200},{12,204},{16,208},{20,212},{24,216},{28,22... | collective-permute-start | bytes 589832 | tf_op jit(solution)/shard_map/ppermute | solution.py:38
  48.9 7.9 %collective-permute-start.19 = (bf16[32,2048]{1,0:T(8,128)(2,1)S(1)}, bf16[32,2048]{1,0:T(8,128)(2,1)S(1)}, u32[]{:S(2)}, u32[]{:S(2)}) collective-permute-start(bf16[32,2048]{1,0:T(8,128)(2,1)S(1)} %slice.133), channel_id=1, source_target_pairs={{0,56},{4,60},{8,0},{12,4},{16,8},{20,12},{24,16},{28,20},{32,24},... | collective-permute-start | bytes 393224 | tf_op jit(solution)/shard_map/ppermute | solution.py:38
  51.6 12.8 %collective-permute-start.12 = (bf16[2,4,64,128]{3,2,1,0:T(8,128)(2,1)}, bf16[2,4,64,128]{3,2,1,0:T(8,128)(2,1)S(1)}, u32[]{:S(2)}, u32[]{:S(2)}) collective-permute-start(bf16[2,4,64,128]{3,2,1,0:T(8,128)(2,1)} %get-tuple-element.37), channel_id=1, source_target_pairs={{0,64},{4,68},{8,72},{12,76},{16,80},{20,84},{24,88},{28,92},{32,9... | collective-permute-start | bytes 393224 | tf_op jit(solution)/shard_map/ppermute | solution.py:38
  56.8 9.7 %collective-permute-start.13 = (bf16[2,4,64,128]{3,2,1,0:T(8,128)(2,1)S(1)}, bf16[2,4,64,128]{3,2,1,0:T(8,128)(2,1)S(1)}, u32[]{:S(2)}, u32[]{:S(2)}) collective-permute-start(bf16[2,4,64,128]{3,2,1,0:T(8,128)(2,1)S(1)} %copy-done.32), channel_id=1, source_target_pairs={{0,128},{4,132},{8,136},{12,140},{16,144},{20,148},{24,152},{28,15... | collective-permute-start | bytes 393224 | tf_op jit(solution)/shard_map/ppermute | solution.py:38
  60.3 10.8 %collective-permute-start.14 = (bf16[2,4,64,128]{3,2,1,0:T(8,128)(2,1)S(1)}, bf16[2,4,64,128]{3,2,1,0:T(8,128)(2,1)S(1)}, u32[]{:S(2)}, u32[]{:S(2)}) collective-permute-start(bf16[2,4,64,128]{3,2,1,0:T(8,128)(2,1)S(1)} %copy-done.31), channel_id=1, source_target_pairs={{0,192},{4,196},{8,200},{12,204},{16,208},{20,212},{24,216},{28,22... | collective-permute-start | bytes 393224 | tf_op jit(solution)/shard_map/ppermute | solution.py:38
  62.4 8.7 %collective-permute-start.20 = (bf16[2,6,64,128]{3,2,1,0:T(8,128)(2,1)}, bf16[2,6,64,128]{3,2,1,0:T(8,128)(2,1)S(1)}, u32[]{:S(2)}, u32[]{:S(2)}) collective-permute-start(bf16[2,6,64,128]{3,2,1,0:T(8,128)(2,1)} %get-tuple-element.41), channel_id=1, source_target_pairs={{0,64},{4,68},{8,72},{12,76},{16,80},{20,84},{24,88},{28,92},{32,9... | collective-permute-start | bytes 589832 | tf_op jit(solution)/shard_map/ppermute | solution.py:38
  62.5 8.8 %collective-permute-start.21 = (bf16[2,6,64,128]{3,2,1,0:T(8,128)(2,1)}, bf16[2,6,64,128]{3,2,1,0:T(8,128)(2,1)S(1)}, u32[]{:S(2)}, u32[]{:S(2)}) collective-permute-start(bf16[2,6,64,128]{3,2,1,0:T(8,128)(2,1)} %get-tuple-element.42), channel_id=1, source_target_pairs={{0,128},{4,132},{8,136},{12,140},{16,144},{20,148},{24,152},{28,15... | collective-permute-start | bytes 589832 | tf_op jit(solution)/shard_map/ppermute | solution.py:38
  64.3 10.6 %collective-permute-start.22 = (bf16[2,6,64,128]{3,2,1,0:T(8,128)(2,1)}, bf16[2,6,64,128]{3,2,1,0:T(8,128)(2,1)S(1)}, u32[]{:S(2)}, u32[]{:S(2)}) collective-permute-start(bf16[2,6,64,128]{3,2,1,0:T(8,128)(2,1)} %get-tuple-element.43), channel_id=1, source_target_pairs={{0,192},{4,196},{8,200},{12,204},{16,208},{20,212},{24,216},{28,22... | collective-permute-start | bytes 589832 | tf_op jit(solution)/shard_map/ppermute | solution.py:38
  66.5 13.3 %collective-permute-start.9 = (bf16[4,6,64,128]{3,2,1,0:T(8,128)(2,1)S(1)}, bf16[4,6,64,128]{3,2,1,0:T(8,128)(2,1)S(1)}, u32[]{:S(2)}, u32[]{:S(2)}) collective-permute-start(bf16[4,6,64,128]{3,2,1,0:T(8,128)(2,1)S(1)} %pad_maximum_fusion), channel_id=1, source_target_pairs={{0,4},{4,0},{8,12},{12,8},{16,20},{20,16},{24,28},{28,24},{32,36},... | collective-permute-start | bytes 1179656 | tf_op jit(solution)/shard_map/ppermute | solution.py:38
  75.0 5.2 %collective-permute-start.23 = (bf16[4,6,64,128]{3,2,1,0:T(8,128)(2,1)S(1)}, bf16[4,6,64,128]{3,2,1,0:T(8,128)(2,1)S(1)}, u32[]{:S(2)}, u32[]{:S(2)}) collective-permute-start(bf16[4,6,64,128]{3,2,1,0:T(8,128)(2,1)S(1)} %pad_maximum_fusion.1), channel_id=1, source_target_pairs={{0,4},{4,0},{8,12},{12,8},{16,20},{20,16},{24,28},{28,24},{32,36},... | collective-permute-start | bytes 1179656 | tf_op jit(solution)/shard_map/ppermute | solution.py:38
  86.1 13.9 %collective-permute-start.24 = (bf16[64,2048]{1,0:T(8,128)(2,1)}, bf16[64,2048]{1,0:T(8,128)(2,1)S(1)}, u32[]{:S(2)}, u32[]{:S(2)}) collective-permute-start(bf16[64,2048]{1,0:T(8,128)(2,1)} %get-tuple-element.45.own_ref), channel_id=1, source_target_pairs={{0,1},{1,2},{2,3},{3,0},{4,5},{5,6},{6,7},{7,4},{8,9},{9,10},{10,1... | collective-permute-start | bytes 786440 | tf_op jit(solution)/shard_map/ppermute | solution.py:496
  87.4 12.7 %collective-permute-start.25 = (bf16[64,2048]{1,0:T(8,128)(2,1)}, bf16[64,2048]{1,0:T(8,128)(2,1)S(1)}, u32[]{:S(2)}, u32[]{:S(2)}) collective-permute-start(bf16[64,2048]{1,0:T(8,128)(2,1)} %get-tuple-element.45.own_ref), channel_id=1, source_target_pairs={{0,3},{1,0},{2,1},{3,2},{4,7},{5,4},{6,5},{7,6},{8,11},{9,8},{10,9... | collective-permute-start | bytes 786440 | tf_op jit(solution)/shard_map/ppermute | solution.py:496
  88.9 12.7 %collective-permute-start.26 = (bf16[64,2048]{1,0:T(8,128)(2,1)}, bf16[64,2048]{1,0:T(8,128)(2,1)S(1)}, u32[]{:S(2)}, u32[]{:S(2)}) collective-permute-start(bf16[64,2048]{1,0:T(8,128)(2,1)} %get-tuple-element.45.own_ref), channel_id=1, source_target_pairs={{0,2},{1,3},{2,0},{3,1},{4,6},{5,7},{6,4},{7,5},{8,10},{9,11},{10,... | collective-permute-start | bytes 786440 | tf_op jit(solution)/shard_map/ppermute | solution.py:496
  90.4 9.7 %all-to-all-start = ((s32[8,1,16]{2,1,0:T(1,128)}), s32[8,1,16]{2,1,0:T(1,128)S(1)}, u32[]{:S(2)}, u32[]{:S(2)}) async-start(s32[8,1,16]{2,1,0:T(1,128)} %get-tuple-element.44), calls=%async_computation | async-start | bytes 8192 | tf_op jit(solution)/shard_map/all_to_all | solution.py:500
  110.6 5.4 %collective-permute-start.28 = (f32[72,128]{1,0:T(8,128)S(1)}, f32[72,128]{1,0:T(8,128)S(1)}, u32[]{:S(2)}, u32[]{:S(2)}) collective-permute-start(f32[72,128]{1,0:T(8,128)S(1)} %add.111._), channel_id=1, source_target_pairs={{0,8},{4,12},{8,0},{12,4},{16,24},{20,28},{24,16},{28,20},{32,40},... | collective-permute-start | bytes 110600 | tf_op jit(solution)/shard_map/ppermute | solution.py:38
  116.0 58.6 %all-to-all-start.1 = ((bf16[64,128,128]{2,1,0:T(8,128)(2,1)}), bf16[64,128,128]{2,1,0:T(8,128)(2,1)S(1)}, u32[]{:S(2)}, u32[]{:S(2)}) async-start(bf16[64,128,128]{2,1,0:T(8,128)(2,1)} %back_remote.1._), calls=%async_computation.1 | async-start | bytes 4194304 | tf_op jit(solution)/shard_map/all_to_all | solution.py:509
  128.3 6.0 %collective-permute-start.30 = (f32[72,128]{1,0:T(8,128)S(1)}, f32[72,128]{1,0:T(8,128)S(1)}, u32[]{:S(2)}, u32[]{:S(2)}) collective-permute-start(f32[72,128]{1,0:T(8,128)S(1)} %add.112), channel_id=1, source_target_pairs={{0,128},{4,132},{8,136},{12,140},{16,144},{20,148},{24,152},{28,15... | collective-permute-start | bytes 110600 | tf_op jit(solution)/shard_map/ppermute | solution.py:38
  130.9 5.9 %collective-permute-start.31 = (f32[72,128]{1,0:T(8,128)S(1)}, f32[72,128]{1,0:T(8,128)S(1)}, u32[]{:S(2)}, u32[]{:S(2)}) collective-permute-start(f32[72,128]{1,0:T(8,128)S(1)} %add.112), channel_id=1, source_target_pairs={{0,192},{4,196},{8,200},{12,204},{16,208},{20,212},{24,216},{28,22... | collective-permute-start | bytes 110600 | tf_op jit(solution)/shard_map/ppermute | solution.py:38
  136.8 42.0 %collective-permute-start.32 = (f32[72,128]{1,0:T(8,128)S(1)}, f32[72,128]{1,0:T(8,128)S(1)}, u32[]{:S(2)}, u32[]{:S(2)}) collective-permute-start(f32[72,128]{1,0:T(8,128)S(1)} %add_add_fusion.1), channel_id=1, source_target_pairs={{0,16},{4,20},{8,24},{12,28},{16,0},{20,4},{24,8},{28,12},{32,48},... | collective-permute-start | bytes 110600 | tf_op jit(solution)/shard_map/ppermute | solution.py:38
  138.6 40.1 %collective-permute-start.33 = (f32[72,128]{1,0:T(8,128)S(1)}, f32[72,128]{1,0:T(8,128)S(1)}, u32[]{:S(2)}, u32[]{:S(2)}) collective-permute-start(f32[72,128]{1,0:T(8,128)S(1)} %add_add_fusion.1), channel_id=1, source_target_pairs={{0,32},{4,36},{8,40},{12,44},{16,48},{20,52},{24,56},{28,60},{32,0... | collective-permute-start | bytes 110600 | tf_op jit(solution)/shard_map/ppermute | solution.py:38
  141.3 37.5 %collective-permute-start.34 = (f32[72,128]{1,0:T(8,128)S(1)}, f32[72,128]{1,0:T(8,128)S(1)}, u32[]{:S(2)}, u32[]{:S(2)}) collective-permute-start(f32[72,128]{1,0:T(8,128)S(1)} %add_add_fusion.1), channel_id=1, source_target_pairs={{0,48},{4,52},{8,56},{12,60},{16,32},{20,36},{24,40},{28,44},{32,1... | collective-permute-start | bytes 110600 | tf_op jit(solution)/shard_map/ppermute | solution.py:38
  (40 other events, 386.2 us)
Sparse Core Ops, SparseCore 0:
  16.3 25.5 all-gather.1

commit v12 on v11

--- a/solution.py
+++ b/solution.py
@@ -73,7 +73,7 @@
     return lax.dot_general(a, b, ((dims[:1], dims[1:]), ((), ())), preferred_element_type=F32)
 
 
-STEP = 4
+STEP = 8
 
 
 def agg_local_kernel(cols_ref, feats_ref, tiles_ref, out_ref):

time: 189 us -> 186 us (0.984)
  Pallas kernels: 32 us -> 28 us
  starting transfers between devices: 65.5 us -> 67.4 us
  transfers between devices with their start and end apart: 39 -> 39, of which waited for: 13 -> 13; matrix products, arithmetic and copies ran while one was open for 5% -> 5% of each run, Pallas kernels for 14% -> 12%
where the time goes in v12:
time: 186 us; the launch traced here: 185 us
  starting transfers between devices  67.4 us (36%)
  waiting for transfers between devices  61.5 us (33%)
  Pallas kernels  28 us (15%)
  between operations  14.6 us (8%)
  local copies, waits for them, and re-layouts  6.88 us (4%)
  other arithmetic  6.82 us (4%)
    ppermute x33, starting transfers between devices, shift(): return lax.ppermute(x, 'rows', pairs)  52.7 us
    all_to_all x1, waiting for transfers between devices, local(): recv = lax.all_to_all(send, 'rows', split_axis=0, concat_axis=0, tiled=True)  32.4 us
    ppermute x33, waiting for transfers between devices, shift(): return lax.ppermute(x, 'rows', pairs)  21.9 us
    all_to_all x1, starting transfers between devices, local(): recv = lax.all_to_all(send, 'rows', split_axis=0, concat_axis=0, tiled=True)  7.11 us
    pallas_call x3, Pallas kernels, pack(): pl.pallas_call(functools.partial(pack_kernel, first, count, len(sources)...  6.43 us
    all_to_all x1, waiting for transfers between devices, local(): lax.all_to_all(held, 'rows', 0, 0, tiled=True, axis_index_groups=along_z)  5.7 us
    pallas_call x1, Pallas kernels, mid(): pl.pallas_call(mid_kernel, grid=(nodes // chunk,), out_shape=(jax.ShapeDt...  4.99 us
    ppermute x3, starting transfers between devices, local(): lax.ppermute(agg, 'feat', [(k, (k + s) % fpeers) for k in range(fpeers)])  4.22 us
  transfers between devices with their start and end apart: 39, of which 13 were waited for; matrix products, arithmetic and copies ran while one was open for 5% of the time, Pallas kernels for 12%

profile of v12, /device:TPU:1, one launch (start us, length us, event | category | flops | bytes accessed | tf_op | source)
XLA Modules:
  0.0 185.2 jit_solution(1801988341907410556)
XLA Ops:
  7.2 6.5 %collective-permute-start.4 = (bf16[64,2048]{1,0:T(8,128)(2,1)}, bf16[64,2048]{1,0:T(8,128)(2,1)S(1)}, u32[]{:S(2)}, u32[]{:S(2)}) collective-permute-start(bf16[64,2048]{1,0:T(8,128)(2,1)} %refs_1_.1), channel_id=1, source_target_pairs={{0,56},{4,60},{8,0},{12,4},{16,8},{20,12},{24,16},{28,20},{32,24},... | collective-permute-start | bytes 786440 | tf_op jit(solution)/shard_map/ppermute | solution.py:38
  14.5 1.7 fusion.1
  17.4 4.6 %collective-permute-done.5.refs_3_ = bf16[64,2048]{1,0:T(8,128)(2,1)S(1)} collective-permute-done((bf16[64,2048]{1,0:T(8,128)(2,1)}, bf16[64,2048]{1,0:T(8,128)(2,1)S(1)}, u32[]{:S(2)}, u32[]{:S(2)}) %collective-permute-start.5) | collective-permute-done | bytes 262176 | tf_op jit(solution)/shard_map/ppermute | solution.py:38
  22.6 2.6 %collective-permute-start.10 = (bf16[64,2048]{1,0:T(8,128)(2,1)S(1)}, bf16[64,2048]{1,0:T(8,128)(2,1)S(1)}, u32[]{:S(2)}, u32[]{:S(2)}) collective-permute-start(bf16[64,2048]{1,0:T(8,128)(2,1)S(1)} %collective-permute-done.4.refs_2_), channel_id=1, source_target_pairs={{0,56},{4,60},{8,0},{12,4},{16,8},{20,12},{24,16},{28,20},{32,24},... | collective-permute-start | bytes 786440 | tf_op jit(solution)/shard_map/ppermute | solution.py:38
  25.3 3.8 %collective-permute-done.11.refs_2_ = bf16[64,2048]{1,0:T(8,128)(2,1)S(1)} collective-permute-done((bf16[64,2048]{1,0:T(8,128)(2,1)S(1)}, bf16[64,2048]{1,0:T(8,128)(2,1)S(1)}, u32[]{:S(2)}, u32[]{:S(2)}) %collective-permute-start.11) | collective-permute-done | bytes 262176 | tf_op jit(solution)/shard_map/ppermute | solution.py:38
  29.3 2.8 %collective-permute-start = (s32[4,16]{1,0:T(4,128)S(1)}, s32[4,16]{1,0:T(4,128)S(1)}, u32[]{:S(2)}, u32[]{:S(2)}) collective-permute-start(s32[4,16]{1,0:T(4,128)S(1)} %squeeze.15), channel_id=1, source_target_pairs={{0,4},{4,0},{8,12},{12,8},{16,20},{20,16},{24,28},{28,24},{32,36},... | collective-permute-start | bytes 776 | tf_op jit(solution)/shard_map/ppermute | solution.py:38
  32.2 3.0 %collective-permute-start.16 = (bf16[64,2048]{1,0:T(8,128)(2,1)S(1)}, bf16[64,2048]{1,0:T(8,128)(2,1)S(1)}, u32[]{:S(2)}, u32[]{:S(2)}) collective-permute-start(bf16[64,2048]{1,0:T(8,128)(2,1)S(1)} %collective-permute-done.10.refs_1_), channel_id=1, source_target_pairs={{0,56},{4,60},{8,0},{12,4},{16,8},{20,12},{24,16},{28,20},{32,24},... | collective-permute-start | bytes 786440 | tf_op jit(solution)/shard_map/ppermute | solution.py:38
  39.7 2.3 %collective-permute-done.2 = s32[2,16]{1,0:T(2,128)S(1)} collective-permute-done((s32[2,16]{1,0:T(2,128)S(1)}, s32[2,16]{1,0:T(2,128)S(1)}, u32[]{:S(2)}, u32[]{:S(2)}) %collective-permute-start.2) | collective-permute-done | bytes 160 | tf_op jit(solution)/shard_map/ppermute | solution.py:38
  42.7 2.2 %pack.3 = (bf16[2,6,64,128]{3,2,1,0:T(8,128)(2,1)}, bf16[2,6,64,128]{3,2,1,0:T(8,128)(2,1)}, bf16[2,6,64,128]{3,2,1,0:T(8,128)(2,1)}, bf16[2,6,64,128]{3,2,1,0:T(8,128)(2,1)}) custom-call(s32[128]{0:T(128)} %reshape.217.refs_0_, bf16[64,2048]{1,0:T(8,128)(2,1)} %refs_1_.1, bf16[64,2048]{1,0:T(8,128)(2,1)} %copy-done.26, bf16[64,2048]{1,0:T(8,128)(2,1)} %copy-done.27), custom_call_target="tpu_custom_call" | custom-call | bytes 3145728 | tf_op jit(solution)/shard_map/pack/pallas_call | solution.py:62
  45.2 2.2 %collective-permute-start.7 = (bf16[2,6,64,128]{3,2,1,0:T(8,128)(2,1)}, bf16[2,6,64,128]{3,2,1,0:T(8,128)(2,1)S(1)}, u32[]{:S(2)}, u32[]{:S(2)}) collective-permute-start(bf16[2,6,64,128]{3,2,1,0:T(8,128)(2,1)} %get-tuple-element.34), channel_id=1, source_target_pairs={{0,128},{4,132},{8,136},{12,140},{16,144},{20,148},{24,152},{28,15... | collective-permute-start | bytes 589832 | tf_op jit(solution)/shard_map/ppermute | solution.py:38
  49.6 2.0 %pack.4 = (bf16[2,4,64,128]{3,2,1,0:T(8,128)(2,1)}, bf16[2,4,64,128]{3,2,1,0:T(8,128)(2,1)}, bf16[2,4,64,128]{3,2,1,0:T(8,128)(2,1)}, bf16[2,4,64,128]{3,2,1,0:T(8,128)(2,1)}) custom-call(s32[128]{0:T(128)} %reshape.217.refs_0_, bf16[64,2048]{1,0:T(8,128)(2,1)} %copy-done.25, bf16[64,2048]{1,0:T(8,128)(2,1)} %copy-done.24, ...), custom_call_target="tpu_custom_call" | custom-call | bytes 3145728 | tf_op jit(solution)/shard_map/pack/pallas_call | solution.py:62
  52.5 3.0 %agg_local.1.refs_6_.local_ref = f32[64,2048]{1,0:T(8,128)} custom-call(s32[64]{0:T(128)} %reshape.216.cols_ref, bf16[64,2048]{1,0:T(8,128)(2,1)} %refs_1_.1, bf16[16,8,128,128]{3,2,1,0:T(8,128)(2,1)} %bitcast.26), custom_call_target="tpu_custom_call" | custom-call | flops 134217728 | bytes 3145728 | tf_op jit(solution)/shard_map/agg_local/pallas_call | solution.py:98
  56.9 2.2 %pack.5 = (bf16[2,6,64,128]{3,2,1,0:T(8,128)(2,1)}, bf16[2,6,64,128]{3,2,1,0:T(8,128)(2,1)}, bf16[2,6,64,128]{3,2,1,0:T(8,128)(2,1)}, bf16[2,6,64,128]{3,2,1,0:T(8,128)(2,1)}) custom-call(s32[128]{0:T(128)} %reshape.217.refs_0_, bf16[64,2048]{1,0:T(8,128)(2,1)} %copy-done.6, bf16[64,2048]{1,0:T(8,128)(2,1)} %copy-done.5, bf16[32,2048]{1,0:T(8,128)(2,1)} %copy-done.28, ...), custom_call_target="tpu_custom_call" | custom-call | bytes 3145728 | tf_op jit(solution)/shard_map/pack/pallas_call | solution.py:62
  59.1 2.1 %collective-permute-start.14 = (bf16[2,4,64,128]{3,2,1,0:T(8,128)(2,1)S(1)}, bf16[2,4,64,128]{3,2,1,0:T(8,128)(2,1)S(1)}, u32[]{:S(2)}, u32[]{:S(2)}) collective-permute-start(bf16[2,4,64,128]{3,2,1,0:T(8,128)(2,1)S(1)} %copy-done.31), channel_id=1, source_target_pairs={{0,192},{4,196},{8,200},{12,204},{16,208},{20,212},{24,216},{28,22... | collective-permute-start | bytes 393224 | tf_op jit(solution)/shard_map/ppermute | solution.py:38
  61.4 1.8 collective-permute-start.21
  63.2 2.0 %collective-permute-start.22 = (bf16[2,6,64,128]{3,2,1,0:T(8,128)(2,1)}, bf16[2,6,64,128]{3,2,1,0:T(8,128)(2,1)S(1)}, u32[]{:S(2)}, u32[]{:S(2)}) collective-permute-start(bf16[2,6,64,128]{3,2,1,0:T(8,128)(2,1)} %get-tuple-element.43), channel_id=1, source_target_pairs={{0,192},{4,196},{8,200},{12,204},{16,208},{20,212},{24,216},{28,22... | collective-permute-start | bytes 589832 | tf_op jit(solution)/shard_map/ppermute | solution.py:38
  65.3 4.5 %collective-permute-start.9 = (bf16[4,6,64,128]{3,2,1,0:T(8,128)(2,1)S(1)}, bf16[4,6,64,128]{3,2,1,0:T(8,128)(2,1)S(1)}, u32[]{:S(2)}, u32[]{:S(2)}) collective-permute-start(bf16[4,6,64,128]{3,2,1,0:T(8,128)(2,1)S(1)} %pad_maximum_fusion), channel_id=1, source_target_pairs={{0,4},{4,0},{8,12},{12,8},{16,20},{20,16},{24,28},{28,24},{32,36},... | collective-permute-start | bytes 1179656 | tf_op jit(solution)/shard_map/ppermute | solution.py:38
  70.2 3.6 %collective-permute-done.22.refs_13_ = bf16[2,6,64,128]{3,2,1,0:T(8,128)(2,1)S(1)} collective-permute-done((bf16[2,6,64,128]{3,2,1,0:T(8,128)(2,1)}, bf16[2,6,64,128]{3,2,1,0:T(8,128)(2,1)S(1)}, u32[]{:S(2)}, u32[]{:S(2)}) %collective-permute-start.22) | collective-permute-done | bytes 196640 | tf_op jit(solution)/shard_map/ppermute | solution.py:38
  73.8 2.5 %collective-permute-start.23 = (bf16[4,6,64,128]{3,2,1,0:T(8,128)(2,1)S(1)}, bf16[4,6,64,128]{3,2,1,0:T(8,128)(2,1)S(1)}, u32[]{:S(2)}, u32[]{:S(2)}) collective-permute-start(bf16[4,6,64,128]{3,2,1,0:T(8,128)(2,1)S(1)} %pad_maximum_fusion.1), channel_id=1, source_target_pairs={{0,4},{4,0},{8,12},{12,8},{16,20},{20,16},{24,28},{28,24},{32,36},... | collective-permute-start | bytes 1179656 | tf_op jit(solution)/shard_map/ppermute | solution.py:38
  80.1 3.8 %agg_remote.1 = (bf16[64,2048]{1,0:T(8,128)(2,1)}, s32[8,1,16]{2,1,0:T(1,128)}) custom-call(s32[64]{0:T(128)} %copy-done.30, s32[8,1,16]{2,1,0:T(1,128)} %copy.42.held_ref, bf16[16,8,128,128]{3,2,1,0:T(8,128)(2,1)} %bitcast.27, f32[64,2048]{1,0:T(8,128)} %agg_local.1.refs_6_.local_ref, bf16[2,6,64,128]{3,2,1,0:T(8,128)(2,1)} %get-tuple-element.32.refs_3_.refs_0_, ...), custom_call_target="tpu_custom_call" | custom-call | flops 134217728 | bytes 5242880 | tf_op jit(solution)/shard_map/agg_remote/pallas_call | solution.py:149
  88.1 3.3 %all-to-all-start = ((s32[8,1,16]{2,1,0:T(1,128)}), s32[8,1,16]{2,1,0:T(1,128)S(1)}, u32[]{:S(2)}, u32[]{:S(2)}) async-start(s32[8,1,16]{2,1,0:T(1,128)} %get-tuple-element.44), calls=%async_computation | async-start | bytes 8192 | tf_op jit(solution)/shard_map/all_to_all | solution.py:500
  92.1 5.7 %all-to-all-done._.held_ref = s32[8,1,16]{2,1,0:T(1,128)S(1)} async-done(((s32[8,1,16]{2,1,0:T(1,128)}), s32[8,1,16]{2,1,0:T(1,128)S(1)}, u32[]{:S(2)}, u32[]{:S(2)}) %all-to-all-start) | async-done | bytes 544 | tf_op jit(solution)/shard_map/all_to_all | solution.py:500
  100.1 5.0 %mid.1 = (bf16[64,2048]{1,0:T(8,128)(2,1)}, bf16[64,2048]{1,0:T(8,128)(2,1)}, f32[72,128]{1,0:T(8,128)}, f32[72,128]{1,0:T(8,128)}) custom-call(s32[2]{0:T(128)} %pad_add_fusion.2.me_ref, s32[8,1,16]{2,1,0:T(1,128)} %copy-done.1, bf16[64,2048]{1,0:T(8,128)(2,1)} %get-tuple-element.45.own_ref, bf16[64,2048]{1,0:T(8,128)(2,1)} %copy-done.21, ...), custom_call_target="tpu_custom_call" | custom-call | flops 402653184 | bytes 3145728 | tf_op jit(solution)/shard_map/mid/pallas_call | solution.py:244
  109.2 3.6 %back_remote.1._ = bf16[64,128,128]{2,1,0:T(8,128)(2,1)} custom-call(s32[64]{0:T(128)} %get-tuple-element.68.slots_ref, bf16[64,2048]{1,0:T(8,128)(2,1)} %get-tuple-element.47.g_ref, bf16[16,8,128,128]{3,2,1,0:T(8,128)(2,1)} %bitcast.28, f32[72,128]{1,0:T(8,128)} %copy-done.16), custom_call_target="tpu_custom_call" | custom-call | flops 134217728 | bytes 5242880 | tf_op jit(solution)/shard_map/back_remote/pallas_call | solution.py:312
  112.8 7.1 %all-to-all-start.1 = ((bf16[64,128,128]{2,1,0:T(8,128)(2,1)}), bf16[64,128,128]{2,1,0:T(8,128)(2,1)S(1)}, u32[]{:S(2)}, u32[]{:S(2)}) async-start(bf16[64,128,128]{2,1,0:T(8,128)(2,1)} %back_remote.1._), calls=%async_computation.1 | async-start | bytes 4194304 | tf_op jit(solution)/shard_map/all_to_all | solution.py:509
  120.0 3.0 %back_local.1.local_ref = f32[64,2048]{1,0:T(8,128)} custom-call(s32[64]{0:T(128)} %reshape.216.cols_ref, bf16[64,2048]{1,0:T(8,128)(2,1)} %get-tuple-element.47.g_ref, bf16[16,8,128,128]{3,2,1,0:T(8,128)(2,1)} %bitcast.29, bf16[64,128,128]{2,1,0:T(8,128)(2,1)} %back_remote.1._), custom_call_target="tpu_custom_call" | custom-call | flops 134217728 | bytes 3145728 | tf_op jit(solution)/shard_map/back_local/pallas_call | solution.py:351
  124.5 2.6 %collective-permute-start.30 = (f32[72,128]{1,0:T(8,128)S(1)}, f32[72,128]{1,0:T(8,128)S(1)}, u32[]{:S(2)}, u32[]{:S(2)}) collective-permute-start(f32[72,128]{1,0:T(8,128)S(1)} %add.112), channel_id=1, source_target_pairs={{0,128},{4,132},{8,136},{12,140},{16,144},{20,148},{24,152},{28,15... | collective-permute-start | bytes 110600 | tf_op jit(solution)/shard_map/ppermute | solution.py:38
  127.1 3.8 %collective-permute-done.30 = f32[72,128]{1,0:T(8,128)S(1)} collective-permute-done((f32[72,128]{1,0:T(8,128)S(1)}, f32[72,128]{1,0:T(8,128)S(1)}, u32[]{:S(2)}, u32[]{:S(2)}) %collective-permute-start.30) | collective-permute-done | bytes 36896 | tf_op jit(solution)/shard_map/ppermute | solution.py:38
  131.7 4.1 %collective-permute-start.32 = (f32[72,128]{1,0:T(8,128)S(1)}, f32[72,128]{1,0:T(8,128)S(1)}, u32[]{:S(2)}, u32[]{:S(2)}) collective-permute-start(f32[72,128]{1,0:T(8,128)S(1)} %add_add_fusion.1), channel_id=1, source_target_pairs={{0,16},{4,20},{8,24},{12,28},{16,0},{20,4},{24,8},{28,12},{32,48},... | collective-permute-start | bytes 110600 | tf_op jit(solution)/shard_map/ppermute | solution.py:38
  137.3 1.9 %collective-permute-start.34 = (f32[72,128]{1,0:T(8,128)S(1)}, f32[72,128]{1,0:T(8,128)S(1)}, u32[]{:S(2)}, u32[]{:S(2)}) collective-permute-start(f32[72,128]{1,0:T(8,128)S(1)} %add_add_fusion.1), channel_id=1, source_target_pairs={{0,48},{4,52},{8,56},{12,60},{16,32},{20,36},{24,40},{28,44},{32,1... | collective-permute-start | bytes 110600 | tf_op jit(solution)/shard_map/ppermute | solution.py:38
  139.3 32.4 %all-to-all-done.1.recv_ref = bf16[64,128,128]{2,1,0:T(8,128)(2,1)S(1)} async-done(((bf16[64,128,128]{2,1,0:T(8,128)(2,1)}), bf16[64,128,128]{2,1,0:T(8,128)(2,1)S(1)}, u32[]{:S(2)}, u32[]{:S(2)}) %all-to-all-start.1) | async-done | bytes 2097184 | tf_op jit(solution)/shard_map/all_to_all | solution.py:509
  172.7 3.1 %finish.1 = f32[64,2048]{1,0:T(8,128)} custom-call(s32[2]{0:T(128)S(1)} %pad_add_fusion.3.place_ref, s32[8,1,16]{2,1,0:T(1,128)S(1)} %copy-done.2, bf16[64,128,128]{2,1,0:T(8,128)(2,1)S(1)} %all-to-all-done.1.recv_ref, f32[64,2048]{1,0:T(8,128)S(1)} %copy-done), custom_call_target="tpu_custom_call" | custom-call | flops 1048576 | bytes 4194304 | tf_op jit(solution)/shard_map/finish/pallas_call | solution.py:402
  (175 shorter events, 35.7 us)
Async XLA Ops:
  7.2 92.2 %all-gather.2.cloned.1.call-start = ((), (), s32[]{:S(2)}) async-start(), calls=%async_computation.2 | async-start | bytes 1556480 | tf_op jit(solution)/shard_map/all_gather | solution.py:487
  7.2 15.3 %collective-permute-start.4 = (bf16[64,2048]{1,0:T(8,128)(2,1)}, bf16[64,2048]{1,0:T(8,128)(2,1)S(1)}, u32[]{:S(2)}, u32[]{:S(2)}) collective-permute-start(bf16[64,2048]{1,0:T(8,128)(2,1)} %refs_1_.1), channel_id=1, source_target_pairs={{0,56},{4,60},{8,0},{12,4},{16,8},{20,12},{24,16},{28,20},{32,24},... | collective-permute-start | bytes 786440 | tf_op jit(solution)/shard_map/ppermute | solution.py:38
  13.7 8.3 %collective-permute-start.5 = (bf16[64,2048]{1,0:T(8,128)(2,1)}, bf16[64,2048]{1,0:T(8,128)(2,1)S(1)}, u32[]{:S(2)}, u32[]{:S(2)}) collective-permute-start(bf16[64,2048]{1,0:T(8,128)(2,1)} %refs_1_.1), channel_id=1, source_target_pairs={{0,8},{4,12},{8,16},{12,20},{16,24},{20,28},{24,32},{28,36},{32,40... | collective-permute-start | bytes 786440 | tf_op jit(solution)/shard_map/ppermute | solution.py:38
  22.0 7.1 %collective-permute-start.11 = (bf16[64,2048]{1,0:T(8,128)(2,1)S(1)}, bf16[64,2048]{1,0:T(8,128)(2,1)S(1)}, u32[]{:S(2)}, u32[]{:S(2)}) collective-permute-start(bf16[64,2048]{1,0:T(8,128)(2,1)S(1)} %collective-permute-done.5.refs_3_), channel_id=1, source_target_pairs={{0,8},{4,12},{8,16},{12,20},{16,24},{20,28},{24,32},{28,36},{32,40... | collective-permute-start | bytes 786440 | tf_op jit(solution)/shard_map/ppermute | solution.py:38
  22.6 9.6 %collective-permute-start.10 = (bf16[64,2048]{1,0:T(8,128)(2,1)S(1)}, bf16[64,2048]{1,0:T(8,128)(2,1)S(1)}, u32[]{:S(2)}, u32[]{:S(2)}) collective-permute-start(bf16[64,2048]{1,0:T(8,128)(2,1)S(1)} %collective-permute-done.4.refs_2_), channel_id=1, source_target_pairs={{0,56},{4,60},{8,0},{12,4},{16,8},{20,12},{24,16},{28,20},{32,24},... | collective-permute-start | bytes 786440 | tf_op jit(solution)/shard_map/ppermute | solution.py:38
  29.1 10.5 %collective-permute-start.17 = (bf16[64,2048]{1,0:T(8,128)(2,1)S(1)}, bf16[64,2048]{1,0:T(8,128)(2,1)S(1)}, u32[]{:S(2)}, u32[]{:S(2)}) collective-permute-start(bf16[64,2048]{1,0:T(8,128)(2,1)S(1)} %collective-permute-done.11.refs_2_), channel_id=1, source_target_pairs={{0,8},{4,12},{8,16},{12,20},{16,24},{20,28},{24,32},{28,36},{32,40... | collective-permute-start | bytes 786440 | tf_op jit(solution)/shard_map/ppermute | solution.py:38
  29.3 5.9 %collective-permute-start = (s32[4,16]{1,0:T(4,128)S(1)}, s32[4,16]{1,0:T(4,128)S(1)}, u32[]{:S(2)}, u32[]{:S(2)}) collective-permute-start(s32[4,16]{1,0:T(4,128)S(1)} %squeeze.15), channel_id=1, source_target_pairs={{0,4},{4,0},{8,12},{12,8},{16,20},{20,16},{24,28},{28,24},{32,36},... | collective-permute-start | bytes 776 | tf_op jit(solution)/shard_map/ppermute | solution.py:38
  32.2 16.7 %collective-permute-start.16 = (bf16[64,2048]{1,0:T(8,128)(2,1)S(1)}, bf16[64,2048]{1,0:T(8,128)(2,1)S(1)}, u32[]{:S(2)}, u32[]{:S(2)}) collective-permute-start(bf16[64,2048]{1,0:T(8,128)(2,1)S(1)} %collective-permute-done.10.refs_1_), channel_id=1, source_target_pairs={{0,56},{4,60},{8,0},{12,4},{16,8},{20,12},{24,16},{28,20},{32,24},... | collective-permute-start | bytes 786440 | tf_op jit(solution)/shard_map/ppermute | solution.py:38
  35.2 4.6 %collective-permute-start.3 = (s32[2,16]{1,0:T(2,128)S(1)}, s32[2,16]{1,0:T(2,128)S(1)}, u32[]{:S(2)}, u32[]{:S(2)}) collective-permute-start(s32[2,16]{1,0:T(2,128)S(1)} %bitcast.36), channel_id=1, source_target_pairs={{0,64},{4,68},{8,72},{12,76},{16,80},{20,84},{24,88},{28,92},{32,9... | collective-permute-start | bytes 392 | tf_op jit(solution)/shard_map/ppermute | solution.py:38
  39.6 11.9 %collective-permute-start.18 = (bf16[32,2048]{1,0:T(8,128)(2,1)S(1)}, bf16[32,2048]{1,0:T(8,128)(2,1)S(1)}, u32[]{:S(2)}, u32[]{:S(2)}) collective-permute-start(bf16[32,2048]{1,0:T(8,128)(2,1)S(1)} %slice.132), channel_id=1, source_target_pairs={{0,8},{4,12},{8,16},{12,20},{16,24},{20,28},{24,32},{28,36},{32,40... | collective-permute-start | bytes 393224 | tf_op jit(solution)/shard_map/ppermute | solution.py:38
  44.9 14.2 %collective-permute-start.6 = (bf16[2,6,64,128]{3,2,1,0:T(8,128)(2,1)}, bf16[2,6,64,128]{3,2,1,0:T(8,128)(2,1)S(1)}, u32[]{:S(2)}, u32[]{:S(2)}) collective-permute-start(bf16[2,6,64,128]{3,2,1,0:T(8,128)(2,1)} %get-tuple-element.33), channel_id=1, source_target_pairs={{0,64},{4,68},{8,72},{12,76},{16,80},{20,84},{24,88},{28,92},{32,9... | collective-permute-start | bytes 589832 | tf_op jit(solution)/shard_map/ppermute | solution.py:38
  45.2 16.1 %collective-permute-start.7 = (bf16[2,6,64,128]{3,2,1,0:T(8,128)(2,1)}, bf16[2,6,64,128]{3,2,1,0:T(8,128)(2,1)S(1)}, u32[]{:S(2)}, u32[]{:S(2)}) collective-permute-start(bf16[2,6,64,128]{3,2,1,0:T(8,128)(2,1)} %get-tuple-element.34), channel_id=1, source_target_pairs={{0,128},{4,132},{8,136},{12,140},{16,144},{20,148},{24,152},{28,15... | collective-permute-start | bytes 589832 | tf_op jit(solution)/shard_map/ppermute | solution.py:38
  47.4 14.0 %collective-permute-start.8 = (bf16[2,6,64,128]{3,2,1,0:T(8,128)(2,1)}, bf16[2,6,64,128]{3,2,1,0:T(8,128)(2,1)S(1)}, u32[]{:S(2)}, u32[]{:S(2)}) collective-permute-start(bf16[2,6,64,128]{3,2,1,0:T(8,128)(2,1)} %get-tuple-element.35), channel_id=1, source_target_pairs={{0,192},{4,196},{8,200},{12,204},{16,208},{20,212},{24,216},{28,22... | collective-permute-start | bytes 589832 | tf_op jit(solution)/shard_map/ppermute | solution.py:38
  48.9 6.7 %collective-permute-start.19 = (bf16[32,2048]{1,0:T(8,128)(2,1)S(1)}, bf16[32,2048]{1,0:T(8,128)(2,1)S(1)}, u32[]{:S(2)}, u32[]{:S(2)}) collective-permute-start(bf16[32,2048]{1,0:T(8,128)(2,1)S(1)} %slice.133), channel_id=1, source_target_pairs={{0,56},{4,60},{8,0},{12,4},{16,8},{20,12},{24,16},{28,20},{32,24},... | collective-permute-start | bytes 393224 | tf_op jit(solution)/shard_map/ppermute | solution.py:38
  51.6 11.6 %collective-permute-start.12 = (bf16[2,4,64,128]{3,2,1,0:T(8,128)(2,1)}, bf16[2,4,64,128]{3,2,1,0:T(8,128)(2,1)S(1)}, u32[]{:S(2)}, u32[]{:S(2)}) collective-permute-start(bf16[2,4,64,128]{3,2,1,0:T(8,128)(2,1)} %get-tuple-element.37), channel_id=1, source_target_pairs={{0,64},{4,68},{8,72},{12,76},{16,80},{20,84},{24,88},{28,92},{32,9... | collective-permute-start | bytes 393224 | tf_op jit(solution)/shard_map/ppermute | solution.py:38
  55.6 9.7 %collective-permute-start.13 = (bf16[2,4,64,128]{3,2,1,0:T(8,128)(2,1)S(1)}, bf16[2,4,64,128]{3,2,1,0:T(8,128)(2,1)S(1)}, u32[]{:S(2)}, u32[]{:S(2)}) collective-permute-start(bf16[2,4,64,128]{3,2,1,0:T(8,128)(2,1)S(1)} %copy-done.32), channel_id=1, source_target_pairs={{0,128},{4,132},{8,136},{12,140},{16,144},{20,148},{24,152},{28,15... | collective-permute-start | bytes 393224 | tf_op jit(solution)/shard_map/ppermute | solution.py:38
  59.1 10.8 %collective-permute-start.14 = (bf16[2,4,64,128]{3,2,1,0:T(8,128)(2,1)S(1)}, bf16[2,4,64,128]{3,2,1,0:T(8,128)(2,1)S(1)}, u32[]{:S(2)}, u32[]{:S(2)}) collective-permute-start(bf16[2,4,64,128]{3,2,1,0:T(8,128)(2,1)S(1)} %copy-done.31), channel_id=1, source_target_pairs={{0,192},{4,196},{8,200},{12,204},{16,208},{20,212},{24,216},{28,22... | collective-permute-start | bytes 393224 | tf_op jit(solution)/shard_map/ppermute | solution.py:38
  61.2 8.7 %collective-permute-start.20 = (bf16[2,6,64,128]{3,2,1,0:T(8,128)(2,1)}, bf16[2,6,64,128]{3,2,1,0:T(8,128)(2,1)S(1)}, u32[]{:S(2)}, u32[]{:S(2)}) collective-permute-start(bf16[2,6,64,128]{3,2,1,0:T(8,128)(2,1)} %get-tuple-element.41), channel_id=1, source_target_pairs={{0,64},{4,68},{8,72},{12,76},{16,80},{20,84},{24,88},{28,92},{32,9... | collective-permute-start | bytes 589832 | tf_op jit(solution)/shard_map/ppermute | solution.py:38
  61.4 8.8 %collective-permute-start.21 = (bf16[2,6,64,128]{3,2,1,0:T(8,128)(2,1)}, bf16[2,6,64,128]{3,2,1,0:T(8,128)(2,1)S(1)}, u32[]{:S(2)}, u32[]{:S(2)}) collective-permute-start(bf16[2,6,64,128]{3,2,1,0:T(8,128)(2,1)} %get-tuple-element.42), channel_id=1, source_target_pairs={{0,128},{4,132},{8,136},{12,140},{16,144},{20,148},{24,152},{28,15... | collective-permute-start | bytes 589832 | tf_op jit(solution)/shard_map/ppermute | solution.py:38
  63.2 10.6 %collective-permute-start.22 = (bf16[2,6,64,128]{3,2,1,0:T(8,128)(2,1)}, bf16[2,6,64,128]{3,2,1,0:T(8,128)(2,1)S(1)}, u32[]{:S(2)}, u32[]{:S(2)}) collective-permute-start(bf16[2,6,64,128]{3,2,1,0:T(8,128)(2,1)} %get-tuple-element.43), channel_id=1, source_target_pairs={{0,192},{4,196},{8,200},{12,204},{16,208},{20,212},{24,216},{28,22... | collective-permute-start | bytes 589832 | tf_op jit(solution)/shard_map/ppermute | solution.py:38
  65.3 13.3 %collective-permute-start.9 = (bf16[4,6,64,128]{3,2,1,0:T(8,128)(2,1)S(1)}, bf16[4,6,64,128]{3,2,1,0:T(8,128)(2,1)S(1)}, u32[]{:S(2)}, u32[]{:S(2)}) collective-permute-start(bf16[4,6,64,128]{3,2,1,0:T(8,128)(2,1)S(1)} %pad_maximum_fusion), channel_id=1, source_target_pairs={{0,4},{4,0},{8,12},{12,8},{16,20},{20,16},{24,28},{28,24},{32,36},... | collective-permute-start | bytes 1179656 | tf_op jit(solution)/shard_map/ppermute | solution.py:38
  73.8 5.2 %collective-permute-start.23 = (bf16[4,6,64,128]{3,2,1,0:T(8,128)(2,1)S(1)}, bf16[4,6,64,128]{3,2,1,0:T(8,128)(2,1)S(1)}, u32[]{:S(2)}, u32[]{:S(2)}) collective-permute-start(bf16[4,6,64,128]{3,2,1,0:T(8,128)(2,1)S(1)} %pad_maximum_fusion.1), channel_id=1, source_target_pairs={{0,4},{4,0},{8,12},{12,8},{16,20},{20,16},{24,28},{28,24},{32,36},... | collective-permute-start | bytes 1179656 | tf_op jit(solution)/shard_map/ppermute | solution.py:38
  83.9 13.9 %collective-permute-start.24 = (bf16[64,2048]{1,0:T(8,128)(2,1)}, bf16[64,2048]{1,0:T(8,128)(2,1)S(1)}, u32[]{:S(2)}, u32[]{:S(2)}) collective-permute-start(bf16[64,2048]{1,0:T(8,128)(2,1)} %get-tuple-element.45.own_ref), channel_id=1, source_target_pairs={{0,1},{1,2},{2,3},{3,0},{4,5},{5,6},{6,7},{7,4},{8,9},{9,10},{10,1... | collective-permute-start | bytes 786440 | tf_op jit(solution)/shard_map/ppermute | solution.py:496
  85.1 12.7 %collective-permute-start.25 = (bf16[64,2048]{1,0:T(8,128)(2,1)}, bf16[64,2048]{1,0:T(8,128)(2,1)S(1)}, u32[]{:S(2)}, u32[]{:S(2)}) collective-permute-start(bf16[64,2048]{1,0:T(8,128)(2,1)} %get-tuple-element.45.own_ref), channel_id=1, source_target_pairs={{0,3},{1,0},{2,1},{3,2},{4,7},{5,4},{6,5},{7,6},{8,11},{9,8},{10,9... | collective-permute-start | bytes 786440 | tf_op jit(solution)/shard_map/ppermute | solution.py:496
  86.6 12.7 %collective-permute-start.26 = (bf16[64,2048]{1,0:T(8,128)(2,1)}, bf16[64,2048]{1,0:T(8,128)(2,1)S(1)}, u32[]{:S(2)}, u32[]{:S(2)}) collective-permute-start(bf16[64,2048]{1,0:T(8,128)(2,1)} %get-tuple-element.45.own_ref), channel_id=1, source_target_pairs={{0,2},{1,3},{2,0},{3,1},{4,6},{5,7},{6,4},{7,5},{8,10},{9,11},{10,... | collective-permute-start | bytes 786440 | tf_op jit(solution)/shard_map/ppermute | solution.py:496
  88.1 9.7 %all-to-all-start = ((s32[8,1,16]{2,1,0:T(1,128)}), s32[8,1,16]{2,1,0:T(1,128)S(1)}, u32[]{:S(2)}, u32[]{:S(2)}) async-start(s32[8,1,16]{2,1,0:T(1,128)} %get-tuple-element.44), calls=%async_computation | async-start | bytes 8192 | tf_op jit(solution)/shard_map/all_to_all | solution.py:500
  112.8 58.8 %all-to-all-start.1 = ((bf16[64,128,128]{2,1,0:T(8,128)(2,1)}), bf16[64,128,128]{2,1,0:T(8,128)(2,1)S(1)}, u32[]{:S(2)}, u32[]{:S(2)}) async-start(bf16[64,128,128]{2,1,0:T(8,128)(2,1)} %back_remote.1._), calls=%async_computation.1 | async-start | bytes 4194304 | tf_op jit(solution)/shard_map/all_to_all | solution.py:509
  124.5 6.4 %collective-permute-start.30 = (f32[72,128]{1,0:T(8,128)S(1)}, f32[72,128]{1,0:T(8,128)S(1)}, u32[]{:S(2)}, u32[]{:S(2)}) collective-permute-start(f32[72,128]{1,0:T(8,128)S(1)} %add.112), channel_id=1, source_target_pairs={{0,128},{4,132},{8,136},{12,140},{16,144},{20,148},{24,152},{28,15... | collective-permute-start | bytes 110600 | tf_op jit(solution)/shard_map/ppermute | solution.py:38
  127.1 4.6 %collective-permute-start.31 = (f32[72,128]{1,0:T(8,128)S(1)}, f32[72,128]{1,0:T(8,128)S(1)}, u32[]{:S(2)}, u32[]{:S(2)}) collective-permute-start(f32[72,128]{1,0:T(8,128)S(1)} %add.112), channel_id=1, source_target_pairs={{0,192},{4,196},{8,200},{12,204},{16,208},{20,212},{24,216},{28,22... | collective-permute-start | bytes 110600 | tf_op jit(solution)/shard_map/ppermute | solution.py:38
  131.7 44.1 %collective-permute-start.32 = (f32[72,128]{1,0:T(8,128)S(1)}, f32[72,128]{1,0:T(8,128)S(1)}, u32[]{:S(2)}, u32[]{:S(2)}) collective-permute-start(f32[72,128]{1,0:T(8,128)S(1)} %add_add_fusion.1), channel_id=1, source_target_pairs={{0,16},{4,20},{8,24},{12,28},{16,0},{20,4},{24,8},{28,12},{32,48},... | collective-permute-start | bytes 110600 | tf_op jit(solution)/shard_map/ppermute | solution.py:38
  135.8 40.0 %collective-permute-start.33 = (f32[72,128]{1,0:T(8,128)S(1)}, f32[72,128]{1,0:T(8,128)S(1)}, u32[]{:S(2)}, u32[]{:S(2)}) collective-permute-start(f32[72,128]{1,0:T(8,128)S(1)} %add_add_fusion.1), channel_id=1, source_target_pairs={{0,32},{4,36},{8,40},{12,44},{16,48},{20,52},{24,56},{28,60},{32,0... | collective-permute-start | bytes 110600 | tf_op jit(solution)/shard_map/ppermute | solution.py:38
  137.3 38.6 %collective-permute-start.34 = (f32[72,128]{1,0:T(8,128)S(1)}, f32[72,128]{1,0:T(8,128)S(1)}, u32[]{:S(2)}, u32[]{:S(2)}) collective-permute-start(f32[72,128]{1,0:T(8,128)S(1)} %add_add_fusion.1), channel_id=1, source_target_pairs={{0,48},{4,52},{8,56},{12,60},{16,32},{20,36},{24,40},{28,44},{32,1... | collective-permute-start | bytes 110600 | tf_op jit(solution)/shard_map/ppermute | solution.py:38
  (40 other events, 377.2 us)
Sparse Core Ops, SparseCore 0:
  16.3 25.5 all-gather.1
